TPU v7x, 32 devices: a whole 2x2x4 slice. The times are simulated.
32 devices in a mesh: clips: 2 (over x), frames: 8 (over z, y), heads: 2 (over core).
Axes of the slice: x: 2, y: 2, z: 4, core: 2. Of those that a mesh axis runs over, the one named last changes fastest.
Arguments:
- tokens: bfloat16 [16, 16, 56, 576], P(('clips', 'frames'), None, None, 'heads'), parts along dimension 0, may hold values from -6 to 6
- out_grad: bfloat16 [16, 16, 56, 576], P(('clips', 'frames'), None, None, 'heads'), parts along dimension 0, may hold values from -6 to 6
- w_qkv: bfloat16 [3, 576, 576], P(None, None, 'heads'), may hold values from -0.25 to 0.25
- pool_kernel: float32 [2, 27, 576], P(None, None, 'heads'), may hold values from -1.25 to 1.25
Outputs:
- input_grad: bfloat16 [16, 16, 56, 576], P(('clips', 'frames'), None, None, 'heads'), parts along dimension 0
- weight_grad: float32 [6, 576, 576], P('clips', 'frames', 'heads'), parts along dimension 0
- kernel_grad: float32 [4, 27, 576], P('clips', None, 'heads'), parts along dimension 0
There are 2 independent parts, one for each index of `clips`. A program takes and returns all parts, laid end to end along the dimension named above; an argument that names none is the same for every part. Nothing has to cross between parts.
All inputs are finite; a program needn't handle non-finite values.
Results may differ from a plain program's by a relative error of at most 0.023.
Values may be sent and summed in bfloat16 or wider, within the bound.
No kernel may reach another device: no remote copies, remote signals or barrier semaphores. Data moves between devices by JAX's collectives and lax.ppermute only.
A program may use at most 64 MiB of HBM per device.

v0:
```python
import jax
import jax.numpy as jnp
from jax import lax
from jax.sharding import PartitionSpec as P

HEADS = 8


def as_sent(array):

    def short(part):
        return part.astype(jnp.bfloat16) if part.dtype == jnp.float32 else part

    return jax.tree.map(short, array)


def from_behind(value, axis, steps):
    count = lax.axis_size(axis)
    leading, last = (max(0, -steps), min(count, count - steps))
    return lax.ppermute(value, axis, [(source, source + steps) for source in range(leading, last)])


def with_halo(array, sides, width):
    for axis, dim in sides:
        count, length = (lax.axis_size(axis), array.shape[dim])
        up = [(i, (i + 1) % count) for i in range(count - 1)]
        down = [(j, i) for i, j in up]
        last = lax.slice_in_dim(array, length - width, length, axis=dim)
        leading = lax.slice_in_dim(array, 0, width, axis=dim)
        before = lax.ppermute(last, axis, up)
        after = lax.ppermute(leading, axis, down)
        array = jnp.concatenate([before, array, after], axis=dim)
    return array


def spatial_pool(frame, kernel_nine):
    channels = frame.shape[-1]
    taps = kernel_nine.reshape(3, 3, 1, channels)
    pooled = lax.conv_general_dilated(
        frame[None],
        taps,
        (4, 4),
        ((1, 1), (1, 1)),
        dimension_numbers=("NHWC", "HWIO", "NHWC"),
        feature_group_count=channels,
        precision=lax.Precision.HIGHEST,
    )
    return pooled[0]


def head_backward(scale):

    def run_head(item):
        query_head, grad_head, key_head, value_head = item
        scores = (
            jnp.einsum("qd,kd->qk", query_head, key_head, preferred_element_type=jnp.float32)
            * scale
        )
        raised = jnp.exp(scores)
        probs = raised / jnp.sum(raised, axis=-1, keepdims=True)
        probs_low = probs.astype(jnp.bfloat16)
        prob_grad = jnp.einsum(
            "qd,kd->qk", grad_head, value_head, preferred_element_type=jnp.float32
        )
        centre = jnp.sum(probs * prob_grad, axis=-1, keepdims=True)
        score_grad = (probs * (prob_grad - centre) * scale).astype(jnp.bfloat16)
        query_grad = (
            grad_head.astype(jnp.float32)
            + jnp.dot(score_grad, key_head, preferred_element_type=jnp.float32)
        ).astype(jnp.bfloat16)
        key_grad = jnp.einsum(
            "qk,qd->kd", score_grad, query_head, preferred_element_type=jnp.float32
        )
        value_grad = jnp.einsum(
            "qk,qd->kd", probs_low, grad_head, preferred_element_type=jnp.float32
        )
        return (query_grad, key_grad, value_grad)

    return run_head


def shards(tokens, out_grad, w_qkv, pool_kernel):
    local = tokens.shape[-1]
    heads_here = HEADS // lax.axis_size("heads")
    head_dim = local // heads_here
    scale = head_dim ** (-0.5)
    row_count = tokens.shape[1]
    col_count = tokens.shape[2]
    pooled_rows = row_count // 4
    pooled_cols = col_count // 4
    token_count = row_count * col_count
    whole = lax.all_gather(tokens, "heads", axis=3, tiled=True)
    flat = whole.reshape(token_count, -1)
    queries = jnp.dot(flat, w_qkv[0], preferred_element_type=jnp.float32).astype(jnp.bfloat16)
    key_proj = jnp.dot(flat, w_qkv[1], preferred_element_type=jnp.float32).astype(jnp.bfloat16)
    value_proj = jnp.dot(flat, w_qkv[2], preferred_element_type=jnp.float32).astype(jnp.bfloat16)
    own_frame = jnp.concatenate([key_proj, value_proj], axis=1).reshape(
        row_count, col_count, 2 * local
    )
    own_wide = own_frame.astype(jnp.float32)
    kernel_both = jnp.concatenate([pool_kernel[0], pool_kernel[1]], axis=1)
    earlier = spatial_pool(own_wide, kernel_both[0:9])
    middle = spatial_pool(own_wide, kernel_both[9:18])
    later = spatial_pool(own_wide, kernel_both[18:27])
    pooled = (
        from_behind(as_sent(earlier), "frames", 1).astype(earlier.dtype)
        + middle
        + from_behind(later, "frames", -1)
    )
    pooled_low = pooled.astype(jnp.bfloat16).reshape(pooled_rows * pooled_cols, 2 * local)
    all_keys = lax.all_gather(pooled_low, "frames", axis=0, tiled=True)
    key_count = all_keys.shape[0]
    key_heads = all_keys[:, :local].reshape(key_count, heads_here, head_dim).transpose(1, 0, 2)
    value_heads = all_keys[:, local:].reshape(key_count, heads_here, head_dim).transpose(1, 0, 2)
    query_heads = queries.reshape(token_count, heads_here, head_dim).transpose(1, 0, 2)
    grad_heads = out_grad.reshape(token_count, heads_here, head_dim).transpose(1, 0, 2)
    query_parts, key_parts, value_parts = lax.map(
        head_backward(scale), (query_heads, grad_heads, key_heads, value_heads)
    )
    query_back = query_parts.transpose(1, 0, 2).reshape(token_count, local)
    key_terms = jnp.concatenate(
        [
            key_parts.transpose(1, 0, 2).reshape(key_count, local),
            value_parts.transpose(1, 0, 2).reshape(key_count, local),
        ],
        axis=1,
    )
    owned = lax.psum_scatter(
        key_terms.astype(jnp.bfloat16), "frames", scatter_dimension=0, tiled=True
    ).astype(jnp.float32)
    window_grad = with_halo(
        owned.reshape(1, pooled_rows, pooled_cols, 2 * local).astype(jnp.bfloat16),
        (("frames", 0),),
        1,
    ).astype(jnp.float32)
    frame_grad = jnp.zeros((row_count, col_count, 2 * local), jnp.float32)
    kernel_parts = []
    for offset in range(3):
        unused, pull_back = jax.vjp(
            spatial_pool, own_wide, kernel_both[9 * offset : 9 * offset + 9]
        )
        part_frame, part_kernel = pull_back(window_grad[2 - offset])
        frame_grad = frame_grad + part_frame
        kernel_parts.append(part_kernel)
    kernel_local = jnp.concatenate(kernel_parts, axis=0)
    kernel_grad = lax.psum(
        jnp.stack([kernel_local[:, :local], kernel_local[:, local:]]).astype(jnp.bfloat16), "frames"
    ).astype(jnp.float32)
    back_low = frame_grad.astype(jnp.bfloat16).reshape(token_count, 2 * local)
    grads = jnp.stack([query_back, back_low[:, :local], back_low[:, local:]])
    weight_part = lax.psum_scatter(
        jnp.einsum("tc,itd->cid", flat, grads, preferred_element_type=jnp.float32).astype(
            jnp.bfloat16
        ),
        "frames",
        scatter_dimension=0,
        tiled=True,
    ).astype(jnp.float32)
    weight_grad = weight_part.transpose(1, 0, 2)
    summed = lax.psum_scatter(
        jnp.einsum("icd,itd->ct", w_qkv, grads, preferred_element_type=jnp.float32).astype(
            jnp.bfloat16
        ),
        "heads",
        scatter_dimension=0,
        tiled=True,
    ).astype(jnp.float32)
    input_grad = summed.T.astype(jnp.bfloat16).reshape(tokens.shape)
    return (input_grad, weight_grad, kernel_grad)


def solution(mesh):
    in_specs = (
        P(("clips", "frames"), None, None, "heads"),
        P(("clips", "frames"), None, None, "heads"),
        P(None, None, "heads"),
        P(None, None, "heads"),
    )
    out_specs = (
        P(("clips", "frames"), None, None, "heads"),
        P("clips", "frames", "heads"),
        P("clips", None, "heads"),
    )
    return jax.shard_map(shards, mesh=mesh, in_specs=in_specs, out_specs=out_specs, check_vma=False)
```

profile of v0, /device:TPU:0, one launch (start us, length us, event | category | flops | bytes accessed | tf_op | source)
XLA Modules:
  0.0 278.9 jit_solution(3454214540168406668)
XLA Ops:
  7.2 1.9 copy.85
  9.1 3.6 %all_gather.6 = bf16[1,16,56,576]{2,1,0,3:T(8,128)(2,1)S(1)} all-gather(bf16[1,16,56,288]{2,1,0,3:T(8,128)(2,1)S(1)} %copy.85), channel_id=1, replica_groups=mesh['clips'=2,'frames'=8,'heads'=2] {'heads'}, dimensions={3}, use_global_device_ids=true | all-gather | bytes 1548288 | tf_op jit(solution)/shard_map/all_gather | solution.py:92
  12.7 3.0 %copy.86 = bf16[1,16,56,576]{3,2,1,0:T(8,128)(2,1)S(1)} copy(bf16[1,16,56,576]{2,1,0,3:T(8,128)(2,1)S(1)} %all_gather.6) | data formatting | bytes 2064384 | tf_op jit(solution)/shard_map/all_gather | solution.py:92
  15.7 1.9 convolution_convert_fusion.1
  17.6 1.7 convolution_convert_fusion.2
  20.8 1.1 copy.88
  24.0 4.8 %collective-permute-start = (bf16[4,14,576]{2,0,1:T(4,128)(2,1)}, bf16[4,14,576]{2,0,1:T(4,128)(2,1)S(1)}, u32[]{:S(2)}, u32[]{:S(2)}) collective-permute-start(bf16[4,14,576]{2,0,1:T(4,128)(2,1)} %slice_bitcast_fusion.2), channel_id=1, source_target_pairs={{0,2},{2,4},{4,6},{6,8},{8,10},{10,12},{12,14},{1,3},{3,5},{5,7},{... | collective-permute-start | bytes 193544 | tf_op jit(solution)/shard_map/ppermute | solution.py:20
  28.8 4.7 %convolution_select_fusion = f32[4,8,2,576]{3,1,2,0:T(8,128)S(1)} fusion(f32[3,3,1,576]{3,2,1,0:T(1,128)S(1)} %reshape.96, pred[8,2]{0,1:T(4,128)(4,1)S(1)} %copy-done.17, bf16[16,1,7,2,576]{4,2,3,0,1:T(8,128)(2,1)S(1)} %slice.70, bf16[16,1,8,8,576]{4,2,3,0,1:T(8,128)(2,1)S(1)} %copy.90), kind=kOutput, calls=%fused_computation.54 | convolution fusion | flops 8110080 | bytes 1605904 | tf_op jit(solution)/shard_map/conv_general_dilated | solution.py:39
  34.3 1.3 collective-permute-start.1
  35.6 2.4 convolution_convert_fusion.3
  38.9 2.4 reshape.91
  41.2 1.1 copy.99
  42.7 1.0 copy.94
  44.4 1.0 fusion.55
  45.5 34.1 %all_gather.7 = bf16[448,576]{1,0:T(8,128)(2,1)S(1)} all-gather(bf16[56,576]{1,0:T(8,128)(2,1)S(1)} %reshape.97), channel_id=1, replica_groups=mesh['clips'=2,'frames'=8,'heads'=2] {'frames'}, dimensions={0}, use_global_device_ids=true | all-gather | bytes 580608 | tf_op jit(solution)/shard_map/all_gather | solution.py:111
  79.5 0.9 fusion.65
  80.4 1.8 copy.98
  82.4 20.5 %while.14 = (s32[]{:T(128)}, bf16[4,896,72]{1,2,0:T(8,128)(2,1)}, bf16[4,448,72]{1,2,0:T(8,128)(2,1)}, bf16[4,448,72]{1,2,0:T(8,128)(2,1)}, bf16[4,896,72]{1,2,0...) while((s32[]{:T(128)}, bf16[4,896,72]{1,2,0:T(8,128)(2,1)}, ...), condition=%wide.region_3.4_spmd, body=%wide.region_0.3_spmd.sunk | while | flops 294022400 | bytes 17689812 | solution.py:117
  83.9 1.4 multiply_reduce_fusion.2
  86.7 0.9 fusion.105
  89.0 1.4 multiply_reduce_fusion.2
  91.8 0.9 fusion.105
  94.1 1.4 multiply_reduce_fusion.2
  96.9 0.9 fusion.105
  99.2 1.4 multiply_reduce_fusion.2
  102.1 0.9 fusion.105
  103.0 1.1 pad_maximum_fusion.4
  104.1 1.1 copy.102
  105.3 56.0 %reduce-scatter.8.cloned.1.call-done = bf16[56,576]{1,0:T(8,128)(2,1)} async-done(((bf16[448,576]{1,0:T(8,128)(2,1)}), bf16[56,576]{1,0:T(8,128)(2,1)}) %reduce-scatter.8.cloned.1.call-update) | async-done | bytes 64528
  161.3 0.9 convert_element_type.94
  162.3 3.0 %collective-permute-start.3 = (bf16[1,4,14,576]{3,0,2,1:T(2,128)(2,1)S(1)}, bf16[1,4,14,576]{3,0,2,1:T(2,128)(2,1)S(1)}, u32[]{:S(2)}, u32[]{:S(2)}) collective-permute-start(bf16[1,4,14,576]{3,0,2,1:T(2,128)(2,1)S(1)} %convert_element_type.94), channel_id=1, source_target_pairs={{0,2},{2,4},{4,6},{6,8},{8,10},{10,12},{12,14},{1,3},{3,5},{5,7},{... | collective-permute-start | bytes 193544 | tf_op jit(solution)/shard_map/ppermute | solution.py:30
  165.3 1.5 collective-permute-start.2
  166.8 1.3 fusion.67
  168.1 1.3 collective-permute-done.3
  169.4 1.3 fusion.68
  170.7 1.6 collective-permute-done.2
  172.3 2.7 add_convert_fusion
  176.1 4.0 %fusion.29 = bf16[576,3,288]{0,2,1:T(8,128)(2,1)} fusion(bf16[896,576,1]{1,0,2:T(8,128)(2,1)} %bitcast.179, bf16[1,896,288]{1,2,0:T(8,128)(2,1)S(1)} %bitcast.187, bf16[1,896,288]{1,2,0:T(8,128)(2,1)S(1)} %bitcast.185, bf16[1,896,288]{1,2,0:T(8,128)(2,1)} %bitcast.194), kind=kOutput, calls=%fused_computation.42 | convolution fusion | flops 893859840 | bytes 3575808 | tf_op jit(solution)/shard_map/tc,itd->cid/dot_general | solution.py:152
  180.2 3.6 %fusion.30 = bf16[576,896]{1,0:T(8,128)(2,1)} fusion(bf16[3,576,288]{1,2,0:T(8,128)(2,1)} %param.8, bf16[1,896,288]{1,2,0:T(8,128)(2,1)S(1)} %bitcast.188, bf16[1,896,288]{1,2,0:T(8,128)(2,1)S(1)} %bitcast.186, bf16[1,896,288]{1,2,0:T(8,128)(2,1)S(1)} %bitcast.195), kind=kOutput, calls=%fused_computation.43 | convolution fusion | flops 893878272 | bytes 3575808 | tf_op jit(solution)/shard_map/icd,itd->ct/dot_general | solution.py:161
  185.1 1.9 fusion.41
  187.1 1.9 fusion.44
  189.0 1.9 fusion.38
  191.1 35.8 %psum.7 = bf16[2,27,288]{2,1,0:T(8,128)(2,1)S(1)} all-reduce(bf16[2,27,288]{2,1,0:T(8,128)(2,1)S(1)} %pad_maximum_fusion.5), channel_id=1, replica_groups=mesh['clips'=2,'frames'=8,'heads'=2] {'frames'}, use_global_device_ids=true, to_apply=%region_7.8 | all-reduce | flops 15552 | bytes 62208 | tf_op jit(solution)/shard_map/psum | solution.py:146
  227.6 32.2 %all-reduce.4.cloned.1.call-done = bf16[576,3,288]{0,2,1:T(8,128)(2,1)} async-done(((bf16[576,3,288]{0,2,1:T(8,128)(2,1)}), bf16[576,3,288]{0,2,1:T(8,128)(2,1)}) %all-reduce.4.cloned.1.call-update) | async-done | bytes 995344
  259.8 1.1 convert_bitcast_fusion
  261.0 0.9 copy.115
  261.9 8.3 %reduce-scatter.6.cloned.1.call-done = bf16[288,896]{1,0:T(8,128)(2,1)} async-done(((bf16[576,896]{1,0:T(8,128)(2,1)}), bf16[288,896]{1,0:T(8,128)(2,1)}) %reduce-scatter.6.cloned.1.call-update) | async-done | bytes 516112 | tf_op jit(solution)/shard_map/reduce_scatter | solution.py:160
  270.2 2.2 copy.108
  (122 shorter events, 20.1 us)
Async XLA Ops:
  7.2 154.2 %reduce-scatter.8.cloned.1.call-start = ((), (), s32[]{:S(2)}) async-start(), calls=%async_computation.4 | async-start | bytes 645120
  15.7 4.4 %copy-start = (bf16[1,16,56,576]{3,2,1,0:T(8,128)(2,1)}, bf16[1,16,56,576]{3,2,1,0:T(8,128)(2,1)S(1)}, u32[]{:S(2)}) copy-start(bf16[1,16,56,576]{3,2,1,0:T(8,128)(2,1)S(1)} %copy.86) | copy-start | bytes 3096580
  17.6 1.7 copy-start.10
  20.1 0.6 copy-start.4
  22.4 0.7 copy-start.12
  22.4 0.7 copy-start.17
  23.1 5.7 %copy-start.3 = (f32[9,576]{1,0:T(8,128)S(1)}, f32[9,576]{1,0:T(8,128)}, u32[]{:S(2)}) copy-start(f32[9,576]{1,0:T(8,128)} %get-tuple-element.111) | copy-start | bytes 62212
  24.0 19.8 %collective-permute-start = (bf16[4,14,576]{2,0,1:T(4,128)(2,1)}, bf16[4,14,576]{2,0,1:T(4,128)(2,1)S(1)}, u32[]{:S(2)}, u32[]{:S(2)}) collective-permute-start(bf16[4,14,576]{2,0,1:T(4,128)(2,1)} %slice_bitcast_fusion.2), channel_id=1, source_target_pairs={{0,2},{2,4},{4,6},{6,8},{8,10},{10,12},{12,14},{1,3},{3,5},{5,7},{... | collective-permute-start | bytes 193544 | tf_op jit(solution)/shard_map/ppermute | solution.py:20
  28.8 6.8 %copy-start.1 = (bf16[1,16,56,576]{3,2,1,0:T(8,128)(2,1)S(1)}, bf16[1,16,56,576]{3,2,1,0:T(8,128)(2,1)}, u32[]{:S(2)}) copy-start(bf16[1,16,56,576]{3,2,1,0:T(8,128)(2,1)} %copy-done) | copy-start | bytes 3096580
  34.3 9.5 %collective-permute-start.1 = (f32[4,14,576]{2,0,1:T(4,128)}, f32[4,14,576]{2,0,1:T(4,128)}, u32[]{:S(2)}, u32[]{:S(2)}) collective-permute-start(f32[4,14,576]{2,0,1:T(4,128)} %slice_bitcast_fusion), channel_id=1, source_target_pairs={{2,0},{4,2},{6,4},{8,6},{10,8},{12,10},{14,12},{3,1},{5,3},{7,5},{... | collective-permute-start | bytes 387080 | tf_op jit(solution)/shard_map/ppermute | solution.py:20
  38.8 3.5 %copy-start.2 = (bf16[896,288]{0,1:T(8,128)(2,1)S(1)}, bf16[896,288]{0,1:T(8,128)(2,1)}, u32[]{:S(2)}) copy-start(bf16[896,288]{0,1:T(8,128)(2,1)} %convolution_convert_fusion.3) | copy-start | bytes 1548292
  43.7 0.6 copy-start.11
  82.5 1.0 copy-start.6
  83.8 1.4 copy-start.7
  85.3 1.0 copy-start.8
  86.6 0.9 copy-start.9
  87.6 1.0 copy-start.6
  89.0 1.4 copy-start.7
  90.4 1.0 copy-start.8
  91.8 0.9 copy-start.9
  92.7 1.0 copy-start.6
  94.1 1.4 copy-start.7
  95.5 1.0 copy-start.8
  96.9 0.9 copy-start.9
  97.8 1.0 copy-start.6
  99.2 1.4 copy-start.7
  100.7 1.0 copy-start.8
  102.0 0.9 copy-start.9
  103.0 2.3 copy-start.5
  105.2 154.6 %all-reduce.4.cloned.1.call-start = ((), (), s32[]{:S(2)}) async-start(), calls=%async_computation.3 | async-start | bytes 2211840
  162.3 7.2 %collective-permute-start.3 = (bf16[1,4,14,576]{3,0,2,1:T(2,128)(2,1)S(1)}, bf16[1,4,14,576]{3,0,2,1:T(2,128)(2,1)S(1)}, u32[]{:S(2)}, u32[]{:S(2)}) collective-permute-start(bf16[1,4,14,576]{3,0,2,1:T(2,128)(2,1)S(1)} %convert_element_type.94), channel_id=1, source_target_pairs={{0,2},{2,4},{4,6},{6,8},{8,10},{10,12},{12,14},{1,3},{3,5},{5,7},{... | collective-permute-start | bytes 193544 | tf_op jit(solution)/shard_map/ppermute | solution.py:30
  165.3 7.0 %collective-permute-start.2 = (bf16[1,4,14,576]{3,0,2,1:T(2,128)(2,1)S(1)}, bf16[1,4,14,576]{3,0,2,1:T(2,128)(2,1)S(1)}, u32[]{:S(2)}, u32[]{:S(2)}) collective-permute-start(bf16[1,4,14,576]{3,0,2,1:T(2,128)(2,1)S(1)} %convert_element_type.94), channel_id=1, source_target_pairs={{2,0},{4,2},{6,4},{8,6},{10,8},{12,10},{14,12},{3,1},{5,3},{7,5},{... | collective-permute-start | bytes 193544 | tf_op jit(solution)/shard_map/ppermute | solution.py:31
  169.4 1.3 copy-start.14
  176.1 4.1 %copy-start.13 = (bf16[4,896,72]{1,2,0:T(8,128)(2,1)S(1)}, bf16[4,896,72]{1,2,0:T(8,128)(2,1)}, u32[]{:S(2)}) copy-start(bf16[4,896,72]{1,2,0:T(8,128)(2,1)} %get-tuple-element.47) | copy-start | bytes 1548292
  180.1 3.7 %copy-start.16 = (u32[32]{0:T(128)S(1)}, u32[32]{0:T(128)}, u32[]{:S(2)}) copy-start(u32[32]{0:T(128)} %constant.58) | copy-start | bytes 388
  180.1 90.0 %reduce-scatter.6.cloned.1.call-start = ((), (), s32[]{:S(2)}) async-start(), calls=%async_computation.2 | async-start | bytes 1548288 | tf_op jit(solution)/shard_map/reduce_scatter | solution.py:160
  185.1 2.0 copy-start.15
Sparse Core Ops, SparseCore 0:
  105.3 55.9 reduce-scatter.7
  180.2 79.5 all-reduce.3
  262.2 7.9 reduce-scatter.5
where the time goes:
time: 280 us; the launch traced here: 279 us
  waiting for transfers between devices  99.4 us (36%)
  blocking collectives  73.5 us (26%)
  matrix products  44.8 us (16%)
  local copies, waits for them, and re-layouts  30.2 us (11%)
  between operations  14.9 us (5%)
  starting transfers between devices  10.7 us (4%)
  other arithmetic  5.16 us (2%)
    unnamed x5, waiting for transfers between devices  88.2 us
    psum x1, blocking collectives, shards(): lax.psum(jnp.stack([kernel_local[:, :local], kernel_local[:, local:]]).as...  35.8 us
    all_gather x1, blocking collectives, shards(): all_keys = lax.all_gather(pooled_low, 'frames', axis=0, tiled=True)  34.1 us
    conv_general_dilated x9, matrix products, spatial_pool(): lax.conv_general_dilated(frame[None], taps, (4, 4), ((1, 1), (1, 1)), dim...  16.8 us
    reduce_scatter x1, waiting for transfers between devices, shards(): lax.psum_scatter(jnp.einsum('icd,itd->ct', w_qkv, grads, preferred_elemen...  8.26 us
    ppermute x2, starting transfers between devices, from_behind(): lax.ppermute(value, axis, [(source, source + steps) for source in range(l...  6.06 us
    unnamed x35, local copies, waits for them, and re-layouts  5.97 us
    dot_general x4, matrix products, run_head(): jnp.einsum('qd,kd->qk', grad_head, value_head, preferred_element_type=jnp...  5.68 us
  transfers between devices with their start and end apart: 7, of which 5 were waited for; matrix products, arithmetic and copies ran while one was open for 10% of the time, Pallas kernels for 0%

commit v1 on v0

--- a/solution.py
+++ b/solution.py
@@ -31,6 +31,54 @@
         after = lax.ppermute(leading, axis, down)
         array = jnp.concatenate([before, array, after], axis=dim)
     return array
+
+
+def frame_pairs(step, flip):
+    count = lax.axis_size("frames")
+    return [(i, i ^ (2 * step + flip)) for i in range(count)]
+
+
+def gather_frames(block):
+    outer = lax.axis_size("frames") // 2
+    same = [block] + [lax.ppermute(block, "frames", frame_pairs(s, 0)) for s in range(1, outer)]
+    other = lax.ppermute(jnp.concatenate(same), "frames", frame_pairs(0, 1))
+    return jnp.concatenate(same + [other])
+
+
+def scatter_frames(terms):
+    outer = lax.axis_size("frames") // 2
+    half = terms.shape[0] // 2
+    moved = lax.ppermute(terms[half:].astype(jnp.bfloat16), "frames", frame_pairs(0, 1))
+    summed = terms[:half].astype(jnp.float32) + moved.astype(jnp.float32)
+    blocks = summed.reshape(outer, half // outer, *terms.shape[1:])
+    low = blocks.astype(jnp.bfloat16)
+    own = blocks[0]
+    for step in range(1, outer):
+        own = own + lax.ppermute(low[step], "frames", frame_pairs(step, 0)).astype(jnp.float32)
+    return own
+
+
+def scatter_weights(terms, kernel_part):
+    count = lax.axis_size("frames")
+    outer = count // 2
+    rows, width = terms.shape[0] // count, terms.shape[1]
+    place = lax.axis_index("frames")
+    low = terms.astype(jnp.bfloat16).reshape(count, rows, width)
+
+    def block(relative):
+        return lax.dynamic_index_in_dim(low, place ^ relative, 0, False)
+
+    extra = kernel_part.reshape(-1, width)
+    away = [block(2 * step + 1) for step in range(outer)] + [extra.astype(jnp.bfloat16)]
+    moved = lax.ppermute(jnp.concatenate(away), "frames", frame_pairs(0, 1)).astype(jnp.float32)
+    here = jnp.concatenate([block(2 * step).astype(jnp.float32) for step in range(outer)] + [extra])
+    summed = here + moved
+    tail = summed[outer * rows :]
+    own = jnp.concatenate([summed[:rows], tail])
+    for step in range(1, outer):
+        piece = jnp.concatenate([summed[step * rows : (step + 1) * rows], tail]).astype(jnp.bfloat16)
+        own = own + lax.ppermute(piece, "frames", frame_pairs(step, 0)).astype(jnp.float32)
+    return own[:rows], own[rows:].reshape(kernel_part.shape)
 
 
 def spatial_pool(frame, kernel_nine):
@@ -108,7 +156,7 @@
         + from_behind(later, "frames", -1)
     )
     pooled_low = pooled.astype(jnp.bfloat16).reshape(pooled_rows * pooled_cols, 2 * local)
-    all_keys = lax.all_gather(pooled_low, "frames", axis=0, tiled=True)
+    all_keys = gather_frames(pooled_low)
     key_count = all_keys.shape[0]
     key_heads = all_keys[:, :local].reshape(key_count, heads_here, head_dim).transpose(1, 0, 2)
     value_heads = all_keys[:, local:].reshape(key_count, heads_here, head_dim).transpose(1, 0, 2)
@@ -125,9 +173,7 @@
         ],
         axis=1,
     )
-    owned = lax.psum_scatter(
-        key_terms.astype(jnp.bfloat16), "frames", scatter_dimension=0, tiled=True
-    ).astype(jnp.float32)
+    owned = scatter_frames(key_terms)
     window_grad = with_halo(
         owned.reshape(1, pooled_rows, pooled_cols, 2 * local).astype(jnp.bfloat16),
         (("frames", 0),),
@@ -143,20 +189,12 @@
         frame_grad = frame_grad + part_frame
         kernel_parts.append(part_kernel)
     kernel_local = jnp.concatenate(kernel_parts, axis=0)
-    kernel_grad = lax.psum(
-        jnp.stack([kernel_local[:, :local], kernel_local[:, local:]]).astype(jnp.bfloat16), "frames"
-    ).astype(jnp.float32)
+    kernel_part = jnp.stack([kernel_local[:, :local], kernel_local[:, local:]])
     back_low = frame_grad.astype(jnp.bfloat16).reshape(token_count, 2 * local)
     grads = jnp.stack([query_back, back_low[:, :local], back_low[:, local:]])
-    weight_part = lax.psum_scatter(
-        jnp.einsum("tc,itd->cid", flat, grads, preferred_element_type=jnp.float32).astype(
-            jnp.bfloat16
-        ),
-        "frames",
-        scatter_dimension=0,
-        tiled=True,
-    ).astype(jnp.float32)
-    weight_grad = weight_part.transpose(1, 0, 2)
+    weight_terms = jnp.einsum("tc,itd->cid", flat, grads, preferred_element_type=jnp.float32)
+    weight_part, kernel_grad = scatter_weights(weight_terms.reshape(-1, 3 * local), kernel_part)
+    weight_grad = weight_part.reshape(-1, 3, local).transpose(1, 0, 2)
     summed = lax.psum_scatter(
         jnp.einsum("icd,itd->ct", w_qkv, grads, preferred_element_type=jnp.float32).astype(
             jnp.bfloat16

time: 280 us -> 187 us (0.67)
  blocking collectives: 73.5 us -> 3.57 us
  waiting for transfers between devices: 99.4 us -> 42.7 us
  starting transfers between devices: 10.7 us -> 31.1 us
  local copies, waits for them, and re-layouts: 30.2 us -> 37.1 us
  matrix products: 44.8 us -> 48.6 us
  other arithmetic: 5.16 us -> 8.38 us
    unnamed x5 -> x1, waiting for transfers between devices: 88.2 us -> 0.02 us
    ppermute x0 -> x12, waiting for transfers between devices: none -> 42.7 us  [the longest x3 13.3 us: scatter_weights(): lax.ppermute(piece, 'frames', frame_pairs(step, 0)).astype(jnp.float32)]
    psum x1 -> x0, blocking collectives: 35.8 us -> none  [shards(): lax.psum(jnp.stack([kernel_local[:, :local], kernel_local[:, local:]]).as...]
    all_gather x1 -> x0, blocking collectives: 34.1 us -> none  [shards(): all_keys = lax.all_gather(pooled_low, 'frames', axis=0, tiled=True)]
    ppermute x0 -> x12, starting transfers between devices: none -> 20.5 us  [the longest x3 6.29 us: scatter_weights(): lax.ppermute(piece, 'frames', frame_pairs(step, 0)).astype(jnp.float32)]
    reduce_scatter x1, waiting for transfers between devices: 8.26 us -> 0.01 us  [shards(): lax.psum_scatter(jnp.einsum('icd,itd->ct', w_qkv, grads, preferred_elemen...]
    while x32 -> x0, local copies, waits for them, and re-layouts: 4.72 us -> none
    dynamic_slice x0 -> x4, local copies, waits for them, and re-layouts: none -> 4.54 us  [block(): return lax.dynamic_index_in_dim(low, place ^ relative, 0, False)]
  transfers between devices with their start and end apart: 7 -> 17, of which waited for: 5 -> 10; matrix products, arithmetic and copies ran while one was open for 10% -> 21% of each run, Pallas kernels for 0% -> 0%
where the time goes in v1:
time: 187 us; the launch traced here: 186 us
  matrix products  48.6 us (26%)
  waiting for transfers between devices  42.7 us (23%)
  local copies, waits for them, and re-layouts  37.1 us (20%)
  starting transfers between devices  31.1 us (17%)
  between operations  14.7 us (8%)
  other arithmetic  8.38 us (4%)
  blocking collectives  3.57 us (2%)
    conv_general_dilated x9, matrix products, spatial_pool(): lax.conv_general_dilated(frame[None], taps, (4, 4), ((1, 1), (1, 1)), dim...  17.1 us
    ppermute x3, waiting for transfers between devices, scatter_weights(): lax.ppermute(piece, 'frames', frame_pairs(step, 0)).astype(jnp.float32)  13.3 us
    unnamed x40, local copies, waits for them, and re-layouts  9.07 us
    ppermute x1, waiting for transfers between devices, gather_frames(): other = lax.ppermute(jnp.concatenate(same), 'frames', frame_pairs(0, 1))  7.17 us
    ppermute x1, waiting for transfers between devices, scatter_frames(): lax.ppermute(terms[half:].astype(jnp.bfloat16), 'frames', frame_pairs(0, 1))  6.76 us
    ppermute x2, starting transfers between devices, from_behind(): lax.ppermute(value, axis, [(source, source + steps) for source in range(l...  6.7 us
    ppermute x3, starting transfers between devices, scatter_weights(): lax.ppermute(piece, 'frames', frame_pairs(step, 0)).astype(jnp.float32)  6.29 us
    ppermute x1, waiting for transfers between devices, scatter_weights(): lax.ppermute(jnp.concatenate(away), 'frames', frame_pairs(0, 1))  5.84 us
  transfers between devices with their start and end apart: 17, of which 10 were waited for; matrix products, arithmetic and copies ran while one was open for 21% of the time, Pallas kernels for 0%

profile of v1, /device:TPU:0, one launch (start us, length us, event | category | flops | bytes accessed | tf_op | source)
XLA Modules:
  0.0 186.3 jit_solution(10176760055856187791)
XLA Ops:
  7.2 1.9 %copy.68 = bf16[1,16,56,288]{2,1,0,3:T(8,128)(2,1)S(1)} copy(bf16[1,16,56,288]{3,2,1,0:T(8,128)(2,1)} %param.6) | data formatting | bytes 1032192 | tf_op args[0]
  9.1 3.6 %all_gather.3 = bf16[1,16,56,576]{2,1,0,3:T(8,128)(2,1)S(1)} all-gather(bf16[1,16,56,288]{2,1,0,3:T(8,128)(2,1)S(1)} %copy.68), channel_id=1, replica_groups=mesh['clips'=2,'frames'=8,'heads'=2] {'heads'}, dimensions={3}, use_global_device_ids=true | all-gather | bytes 1548288 | tf_op jit(solution)/shard_map/all_gather | solution.py:140
  12.7 3.0 %copy.69 = bf16[1,16,56,576]{3,2,1,0:T(8,128)(2,1)S(1)} copy(bf16[1,16,56,576]{2,1,0,3:T(8,128)(2,1)S(1)} %all_gather.3) | data formatting | bytes 2064384 | tf_op jit(solution)/shard_map/all_gather | solution.py:140
  15.7 1.9 %convolution_convert_fusion.1 = bf16[896,288]{0,1:T(8,128)(2,1)S(1)} fusion(bf16[896,576]{1,0:T(8,128)(2,1)S(1)} %bitcast.204, bf16[3,576,288]{1,2,0:T(8,128)(2,1)} %param.8), kind=kOutput, calls=%fused_computation.46 | convolution fusion | flops 297529344 | bytes 1916928 | tf_op jit(solution)/shard_map/dot_general | solution.py:144
  17.6 1.7 convolution_convert_fusion.2
  22.7 5.4 %collective-permute-start = (bf16[4,14,576]{2,0,1:T(4,128)(2,1)}, bf16[4,14,576]{2,0,1:T(4,128)(2,1)}, u32[]{:S(2)}, u32[]{:S(2)}) collective-permute-start(bf16[4,14,576]{2,0,1:T(4,128)(2,1)} %slice_bitcast_fusion.2), channel_id=1, source_target_pairs={{0,2},{2,4},{4,6},{6,8},{8,10},{10,12},{12,14},{1,3},{3,5},{5,7},{... | collective-permute-start | bytes 193544 | tf_op jit(solution)/shard_map/ppermute | solution.py:20
  28.1 4.7 %convolution_select_fusion = f32[4,8,2,576]{3,1,2,0:T(8,128)S(1)} fusion(f32[3,3,1,576]{3,2,1,0:T(1,128)S(1)} %reshape.125, pred[8,2]{0,1:T(4,128)(4,1)S(1)} %copy-done.11, bf16[16,1,7,2,576]{4,2,3,0,1:T(8,128)(2,1)S(1)} %slice.126, bf16[16,1,8,8,576]{4,2,3,0,1:T(8,128)(2,1)S(1)} %copy.73), kind=kOutput, calls=%fused_computation.57 | convolution fusion | flops 8110080 | bytes 1605904 | tf_op jit(solution)/shard_map/conv_general_dilated | solution.py:87
  34.9 2.4 %convolution_convert_fusion.3 = bf16[896,288]{0,1:T(8,128)(2,1)} fusion(bf16[896,576]{1,0:T(8,128)(2,1)S(1)} %bitcast.206, bf16[3,576,288]{1,2,0:T(8,128)(2,1)} %param.8), kind=kOutput, calls=%fused_computation.48 | convolution fusion | flops 297529344 | bytes 1916928 | tf_op jit(solution)/shard_map/dot_general | solution.py:142
  40.1 1.5 copy.70
  42.7 5.1 %collective-permute-start.4 = (bf16[56,576]{1,0:T(8,128)(2,1)S(1)}, bf16[56,576]{1,0:T(8,128)(2,1)S(1)}, u32[]{:S(2)}, u32[]{:S(2)}) collective-permute-start(bf16[56,576]{1,0:T(8,128)(2,1)S(1)} %reshape.126), channel_id=1, source_target_pairs={{0,12},{2,14},{4,8},{6,10},{8,4},{10,6},{12,0},{14,2},{1,13},{3,15... | collective-permute-start | bytes 193544 | tf_op jit(solution)/shard_map/ppermute | solution.py:43
  48.5 2.2 %collective-permute-done.4 = bf16[56,576]{1,0:T(8,128)(2,1)S(1)} collective-permute-done((bf16[56,576]{1,0:T(8,128)(2,1)S(1)}, bf16[56,576]{1,0:T(8,128)(2,1)S(1)}, u32[]{:S(2)}, u32[]{:S(2)}) %collective-permute-start.4) | collective-permute-done | bytes 64544 | tf_op jit(solution)/shard_map/ppermute | solution.py:43
  50.7 2.9 %collective-permute-done.3 = bf16[56,576]{1,0:T(8,128)(2,1)S(1)} collective-permute-done((bf16[56,576]{1,0:T(8,128)(2,1)S(1)}, bf16[56,576]{1,0:T(8,128)(2,1)S(1)}, u32[]{:S(2)}, u32[]{:S(2)}) %collective-permute-start.3) | collective-permute-done | bytes 64544 | tf_op jit(solution)/shard_map/ppermute | solution.py:43
  53.6 1.4 collective-permute-start.5
  55.1 7.2 %collective-permute-done.5 = bf16[224,576]{1,0:T(8,128)(2,1)S(1)} collective-permute-done((bf16[224,576]{1,0:T(8,128)(2,1)S(1)}, bf16[224,576]{1,0:T(8,128)(2,1)S(1)}, u32[]{:S(2)}, u32[]{:S(2)}) %collective-permute-start.5) | collective-permute-done | bytes 258080 | tf_op jit(solution)/shard_map/ppermute | solution.py:44
  63.5 20.6 %while.14 = (s32[]{:T(128)}, bf16[4,896,72]{1,2,0:T(8,128)(2,1)}, f32[4,448,72]{1,2,0:T(8,128)}, f32[4,448,72]{1,2,0:T(8,128)}, bf16[4,896,72]{1,2,0:T(8,128)(2,...) while((s32[]{:T(128)}, bf16[4,896,72]{1,2,0:T(8,128)(2,1)}, ...), condition=%wide.region_3.4_spmd, body=%wide.region_0.3_spmd.sunk | while | flops 294022400 | bytes 13560933 | solution.py:165
  65.1 1.3 multiply_reduce_fusion.2
  70.2 1.3 multiply_reduce_fusion.2
  75.4 1.3 multiply_reduce_fusion.2
  80.5 1.3 multiply_reduce_fusion.2
  84.1 1.4 copy.86
  86.8 6.8 %collective-permute-done.6 = bf16[224,576]{1,0:T(8,128)(2,1)S(1)} collective-permute-done((bf16[224,576]{1,0:T(8,128)(2,1)S(1)}, bf16[224,576]{1,0:T(8,128)(2,1)S(1)}, u32[]{:S(2)}, u32[]{:S(2)}) %collective-permute-start.6) | collective-permute-done | bytes 258080 | tf_op jit(solution)/shard_map/ppermute | solution.py:51
  94.3 3.0 %collective-permute-start.8 = (bf16[56,576]{1,0:T(8,128)(2,1)S(1)}, bf16[56,576]{1,0:T(8,128)(2,1)S(1)}, u32[]{:S(2)}, u32[]{:S(2)}) collective-permute-start(bf16[56,576]{1,0:T(8,128)(2,1)S(1)} %get-tuple-element.115), channel_id=1, source_target_pairs={{0,8},{2,10},{4,12},{6,14},{8,0},{10,2},{12,4},{14,6},{1,9},{3,11}... | collective-permute-start | bytes 193544 | tf_op jit(solution)/shard_map/ppermute | solution.py:57
  98.2 2.0 %collective-permute-done.9 = bf16[56,576]{1,0:T(8,128)(2,1)S(1)} collective-permute-done((bf16[56,576]{1,0:T(8,128)(2,1)S(1)}, bf16[56,576]{1,0:T(8,128)(2,1)S(1)}, u32[]{:S(2)}, u32[]{:S(2)}) %collective-permute-start.9) | collective-permute-done | bytes 64544 | tf_op jit(solution)/shard_map/ppermute | solution.py:57
  100.1 1.8 collective-permute-done.8
  102.0 2.3 %collective-permute-start.11 = (bf16[1,4,14,576]{3,0,2,1:T(2,128)(2,1)S(1)}, bf16[1,4,14,576]{3,0,2,1:T(2,128)(2,1)S(1)}, u32[]{:S(2)}, u32[]{:S(2)}) collective-permute-start(bf16[1,4,14,576]{3,0,2,1:T(2,128)(2,1)S(1)} %convert_element_type.175), channel_id=1, source_target_pairs={{0,2},{2,4},{4,6},{6,8},{8,10},{10,12},{12,14},{1,3},{3,5},{5,7},{... | collective-permute-start | bytes 193544 | tf_op jit(solution)/shard_map/ppermute | solution.py:30
  104.4 1.5 collective-permute-start.10
  105.8 2.4 %fusion.83 = f32[1,16,56,576]{3,0,2,1:T(1,128)} fusion(bf16[1,4,14,576]{3,0,2,1:T(2,128)(2,1)S(1)} %convert_element_type.175, f32[3,3,576,1]{2,3,1,0:T(1,128)S(1)} %reshape.132), kind=kOutput, calls=%fused_computation.139 | convolution fusion | flops 3117312 | bytes 2149632 | tf_op jit(solution)/shard_map/transpose(jvp())/conv_general_dilated | solution.py:87
  108.2 1.9 %fusion.41 = f32[3,3,576]{2,1,0:T(4,128)S(1)} fusion(bf16[1,4,14,576]{3,0,2,1:T(2,128)(2,1)S(1)} %convert_element_type.175, bf16[1,16,56,576]{3,2,1,0:T(8,128)(2,1)S(1)} %bitcast.196), kind=kOutput, calls=%fused_computation.62 | convolution fusion | flops 519552 | bytes 1117440 | tf_op jit(solution)/shard_map/transpose(jvp())/conv_general_dilated | solution.py:87
  110.2 1.9 %fusion.44 = f32[3,3,576]{2,1,0:T(4,128)S(1)} fusion(bf16[1,4,14,576]{3,0,2,1:T(2,128)(2,1)S(1)} %collective-permute-done.11, bf16[1,16,56,576]{3,2,1,0:T(8,128)(2,1)S(1)} %bitcast.197), kind=kOutput, calls=%fused_computation.63 | convolution fusion | flops 519552 | bytes 1117440 | tf_op jit(solution)/shard_map/transpose(jvp())/conv_general_dilated | solution.py:87
  112.1 1.9 %fusion.38 = f32[3,3,576]{2,1,0:T(4,128)S(1)} fusion(bf16[1,4,14,576]{3,0,2,1:T(2,128)(2,1)S(1)} %collective-permute-done.10, bf16[1,16,56,576]{3,2,1,0:T(8,128)(2,1)S(1)} %bitcast.198), kind=kOutput, calls=%fused_computation.61 | convolution fusion | flops 519552 | bytes 1117440 | tf_op jit(solution)/shard_map/transpose(jvp())/conv_general_dilated | solution.py:87
  114.8 1.3 fusion.84
  116.4 2.7 %add_convert_fusion = bf16[1,16,56,576]{3,0,2,1:T(2,128)(2,1)S(1)} fusion(f32[1,16,56,576]{3,0,2,1:T(1,128)S(1)} %fusion.84, f32[1,16,56,576]{3,0,2,1:T(1,128)S(1)} %copy-done.12, bf16[1,4,14,576]{3,0,2,1:T(2,128)(2,1)S(1)} %collective-permute-done.10, f32[3,3,576,1]{2,3,1,0:T(1,128)S(1)} %reshape.131), kind=kOutput, calls=%fused_computation.36 | convolution fusion | flops 4665600 | bytes 5246208 | tf_op jit(solution)/shard_map/transpose(jvp())/conv_general_dilated | solution.py:87
  120.9 3.5 %fusion.30 = bf16[576,896]{1,0:T(8,128)(2,1)} fusion(bf16[3,576,288]{1,2,0:T(8,128)(2,1)S(1)} %copy-done.10, bf16[1,896,288]{1,2,0:T(8,128)(2,1)S(1)} %bitcast.216, bf16[1,896,288]{1,2,0:T(8,128)(2,1)S(1)} %bitcast.214, bf16[1,896,288]{1,2,0:T(8,128)(2,1)} %bitcast.221), kind=kOutput, calls=%fused_computation.43 | convolution fusion | flops 893878272 | bytes 3575808 | tf_op jit(solution)/shard_map/icd,itd->ct/dot_general | solution.py:199
  124.5 2.5 %fusion.29 = bf16[576,3,288]{0,2,1:T(8,128)(2,1)S(1)} fusion(bf16[896,576,1]{1,0,2:T(8,128)(2,1)S(1)} %bitcast.207, bf16[1,896,288]{1,2,0:T(8,128)(2,1)S(1)} %bitcast.217, bf16[1,896,288]{1,2,0:T(8,128)(2,1)S(1)} %bitcast.215, bf16[1,896,288]{1,2,0:T(8,128)(2,1)} %bitcast.222), kind=kOutput, calls=%fused_computation.42 | convolution fusion | flops 893859840 | bytes 3575808 | tf_op jit(solution)/shard_map/tc,itd->cid/dot_general | solution.py:195
  127.0 2.0 %convert_element_type.157 = bf16[8,72,864]{1,0,2:T(8,128)(2,1)S(1)} reshape(bf16[576,3,288]{0,2,1:T(8,128)(2,1)S(1)} %fusion.29) | data formatting | bytes 1990656 | tf_op jit(solution)/shard_map/convert_element_type | solution.py:66
  129.0 4.4 %constant_dynamic-slice_fusion = (bf16[1,72,864]{1,0,2:T(2,128)(2,1)}, bf16[1,72,864]{1,0,2:T(2,128)(2,1)S(1)}, bf16[1,72,864]{1,0,2:T(2,128)(2,1)S(1)}, bf16[1,...) fusion(bf16[8,72,864]{1,0,2:T(8,128)(2,1)S(1)} %convert_element, ...), kind=kLoop, calls=%fused_computation.121 | loop fusion | flops 62208 | bytes 2115104 | tf_op jit(solution)/shard_map/jit(dynamic_index_in_dim)/dynamic_slice | solution.py:69
  133.5 1.3 copy.106
  134.8 1.3 copy.104
  136.1 1.3 copy.103
  141.5 2.7 %collective-permute-start.12 = (bf16[306,864]{1,0:T(8,128)(2,1)}, bf16[306,864]{1,0:T(8,128)(2,1)}, u32[]{:S(2)}, u32[]{:S(2)}) collective-permute-start(bf16[306,864]{1,0:T(8,128)(2,1)} %convert_dynamic-update-slice_fusion), channel_id=1, source_target_pairs={{0,2},{2,0},{4,6},{6,4},{8,10},{10,8},{12,14},{14,12},{1,3},{3,1},... | collective-permute-start | bytes 1586312 | tf_op jit(solution)/shard_map/ppermute | solution.py:73
  145.2 1.8 concatenate.45
  147.0 5.8 %collective-permute-done.12 = bf16[306,864]{1,0:T(8,128)(2,1)} collective-permute-done((bf16[306,864]{1,0:T(8,128)(2,1)}, bf16[306,864]{1,0:T(8,128)(2,1)}, u32[]{:S(2)}, u32[]{:S(2)}) %collective-permute-start.12) | collective-permute-done | bytes 528800 | tf_op jit(solution)/shard_map/ppermute | solution.py:73
  152.9 1.4 copy.107
  155.1 2.7 %collective-permute-start.13 = (bf16[90,864]{0,1:T(8,128)(2,1)S(1)}, bf16[90,864]{0,1:T(8,128)(2,1)S(1)}, u32[]{:S(2)}, u32[]{:S(2)}) collective-permute-start(bf16[90,864]{0,1:T(8,128)(2,1)S(1)} %get-tuple-element.116), channel_id=1, source_target_pairs={{0,4},{2,6},{4,0},{6,2},{8,12},{10,14},{12,8},{14,10},{1,5},{3,7},... | collective-permute-start | bytes 466568 | tf_op jit(solution)/shard_map/ppermute | solution.py:80
  157.8 3.6 %collective-permute-start.14 = (bf16[90,864]{0,1:T(8,128)(2,1)S(1)}, bf16[90,864]{0,1:T(8,128)(2,1)S(1)}, u32[]{:S(2)}, u32[]{:S(2)}) collective-permute-start(bf16[90,864]{0,1:T(8,128)(2,1)S(1)} %get-tuple-element.117), channel_id=1, source_target_pairs={{0,8},{2,10},{4,12},{6,14},{8,0},{10,2},{12,4},{14,6},{1,9},{3,11}... | collective-permute-start | bytes 466568 | tf_op jit(solution)/shard_map/ppermute | solution.py:80
  161.6 2.0 %collective-permute-done.13 = bf16[90,864]{0,1:T(8,128)(2,1)S(1)} collective-permute-done((bf16[90,864]{0,1:T(8,128)(2,1)S(1)}, bf16[90,864]{0,1:T(8,128)(2,1)S(1)}, u32[]{:S(2)}, u32[]{:S(2)}) %collective-permute-start.13) | collective-permute-done | bytes 155552 | tf_op jit(solution)/shard_map/ppermute | solution.py:80
  163.7 11.2 %collective-permute-done.14 = bf16[90,864]{0,1:T(8,128)(2,1)S(1)} collective-permute-done((bf16[90,864]{0,1:T(8,128)(2,1)S(1)}, bf16[90,864]{0,1:T(8,128)(2,1)S(1)}, u32[]{:S(2)}, u32[]{:S(2)}) %collective-permute-start.14) | collective-permute-done | bytes 155552 | tf_op jit(solution)/shard_map/ppermute | solution.py:80
  177.3 2.2 %copy.92 = bf16[896,288]{1,0:T(8,128)(2,1)} copy(bf16[896,288]{0,1:T(8,128)(2,1)} %bitcast.213) | data formatting | bytes 1032192 | tf_op jit(solution)/shard_map/convert_element_type | solution.py:206
  (142 shorter events, 40.7 us)
Async XLA Ops:
  7.2 170.2 %reduce-scatter.2.cloned.1.call-start = ((), (), s32[]{:S(2)}) async-start(), calls=%async_computation.1 | async-start | bytes 1548288 | tf_op jit(solution)/shard_map/reduce_scatter | solution.py:198
  15.7 3.6 %copy-start.1 = (bf16[1,16,56,576]{3,2,1,0:T(8,128)(2,1)}, bf16[1,16,56,576]{3,2,1,0:T(8,128)(2,1)S(1)}, u32[]{:S(2)}) copy-start(bf16[1,16,56,576]{3,2,1,0:T(8,128)(2,1)S(1)} %copy.69) | copy-start | bytes 3096580
  17.6 1.7 copy-start.9
  21.2 0.7 copy-start.11
  21.8 11.0 %copy-start.6 = (bf16[16,1,7,2,576]{4,2,3,0,1:T(8,128)(2,1)}, bf16[16,1,7,2,576]{4,2,3,0,1:T(8,128)(2,1)S(1)}, u32[]{:S(2)}) copy-start(bf16[16,1,7,2,576]{4,2,3,0,1:T(8,128)(2,1)S(1)} %slice.126) | copy-start | bytes 774148
  22.7 19.0 %collective-permute-start = (bf16[4,14,576]{2,0,1:T(4,128)(2,1)}, bf16[4,14,576]{2,0,1:T(4,128)(2,1)}, u32[]{:S(2)}, u32[]{:S(2)}) collective-permute-start(bf16[4,14,576]{2,0,1:T(4,128)(2,1)} %slice_bitcast_fusion.2), channel_id=1, source_target_pairs={{0,2},{2,4},{4,6},{6,8},{8,10},{10,12},{12,14},{1,3},{3,5},{5,7},{... | collective-permute-start | bytes 193544 | tf_op jit(solution)/shard_map/ppermute | solution.py:20
  28.1 6.8 %copy-start.2 = (bf16[1,16,56,576]{3,2,1,0:T(8,128)(2,1)S(1)}, bf16[1,16,56,576]{3,2,1,0:T(8,128)(2,1)}, u32[]{:S(2)}) copy-start(bf16[1,16,56,576]{3,2,1,0:T(8,128)(2,1)} %copy-done.1) | copy-start | bytes 3096580
  33.6 8.1 %collective-permute-start.1 = (f32[4,14,576]{2,0,1:T(4,128)}, f32[4,14,576]{2,0,1:T(4,128)}, u32[]{:S(2)}, u32[]{:S(2)}) collective-permute-start(f32[4,14,576]{2,0,1:T(4,128)} %slice_bitcast_fusion), channel_id=1, source_target_pairs={{2,0},{4,2},{6,4},{8,6},{10,8},{12,10},{14,12},{3,1},{5,3},{7,5},{... | collective-permute-start | bytes 387080 | tf_op jit(solution)/shard_map/ppermute | solution.py:20
  37.3 1.1 copy-start.4
  42.7 8.0 %collective-permute-start.4 = (bf16[56,576]{1,0:T(8,128)(2,1)S(1)}, bf16[56,576]{1,0:T(8,128)(2,1)S(1)}, u32[]{:S(2)}, u32[]{:S(2)}) collective-permute-start(bf16[56,576]{1,0:T(8,128)(2,1)S(1)} %reshape.126), channel_id=1, source_target_pairs={{0,12},{2,14},{4,8},{6,10},{8,4},{10,6},{12,0},{14,2},{1,13},{3,15... | collective-permute-start | bytes 193544 | tf_op jit(solution)/shard_map/ppermute | solution.py:43
  47.8 5.8 %collective-permute-start.3 = (bf16[56,576]{1,0:T(8,128)(2,1)S(1)}, bf16[56,576]{1,0:T(8,128)(2,1)S(1)}, u32[]{:S(2)}, u32[]{:S(2)}) collective-permute-start(bf16[56,576]{1,0:T(8,128)(2,1)S(1)} %reshape.126), channel_id=1, source_target_pairs={{0,8},{2,10},{4,12},{6,14},{8,0},{10,2},{12,4},{14,6},{1,9},{3,11}... | collective-permute-start | bytes 193544 | tf_op jit(solution)/shard_map/ppermute | solution.py:43
  47.8 5.8 %collective-permute-start.2 = (bf16[56,576]{1,0:T(8,128)(2,1)S(1)}, bf16[56,576]{1,0:T(8,128)(2,1)S(1)}, u32[]{:S(2)}, u32[]{:S(2)}) collective-permute-start(bf16[56,576]{1,0:T(8,128)(2,1)S(1)} %reshape.126), channel_id=1, source_target_pairs={{0,4},{2,6},{4,0},{6,2},{8,12},{10,14},{12,8},{14,10},{1,5},{3,7},... | collective-permute-start | bytes 193544 | tf_op jit(solution)/shard_map/ppermute | solution.py:43
  53.6 8.6 %collective-permute-start.5 = (bf16[224,576]{1,0:T(8,128)(2,1)S(1)}, bf16[224,576]{1,0:T(8,128)(2,1)S(1)}, u32[]{:S(2)}, u32[]{:S(2)}) collective-permute-start(bf16[224,576]{1,0:T(8,128)(2,1)S(1)} %pad_maximum_fusion.5), channel_id=1, source_target_pairs={{0,2},{2,0},{4,6},{6,4},{8,10},{10,8},{12,14},{14,12},{1,3},{3,1},... | collective-permute-start | bytes 774152 | tf_op jit(solution)/shard_map/ppermute | solution.py:44
  84.1 1.4 copy-start.5
  85.8 7.7 %collective-permute-start.6 = (bf16[224,576]{1,0:T(8,128)(2,1)S(1)}, bf16[224,576]{1,0:T(8,128)(2,1)S(1)}, u32[]{:S(2)}, u32[]{:S(2)}) collective-permute-start(bf16[224,576]{1,0:T(8,128)(2,1)S(1)} %fusion.49), channel_id=1, source_target_pairs={{0,2},{2,0},{4,6},{6,4},{8,10},{10,8},{12,14},{14,12},{1,3},{3,1},... | collective-permute-start | bytes 774152 | tf_op jit(solution)/shard_map/ppermute | solution.py:51
  93.8 4.4 %collective-permute-start.7 = (bf16[56,576]{1,0:T(8,128)(2,1)S(1)}, bf16[56,576]{1,0:T(8,128)(2,1)S(1)}, u32[]{:S(2)}, u32[]{:S(2)}) collective-permute-start(bf16[56,576]{1,0:T(8,128)(2,1)S(1)} %get-tuple-element.113), channel_id=1, source_target_pairs={{0,4},{2,6},{4,0},{6,2},{8,12},{10,14},{12,8},{14,10},{1,5},{3,7},... | collective-permute-start | bytes 193544 | tf_op jit(solution)/shard_map/ppermute | solution.py:57
  93.8 6.3 %collective-permute-start.9 = (bf16[56,576]{1,0:T(8,128)(2,1)S(1)}, bf16[56,576]{1,0:T(8,128)(2,1)S(1)}, u32[]{:S(2)}, u32[]{:S(2)}) collective-permute-start(bf16[56,576]{1,0:T(8,128)(2,1)S(1)} %get-tuple-element.114), channel_id=1, source_target_pairs={{0,12},{2,14},{4,8},{6,10},{8,4},{10,6},{12,0},{14,2},{1,13},{3,15... | collective-permute-start | bytes 193544 | tf_op jit(solution)/shard_map/ppermute | solution.py:57
  94.3 7.6 %collective-permute-start.8 = (bf16[56,576]{1,0:T(8,128)(2,1)S(1)}, bf16[56,576]{1,0:T(8,128)(2,1)S(1)}, u32[]{:S(2)}, u32[]{:S(2)}) collective-permute-start(bf16[56,576]{1,0:T(8,128)(2,1)S(1)} %get-tuple-element.115), channel_id=1, source_target_pairs={{0,8},{2,10},{4,12},{6,14},{8,0},{10,2},{12,4},{14,6},{1,9},{3,11}... | collective-permute-start | bytes 193544 | tf_op jit(solution)/shard_map/ppermute | solution.py:57
  102.0 8.1 %collective-permute-start.11 = (bf16[1,4,14,576]{3,0,2,1:T(2,128)(2,1)S(1)}, bf16[1,4,14,576]{3,0,2,1:T(2,128)(2,1)S(1)}, u32[]{:S(2)}, u32[]{:S(2)}) collective-permute-start(bf16[1,4,14,576]{3,0,2,1:T(2,128)(2,1)S(1)} %convert_element_type.175), channel_id=1, source_target_pairs={{0,2},{2,4},{4,6},{6,8},{8,10},{10,12},{12,14},{1,3},{3,5},{5,7},{... | collective-permute-start | bytes 193544 | tf_op jit(solution)/shard_map/ppermute | solution.py:30
  104.4 7.7 %collective-permute-start.10 = (bf16[1,4,14,576]{3,0,2,1:T(2,128)(2,1)S(1)}, bf16[1,4,14,576]{3,0,2,1:T(2,128)(2,1)S(1)}, u32[]{:S(2)}, u32[]{:S(2)}) collective-permute-start(bf16[1,4,14,576]{3,0,2,1:T(2,128)(2,1)S(1)} %convert_element_type.175), channel_id=1, source_target_pairs={{2,0},{4,2},{6,4},{8,6},{10,8},{12,10},{14,12},{3,1},{5,3},{7,5},{... | collective-permute-start | bytes 193544 | tf_op jit(solution)/shard_map/ppermute | solution.py:31
  114.8 1.6 copy-start.12
  119.7 1.2 copy-start.10
  120.9 3.6 %copy-start.3 = (bf16[1,16,56,576]{3,2,1,0:T(8,128)(2,1)S(1)}, bf16[1,16,56,576]{3,2,1,0:T(8,128)(2,1)}, u32[]{:S(2)}) copy-start(bf16[1,16,56,576]{3,2,1,0:T(8,128)(2,1)} %copy-done.1) | copy-start | bytes 3096580
  133.5 3.9 %copy-start = (bf16[1,72,864]{1,0,2:T(2,128)(2,1)S(1)}, bf16[1,72,864]{1,0,2:T(2,128)(2,1)}, u32[]{:S(2)}) copy-start(bf16[1,72,864]{1,0,2:T(2,128)(2,1)} %get-tuple-element.105) | copy-start | bytes 373252
  133.5 7.2 %copy-start.7 = (f32[1,27,288]{2,1,0:T(8,128)S(1)}, f32[1,27,288]{2,1,0:T(8,128)}, u32[]{:S(2)}) copy-start(f32[1,27,288]{2,1,0:T(8,128)} %get-tuple-element.123) | copy-start | bytes 93316
  133.5 7.2 %copy-start.8 = (f32[1,27,288]{2,1,0:T(8,128)S(1)}, f32[1,27,288]{2,1,0:T(8,128)}, u32[]{:S(2)}) copy-start(f32[1,27,288]{2,1,0:T(8,128)} %get-tuple-element.124) | copy-start | bytes 93316
  141.5 11.4 %collective-permute-start.12 = (bf16[306,864]{1,0:T(8,128)(2,1)}, bf16[306,864]{1,0:T(8,128)(2,1)}, u32[]{:S(2)}, u32[]{:S(2)}) collective-permute-start(bf16[306,864]{1,0:T(8,128)(2,1)} %convert_dynamic-update-slice_fusion), channel_id=1, source_target_pairs={{0,2},{2,0},{4,6},{6,4},{8,10},{10,8},{12,14},{14,12},{1,3},{3,1},... | collective-permute-start | bytes 1586312 | tf_op jit(solution)/shard_map/ppermute | solution.py:73
  155.1 8.5 %collective-permute-start.13 = (bf16[90,864]{0,1:T(8,128)(2,1)S(1)}, bf16[90,864]{0,1:T(8,128)(2,1)S(1)}, u32[]{:S(2)}, u32[]{:S(2)}) collective-permute-start(bf16[90,864]{0,1:T(8,128)(2,1)S(1)} %get-tuple-element.116), channel_id=1, source_target_pairs={{0,4},{2,6},{4,0},{6,2},{8,12},{10,14},{12,8},{14,10},{1,5},{3,7},... | collective-permute-start | bytes 466568 | tf_op jit(solution)/shard_map/ppermute | solution.py:80
  157.8 17.1 %collective-permute-start.14 = (bf16[90,864]{0,1:T(8,128)(2,1)S(1)}, bf16[90,864]{0,1:T(8,128)(2,1)S(1)}, u32[]{:S(2)}, u32[]{:S(2)}) collective-permute-start(bf16[90,864]{0,1:T(8,128)(2,1)S(1)} %get-tuple-element.117), channel_id=1, source_target_pairs={{0,8},{2,10},{4,12},{6,14},{8,0},{10,2},{12,4},{14,6},{1,9},{3,11}... | collective-permute-start | bytes 466568 | tf_op jit(solution)/shard_map/ppermute | solution.py:80
  161.4 13.5 %collective-permute-start.15 = (bf16[90,864]{0,1:T(8,128)(2,1)S(1)}, bf16[90,864]{0,1:T(8,128)(2,1)S(1)}, u32[]{:S(2)}, u32[]{:S(2)}) collective-permute-start(bf16[90,864]{0,1:T(8,128)(2,1)S(1)} %concatenate.54), channel_id=1, source_target_pairs={{0,12},{2,14},{4,8},{6,10},{8,4},{10,6},{12,0},{14,2},{1,13},{3,15... | collective-permute-start | bytes 466568 | tf_op jit(solution)/shard_map/ppermute | solution.py:80
Sparse Core Ops, SparseCore 0:
  127.2 10.1 reduce-scatter.1

commit v2 on v1

v2 whole, which is shorter than its diff:
```python
import functools
import math

import jax
import jax.numpy as jnp
from jax import lax
from jax.experimental import pallas as pl
from jax.experimental.pallas import tpu as pltpu
from jax.sharding import PartitionSpec as P

HEADS = 8
LANES = 128
F32 = jnp.float32
BF16 = jnp.bfloat16
PARAMS = pltpu.CompilerParams(vmem_limit_bytes=56 * 1024 * 1024)
NN = (((1,), (0,)), ((), ()))
NT = (((1,), (1,)), ((), ()))
TN = (((0,), (0,)), ((), ()))


def mul(left, right, dims=NN):
    return lax.dot_general(left, right, dims, preferred_element_type=F32)


def vmem():
    return pl.BlockSpec(memory_space=pltpu.VMEM)


def smem():
    return pl.BlockSpec(memory_space=pltpu.SMEM)


def lane_tiles(channels):
    return [
        (k, k * LANES, min(LANES, channels - k * LANES)) for k in range(pl.cdiv(channels, LANES))
    ]


def pool_body(geometry, place, own, other, weights, taps, to_pair, to_next, middle, windows, wide):
    rows, cols, local = geometry
    pooled_rows, pooled_cols = rows // 4, cols // 4
    even = place[0] % 2 == 0
    starts = lax.broadcasted_iota(jnp.int32, (pooled_cols, LANES), 0) == 0
    for side in range(2):
        full = mul(own[...], weights[side + 1, :local, :]) + mul(
            other[...], weights[side + 1, local:, :]
        )
        full = full.astype(BF16).astype(F32)
        for tile, low, width in lane_tiles(local):
            wide[tile, 0:8, :] = jnp.zeros((8, LANES), F32)
            wide[tile, 8:, :width] = full[:, low : low + width]
            for b in range(3):
                for e in range(3):
                    for i in range(pooled_rows):
                        row = 4 * i + b - 1
                        if row < 0:
                            piece = jnp.zeros((pooled_cols, LANES), F32)
                        else:
                            piece = wide[tile, pl.ds(row * cols + e + 7, pooled_cols, stride=4), :]
                            if e == 0:
                                piece = jnp.where(starts, 0.0, piece)
                        at = slice(i * pooled_cols, (i + 1) * pooled_cols)
                        windows[side, 3 * b + e, at, low : low + width] = piece[:, :width]
        sums = []
        for a in range(3):
            total = windows[side, 0] * taps[side, 9 * a : 9 * a + 1, :]
            for k in range(1, 9):
                total = total + windows[side, k] * taps[side, 9 * a + k : 9 * a + k + 1, :]
            sums.append(total)
        lanes = slice(side * local, (side + 1) * local)
        earlier, center, later = sums
        to_pair[:, lanes] = jnp.where(even, earlier, later).astype(BF16)
        to_next[:, lanes] = jnp.where(even, later, earlier).astype(BF16)
        middle[:, lanes] = center


def pool_call(place, own, other, weights, taps, rows, cols):
    local = own.shape[1]
    count = rows * cols // 16
    return pl.pallas_call(
        functools.partial(pool_body, (rows, cols, local)),
        out_shape=(
            jax.ShapeDtypeStruct((count, 2 * local), BF16),
            jax.ShapeDtypeStruct((count, 2 * local), BF16),
            jax.ShapeDtypeStruct((count, 2 * local), F32),
            jax.ShapeDtypeStruct((2, 9, count, local), F32),
        ),
        in_specs=[smem()] + [vmem()] * 4,
        out_specs=(vmem(),) * 4,
        scratch_shapes=[pltpu.VMEM((pl.cdiv(local, LANES), rows * cols + 8, LANES), F32)],
        compiler_params=PARAMS,
        name="project_pool",
    )(place, own, other, weights, taps)


def spread_rows(head_dim, local, heads):
    rows = lax.broadcasted_iota(jnp.int32, (heads * LANES, local), 0)
    cols = lax.broadcasted_iota(jnp.int32, (heads * LANES, local), 1)
    chosen = rows < 0
    for h in range(heads):
        inside = (cols >= h * head_dim) & (cols < (h + 1) * head_dim)
        chosen = chosen | (inside & (rows == cols + h * (LANES - head_dim)))
    return chosen.astype(F32).astype(BF16)


def query_body(geometry, own, other, near_t, far_t, out_grad, query_t, grad_t):
    head_dim, local, heads = geometry
    spread = spread_rows(head_dim, local, heads)
    near = mul(spread, near_t[...]).astype(BF16)
    far = mul(spread, far_t[...]).astype(BF16)
    query = mul(near, own[...], NT) + mul(far, other[...], NT)
    query_t[...] = query.astype(BF16)
    grad_t[...] = mul(spread, out_grad[...], NT).astype(BF16)


def query_call(own, other, near, far, out_grad, head_dim):
    tokens, local = own.shape
    heads = local // head_dim
    shape = jax.ShapeDtypeStruct((heads * LANES, tokens), BF16)
    return pl.pallas_call(
        functools.partial(query_body, (head_dim, local, heads)),
        out_shape=(shape, shape),
        in_specs=[vmem()] * 5,
        out_specs=(vmem(),) * 2,
        compiler_params=PARAMS,
        name="project_query",
    )(own, other, near, far, out_grad)


def attend_body(geometry, keys, query_t, grad_t, key_grads, query_grad, total):
    head_dim, local, heads = geometry
    head = pl.program_id(0)
    scale = head_dim ** (-0.5)
    rows = lax.broadcasted_iota(jnp.int32, (2 * local, 2 * LANES), 0)
    cols = lax.broadcasted_iota(jnp.int32, (2 * local, 2 * LANES), 1)
    lane = cols % LANES
    source = lane + (cols // LANES) * local + head * head_dim
    chosen = ((rows == source) & (lane < head_dim)).astype(F32).astype(BF16)
    both = mul(keys[...], chosen).astype(BF16)
    key, value = both[:, :LANES], both[:, LANES:]
    query = query_t[...]
    grad = grad_t[...]
    scores = mul(key, query)
    raised = jnp.exp2(scores * (scale * math.log2(math.e)))
    inverse = 1.0 / jnp.sum(raised, axis=0, keepdims=True)
    prob_grad = mul(value, grad)
    centre = jnp.sum(raised * prob_grad, axis=0, keepdims=True) * inverse
    probs = raised * inverse
    score_grad = (probs * (prob_grad - centre) * scale).astype(BF16)
    value_back = mul(probs.astype(BF16), grad, NT)
    key_back = mul(score_grad, query, NT)
    square = lax.broadcasted_iota(jnp.int32, (LANES, LANES), 0) == lax.broadcasted_iota(
        jnp.int32, (LANES, LANES), 1
    )
    key_t = mul(square.astype(F32).astype(BF16), key, NT).astype(BF16)
    back_t = mul(key_t, score_grad) + grad.astype(F32)
    query_grad[...] = back_t.T.astype(BF16)
    joined = jnp.concatenate([key_back, value_back], axis=1).astype(BF16)
    placed = mul(joined, chosen, NT)

    @pl.when(head == 0)
    def _():
        total[...] = placed

    @pl.when(head > 0)
    def _():
        total[...] += placed

    @pl.when(head == heads - 1)
    def _():
        key_grads[...] = total[...].astype(BF16)


def attend_call(keys, query_t, grad_t, head_dim):
    key_count, both = keys.shape
    local = both // 2
    heads = local // head_dim
    tokens = query_t.shape[1]
    return pl.pallas_call(
        functools.partial(attend_body, (head_dim, local, heads)),
        grid=(heads,),
        out_shape=(
            jax.ShapeDtypeStruct((key_count, both), BF16),
            jax.ShapeDtypeStruct((tokens, heads * LANES), BF16),
        ),
        in_specs=[
            pl.BlockSpec((key_count, both), lambda h: (0, 0)),
            pl.BlockSpec((LANES, tokens), lambda h: (h, 0)),
            pl.BlockSpec((LANES, tokens), lambda h: (h, 0)),
        ],
        out_specs=(
            pl.BlockSpec((key_count, both), lambda h: (0, 0)),
            pl.BlockSpec((tokens, LANES), lambda h: (0, h)),
        ),
        scratch_shapes=[pltpu.VMEM((key_count, both), F32)],
        compiler_params=PARAMS,
        name="attend_backward",
    )(keys, query_t, grad_t)


def query_side_body(geometry, query_pad, own, other, weights, weight_terms, token_terms):
    head_dim, local, heads = geometry
    spread = spread_rows(head_dim, local, heads)
    query_back = mul(query_pad[...], spread).astype(BF16)
    weight_terms[:local, :] = mul(own[...], query_back, TN)
    weight_terms[local:, :] = mul(other[...], query_back, TN)
    token_terms[0] = mul(query_back, weights[0, :local, :], NT)
    token_terms[1] = mul(query_back, weights[0, local:, :], NT)


def query_side_call(query_pad, own, other, weights, head_dim):
    tokens, local = own.shape
    return pl.pallas_call(
        functools.partial(query_side_body, (head_dim, local, local // head_dim)),
        out_shape=(
            jax.ShapeDtypeStruct((2 * local, local), F32),
            jax.ShapeDtypeStruct((2, tokens, local), F32),
        ),
        in_specs=[vmem()] * 4,
        out_specs=(vmem(),) * 2,
        compiler_params=PARAMS,
        name="query_side",
    )(query_pad, own, other, weights)


def pull_body(
    geometry,
    place,
    mine,
    before,
    after,
    windows,
    taps,
    own,
    other,
    weights,
    query_weight,
    query_token,
    here,
    away,
    token_near,
    token_far,
    wide,
    staged,
    folded,
):
    rows, cols, local, count = geometry
    pooled_rows, pooled_cols = rows // 4, cols // 4
    position, core = place[0], place[1]
    pooled = pooled_rows * pooled_cols
    block_rows = 2 * local // count
    outer = count // 2
    starts = lax.broadcasted_iota(jnp.int32, (pooled, local), 0) % pooled_cols == 0
    here[outer * block_rows :, :] = jnp.zeros((here.shape[0] - outer * block_rows, 3 * local), F32)
    away[outer * block_rows :, :] = jnp.zeros((here.shape[0] - outer * block_rows, 3 * local), BF16)
    near = query_token[0]
    far = query_token[1]
    columns = [(query_weight[:local, :], query_weight[local:, :])]
    for side in range(2):
        lanes = slice(side * local, (side + 1) * local)
        grads = [after[:, lanes].astype(F32), mine[:, lanes], before[:, lanes].astype(F32)]
        wide[...] = jnp.zeros(wide.shape, F32)
        for b in range(3):
            for e in range(3):
                k = 3 * b + e
                window = windows[side, k]
                spread = None
                for a in range(3):
                    term = grads[a] * taps[side, 9 * a + k : 9 * a + k + 1, :]
                    spread = term if spread is None else spread + term
                    tap = jnp.sum(grads[a] * window, axis=0, keepdims=True)
                    at = outer * block_rows + 9 * a + k
                    here[at : at + 1, lanes] = tap
                    folded[9 * a + k : 9 * a + k + 1, lanes] = tap
                if e == 0:
                    spread = jnp.where(starts, 0.0, spread)
                for tile, low, width in lane_tiles(local):
                    part = spread[:, low : low + width]
                    if width < LANES:
                        part = jnp.concatenate(
                            [part, jnp.zeros((pooled, LANES - width), F32)], axis=1
                        )
                    staged[tile] = part
                    for i in range(pooled_rows):
                        row = 4 * i + b - 1
                        if row >= 0:
                            at = slice(i * pooled_cols, (i + 1) * pooled_cols)
                            wide[tile, pl.ds(row * cols + e + 7, pooled_cols, stride=4), :] = (
                                staged[tile, at, :]
                            )
        back = jnp.concatenate(
            [wide[tile, 8:, :width] for tile, low, width in lane_tiles(local)], axis=1
        ).astype(BF16)
        near = near + mul(back, weights[side + 1, :local, :], NT)
        far = far + mul(back, weights[side + 1, local:, :], NT)
        columns.append((mul(own[...], back, TN), mul(other[...], back, TN)))
    token_near[...] = near
    token_far[...] = far.astype(BF16)
    away[outer * block_rows : outer * block_rows + 32, : 2 * local] = folded[...].astype(BF16)
    for half in range(2):
        actual = jnp.where(half == 0, core, 1 - core)
        for j in range(count // 2):
            relative = position ^ (actual * (count // 2) + j)
            at = pl.multiple_of((relative // 2) * block_rows, 8)
            rows_here = slice(j * block_rows, (j + 1) * block_rows)
            for side in range(3):
                lanes = slice(side * local, (side + 1) * local)
                value = columns[side][half][rows_here, :]

                @pl.when(relative % 2 == 0)
                def _(value=value, at=at, lanes=lanes):
                    here[pl.ds(at, block_rows), lanes] = value

                @pl.when(relative % 2 == 1)
                def _(value=value, at=at, lanes=lanes):
                    away[pl.ds(at, block_rows), lanes] = value.astype(BF16)


def pull_call(place, mine, before, after, windows, taps, own, other, weights, query_weight, query_token, rows, cols, count):
    tokens, local = own.shape
    half = local
    size = half + 32
    return pl.pallas_call(
        functools.partial(pull_body, (rows, cols, local, count)),
        out_shape=(
            jax.ShapeDtypeStruct((size, 3 * local), F32),
            jax.ShapeDtypeStruct((size, 3 * local), BF16),
            jax.ShapeDtypeStruct((tokens, local), F32),
            jax.ShapeDtypeStruct((tokens, local), BF16),
        ),
        in_specs=[smem()] + [vmem()] * 10,
        out_specs=(vmem(),) * 4,
        scratch_shapes=[
            pltpu.VMEM((pl.cdiv(local, LANES), tokens + 8, LANES), F32),
            pltpu.VMEM((pl.cdiv(local, LANES), rows * cols // 16, LANES), F32),
            pltpu.VMEM((32, 2 * local), F32),
        ],
        compiler_params=PARAMS,
        name="pull_back",
    )(place, mine, before, after, windows, taps, own, other, weights, query_weight, query_token)


def frame_pairs(step, flip):
    count = lax.axis_size("frames")
    return [(i, i ^ (2 * step + flip)) for i in range(count)]


def next_pairs():
    count = lax.axis_size("frames")
    return [(i, (i + (1 if i % 2 else -1)) % count) for i in range(count)]


def exchange(block, pairs):
    return lax.ppermute(block, "frames", pairs)


def gather_frames(block):
    outer = lax.axis_size("frames") // 2
    same = [block] + [exchange(block, frame_pairs(s, 0)) for s in range(1, outer)]
    other = exchange(jnp.concatenate(same), frame_pairs(0, 1))
    return jnp.concatenate(same + [other])


def scatter_frames(terms):
    outer = lax.axis_size("frames") // 2
    half = terms.shape[0] // 2
    moved = exchange(terms[half:], frame_pairs(0, 1))
    summed = terms[:half].astype(F32) + moved.astype(F32)
    rows = half // outer
    low = summed.astype(BF16)
    own = summed[:rows]
    for step in range(1, outer):
        piece = low[step * rows : (step + 1) * rows]
        own = own + exchange(piece, frame_pairs(step, 0)).astype(F32)
    return own


def scatter_weights(here, away, rows):
    outer = lax.axis_size("frames") // 2
    moved = exchange(away, frame_pairs(0, 1))
    summed = here + moved.astype(F32)
    tail = summed[outer * rows :]
    own = jnp.concatenate([summed[:rows], tail])
    low = summed.astype(BF16)
    for step in range(1, outer):
        piece = jnp.concatenate([low[step * rows : (step + 1) * rows], low[outer * rows :]])
        own = own + exchange(piece, frame_pairs(step, 0)).astype(F32)
    return own[:rows], own[rows:]


def shards(tokens, out_grad, w_qkv, pool_kernel):
    local = tokens.shape[-1]
    heads_here = HEADS // lax.axis_size("heads")
    head_dim = local // heads_here
    rows, cols = tokens.shape[1], tokens.shape[2]
    token_count = rows * cols
    count = lax.axis_size("frames")
    frame = lax.axis_index("frames")
    core = lax.axis_index("heads")
    even = frame % 2 == 0
    place = jnp.stack([frame, core]).astype(jnp.int32)
    own = tokens.reshape(token_count, local)
    grad = out_grad.reshape(token_count, local)
    other = lax.ppermute(own, "heads", [(0, 1), (1, 0)])
    weights = jnp.where(core == 0, w_qkv, jnp.roll(w_qkv, local, axis=1))
    to_pair, to_next, middle, windows = pool_call(
        place, own, other, weights, pool_kernel, rows, cols
    )
    from_pair = exchange(to_pair, frame_pairs(0, 1))
    from_next = exchange(to_next, next_pairs())
    at_end = (frame == 0) | (frame == count - 1)
    pooled = middle + from_pair.astype(F32) + jnp.where(at_end, 0.0, from_next.astype(F32))
    query_t, grad_t = query_call(
        own, other, weights[0, :local].T, weights[0, local:].T, grad, head_dim
    )
    keys = gather_frames(pooled.astype(BF16))
    key_grads, query_pad = attend_call(keys, query_t, grad_t, head_dim)
    owned = scatter_frames(key_grads)
    query_weight, query_token = query_side_call(query_pad, own, other, weights, head_dim)
    low = owned.astype(BF16)
    pair = exchange(low, frame_pairs(0, 1))
    beside = jnp.where(at_end, 0.0, exchange(low, next_pairs()).astype(F32)).astype(BF16)
    before = jnp.where(even, beside, pair)
    after = jnp.where(even, pair, beside)
    here, away, near, far = pull_call(
        place, owned, before, after, windows, pool_kernel, own, other, weights,
        query_weight, query_token, rows, cols, count,
    )
    weight_part, kernel_part = scatter_weights(here, away, 2 * local // count)
    weight_grad = jnp.stack([weight_part[:, s * local : (s + 1) * local] for s in range(3)])
    kernel_grad = jnp.stack([kernel_part[:27, s * local : (s + 1) * local] for s in range(2)])
    input_grad = near + lax.ppermute(far, "heads", [(0, 1), (1, 0)]).astype(F32)
    return input_grad.astype(BF16).reshape(tokens.shape), weight_grad, kernel_grad


def solution(mesh):
    in_specs = (
        P(("clips", "frames"), None, None, "heads"),
        P(("clips", "frames"), None, None, "heads"),
        P(None, None, "heads"),
        P(None, None, "heads"),
    )
    out_specs = (
        P(("clips", "frames"), None, None, "heads"),
        P("clips", "frames", "heads"),
        P("clips", None, "heads"),
    )
    return jax.shard_map(shards, mesh=mesh, in_specs=in_specs, out_specs=out_specs, check_vma=False)
```

time: 187 us -> 120 us (0.64)
  matrix products: 48.6 us -> 0 us
  Pallas kernels: 0 us -> 37.5 us
  local copies, waits for them, and re-layouts: 37.1 us -> 12.8 us
  between operations: 14.7 us -> 0.84 us
  starting transfers between devices: 31.1 us -> 23.1 us
  waiting for transfers between devices: 42.7 us -> 37.6 us
  blocking collectives: 3.57 us -> 0 us
    pallas_call x0 -> x5, Pallas kernels: none -> 37.5 us  [the longest x1 11.5 us: attend_call(): pl.pallas_call(functools.partial(attend_body, (head_dim, local, heads)),...]
    dot_general x25 -> x0, matrix products: 31.5 us -> none  [the longest x4 5.28 us: run_head(): jnp.einsum('qd,kd->qk', grad_head, value_head, preferred_element_type=jnp...]
    conv_general_dilated x9 -> x0, matrix products: 17.1 us -> none  [spatial_pool(): lax.conv_general_dilated(frame[None], taps, (4, 4), ((1, 1), (1, 1)), dim...]
    ppermute x16 -> x18, starting transfers between devices: 31 us -> 23.1 us  [the longest x16 22.5 us: exchange(): return lax.ppermute(block, 'frames', pairs)]
    ppermute x16 -> x18, waiting for transfers between devices: 42.7 us -> 37.6 us  [the longest x16 35.8 us: exchange(): return lax.ppermute(block, 'frames', pairs)]
    unnamed x40 -> x14, local copies, waits for them, and re-layouts: 9.07 us -> 4.13 us
    convert_element_type x6 -> x0, local copies, waits for them, and re-layouts: 4.88 us -> none  [the longest x1 2.16 us: shards(): input_grad = summed.T.astype(jnp.bfloat16).reshape(tokens.shape)]
    dynamic_slice x4 -> x0, local copies, waits for them, and re-layouts: 4.54 us -> none  [block(): return lax.dynamic_index_in_dim(low, place ^ relative, 0, False)]
  transfers between devices with their start and end apart: 17 -> 18, of which waited for: 10 -> 11; matrix products, arithmetic and copies ran while one was open for 21% -> 9% of each run, Pallas kernels for 0% -> 9%
where the time goes in v2:
time: 120 us; the launch traced here: 119 us
  waiting for transfers between devices  37.6 us (31%)
  Pallas kernels  37.5 us (31%)
  starting transfers between devices  23.1 us (19%)
  local copies, waits for them, and re-layouts  12.8 us (11%)
  other arithmetic  7.48 us (6%)
    ppermute x16, waiting for transfers between devices, exchange(): return lax.ppermute(block, 'frames', pairs)  35.8 us
    ppermute x16, starting transfers between devices, exchange(): return lax.ppermute(block, 'frames', pairs)  22.5 us
    pallas_call x1, Pallas kernels, attend_call(): pl.pallas_call(functools.partial(attend_body, (head_dim, local, heads)),...  11.5 us
    pallas_call x1, Pallas kernels, pull_call(): pl.pallas_call(functools.partial(pull_body, (rows, cols, local, count)),...  10.6 us
    pallas_call x1, Pallas kernels, query_side_call(): pl.pallas_call(functools.partial(query_side_body, (head_dim, local, local...  5.58 us
    pallas_call x1, Pallas kernels, pool_call(): pl.pallas_call(functools.partial(pool_body, (rows, cols, local)), out_sha...  5.03 us
    pallas_call x1, Pallas kernels, query_call(): pl.pallas_call(functools.partial(query_body, (head_dim, local, heads)), o...  4.78 us
    unnamed x14, local copies, waits for them, and re-layouts  4.13 us
  transfers between devices with their start and end apart: 18, of which 11 were waited for; matrix products, arithmetic and copies ran while one was open for 9% of the time, Pallas kernels for 9%

profile of v2, /device:TPU:0, one launch (start us, length us, event | category | flops | bytes accessed | tf_op | source)
XLA Modules:
  0.0 119.3 jit_solution(17093138274457200098)
XLA Ops:
  0.6 1.5 %copy.15 = bf16[896,288]{0,1:T(8,128)(2,1)S(1)} copy(bf16[896,288]{1,0:T(8,128)(2,1)} %bitcast.23) | data formatting | bytes 1032192 | tf_op jit(solution)/shard_map/reshape | solution.py:402
  2.1 0.5 collective-permute-start
  2.6 1.5 %copy.20.taps = f32[2,27,288]{2,1,0:T(8,128)} copy(f32[2,27,288]{2,0,1:T(2,128)} %param.7) | data formatting | bytes 124416 | tf_op args[3]
  4.2 1.0 copy.18
  5.2 0.6 pad_add_fusion.place
  6.0 1.4 %maximum_select_fusion.weights = bf16[3,576,288]{2,1,0:T(8,128)(2,1)} fusion(bf16[3,576,288]{2,1,0:T(8,128)(2,1)S(1)} %copy.18, bf16[3,288,288]{2,1,0:T(8,128)(2,1)S(1)} %get-tuple-element.46, bf16[3,288,288]{2,1,0:T(8,128)(2,1)S(1)} %get-tuple-element.45, pred[]{:T(512)S(6)} %eq.14), kind=kLoop, calls=%fused_computation.1 | loop fusion | flops 2488320 | bytes 2985985 | tf_op jit(solution)/shard_map/jit(_where)/select_n | solution.py:405
  7.4 1.1 copy.19.other
  8.5 5.0 %project_pool.1 = (bf16[56,576]{1,0:T(8,128)(2,1)}, bf16[56,576]{1,0:T(8,128)(2,1)}, f32[56,576]{1,0:T(8,128)}, f32[2,9,56,288]{3,2,1,0:T(8,128)}) custom-call(s32[2]{0:T(128)} %pad_add_fusion.place, bf16[896,288]{1,0:T(8,128)(2,1)} %bitcast.24, bf16[896,288]{1,0:T(8,128)(2,1)} %copy.19.other, bf16[3,576,288]{2,1,0:T(8,128)(2,1)} %maximum_select_fusion.weights, ...), custom_call_target="tpu_custom_call" | custom-call | tf_op jit(solution)/shard_map/project_pool/pallas_call | solution.py:80
  13.6 2.5 %collective-permute-start.1 = (bf16[56,576]{1,0:T(8,128)(2,1)}, bf16[56,576]{1,0:T(8,128)(2,1)S(1)}, u32[]{:S(2)}, u32[]{:S(2)}) collective-permute-start(bf16[56,576]{1,0:T(8,128)(2,1)} %get-tuple-element.18), channel_id=1, source_target_pairs={{0,2},{2,0},{4,6},{6,4},{8,10},{10,8},{12,14},{14,12},{1,3},{3,1},... | collective-permute-start | bytes 193544 | tf_op jit(solution)/shard_map/ppermute | solution.py:354
  16.1 3.5 %collective-permute-start.2 = (bf16[56,576]{1,0:T(8,128)(2,1)}, bf16[56,576]{1,0:T(8,128)(2,1)S(1)}, u32[]{:S(2)}, u32[]{:S(2)}) collective-permute-start(bf16[56,576]{1,0:T(8,128)(2,1)} %get-tuple-element.19), channel_id=1, source_target_pairs={{0,14},{2,4},{4,2},{6,8},{8,6},{10,12},{12,10},{14,0},{1,15},{3,5}... | collective-permute-start | bytes 193544 | tf_op jit(solution)/shard_map/ppermute | solution.py:354
  19.7 0.5 collective-permute-done.1
  20.1 3.2 %collective-permute-done.2 = bf16[56,576]{1,0:T(8,128)(2,1)S(1)} collective-permute-done((bf16[56,576]{1,0:T(8,128)(2,1)}, bf16[56,576]{1,0:T(8,128)(2,1)S(1)}, u32[]{:S(2)}, u32[]{:S(2)}) %collective-permute-start.2) | collective-permute-done | bytes 64544 | tf_op jit(solution)/shard_map/ppermute | solution.py:354
  23.4 0.9 constant_dynamic-update-slice_fusion.4
  24.3 1.9 %collective-permute-start.5 = (bf16[56,576]{1,0:T(8,128)(2,1)S(1)}, bf16[56,576]{1,0:T(8,128)(2,1)S(1)}, u32[]{:S(2)}, u32[]{:S(2)}) collective-permute-start(bf16[56,576]{1,0:T(8,128)(2,1)S(1)} %get-tuple-element.42), channel_id=1, source_target_pairs={{0,12},{2,14},{4,8},{6,10},{8,4},{10,6},{12,0},{14,2},{1,13},{3,15... | collective-permute-start | bytes 193544 | tf_op jit(solution)/shard_map/ppermute | solution.py:354
  26.2 2.6 %collective-permute-start.3 = (bf16[56,576]{1,0:T(8,128)(2,1)S(1)}, bf16[56,576]{1,0:T(8,128)(2,1)S(1)}, u32[]{:S(2)}, u32[]{:S(2)}) collective-permute-start(bf16[56,576]{1,0:T(8,128)(2,1)S(1)} %get-tuple-element.42), channel_id=1, source_target_pairs={{0,4},{2,6},{4,0},{6,2},{8,12},{10,14},{12,8},{14,10},{1,5},{3,7},... | collective-permute-start | bytes 193544 | tf_op jit(solution)/shard_map/ppermute | solution.py:354
  28.8 1.1 slice_bitcast_fusion
  29.9 0.8 copy.23.far_t
  30.7 0.8 copy.22.near_t
  31.5 4.8 %project_query.1 = (bf16[512,896]{1,0:T(8,128)(2,1)}, bf16[512,896]{1,0:T(8,128)(2,1)}) custom-call(bf16[896,288]{1,0:T(8,128)(2,1)} %bitcast.25, bf16[896,288]{1,0:T(8,128)(2,1)} %copy.19.other, bf16[288,288]{1,0:T(8,128)(2,1)} %copy.22.near_t, bf16[288,288]{1,0:T(8,128)(2,1)} %copy.23.far_t, bf16[896,288]{1,0:T(8,128)(2,1)} %bitcast.28), custom_call_target="tpu_custom_call" | custom-call | tf_op jit(solution)/shard_map/project_query/pallas_call | solution.py:120
  36.8 6.9 %collective-permute-done.6 = bf16[224,576]{1,0:T(8,128)(2,1)S(1)} collective-permute-done((bf16[224,576]{1,0:T(8,128)(2,1)S(1)}, bf16[224,576]{1,0:T(8,128)(2,1)S(1)}, u32[]{:S(2)}, u32[]{:S(2)}) %collective-permute-start.6) | collective-permute-done | bytes 258080 | tf_op jit(solution)/shard_map/ppermute | solution.py:354
  43.8 0.8 copy-done.3
  44.6 11.5 %attend_backward.1 = (bf16[448,576]{1,0:T(8,128)(2,1)}, bf16[896,512]{1,0:T(8,128)(2,1)}) custom-call(bf16[448,576]{1,0:T(8,128)(2,1)} %copy-done.3, bf16[512,896]{1,0:T(8,128)(2,1)} %get-tuple-element.20.query_t, bf16[512,896]{1,0:T(8,128)(2,1)} %get-tuple-element.21.grad_t), custom_call_target="tpu_custom_call" | custom-call | tf_op jit(solution)/shard_map/attend_backward/pallas_call | solution.py:179
  56.1 1.0 slice.78
  57.1 0.7 collective-permute-start.7
  57.8 6.0 %collective-permute-done.7 = bf16[224,576]{1,0:T(8,128)(2,1)S(1)} collective-permute-done((bf16[224,576]{1,0:T(8,128)(2,1)S(1)}, bf16[224,576]{1,0:T(8,128)(2,1)S(1)}, u32[]{:S(2)}, u32[]{:S(2)}) %collective-permute-start.7) | collective-permute-done | bytes 258080 | tf_op jit(solution)/shard_map/ppermute | solution.py:354
  63.8 1.1 convert_add_fusion.1
  65.3 2.6 %collective-permute-start.10 = (bf16[56,576]{1,0:T(8,128)(2,1)S(1)}, bf16[56,576]{1,0:T(8,128)(2,1)S(1)}, u32[]{:S(2)}, u32[]{:S(2)}) collective-permute-start(bf16[56,576]{1,0:T(8,128)(2,1)S(1)} %get-tuple-element.57), channel_id=1, source_target_pairs={{0,12},{2,14},{4,8},{6,10},{8,4},{10,6},{12,0},{14,2},{1,13},{3,15... | collective-permute-start | bytes 193544 | tf_op jit(solution)/shard_map/ppermute | solution.py:354
  67.9 0.5 collective-permute-start.9
  68.4 1.5 %collective-permute-done.8 = bf16[56,576]{1,0:T(8,128)(2,1)S(1)} collective-permute-done((bf16[56,576]{1,0:T(8,128)(2,1)S(1)}, bf16[56,576]{1,0:T(8,128)(2,1)S(1)}, u32[]{:S(2)}, u32[]{:S(2)}) %collective-permute-start.8) | collective-permute-done | bytes 64544 | tf_op jit(solution)/shard_map/ppermute | solution.py:354
  69.9 1.6 %collective-permute-done.10 = bf16[56,576]{1,0:T(8,128)(2,1)S(1)} collective-permute-done((bf16[56,576]{1,0:T(8,128)(2,1)S(1)}, bf16[56,576]{1,0:T(8,128)(2,1)S(1)}, u32[]{:S(2)}, u32[]{:S(2)}) %collective-permute-start.10) | collective-permute-done | bytes 64544 | tf_op jit(solution)/shard_map/ppermute | solution.py:354
  71.5 3.0 %collective-permute-done.9 = bf16[56,576]{1,0:T(8,128)(2,1)S(1)} collective-permute-done((bf16[56,576]{1,0:T(8,128)(2,1)S(1)}, bf16[56,576]{1,0:T(8,128)(2,1)S(1)}, u32[]{:S(2)}, u32[]{:S(2)}) %collective-permute-start.9) | collective-permute-done | bytes 64544 | tf_op jit(solution)/shard_map/ppermute | solution.py:354
  74.5 0.7 fusion.6
  75.2 0.8 collective-permute-start.12
  76.1 2.0 %collective-permute-start.11 = (bf16[56,576]{1,0:T(8,128)(2,1)S(1)}, bf16[56,576]{1,0:T(8,128)(2,1)S(1)}, u32[]{:S(2)}, u32[]{:S(2)}) collective-permute-start(bf16[56,576]{1,0:T(8,128)(2,1)S(1)} %get-tuple-element.39), channel_id=1, source_target_pairs={{0,14},{2,4},{4,2},{6,8},{8,6},{10,12},{12,10},{14,0},{1,15},{3,5}... | collective-permute-start | bytes 193544 | tf_op jit(solution)/shard_map/ppermute | solution.py:354
  78.0 5.6 %query_side.1 = (f32[576,288]{1,0:T(8,128)}, f32[2,896,288]{2,1,0:T(8,128)}) custom-call(bf16[896,512]{1,0:T(8,128)(2,1)} %get-tuple-element.24.query_pad, bf16[896,288]{1,0:T(8,128)(2,1)} %bitcast.26, bf16[896,288]{1,0:T(8,128)(2,1)} %copy.19.other, bf16[3,576,288]{2,1,0:T(8,128)(2,1)} %maximum_select_fusion.weights), custom_call_target="tpu_custom_call" | custom-call | tf_op jit(solution)/shard_map/query_side/pallas_call | solution.py:213
  83.6 0.7 broadcast_select_fusion
  84.3 10.6 %pull_back.1 = (f32[320,864]{1,0:T(8,128)}, bf16[320,864]{1,0:T(8,128)(2,1)}, f32[896,288]{1,0:T(8,128)}, bf16[896,288]{1,0:T(8,128)(2,1)}) custom-call(s32[2]{0:T(128)} %pad_add_fusion.place, f32[56,576]{1,0:T(8,128)} %get-tuple-element.40.mine, bf16[56,576]{1,0:T(8,128)(2,1)} %get-tuple-element.60.before, bf16[56,576]{1,0:T(8,128)(2,1)} %get-tuple-element.59.after, ...), custom_call_target="tpu_custom_call" | custom-call | tf_op jit(solution)/shard_map/pull_back/pallas_call | solution.py:323
  94.9 1.5 %copy.27 = bf16[896,288]{0,1:T(8,128)(2,1)S(1)} copy(bf16[896,288]{1,0:T(8,128)(2,1)} %get-tuple-element.28) | data formatting | bytes 1032192 | tf_op jit(solution)/shard_map/pull_back/pallas_call | solution.py:323
  96.5 1.9 %collective-permute-done.13 = bf16[896,288]{0,1:T(8,128)(2,1)S(1)} collective-permute-done((bf16[896,288]{0,1:T(8,128)(2,1)S(1)}, bf16[896,288]{0,1:T(8,128)(2,1)S(1)}, u32[]{:S(2)}, u32[]{:S(2)}) %collective-permute-start.13) | collective-permute-done | bytes 516128 | tf_op jit(solution)/shard_map/ppermute | solution.py:432
  98.7 6.1 %collective-permute-done.14 = bf16[320,864]{1,0:T(8,128)(2,1)S(1)} collective-permute-done((bf16[320,864]{1,0:T(8,128)(2,1)}, bf16[320,864]{1,0:T(8,128)(2,1)S(1)}, u32[]{:S(2)}, u32[]{:S(2)}) %collective-permute-start.14) | collective-permute-done | bytes 552992 | tf_op jit(solution)/shard_map/ppermute | solution.py:354
  105.1 0.8 collective-permute-start.15
  105.8 1.2 %collective-permute-start.16 = (bf16[104,864]{1,0:T(8,128)(2,1)S(1)}, bf16[104,864]{1,0:T(8,128)(2,1)S(1)}, u32[]{:S(2)}, u32[]{:S(2)}) collective-permute-start(bf16[104,864]{1,0:T(8,128)(2,1)S(1)} %get-tuple-element.62), channel_id=1, source_target_pairs={{0,8},{2,10},{4,12},{6,14},{8,0},{10,2},{12,4},{14,6},{1,9},{3,11}... | collective-permute-start | bytes 539144 | tf_op jit(solution)/shard_map/ppermute | solution.py:354
  107.0 2.5 %collective-permute-start.17 = (bf16[104,864]{1,0:T(8,128)(2,1)S(1)}, bf16[104,864]{1,0:T(8,128)(2,1)S(1)}, u32[]{:S(2)}, u32[]{:S(2)}) collective-permute-start(bf16[104,864]{1,0:T(8,128)(2,1)S(1)} %concatenate.29), channel_id=1, source_target_pairs={{0,12},{2,14},{4,8},{6,10},{8,4},{10,6},{12,0},{14,2},{1,13},{3,15... | collective-permute-start | bytes 539144 | tf_op jit(solution)/shard_map/ppermute | solution.py:354
  109.5 1.0 add_convert_fusion
  110.6 1.8 %collective-permute-done.15 = bf16[104,864]{1,0:T(8,128)(2,1)S(1)} collective-permute-done((bf16[104,864]{1,0:T(8,128)(2,1)S(1)}, bf16[104,864]{1,0:T(8,128)(2,1)S(1)}, u32[]{:S(2)}, u32[]{:S(2)}) %collective-permute-start.15) | collective-permute-done | bytes 179744 | tf_op jit(solution)/shard_map/ppermute | solution.py:354
  112.4 5.2 %collective-permute-done.16 = bf16[104,864]{1,0:T(8,128)(2,1)S(1)} collective-permute-done((bf16[104,864]{1,0:T(8,128)(2,1)S(1)}, bf16[104,864]{1,0:T(8,128)(2,1)S(1)}, u32[]{:S(2)}, u32[]{:S(2)}) %collective-permute-start.16) | collective-permute-done | bytes 179744 | tf_op jit(solution)/shard_map/ppermute | solution.py:354
  117.9 0.7 copy.29
  118.6 0.8 pad_maximum_fusion
  (38 shorter events, 2.1 us)
Async XLA Ops:
  0.6 3.5 %copy-start.2 = (bf16[3,576,288]{1,2,0:T(8,128)(2,1)S(1)}, bf16[3,576,288]{1,2,0:T(8,128)(2,1)}, u32[]{:S(2)}) copy-start(bf16[3,576,288]{1,2,0:T(8,128)(2,1)} %param.6) | copy-start | bytes 2985988
  2.1 5.3 %collective-permute-start = (bf16[896,288]{0,1:T(8,128)(2,1)S(1)}, bf16[896,288]{0,1:T(8,128)(2,1)S(1)}, u32[]{:S(2)}, u32[]{:S(2)}) collective-permute-start(bf16[896,288]{0,1:T(8,128)(2,1)S(1)} %copy.15), channel_id=1, source_target_pairs={{0,1},{1,0},{2,3},{3,2},{4,5},{5,4},{6,7},{7,6},{8,9},{9,8},{10,11... | collective-permute-start | bytes 1548296 | tf_op jit(solution)/shard_map/ppermute | solution.py:404
  13.6 6.6 %collective-permute-start.1 = (bf16[56,576]{1,0:T(8,128)(2,1)}, bf16[56,576]{1,0:T(8,128)(2,1)S(1)}, u32[]{:S(2)}, u32[]{:S(2)}) collective-permute-start(bf16[56,576]{1,0:T(8,128)(2,1)} %get-tuple-element.18), channel_id=1, source_target_pairs={{0,2},{2,0},{4,6},{6,4},{8,10},{10,8},{12,14},{14,12},{1,3},{3,1},... | collective-permute-start | bytes 193544 | tf_op jit(solution)/shard_map/ppermute | solution.py:354
  16.1 7.2 %collective-permute-start.2 = (bf16[56,576]{1,0:T(8,128)(2,1)}, bf16[56,576]{1,0:T(8,128)(2,1)S(1)}, u32[]{:S(2)}, u32[]{:S(2)}) collective-permute-start(bf16[56,576]{1,0:T(8,128)(2,1)} %get-tuple-element.19), channel_id=1, source_target_pairs={{0,14},{2,4},{4,2},{6,8},{8,6},{10,12},{12,10},{14,0},{1,15},{3,5}... | collective-permute-start | bytes 193544 | tf_op jit(solution)/shard_map/ppermute | solution.py:354
  24.3 12.0 %collective-permute-start.5 = (bf16[56,576]{1,0:T(8,128)(2,1)S(1)}, bf16[56,576]{1,0:T(8,128)(2,1)S(1)}, u32[]{:S(2)}, u32[]{:S(2)}) collective-permute-start(bf16[56,576]{1,0:T(8,128)(2,1)S(1)} %get-tuple-element.42), channel_id=1, source_target_pairs={{0,12},{2,14},{4,8},{6,10},{8,4},{10,6},{12,0},{14,2},{1,13},{3,15... | collective-permute-start | bytes 193544 | tf_op jit(solution)/shard_map/ppermute | solution.py:354
  26.2 10.1 %collective-permute-start.4 = (bf16[56,576]{1,0:T(8,128)(2,1)S(1)}, bf16[56,576]{1,0:T(8,128)(2,1)S(1)}, u32[]{:S(2)}, u32[]{:S(2)}) collective-permute-start(bf16[56,576]{1,0:T(8,128)(2,1)S(1)} %get-tuple-element.42), channel_id=1, source_target_pairs={{0,8},{2,10},{4,12},{6,14},{8,0},{10,2},{12,4},{14,6},{1,9},{3,11}... | collective-permute-start | bytes 193544 | tf_op jit(solution)/shard_map/ppermute | solution.py:354
  26.2 10.1 %collective-permute-start.3 = (bf16[56,576]{1,0:T(8,128)(2,1)S(1)}, bf16[56,576]{1,0:T(8,128)(2,1)S(1)}, u32[]{:S(2)}, u32[]{:S(2)}) collective-permute-start(bf16[56,576]{1,0:T(8,128)(2,1)S(1)} %get-tuple-element.42), channel_id=1, source_target_pairs={{0,4},{2,6},{4,0},{6,2},{8,12},{10,14},{12,8},{14,10},{1,5},{3,7},... | collective-permute-start | bytes 193544 | tf_op jit(solution)/shard_map/ppermute | solution.py:354
  36.4 7.4 %collective-permute-start.6 = (bf16[224,576]{1,0:T(8,128)(2,1)S(1)}, bf16[224,576]{1,0:T(8,128)(2,1)S(1)}, u32[]{:S(2)}, u32[]{:S(2)}) collective-permute-start(bf16[224,576]{1,0:T(8,128)(2,1)S(1)} %pad_maximum_fusion.1), channel_id=1, source_target_pairs={{0,2},{2,0},{4,6},{6,4},{8,10},{10,8},{12,14},{14,12},{1,3},{3,1},... | collective-permute-start | bytes 774152 | tf_op jit(solution)/shard_map/ppermute | solution.py:354
  43.8 0.8 copy-start.3
  57.1 6.7 %collective-permute-start.7 = (bf16[224,576]{1,0:T(8,128)(2,1)S(1)}, bf16[224,576]{1,0:T(8,128)(2,1)S(1)}, u32[]{:S(2)}, u32[]{:S(2)}) collective-permute-start(bf16[224,576]{1,0:T(8,128)(2,1)S(1)} %slice.78), channel_id=1, source_target_pairs={{0,2},{2,0},{4,6},{6,4},{8,10},{10,8},{12,14},{14,12},{1,3},{3,1},... | collective-permute-start | bytes 774152 | tf_op jit(solution)/shard_map/ppermute | solution.py:354
  64.9 5.0 %collective-permute-start.8 = (bf16[56,576]{1,0:T(8,128)(2,1)S(1)}, bf16[56,576]{1,0:T(8,128)(2,1)S(1)}, u32[]{:S(2)}, u32[]{:S(2)}) collective-permute-start(bf16[56,576]{1,0:T(8,128)(2,1)S(1)} %get-tuple-element.56), channel_id=1, source_target_pairs={{0,4},{2,6},{4,0},{6,2},{8,12},{10,14},{12,8},{14,10},{1,5},{3,7},... | collective-permute-start | bytes 193544 | tf_op jit(solution)/shard_map/ppermute | solution.py:354
  65.3 6.2 %collective-permute-start.10 = (bf16[56,576]{1,0:T(8,128)(2,1)S(1)}, bf16[56,576]{1,0:T(8,128)(2,1)S(1)}, u32[]{:S(2)}, u32[]{:S(2)}) collective-permute-start(bf16[56,576]{1,0:T(8,128)(2,1)S(1)} %get-tuple-element.57), channel_id=1, source_target_pairs={{0,12},{2,14},{4,8},{6,10},{8,4},{10,6},{12,0},{14,2},{1,13},{3,15... | collective-permute-start | bytes 193544 | tf_op jit(solution)/shard_map/ppermute | solution.py:354
  67.9 6.7 %collective-permute-start.9 = (bf16[56,576]{1,0:T(8,128)(2,1)S(1)}, bf16[56,576]{1,0:T(8,128)(2,1)S(1)}, u32[]{:S(2)}, u32[]{:S(2)}) collective-permute-start(bf16[56,576]{1,0:T(8,128)(2,1)S(1)} %get-tuple-element.58), channel_id=1, source_target_pairs={{0,8},{2,10},{4,12},{6,14},{8,0},{10,2},{12,4},{14,6},{1,9},{3,11}... | collective-permute-start | bytes 193544 | tf_op jit(solution)/shard_map/ppermute | solution.py:354
  75.2 8.4 %collective-permute-start.12 = (bf16[56,576]{1,0:T(8,128)(2,1)S(1)}, bf16[56,576]{1,0:T(8,128)(2,1)S(1)}, u32[]{:S(2)}, u32[]{:S(2)}) collective-permute-start(bf16[56,576]{1,0:T(8,128)(2,1)S(1)} %get-tuple-element.39), channel_id=1, source_target_pairs={{0,2},{2,0},{4,6},{6,4},{8,10},{10,8},{12,14},{14,12},{1,3},{3,1},... | collective-permute-start | bytes 193544 | tf_op jit(solution)/shard_map/ppermute | solution.py:354
  76.1 7.5 %collective-permute-start.11 = (bf16[56,576]{1,0:T(8,128)(2,1)S(1)}, bf16[56,576]{1,0:T(8,128)(2,1)S(1)}, u32[]{:S(2)}, u32[]{:S(2)}) collective-permute-start(bf16[56,576]{1,0:T(8,128)(2,1)S(1)} %get-tuple-element.39), channel_id=1, source_target_pairs={{0,14},{2,4},{4,2},{6,8},{8,6},{10,12},{12,10},{14,0},{1,15},{3,5}... | collective-permute-start | bytes 193544 | tf_op jit(solution)/shard_map/ppermute | solution.py:354
  94.9 9.9 %copy-start.1 = (f32[320,864]{1,0:T(8,128)S(1)}, f32[320,864]{1,0:T(8,128)}, u32[]{:S(2)}) copy-start(f32[320,864]{1,0:T(8,128)} %get-tuple-element.29) | copy-start | bytes 3317764
  94.9 9.9 %collective-permute-start.14 = (bf16[320,864]{1,0:T(8,128)(2,1)}, bf16[320,864]{1,0:T(8,128)(2,1)S(1)}, u32[]{:S(2)}, u32[]{:S(2)}) collective-permute-start(bf16[320,864]{1,0:T(8,128)(2,1)} %get-tuple-element.30), channel_id=1, source_target_pairs={{0,2},{2,0},{4,6},{6,4},{8,10},{10,8},{12,14},{14,12},{1,3},{3,1},... | collective-permute-start | bytes 1658888 | tf_op jit(solution)/shard_map/ppermute | solution.py:354
  96.4 2.0 %collective-permute-start.13 = (bf16[896,288]{0,1:T(8,128)(2,1)S(1)}, bf16[896,288]{0,1:T(8,128)(2,1)S(1)}, u32[]{:S(2)}, u32[]{:S(2)}) collective-permute-start(bf16[896,288]{0,1:T(8,128)(2,1)S(1)} %copy.27), channel_id=1, source_target_pairs={{0,1},{1,0},{2,3},{3,2},{4,5},{5,4},{6,7},{7,6},{8,9},{9,8},{10,11... | collective-permute-start | bytes 1548296 | tf_op jit(solution)/shard_map/ppermute | solution.py:432
  104.9 4.6 %copy-start = (f32[896,288]{1,0:T(8,128)S(1)}, f32[896,288]{1,0:T(8,128)}, u32[]{:S(2)}) copy-start(f32[896,288]{1,0:T(8,128)} %get-tuple-element.27) | copy-start | bytes 3096580
  105.1 7.4 %collective-permute-start.15 = (bf16[104,864]{1,0:T(8,128)(2,1)S(1)}, bf16[104,864]{1,0:T(8,128)(2,1)S(1)}, u32[]{:S(2)}, u32[]{:S(2)}) collective-permute-start(bf16[104,864]{1,0:T(8,128)(2,1)S(1)} %get-tuple-element.61), channel_id=1, source_target_pairs={{0,4},{2,6},{4,0},{6,2},{8,12},{10,14},{12,8},{14,10},{1,5},{3,7},... | collective-permute-start | bytes 539144 | tf_op jit(solution)/shard_map/ppermute | solution.py:354
  105.8 11.7 %collective-permute-start.16 = (bf16[104,864]{1,0:T(8,128)(2,1)S(1)}, bf16[104,864]{1,0:T(8,128)(2,1)S(1)}, u32[]{:S(2)}, u32[]{:S(2)}) collective-permute-start(bf16[104,864]{1,0:T(8,128)(2,1)S(1)} %get-tuple-element.62), channel_id=1, source_target_pairs={{0,8},{2,10},{4,12},{6,14},{8,0},{10,2},{12,4},{14,6},{1,9},{3,11}... | collective-permute-start | bytes 539144 | tf_op jit(solution)/shard_map/ppermute | solution.py:354
  107.0 10.5 %collective-permute-start.17 = (bf16[104,864]{1,0:T(8,128)(2,1)S(1)}, bf16[104,864]{1,0:T(8,128)(2,1)S(1)}, u32[]{:S(2)}, u32[]{:S(2)}) collective-permute-start(bf16[104,864]{1,0:T(8,128)(2,1)S(1)} %concatenate.29), channel_id=1, source_target_pairs={{0,12},{2,14},{4,8},{6,10},{8,4},{10,6},{12,0},{14,2},{1,13},{3,15... | collective-permute-start | bytes 539144 | tf_op jit(solution)/shard_map/ppermute | solution.py:354

commit v3 on v2

v3 whole, which is shorter than its diff:
```python
import functools
import math

import jax
import jax.numpy as jnp
from jax import lax
from jax.experimental import pallas as pl
from jax.experimental.pallas import tpu as pltpu
from jax.sharding import PartitionSpec as P

HEADS = 8
LANES = 128
F32 = jnp.float32
BF16 = jnp.bfloat16
PARAMS = pltpu.CompilerParams(vmem_limit_bytes=16 * 1024 * 1024)
NN = (((1,), (0,)), ((), ()))
NT = (((1,), (1,)), ((), ()))
TN = (((0,), (0,)), ((), ()))


def mul(left, right, dims=NN):
    return lax.dot_general(left, right, dims, preferred_element_type=F32)


def near_core(*arrays):
    return tuple(pltpu.with_memory_space_constraint(x, pltpu.VMEM) for x in arrays)


def vmem():
    return pl.BlockSpec(memory_space=pltpu.VMEM)


def smem():
    return pl.BlockSpec(memory_space=pltpu.SMEM)


def lane_tiles(channels):
    return [
        (k, k * LANES, min(LANES, channels - k * LANES)) for k in range(pl.cdiv(channels, LANES))
    ]


def round_up(size, step):
    return pl.cdiv(size, step) * step


def pool_body(
    geometry, place, own, other, weights, taps, to_pair, to_next, inner, stored, windows, wide
):
    rows, cols, local = geometry
    pooled_rows, pooled_cols = rows // 4, cols // 4
    even = place[0] % 2 == 0
    first = place[1] == 0
    mine, theirs = own[:, :local].astype(F32), other[:, :local].astype(F32)
    low_half = jnp.where(first, mine, theirs)
    high_half = jnp.where(first, theirs, mine)
    joined = jnp.concatenate([low_half, high_half], axis=1).astype(BF16)
    starts = lax.broadcasted_iota(jnp.int32, (pooled_cols, LANES), 0) == 0
    for side in range(2):
        full = mul(joined, weights[side + 1], NT).astype(BF16).astype(F32)
        for tile, low, width in lane_tiles(local):
            wide[tile, 0:8, :] = jnp.zeros((8, LANES), F32)
            wide[tile, 8:, :width] = full[:, low : low + width]
            for b in range(3):
                for e in range(3):
                    for i in range(pooled_rows):
                        row = 4 * i + b - 1
                        if row < 0:
                            piece = jnp.zeros((pooled_cols, LANES), F32)
                        else:
                            piece = wide[tile, pl.ds(row * cols + e + 7, pooled_cols, stride=4), :]
                            if e == 0:
                                piece = jnp.where(starts, 0.0, piece)
                        at = slice(i * pooled_cols, (i + 1) * pooled_cols)
                        windows[3 * b + e, at, low : low + width] = piece[:, :width]
        for k in range(9):
            stored[side, k] = windows[k].astype(BF16)
        sums = []
        for a in range(3):
            total = windows[0] * taps[9 * a, side : side + 1, :]
            for k in range(1, 9):
                total = total + windows[k] * taps[9 * a + k, side : side + 1, :]
            sums.append(total)
        lanes = slice(side * local, (side + 1) * local)
        earlier, center, later = sums
        to_pair[:, lanes] = center.astype(BF16)
        to_next[:, lanes] = jnp.where(even, later, earlier).astype(BF16)
        inner[:, lanes] = jnp.where(even, earlier, later)


def pool_call(place, own, other, weights, taps, rows, cols):
    local = weights.shape[1]
    count = rows * cols // 16
    return pl.pallas_call(
        functools.partial(pool_body, (rows, cols, local)),
        out_shape=(
            pltpu.VMEM((count, 2 * local), BF16),
            pltpu.VMEM((count, 2 * local), BF16),
            pltpu.VMEM((count, 2 * local), F32),
            jax.ShapeDtypeStruct((2, 9, count, local), BF16),
        ),
        in_specs=[smem()] + [vmem()] * 4,
        out_specs=(vmem(),) * 4,
        scratch_shapes=[
            pltpu.VMEM((9, count, local), F32),
            pltpu.VMEM((pl.cdiv(local, LANES), rows * cols + 8, LANES), F32)],
        compiler_params=PARAMS,
        name="project_pool",
    )(place, *near_core(own, other), weights, taps)


def spread_rows(head_dim, local, heads):
    rows = lax.broadcasted_iota(jnp.int32, (heads * LANES, local), 0)
    cols = lax.broadcasted_iota(jnp.int32, (heads * LANES, local), 1)
    chosen = rows < 0
    for h in range(heads):
        inside = (cols >= h * head_dim) & (cols < (h + 1) * head_dim)
        chosen = chosen | (inside & (rows == cols + h * (LANES - head_dim)))
    return chosen.astype(F32).astype(BF16)


def identity(size):
    rows = lax.broadcasted_iota(jnp.int32, (size, size), 0)
    cols = lax.broadcasted_iota(jnp.int32, (size, size), 1)
    return (rows == cols).astype(F32).astype(BF16)


def query_body(geometry, place, own, other, weights, out_grad, query_t, grad_t, tokens_t):
    head_dim, local, heads = geometry
    spread = spread_rows(head_dim, local, heads)
    turn = identity(local)
    near = pl.multiple_of(place[1] * local, 16)
    far = pl.multiple_of((1 - place[1]) * local, 16)
    tokens_t[pl.ds(near, local), :] = mul(turn, own[:, :local], NT).astype(BF16)
    tokens_t[pl.ds(far, local), :] = mul(turn, other[:, :local], NT).astype(BF16)
    query_t[...] = mul(mul(spread, weights[0]).astype(BF16), tokens_t[...]).astype(BF16)
    grad_t[...] = mul(spread, out_grad[...], NT).astype(BF16)


def query_call(place, own, other, weights, out_grad, head_dim):
    tokens, local = out_grad.shape
    heads = local // head_dim
    shape = pltpu.VMEM((heads * LANES, tokens), BF16)
    return pl.pallas_call(
        functools.partial(query_body, (head_dim, local, heads)),
        out_shape=(shape, shape, pltpu.VMEM((2 * local, tokens), BF16)),
        in_specs=[smem()] + [vmem()] * 4,
        out_specs=(vmem(),) * 3,
        compiler_params=PARAMS,
        name="project_query",
    )(place, *near_core(own, other), weights, out_grad)


def choose_head(head_dim, local, head):
    rows = lax.broadcasted_iota(jnp.int32, (2 * local, 2 * LANES), 0)
    cols = lax.broadcasted_iota(jnp.int32, (2 * local, 2 * LANES), 1)
    lane = cols % LANES
    source = lane + (cols // LANES) * local + head * head_dim
    return ((rows == source) & (lane < head_dim)).astype(F32).astype(BF16)


def head_products(head_dim, keys, chosen, query, grad):
    both = mul(keys, chosen).astype(BF16)
    key, value = both[:, :LANES], both[:, LANES:]
    factor = head_dim ** (-0.5) * math.log2(math.e)
    raised = jnp.exp2(mul(key, query) * factor)
    return key, raised, mul(value, grad)


def measure_body(geometry, keys, query_t, grad_t, sums):
    head_dim, local, heads = geometry
    chosen = choose_head(head_dim, local, pl.program_id(0))
    key, raised, prob_grad = head_products(head_dim, keys[...], chosen, query_t[...], grad_t[...])
    sums[0, 0:1, :] = jnp.sum(raised, axis=0, keepdims=True)
    sums[0, 1:2, :] = jnp.sum(raised * prob_grad, axis=0, keepdims=True)


def attend_body(geometry, final, keys, query_t, grad_t, sums, *rest):
    head_dim, local, heads = geometry
    if final:
        partial_t, key_grads, query_grad, total = rest
    else:
        key_grads, totals, partial_t, total = rest
    head = pl.program_id(0)
    scale = head_dim ** (-0.5)
    chosen = choose_head(head_dim, local, head)
    query, grad = query_t[...], grad_t[...]
    key, raised, prob_grad = head_products(head_dim, keys[...], chosen, query, grad)
    if final:
        inverse, centre = sums[0, 0:1, :], sums[0, 1:2, :]
    else:
        inverse = 1.0 / (sums[0, 0:1, :] + jnp.sum(raised, axis=0, keepdims=True))
        weighted = sums[0, 1:2, :] + jnp.sum(raised * prob_grad, axis=0, keepdims=True)
        centre = weighted * inverse
        totals[0, 0:1, :] = inverse
        totals[0, 1:2, :] = centre
    probs = raised * inverse
    score_grad = (probs * (prob_grad - centre) * scale).astype(BF16)
    value_back = mul(probs.astype(BF16), grad, NT)
    key_back = mul(score_grad, query, NT)
    key_t = mul(identity(LANES), key, NT).astype(BF16)
    back_t = mul(key_t, score_grad)
    if final:
        query_grad[...] = (back_t + partial_t[...] + grad.astype(F32)).T.astype(BF16)
    else:
        partial_t[...] = back_t
    joined = jnp.concatenate([key_back, value_back], axis=1).astype(BF16)
    placed = mul(joined, chosen, NT)

    @pl.when(head == 0)
    def _():
        total[...] = placed

    @pl.when(head > 0)
    def _():
        total[...] += placed

    @pl.when(head == heads - 1)
    def _():
        key_grads[...] = total[...].astype(BF16)


def attend_specs(keys, query_t):
    key_count, both = keys.shape
    tokens = query_t.shape[1]
    key_spec = pl.BlockSpec((key_count, both), lambda h: (0, 0))
    lane_spec = pl.BlockSpec((LANES, tokens), lambda h: (h, 0))
    sum_spec = pl.BlockSpec((1, 8, tokens), lambda h: (h, 0, 0))
    return key_spec, lane_spec, sum_spec


def measure_call(keys, query_t, grad_t, head_dim):
    local, tokens = keys.shape[1] // 2, query_t.shape[1]
    heads = local // head_dim
    key_spec, lane_spec, sum_spec = attend_specs(keys, query_t)
    return pl.pallas_call(
        functools.partial(measure_body, (head_dim, local, heads)),
        grid=(heads,),
        out_shape=pltpu.VMEM((heads, 8, tokens), F32),
        in_specs=[key_spec, lane_spec, lane_spec],
        out_specs=sum_spec,
        compiler_params=PARAMS,
        name="attend_measure",
    )(*near_core(keys, query_t, grad_t))


def attend_call(keys, query_t, grad_t, sums, head_dim):
    key_count, both = keys.shape
    local, tokens = both // 2, query_t.shape[1]
    heads = local // head_dim
    key_spec, lane_spec, sum_spec = attend_specs(keys, query_t)
    return pl.pallas_call(
        functools.partial(attend_body, (head_dim, local, heads), False),
        grid=(heads,),
        out_shape=(
            pltpu.VMEM((key_count, both), BF16),
            pltpu.VMEM((heads, 8, tokens), F32),
            pltpu.VMEM((heads * LANES, tokens), F32),
        ),
        in_specs=[key_spec, lane_spec, lane_spec, sum_spec],
        out_specs=(key_spec, sum_spec, lane_spec),
        scratch_shapes=[pltpu.VMEM((key_count, both), F32)],
        compiler_params=PARAMS,
        name="attend_other",
    )(*near_core(keys, query_t, grad_t, sums))


def attend_final_call(keys, query_t, grad_t, totals, partial_t, head_dim):
    key_count, both = keys.shape
    local, tokens = both // 2, query_t.shape[1]
    heads = local // head_dim
    key_spec, lane_spec, sum_spec = attend_specs(keys, query_t)
    return pl.pallas_call(
        functools.partial(attend_body, (head_dim, local, heads), True),
        grid=(heads,),
        out_shape=(
            pltpu.VMEM((key_count, both), BF16),
            pltpu.VMEM((tokens, heads * LANES), BF16),
        ),
        in_specs=[key_spec, lane_spec, lane_spec, sum_spec, lane_spec],
        out_specs=(key_spec, pl.BlockSpec((tokens, LANES), lambda h: (0, h))),
        scratch_shapes=[pltpu.VMEM((key_count, both), F32)],
        compiler_params=PARAMS,
        name="attend_same",
    )(*near_core(keys, query_t, grad_t, totals, partial_t))


def store_blocks(position, count, rows, columns, here, away):
    padded = round_up(rows, 8)
    for j in range(count):
        relative = position ^ j
        at = pl.multiple_of((relative // 2) * padded, 8)
        block = slice(j * rows, (j + 1) * rows)
        value = jnp.concatenate([column[block, :] for column in columns], axis=1)

        @pl.when(relative % 2 == 0)
        def _(value=value, at=at):
            here[pl.ds(at, rows), : value.shape[1]] = value

        @pl.when(relative % 2 == 1)
        def _(value=value, at=at):
            away[pl.ds(at, rows), : value.shape[1]] = value.astype(BF16)


def query_side_body(geometry, place, query_pad, tokens_t, query_back, here, away):
    head_dim, local, heads, count = geometry
    spread = spread_rows(head_dim, local, heads)
    back = mul(query_pad[...], spread).astype(BF16)
    query_back[...] = back
    here[...] = jnp.zeros(here.shape, F32)
    away[...] = jnp.zeros(away.shape, BF16)
    column = mul(tokens_t[...], back)
    store_blocks(place[0], count, 2 * local // count, [column], here, away)


def query_side_call(place, query_pad, tokens_t, head_dim, count):
    both, tokens = tokens_t.shape
    local = both // 2
    shape = (count // 2 * round_up(both // count, 8), round_up(local, LANES))
    return pl.pallas_call(
        functools.partial(query_side_body, (head_dim, local, local // head_dim, count)),
        out_shape=(
            pltpu.VMEM((tokens, local), BF16),
            pltpu.VMEM(shape, F32),
            pltpu.VMEM(shape, BF16),
        ),
        in_specs=[smem()] + [vmem()] * 2,
        out_specs=(vmem(),) * 3,
        compiler_params=PARAMS,
        name="query_side",
    )(place, *near_core(query_pad, tokens_t))


def pull_body(
    geometry,
    place,
    mine,
    swapped,
    beside,
    windows,
    taps,
    tokens_t,
    weights,
    query_back,
    here,
    away,
    token_near,
    token_far,
    wide,
    staged,
    folded,
):
    rows, cols, local, count = geometry
    pooled_rows, pooled_cols = rows // 4, cols // 4
    position, core = place[0], place[1]
    even = position % 2 == 0
    pooled = pooled_rows * pooled_cols
    block_rows = 2 * local // count
    outer = count // 2
    starts = lax.broadcasted_iota(jnp.int32, (pooled, local), 0) % pooled_cols == 0
    folded[...] = jnp.zeros(folded.shape, F32)
    here[...] = jnp.zeros(here.shape, F32)
    away[...] = jnp.zeros(away.shape, BF16)
    token_sum = mul(query_back[...], weights[0])
    columns = []
    for side in range(2):
        lanes = slice(side * local, (side + 1) * local)
        partner, distant = swapped[:, lanes].astype(F32), beside[:, lanes].astype(F32)
        grads = [
            jnp.where(even, partner, distant),
            mine[:, lanes].astype(F32),
            jnp.where(even, distant, partner),
        ]
        wide[...] = jnp.zeros(wide.shape, F32)
        for b in range(3):
            for e in range(3):
                k = 3 * b + e
                window = windows[side, k].astype(F32)
                spread = None
                for a in range(3):
                    term = grads[a] * taps[9 * a + k, side : side + 1, :]
                    spread = term if spread is None else spread + term
                    tap = jnp.sum(grads[a] * window, axis=0, keepdims=True)
                    folded[9 * a + k : 9 * a + k + 1, lanes] = tap
                if e == 0:
                    spread = jnp.where(starts, 0.0, spread)
                for tile, low, width in lane_tiles(local):
                    part = spread[:, low : low + width]
                    if width < LANES:
                        part = jnp.concatenate(
                            [part, jnp.zeros((pooled, LANES - width), F32)], axis=1
                        )
                    staged[tile] = part
                    for i in range(pooled_rows):
                        row = 4 * i + b - 1
                        if row >= 0:
                            at = slice(i * pooled_cols, (i + 1) * pooled_cols)
                            wide[tile, pl.ds(row * cols + e + 7, pooled_cols, stride=4), :] = (
                                staged[tile, at, :]
                            )
        back = jnp.concatenate(
            [wide[tile, 8:, :width] for tile, low, width in lane_tiles(local)], axis=1
        ).astype(BF16)
        token_sum = token_sum + mul(back, weights[side + 1])
        columns.append(mul(tokens_t[...], back))
    first = core == 0
    low_half, high_half = token_sum[:, :local], token_sum[:, local:]
    token_near[...] = jnp.where(first, low_half, high_half)
    token_far[:, :local] = jnp.where(first, high_half, low_half).astype(BF16)
    token_far[:, local:] = jnp.zeros((token_far.shape[0], token_far.shape[1] - local), BF16)
    blocks_end = outer * round_up(block_rows, 8)
    here[blocks_end:, :] = folded[...]
    away[blocks_end:, :] = folded[...].astype(BF16)
    store_blocks(position, count, block_rows, columns, here, away)


def pull_call(
    place, mine, swapped, beside, windows, taps, tokens_t, weights, query_back, rows, cols, count
):
    both, tokens = tokens_t.shape
    local = both // 2
    size = count // 2 * round_up(both // count, 8) + 32
    tiles = pl.cdiv(local, LANES)
    return pl.pallas_call(
        functools.partial(pull_body, (rows, cols, local, count)),
        out_shape=(
            pltpu.VMEM((size, both), F32),
            pltpu.VMEM((size, both), BF16),
            pltpu.VMEM((tokens, local), F32),
            pltpu.VMEM((tokens, tiles * LANES), BF16),
        ),
        in_specs=[smem()] + [vmem()] * 8,
        out_specs=(vmem(),) * 4,
        scratch_shapes=[
            pltpu.VMEM((tiles, tokens + 8, LANES), F32),
            pltpu.VMEM((tiles, rows * cols // 16, LANES), F32),
            pltpu.VMEM((32, both), F32),
        ],
        compiler_params=PARAMS,
        name="pull_back",
    )(
        place,
        *near_core(mine, swapped, beside),
        windows,
        taps,
        *near_core(tokens_t),
        weights,
        *near_core(query_back),
    )


def frame_pairs(step, flip):
    count = lax.axis_size("frames")
    return [(i, i ^ (2 * step + flip)) for i in range(count)]


def outer_pairs(direction):
    count = lax.axis_size("frames")
    moves = [(i, i + direction * (2 if i % 2 else -2)) for i in range(count)]
    return [(i, j) for i, j in moves if 0 <= j < count]


def exchange(block, pairs):
    return lax.ppermute(block, "frames", pairs)


def across(block):
    return lax.ppermute(block, "heads", [(0, 1), (1, 0)])


def scatter_weights(here, moved, rows):
    outer = lax.axis_size("frames") // 2
    summed = here + moved.astype(F32)
    end = outer * rows
    own = jnp.concatenate([summed[:rows], summed[end:]])
    low = summed.astype(BF16)
    pieces = []
    for step in range(1, outer):
        piece = jnp.concatenate([low[step * rows : (step + 1) * rows], low[end:]])
        pieces.append(exchange(piece, frame_pairs(step, 0)))
    return own, pieces


def add_all(own, pieces):
    for piece in pieces:
        own = own + piece.astype(F32)
    return own


def shards(tokens, out_grad, w_qkv, pool_kernel):
    local = tokens.shape[-1]
    heads_here = HEADS // lax.axis_size("heads")
    head_dim = local // heads_here
    rows, cols = tokens.shape[1], tokens.shape[2]
    token_count = rows * cols
    count = lax.axis_size("frames")
    frame = lax.axis_index("frames")
    core = lax.axis_index("heads")
    place = jnp.stack([frame, core]).astype(jnp.int32)
    outer = count // 2
    spare = round_up(local, LANES) - local
    own = jnp.pad(tokens.reshape(token_count, local), ((0, 0), (0, spare)))
    grad = out_grad.reshape(token_count, local)
    other = across(own)
    weights = w_qkv.transpose(0, 2, 1)
    taps = pool_kernel.transpose(1, 0, 2)
    to_pair, to_next, inner, windows = pool_call(place, own, other, weights, taps, rows, cols)
    from_next = exchange(to_next, outer_pairs(1))
    from_pair = exchange(to_pair, frame_pairs(0, 1))
    block = (inner + from_pair.astype(F32) + from_next.astype(F32)).astype(BF16)
    others = [exchange(block, frame_pairs(s, 0)) for s in range(1, outer)]
    query_t, grad_t, tokens_t = query_call(place, own, other, weights, grad, head_dim)
    others, query_t, grad_t, tokens_t = lax.optimization_barrier(
        (others, query_t, grad_t, tokens_t)
    )
    same_keys = jnp.concatenate([block] + others)
    other_keys = exchange(same_keys, frame_pairs(0, 1))
    sums = measure_call(same_keys, query_t, grad_t, head_dim)
    other_grads, totals, partial_t = attend_call(other_keys, query_t, grad_t, sums, head_dim)
    moved = exchange(other_grads, frame_pairs(0, 1))
    same_grads, query_pad = attend_final_call(
        same_keys, query_t, grad_t, totals, partial_t, head_dim
    )
    summed = same_grads.astype(F32) + moved.astype(F32)
    step_rows = block.shape[0]
    low = summed.astype(BF16)
    pieces = [
        exchange(low[s * step_rows : (s + 1) * step_rows], frame_pairs(s, 0))
        for s in range(1, outer)
    ]
    query_back, query_here, query_away = query_side_call(
        place, query_pad, tokens_t, head_dim, count
    )
    query_moved = exchange(query_away, frame_pairs(0, 1))
    pieces, query_back, query_here = lax.optimization_barrier((pieces, query_back, query_here))
    swapped = add_all(summed[:step_rows], pieces).astype(BF16)
    beside = exchange(swapped, outer_pairs(-1))
    mine = exchange(swapped, frame_pairs(0, 1))
    block_rows = 2 * local // count
    padded = round_up(block_rows, 8)
    query_own, query_pieces = scatter_weights(query_here, query_moved, padded)
    beside, mine, query_pieces = lax.optimization_barrier((beside, mine, query_pieces))
    here, away, near, far = pull_call(
        place, mine, swapped, beside, windows, taps, tokens_t, weights, query_back, rows, cols, count
    )
    moved = exchange(away, frame_pairs(0, 1))
    query_sum = add_all(query_own, query_pieces)[:block_rows, :local]
    input_grad = (near + across(far)[:, :local].astype(F32)).astype(BF16)
    own_sum, pieces = scatter_weights(here, moved, padded)
    pieces, input_grad, query_sum = lax.optimization_barrier((pieces, input_grad, query_sum))
    total = add_all(own_sum, pieces)
    weight_grad = jnp.stack([query_sum, total[:block_rows, :local], total[:block_rows, local:]])
    tail = total[padded : padded + 27]
    kernel_grad = jnp.stack([tail[:, :local], tail[:, local:]])
    return input_grad.reshape(tokens.shape), weight_grad, kernel_grad


def solution(mesh):
    in_specs = (
        P(("clips", "frames"), None, None, "heads"),
        P(("clips", "frames"), None, None, "heads"),
        P(None, None, "heads"),
        P(None, None, "heads"),
    )
    out_specs = (
        P(("clips", "frames"), None, None, "heads"),
        P("clips", "frames", "heads"),
        P("clips", None, "heads"),
    )
    return jax.shard_map(shards, mesh=mesh, in_specs=in_specs, out_specs=out_specs, check_vma=False)
```

time: 120 us -> 91 us (0.76)
  waiting for transfers between devices: 37.6 us -> 24.7 us
  local copies, waits for them, and re-layouts: 12.8 us -> 2.26 us
  Pallas kernels: 37.5 us -> 27.3 us
  starting transfers between devices: 23.1 us -> 33.2 us
  other arithmetic: 7.48 us -> 2.39 us
    ppermute x16 -> x20, waiting for transfers between devices: 35.8 us -> 23 us  [exchange(): return lax.ppermute(block, 'frames', pairs)]
    ppermute x16 -> x20, starting transfers between devices: 22.5 us -> 32.6 us  [exchange(): return lax.ppermute(block, 'frames', pairs)]
    pallas_call x1, Pallas kernels: 10.6 us -> 5.54 us  [pull_call(): pl.pallas_call(functools.partial(pull_body, (rows, cols, local, count)),...]
    pallas_call x1, Pallas kernels: 5.58 us -> 1.94 us  [query_side_call(): pl.pallas_call(functools.partial(query_side_body, (head_dim, local, local...]
    unnamed x14 -> x7, local copies, waits for them, and re-layouts: 4.13 us -> 0.71 us
    pallas_call x1 -> x3, Pallas kernels: 11.5 us -> 14.4 us  [the longest x1 5.89 us: attend_call(): pl.pallas_call(functools.partial(attend_body, (head_dim, local, heads), F...]
    transpose x3 -> x0, local copies, waits for them, and re-layouts: 2.76 us -> none  [the longest x2 1.92 us: shards(): weights[0, local:]]
    pallas_call x1, Pallas kernels: 5.03 us -> 2.42 us  [pool_call(): pl.pallas_call(functools.partial(pool_body, (rows, cols, local)), out_sha...]
  transfers between devices with their start and end apart: 18 -> 22, of which waited for: 11 -> 10; matrix products, arithmetic and copies ran while one was open for 9% -> 2% of each run, Pallas kernels for 9% -> 15%
where the time goes in v3:
time: 91 us; the launch traced here: 90.8 us
  starting transfers between devices  33.2 us (36%)
  Pallas kernels  27.3 us (30%)
  waiting for transfers between devices  24.7 us (27%)
  other arithmetic  2.39 us (3%)
  local copies, waits for them, and re-layouts  2.26 us (2%)
    ppermute x20, starting transfers between devices, exchange(): return lax.ppermute(block, 'frames', pairs)  32.6 us
    ppermute x20, waiting for transfers between devices, exchange(): return lax.ppermute(block, 'frames', pairs)  23 us
    pallas_call x1, Pallas kernels, attend_call(): pl.pallas_call(functools.partial(attend_body, (head_dim, local, heads), F...  5.89 us
    pallas_call x1, Pallas kernels, attend_final_call(): pl.pallas_call(functools.partial(attend_body, (head_dim, local, heads), T...  5.59 us
    pallas_call x1, Pallas kernels, pull_call(): pl.pallas_call(functools.partial(pull_body, (rows, cols, local, count)),...  5.54 us
    pallas_call x1, Pallas kernels, query_call(): pl.pallas_call(functools.partial(query_body, (head_dim, local, heads)), o...  2.99 us
    pallas_call x1, Pallas kernels, measure_call(): pl.pallas_call(functools.partial(measure_body, (head_dim, local, heads)),...  2.92 us
    pallas_call x1, Pallas kernels, pool_call(): pl.pallas_call(functools.partial(pool_body, (rows, cols, local)), out_sha...  2.42 us
  transfers between devices with their start and end apart: 22, of which 10 were waited for; matrix products, arithmetic and copies ran while one was open for 2% of the time, Pallas kernels for 15%

profile of v3, /device:TPU:0, one launch (start us, length us, event | category | flops | bytes accessed | tf_op | source)
XLA Modules:
  0.0 90.8 jit_solution(13346625747739890544)
XLA Ops:
  0.7 1.3 %pad.4.own = bf16[896,384]{1,0:T(8,128)(2,1)S(1)} pad(bf16[896,288]{1,0:T(8,128)(2,1)} %bitcast.22, bf16[]{:T(256)} %constant.10.clone.1), padding=0_0x0_96 | pad | bytes 1204226 | tf_op jit(solution)/shard_map/jit(_pad)/pad | solution.py:502
  1.9 0.5 collective-permute-start
  2.4 0.1 pad_add_fusion.place
  2.5 1.7 %collective-permute-done.other = bf16[896,384]{1,0:T(8,128)(2,1)S(1)} collective-permute-done((bf16[896,384]{1,0:T(8,128)(2,1)S(1)}, bf16[896,384]{1,0:T(8,128)(2,1)S(1)}, u32[]{:S(2)}, u32[]{:S(2)}) %collective-permute-start) | collective-permute-done | bytes 688160 | tf_op jit(solution)/shard_map/ppermute | solution.py:468
  4.2 2.4 %project_pool.1 = (bf16[56,576]{1,0:T(8,128)(2,1)S(1)}, bf16[56,576]{1,0:T(8,128)(2,1)S(1)}, f32[56,576]{1,0:T(8,128)S(1)}, bf16[2,9,56,288]{3,2,1,0:T(8,128)(2,1)S(1)}) custom-call(s32[2]{0:T(128)S(1)} %pad_add_fusion.place, bf16[896,384]{1,0:T(8,128)(2,1)S(1)} %pad.4.own, bf16[896,384]{1,0:T(8,128)(2,1)S(1)} %collective-permute-done.other, ...), custom_call_target="tpu_custom_call" | custom-call | tf_op jit(solution)/shard_map/project_pool/pallas_call | solution.py:94
  6.6 3.0 %collective-permute-start.1 = (bf16[56,576]{1,0:T(8,128)(2,1)S(1)}, bf16[56,576]{1,0:T(8,128)(2,1)S(1)}, u32[]{:S(2)}, u32[]{:S(2)}) collective-permute-start(bf16[56,576]{1,0:T(8,128)(2,1)S(1)} %get-tuple-element.44), channel_id=1, source_target_pairs={{0,2},{2,0},{4,6},{6,4},{8,10},{10,8},{12,14},{14,12},{1,3},{3,1},... | collective-permute-start | bytes 193544 | tf_op jit(solution)/shard_map/ppermute | solution.py:464
  9.6 1.3 %collective-permute-start.2 = (bf16[56,576]{1,0:T(8,128)(2,1)S(1)}, bf16[56,576]{1,0:T(8,128)(2,1)S(1)}, u32[]{:S(2)}, u32[]{:S(2)}) collective-permute-start(bf16[56,576]{1,0:T(8,128)(2,1)S(1)} %get-tuple-element.45), channel_id=1, source_target_pairs={{2,6},{4,0},{6,10},{8,4},{10,14},{12,8},{3,7},{5,1},{7,11},{9,5},{... | collective-permute-start | bytes 193544 | tf_op jit(solution)/shard_map/ppermute | solution.py:464
  10.9 1.2 %collective-permute-done.1 = bf16[56,576]{1,0:T(8,128)(2,1)S(1)} collective-permute-done((bf16[56,576]{1,0:T(8,128)(2,1)S(1)}, bf16[56,576]{1,0:T(8,128)(2,1)S(1)}, u32[]{:S(2)}, u32[]{:S(2)}) %collective-permute-start.1) | collective-permute-done | bytes 64544 | tf_op jit(solution)/shard_map/ppermute | solution.py:464
  12.1 3.7 %collective-permute-done.2 = bf16[56,576]{1,0:T(8,128)(2,1)S(1)} collective-permute-done((bf16[56,576]{1,0:T(8,128)(2,1)S(1)}, bf16[56,576]{1,0:T(8,128)(2,1)S(1)}, u32[]{:S(2)}, u32[]{:S(2)}) %collective-permute-start.2) | collective-permute-done | bytes 64544 | tf_op jit(solution)/shard_map/ppermute | solution.py:464
  15.8 1.7 %collective-permute-start.5 = (bf16[56,576]{1,0:T(8,128)(2,1)S(1)}, bf16[56,576]{1,0:T(8,128)(2,1)S(1)}, u32[]{:S(2)}, u32[]{:S(2)}) collective-permute-start(bf16[56,576]{1,0:T(8,128)(2,1)S(1)} %add_convert_fusion.1), channel_id=1, source_target_pairs={{0,12},{2,14},{4,8},{6,10},{8,4},{10,6},{12,0},{14,2},{1,13},{3,15... | collective-permute-start | bytes 193544 | tf_op jit(solution)/shard_map/ppermute | solution.py:464
  17.6 1.4 %collective-permute-start.4 = (bf16[56,576]{1,0:T(8,128)(2,1)S(1)}, bf16[56,576]{1,0:T(8,128)(2,1)S(1)}, u32[]{:S(2)}, u32[]{:S(2)}) collective-permute-start(bf16[56,576]{1,0:T(8,128)(2,1)S(1)} %add_convert_fusion.1), channel_id=1, source_target_pairs={{0,8},{2,10},{4,12},{6,14},{8,0},{10,2},{12,4},{14,6},{1,9},{3,11}... | collective-permute-start | bytes 193544 | tf_op jit(solution)/shard_map/ppermute | solution.py:464
  19.0 1.3 %collective-permute-start.3 = (bf16[56,576]{1,0:T(8,128)(2,1)S(1)}, bf16[56,576]{1,0:T(8,128)(2,1)S(1)}, u32[]{:S(2)}, u32[]{:S(2)}) collective-permute-start(bf16[56,576]{1,0:T(8,128)(2,1)S(1)} %add_convert_fusion.1), channel_id=1, source_target_pairs={{0,4},{2,6},{4,0},{6,2},{8,12},{10,14},{12,8},{14,10},{1,5},{3,7},... | collective-permute-start | bytes 193544 | tf_op jit(solution)/shard_map/ppermute | solution.py:464
  20.3 3.0 %project_query.1 = (bf16[512,896]{1,0:T(8,128)(2,1)S(1)}, bf16[512,896]{1,0:T(8,128)(2,1)S(1)}, bf16[576,896]{1,0:T(8,128)(2,1)S(1)}) custom-call(s32[2]{0:T(128)S(1)} %pad_add_fusion.place, bf16[896,384]{1,0:T(8,128)(2,1)S(1)} %pad.4.own, bf16[896,384]{1,0:T(8,128)(2,1)S(1)} %collective-permute-done.other, bf16[3,288,576]{2,1,0:T(8,128)(2,1)S(1)} %bitcast.17, ...), custom_call_target="tpu_custom_call" | custom-call | tf_op jit(solution)/shard_map/project_query/pallas_call | solution.py:144
  23.3 1.1 %collective-permute-done.4 = bf16[56,576]{1,0:T(8,128)(2,1)S(1)} collective-permute-done((bf16[56,576]{1,0:T(8,128)(2,1)S(1)}, bf16[56,576]{1,0:T(8,128)(2,1)S(1)}, u32[]{:S(2)}, u32[]{:S(2)}) %collective-permute-start.4) | collective-permute-done | bytes 64544 | tf_op jit(solution)/shard_map/ppermute | solution.py:464
  24.5 1.2 %collective-permute-start.6 = (bf16[224,576]{1,0:T(8,128)(2,1)S(1)}, bf16[224,576]{1,0:T(8,128)(2,1)S(1)}, u32[]{:S(2)}, u32[]{:S(2)}) collective-permute-start(bf16[224,576]{1,0:T(8,128)(2,1)S(1)} %pad_maximum_fusion.1.keys), channel_id=1, source_target_pairs={{0,2},{2,0},{4,6},{6,4},{8,10},{10,8},{12,14},{14,12},{1,3},{3,1},... | collective-permute-start | bytes 774152 | tf_op jit(solution)/shard_map/ppermute | solution.py:464
  25.6 2.9 %attend_measure.1.sums = f32[4,8,896]{2,1,0:T(8,128)S(1)} custom-call(bf16[224,576]{1,0:T(8,128)(2,1)S(1)} %pad_maximum_fusion.1.keys, bf16[512,896]{1,0:T(8,128)(2,1)S(1)} %get-tuple-element.52.query_t, bf16[512,896]{1,0:T(8,128)(2,1)S(1)} %get-tuple-element.53.grad_t), custom_call_target="tpu_custom_call" | custom-call | tf_op jit(solution)/shard_map/attend_measure/pallas_call | solution.py:236
  28.6 3.5 %collective-permute-done.6.keys = bf16[224,576]{1,0:T(8,128)(2,1)S(1)} collective-permute-done((bf16[224,576]{1,0:T(8,128)(2,1)S(1)}, bf16[224,576]{1,0:T(8,128)(2,1)S(1)}, u32[]{:S(2)}, u32[]{:S(2)}) %collective-permute-start.6) | collective-permute-done | bytes 258080 | tf_op jit(solution)/shard_map/ppermute | solution.py:464
  32.1 5.9 %attend_other.1 = (bf16[224,576]{1,0:T(8,128)(2,1)S(1)}, f32[4,8,896]{2,1,0:T(8,128)S(1)}, f32[512,896]{1,0:T(8,128)S(1)}) custom-call(bf16[224,576]{1,0:T(8,128)(2,1)S(1)} %collective-permute-done.6.keys, bf16[512,896]{1,0:T(8,128)(2,1)S(1)} %get-tuple-element.52.query_t, bf16[512,896]{1,0:T(8,128)(2,1)S(1)} %get-tuple-element.53.grad_t, ...), custom_call_target="tpu_custom_call" | custom-call | tf_op jit(solution)/shard_map/attend_other/pallas_call | solution.py:252
  38.0 1.8 %collective-permute-start.7 = (bf16[224,576]{1,0:T(8,128)(2,1)S(1)}, bf16[224,576]{1,0:T(8,128)(2,1)S(1)}, u32[]{:S(2)}, u32[]{:S(2)}) collective-permute-start(bf16[224,576]{1,0:T(8,128)(2,1)S(1)} %get-tuple-element.57), channel_id=1, source_target_pairs={{0,2},{2,0},{4,6},{6,4},{8,10},{10,8},{12,14},{14,12},{1,3},{3,1},... | collective-permute-start | bytes 774152 | tf_op jit(solution)/shard_map/ppermute | solution.py:464
  39.8 5.6 %attend_same.1 = (bf16[224,576]{1,0:T(8,128)(2,1)S(1)}, bf16[896,512]{1,0:T(8,128)(2,1)S(1)}) custom-call(bf16[224,576]{1,0:T(8,128)(2,1)S(1)} %pad_maximum_fusion.1.keys, bf16[512,896]{1,0:T(8,128)(2,1)S(1)} %get-tuple-element.52.query_t, bf16[512,896]{1,0:T(8,128)(2,1)S(1)} %get-tuple-element.53.grad_t, f32[4,8,896]{2,1,0:T(8,128)S(1)} %get-tuple-element.54.sums, ...), custom_call_target="tpu_custom_call" | custom-call | tf_op jit(solution)/shard_map/attend_same/pallas_call | solution.py:273
  45.4 0.1 fusion.7
  45.5 2.1 %collective-permute-start.10 = (bf16[56,576]{1,0:T(8,128)(2,1)S(1)}, bf16[56,576]{1,0:T(8,128)(2,1)S(1)}, u32[]{:S(2)}, u32[]{:S(2)}) collective-permute-start(bf16[56,576]{1,0:T(8,128)(2,1)S(1)} %get-tuple-element.94), channel_id=1, source_target_pairs={{0,12},{2,14},{4,8},{6,10},{8,4},{10,6},{12,0},{14,2},{1,13},{3,15... | collective-permute-start | bytes 193544 | tf_op jit(solution)/shard_map/ppermute | solution.py:464
  47.6 2.4 %collective-permute-start.8 = (bf16[56,576]{1,0:T(8,128)(2,1)S(1)}, bf16[56,576]{1,0:T(8,128)(2,1)S(1)}, u32[]{:S(2)}, u32[]{:S(2)}) collective-permute-start(bf16[56,576]{1,0:T(8,128)(2,1)S(1)} %get-tuple-element.96), channel_id=1, source_target_pairs={{0,4},{2,6},{4,0},{6,2},{8,12},{10,14},{12,8},{14,10},{1,5},{3,7},... | collective-permute-start | bytes 193544 | tf_op jit(solution)/shard_map/ppermute | solution.py:464
  50.0 1.9 %query_side.1 = (bf16[896,288]{1,0:T(8,128)(2,1)S(1)}, f32[288,384]{1,0:T(8,128)S(1)}, bf16[288,384]{1,0:T(8,128)(2,1)S(1)}) custom-call(s32[2]{0:T(128)S(1)} %pad_add_fusion.place, bf16[896,512]{1,0:T(8,128)(2,1)S(1)} %get-tuple-element.58.query_pad, bf16[576,896]{1,0:T(8,128)(2,1)S(1)} %get-tuple-element.59.tokens_t), custom_call_target="tpu_custom_call" | custom-call | tf_op jit(solution)/shard_map/query_side/pallas_call | solution.py:320
  51.9 1.7 %collective-permute-start.13 = (bf16[288,384]{1,0:T(8,128)(2,1)S(1)}, bf16[288,384]{1,0:T(8,128)(2,1)S(1)}, u32[]{:S(2)}, u32[]{:S(2)}) collective-permute-start(bf16[288,384]{1,0:T(8,128)(2,1)S(1)} %get-tuple-element.66), channel_id=1, source_target_pairs={{0,2},{2,0},{4,6},{6,4},{8,10},{10,8},{12,14},{14,12},{1,3},{3,1},... | collective-permute-start | bytes 663560 | tf_op jit(solution)/shard_map/ppermute | solution.py:464
  53.7 1.3 %collective-permute-start.12 = (bf16[56,576]{1,0:T(8,128)(2,1)S(1)}, bf16[56,576]{1,0:T(8,128)(2,1)S(1)}, u32[]{:S(2)}, u32[]{:S(2)}) collective-permute-start(bf16[56,576]{1,0:T(8,128)(2,1)S(1)} %fusion.4.swapped), channel_id=1, source_target_pairs={{0,2},{2,0},{4,6},{6,4},{8,10},{10,8},{12,14},{14,12},{1,3},{3,1},... | collective-permute-start | bytes 193544 | tf_op jit(solution)/shard_map/ppermute | solution.py:464
  55.0 3.1 %collective-permute-start.11 = (bf16[56,576]{1,0:T(8,128)(2,1)S(1)}, bf16[56,576]{1,0:T(8,128)(2,1)S(1)}, u32[]{:S(2)}, u32[]{:S(2)}) collective-permute-start(bf16[56,576]{1,0:T(8,128)(2,1)S(1)} %fusion.4.swapped), channel_id=1, source_target_pairs={{0,4},{4,8},{6,2},{8,12},{10,6},{14,10},{1,5},{5,9},{7,3},{9,13},{... | collective-permute-start | bytes 193544 | tf_op jit(solution)/shard_map/ppermute | solution.py:464
  58.2 1.8 %collective-permute-start.16 = (bf16[72,384]{1,0:T(8,128)(2,1)S(1)}, bf16[72,384]{1,0:T(8,128)(2,1)S(1)}, u32[]{:S(2)}, u32[]{:S(2)}) collective-permute-start(bf16[72,384]{1,0:T(8,128)(2,1)S(1)} %get-tuple-element.101), channel_id=1, source_target_pairs={{0,12},{2,14},{4,8},{6,10},{8,4},{10,6},{12,0},{14,2},{1,13},{3,15... | collective-permute-start | bytes 165896 | tf_op jit(solution)/shard_map/ppermute | solution.py:464
  60.1 0.1 collective-permute-start.15
  60.2 2.5 %collective-permute-start.14 = (bf16[72,384]{1,0:T(8,128)(2,1)S(1)}, bf16[72,384]{1,0:T(8,128)(2,1)S(1)}, u32[]{:S(2)}, u32[]{:S(2)}) collective-permute-start(bf16[72,384]{1,0:T(8,128)(2,1)S(1)} %get-tuple-element.103), channel_id=1, source_target_pairs={{0,4},{2,6},{4,0},{6,2},{8,12},{10,14},{12,8},{14,10},{1,5},{3,7},... | collective-permute-start | bytes 165896 | tf_op jit(solution)/shard_map/ppermute | solution.py:464
  62.7 1.6 %collective-permute-done.16 = bf16[72,384]{1,0:T(8,128)(2,1)S(1)} collective-permute-done((bf16[72,384]{1,0:T(8,128)(2,1)S(1)}, bf16[72,384]{1,0:T(8,128)(2,1)S(1)}, u32[]{:S(2)}, u32[]{:S(2)}) %collective-permute-start.16) | collective-permute-done | bytes 55328 | tf_op jit(solution)/shard_map/ppermute | solution.py:464
  64.3 1.2 %collective-permute-done.15 = bf16[72,384]{1,0:T(8,128)(2,1)S(1)} collective-permute-done((bf16[72,384]{1,0:T(8,128)(2,1)S(1)}, bf16[72,384]{1,0:T(8,128)(2,1)S(1)}, u32[]{:S(2)}, u32[]{:S(2)}) %collective-permute-start.15) | collective-permute-done | bytes 55328 | tf_op jit(solution)/shard_map/ppermute | solution.py:464
  65.5 5.5 %pull_back.1 = (f32[320,576]{1,0:T(8,128)S(1)}, bf16[320,576]{1,0:T(8,128)(2,1)S(1)}, f32[896,288]{1,0:T(8,128)S(1)}, bf16[896,384]{1,0:T(8,128)(2,1)S(1)}) custom-call(s32[2]{0:T(128)S(1)} %pad_add_fusion.place, bf16[56,576]{1,0:T(8,128)(2,1)S(1)} %collective-permute-done.12.mine, bf16[56,576]{1,0:T(8,128)(2,1)S(1)} %fusion.4.swapped, ...), custom_call_target="tpu_custom_call" | custom-call | tf_op jit(solution)/shard_map/pull_back/pallas_call | solution.py:424
  71.0 1.5 %collective-permute-start.17 = (bf16[320,576]{1,0:T(8,128)(2,1)S(1)}, bf16[320,576]{1,0:T(8,128)(2,1)S(1)}, u32[]{:S(2)}, u32[]{:S(2)}) collective-permute-start(bf16[320,576]{1,0:T(8,128)(2,1)S(1)} %get-tuple-element.72), channel_id=1, source_target_pairs={{0,2},{2,0},{4,6},{6,4},{8,10},{10,8},{12,14},{14,12},{1,3},{3,1},... | collective-permute-start | bytes 1105928 | tf_op jit(solution)/shard_map/ppermute | solution.py:464
  72.5 0.1 collective-permute-start.21
  72.6 6.4 %collective-permute-done.17 = bf16[320,576]{1,0:T(8,128)(2,1)S(1)} collective-permute-done((bf16[320,576]{1,0:T(8,128)(2,1)S(1)}, bf16[320,576]{1,0:T(8,128)(2,1)S(1)}, u32[]{:S(2)}, u32[]{:S(2)}) %collective-permute-start.17) | collective-permute-done | bytes 368672 | tf_op jit(solution)/shard_map/ppermute | solution.py:464
  79.0 0.1 fusion.8
  79.3 1.8 %collective-permute-start.19 = (bf16[104,576]{1,0:T(8,128)(2,1)S(1)}, bf16[104,576]{1,0:T(8,128)(2,1)S(1)}, u32[]{:S(2)}, u32[]{:S(2)}) collective-permute-start(bf16[104,576]{1,0:T(8,128)(2,1)S(1)} %get-tuple-element.104), channel_id=1, source_target_pairs={{0,8},{2,10},{4,12},{6,14},{8,0},{10,2},{12,4},{14,6},{1,9},{3,11}... | collective-permute-start | bytes 359432 | tf_op jit(solution)/shard_map/ppermute | solution.py:464
  81.0 0.6 collective-permute-start.18
  81.7 2.0 %collective-permute-start.20 = (bf16[104,576]{1,0:T(8,128)(2,1)S(1)}, bf16[104,576]{1,0:T(8,128)(2,1)S(1)}, u32[]{:S(2)}, u32[]{:S(2)}) collective-permute-start(bf16[104,576]{1,0:T(8,128)(2,1)S(1)} %concatenate.20), channel_id=1, source_target_pairs={{0,12},{2,14},{4,8},{6,10},{8,4},{10,6},{12,0},{14,2},{1,13},{3,15... | collective-permute-start | bytes 359432 | tf_op jit(solution)/shard_map/ppermute | solution.py:464
  83.7 1.0 %add_convert_fusion = bf16[896,288]{1,0:T(8,128)(2,1)} fusion(f32[896,288]{1,0:T(8,128)S(1)} %get-tuple-element.73, bf16[896,384]{1,0:T(8,128)(2,1)S(1)} %collective-permute-done.21), kind=kLoop, calls=%fused_computation | loop fusion | flops 774144 | bytes 2064384 | tf_op jit(solution)/shard_map/convert_element_type | solution.py:548
  84.8 1.9 %collective-permute-done.19 = bf16[104,576]{1,0:T(8,128)(2,1)S(1)} collective-permute-done((bf16[104,576]{1,0:T(8,128)(2,1)S(1)}, bf16[104,576]{1,0:T(8,128)(2,1)S(1)}, u32[]{:S(2)}, u32[]{:S(2)}) %collective-permute-start.19) | collective-permute-done | bytes 119840 | tf_op jit(solution)/shard_map/ppermute | solution.py:464
  86.7 2.4 %collective-permute-done.20 = bf16[104,576]{1,0:T(8,128)(2,1)S(1)} collective-permute-done((bf16[104,576]{1,0:T(8,128)(2,1)S(1)}, bf16[104,576]{1,0:T(8,128)(2,1)S(1)}, u32[]{:S(2)}, u32[]{:S(2)}) %collective-permute-start.20) | collective-permute-done | bytes 119840 | tf_op jit(solution)/shard_map/ppermute | solution.py:464
  89.1 0.1 fusion.1
  89.1 0.1 slice_bitcast_fusion.3
  89.2 0.1 slice_bitcast_fusion.1
  89.3 0.7 copy.7
  90.0 0.8 pad_maximum_fusion
  (34 shorter events, 0.4 us)
Async XLA Ops:
  0.6 3.6 %copy-start.2 = (f32[2,27,288]{2,0,1:T(2,128)S(1)}, f32[2,27,288]{2,0,1:T(2,128)}, u32[]{:S(2)}) copy-start(f32[2,27,288]{2,0,1:T(2,128)} %param.7) | copy-start | bytes 186628
  0.6 3.6 %copy-start = (bf16[3,576,288]{1,2,0:T(8,128)(2,1)S(1)}, bf16[3,576,288]{1,2,0:T(8,128)(2,1)}, u32[]{:S(2)}) copy-start(bf16[3,576,288]{1,2,0:T(8,128)(2,1)} %param.6) | copy-start | bytes 2985988
  1.9 2.3 %collective-permute-start = (bf16[896,384]{1,0:T(8,128)(2,1)S(1)}, bf16[896,384]{1,0:T(8,128)(2,1)S(1)}, u32[]{:S(2)}, u32[]{:S(2)}) collective-permute-start(bf16[896,384]{1,0:T(8,128)(2,1)S(1)} %pad.4.own), channel_id=1, source_target_pairs={{0,1},{1,0},{2,3},{3,2},{4,5},{5,4},{6,7},{7,6},{8,9},{9,8},{10,11... | collective-permute-start | bytes 2064392 | tf_op jit(solution)/shard_map/ppermute | solution.py:468
  4.2 16.1 %copy-start.1 = (bf16[1,16,56,288]{3,2,1,0:T(8,128)(2,1)S(1)}, bf16[1,16,56,288]{3,2,1,0:T(8,128)(2,1)}, u32[]{:S(2)}) copy-start(bf16[1,16,56,288]{3,2,1,0:T(8,128)(2,1)} %param.5) | copy-start | bytes 1548292
  6.6 5.5 %collective-permute-start.1 = (bf16[56,576]{1,0:T(8,128)(2,1)S(1)}, bf16[56,576]{1,0:T(8,128)(2,1)S(1)}, u32[]{:S(2)}, u32[]{:S(2)}) collective-permute-start(bf16[56,576]{1,0:T(8,128)(2,1)S(1)} %get-tuple-element.44), channel_id=1, source_target_pairs={{0,2},{2,0},{4,6},{6,4},{8,10},{10,8},{12,14},{14,12},{1,3},{3,1},... | collective-permute-start | bytes 193544 | tf_op jit(solution)/shard_map/ppermute | solution.py:464
  9.6 6.2 %collective-permute-start.2 = (bf16[56,576]{1,0:T(8,128)(2,1)S(1)}, bf16[56,576]{1,0:T(8,128)(2,1)S(1)}, u32[]{:S(2)}, u32[]{:S(2)}) collective-permute-start(bf16[56,576]{1,0:T(8,128)(2,1)S(1)} %get-tuple-element.45), channel_id=1, source_target_pairs={{2,6},{4,0},{6,10},{8,4},{10,14},{12,8},{3,7},{5,1},{7,11},{9,5},{... | collective-permute-start | bytes 193544 | tf_op jit(solution)/shard_map/ppermute | solution.py:464
  15.8 7.5 %collective-permute-start.5 = (bf16[56,576]{1,0:T(8,128)(2,1)S(1)}, bf16[56,576]{1,0:T(8,128)(2,1)S(1)}, u32[]{:S(2)}, u32[]{:S(2)}) collective-permute-start(bf16[56,576]{1,0:T(8,128)(2,1)S(1)} %add_convert_fusion.1), channel_id=1, source_target_pairs={{0,12},{2,14},{4,8},{6,10},{8,4},{10,6},{12,0},{14,2},{1,13},{3,15... | collective-permute-start | bytes 193544 | tf_op jit(solution)/shard_map/ppermute | solution.py:464
  17.6 6.8 %collective-permute-start.4 = (bf16[56,576]{1,0:T(8,128)(2,1)S(1)}, bf16[56,576]{1,0:T(8,128)(2,1)S(1)}, u32[]{:S(2)}, u32[]{:S(2)}) collective-permute-start(bf16[56,576]{1,0:T(8,128)(2,1)S(1)} %add_convert_fusion.1), channel_id=1, source_target_pairs={{0,8},{2,10},{4,12},{6,14},{8,0},{10,2},{12,4},{14,6},{1,9},{3,11}... | collective-permute-start | bytes 193544 | tf_op jit(solution)/shard_map/ppermute | solution.py:464
  19.0 5.5 %collective-permute-start.3 = (bf16[56,576]{1,0:T(8,128)(2,1)S(1)}, bf16[56,576]{1,0:T(8,128)(2,1)S(1)}, u32[]{:S(2)}, u32[]{:S(2)}) collective-permute-start(bf16[56,576]{1,0:T(8,128)(2,1)S(1)} %add_convert_fusion.1), channel_id=1, source_target_pairs={{0,4},{2,6},{4,0},{6,2},{8,12},{10,14},{12,8},{14,10},{1,5},{3,7},... | collective-permute-start | bytes 193544 | tf_op jit(solution)/shard_map/ppermute | solution.py:464
  24.5 7.6 %collective-permute-start.6 = (bf16[224,576]{1,0:T(8,128)(2,1)S(1)}, bf16[224,576]{1,0:T(8,128)(2,1)S(1)}, u32[]{:S(2)}, u32[]{:S(2)}) collective-permute-start(bf16[224,576]{1,0:T(8,128)(2,1)S(1)} %pad_maximum_fusion.1.keys), channel_id=1, source_target_pairs={{0,2},{2,0},{4,6},{6,4},{8,10},{10,8},{12,14},{14,12},{1,3},{3,1},... | collective-permute-start | bytes 774152 | tf_op jit(solution)/shard_map/ppermute | solution.py:464
  38.0 7.4 %collective-permute-start.7 = (bf16[224,576]{1,0:T(8,128)(2,1)S(1)}, bf16[224,576]{1,0:T(8,128)(2,1)S(1)}, u32[]{:S(2)}, u32[]{:S(2)}) collective-permute-start(bf16[224,576]{1,0:T(8,128)(2,1)S(1)} %get-tuple-element.57), channel_id=1, source_target_pairs={{0,2},{2,0},{4,6},{6,4},{8,10},{10,8},{12,14},{14,12},{1,3},{3,1},... | collective-permute-start | bytes 774152 | tf_op jit(solution)/shard_map/ppermute | solution.py:464
  45.5 8.1 %collective-permute-start.10 = (bf16[56,576]{1,0:T(8,128)(2,1)S(1)}, bf16[56,576]{1,0:T(8,128)(2,1)S(1)}, u32[]{:S(2)}, u32[]{:S(2)}) collective-permute-start(bf16[56,576]{1,0:T(8,128)(2,1)S(1)} %get-tuple-element.94), channel_id=1, source_target_pairs={{0,12},{2,14},{4,8},{6,10},{8,4},{10,6},{12,0},{14,2},{1,13},{3,15... | collective-permute-start | bytes 193544 | tf_op jit(solution)/shard_map/ppermute | solution.py:464
  47.6 6.0 %collective-permute-start.9 = (bf16[56,576]{1,0:T(8,128)(2,1)S(1)}, bf16[56,576]{1,0:T(8,128)(2,1)S(1)}, u32[]{:S(2)}, u32[]{:S(2)}) collective-permute-start(bf16[56,576]{1,0:T(8,128)(2,1)S(1)} %get-tuple-element.95), channel_id=1, source_target_pairs={{0,8},{2,10},{4,12},{6,14},{8,0},{10,2},{12,4},{14,6},{1,9},{3,11}... | collective-permute-start | bytes 193544 | tf_op jit(solution)/shard_map/ppermute | solution.py:464
  47.6 6.0 %collective-permute-start.8 = (bf16[56,576]{1,0:T(8,128)(2,1)S(1)}, bf16[56,576]{1,0:T(8,128)(2,1)S(1)}, u32[]{:S(2)}, u32[]{:S(2)}) collective-permute-start(bf16[56,576]{1,0:T(8,128)(2,1)S(1)} %get-tuple-element.96), channel_id=1, source_target_pairs={{0,4},{2,6},{4,0},{6,2},{8,12},{10,14},{12,8},{14,10},{1,5},{3,7},... | collective-permute-start | bytes 193544 | tf_op jit(solution)/shard_map/ppermute | solution.py:464
  51.9 6.2 %collective-permute-start.13 = (bf16[288,384]{1,0:T(8,128)(2,1)S(1)}, bf16[288,384]{1,0:T(8,128)(2,1)S(1)}, u32[]{:S(2)}, u32[]{:S(2)}) collective-permute-start(bf16[288,384]{1,0:T(8,128)(2,1)S(1)} %get-tuple-element.66), channel_id=1, source_target_pairs={{0,2},{2,0},{4,6},{6,4},{8,10},{10,8},{12,14},{14,12},{1,3},{3,1},... | collective-permute-start | bytes 663560 | tf_op jit(solution)/shard_map/ppermute | solution.py:464
  53.7 11.8 %collective-permute-start.12 = (bf16[56,576]{1,0:T(8,128)(2,1)S(1)}, bf16[56,576]{1,0:T(8,128)(2,1)S(1)}, u32[]{:S(2)}, u32[]{:S(2)}) collective-permute-start(bf16[56,576]{1,0:T(8,128)(2,1)S(1)} %fusion.4.swapped), channel_id=1, source_target_pairs={{0,2},{2,0},{4,6},{6,4},{8,10},{10,8},{12,14},{14,12},{1,3},{3,1},... | collective-permute-start | bytes 193544 | tf_op jit(solution)/shard_map/ppermute | solution.py:464
  55.0 10.5 %collective-permute-start.11 = (bf16[56,576]{1,0:T(8,128)(2,1)S(1)}, bf16[56,576]{1,0:T(8,128)(2,1)S(1)}, u32[]{:S(2)}, u32[]{:S(2)}) collective-permute-start(bf16[56,576]{1,0:T(8,128)(2,1)S(1)} %fusion.4.swapped), channel_id=1, source_target_pairs={{0,4},{4,8},{6,2},{8,12},{10,6},{14,10},{1,5},{5,9},{7,3},{9,13},{... | collective-permute-start | bytes 193544 | tf_op jit(solution)/shard_map/ppermute | solution.py:464
  58.2 6.0 %collective-permute-start.16 = (bf16[72,384]{1,0:T(8,128)(2,1)S(1)}, bf16[72,384]{1,0:T(8,128)(2,1)S(1)}, u32[]{:S(2)}, u32[]{:S(2)}) collective-permute-start(bf16[72,384]{1,0:T(8,128)(2,1)S(1)} %get-tuple-element.101), channel_id=1, source_target_pairs={{0,12},{2,14},{4,8},{6,10},{8,4},{10,6},{12,0},{14,2},{1,13},{3,15... | collective-permute-start | bytes 165896 | tf_op jit(solution)/shard_map/ppermute | solution.py:464
  60.1 5.4 %collective-permute-start.15 = (bf16[72,384]{1,0:T(8,128)(2,1)S(1)}, bf16[72,384]{1,0:T(8,128)(2,1)S(1)}, u32[]{:S(2)}, u32[]{:S(2)}) collective-permute-start(bf16[72,384]{1,0:T(8,128)(2,1)S(1)} %get-tuple-element.102), channel_id=1, source_target_pairs={{0,8},{2,10},{4,12},{6,14},{8,0},{10,2},{12,4},{14,6},{1,9},{3,11}... | collective-permute-start | bytes 165896 | tf_op jit(solution)/shard_map/ppermute | solution.py:464
  60.2 5.3 %collective-permute-start.14 = (bf16[72,384]{1,0:T(8,128)(2,1)S(1)}, bf16[72,384]{1,0:T(8,128)(2,1)S(1)}, u32[]{:S(2)}, u32[]{:S(2)}) collective-permute-start(bf16[72,384]{1,0:T(8,128)(2,1)S(1)} %get-tuple-element.103), channel_id=1, source_target_pairs={{0,4},{2,6},{4,0},{6,2},{8,12},{10,14},{12,8},{14,10},{1,5},{3,7},... | collective-permute-start | bytes 165896 | tf_op jit(solution)/shard_map/ppermute | solution.py:464
  71.0 8.0 %collective-permute-start.17 = (bf16[320,576]{1,0:T(8,128)(2,1)S(1)}, bf16[320,576]{1,0:T(8,128)(2,1)S(1)}, u32[]{:S(2)}, u32[]{:S(2)}) collective-permute-start(bf16[320,576]{1,0:T(8,128)(2,1)S(1)} %get-tuple-element.72), channel_id=1, source_target_pairs={{0,2},{2,0},{4,6},{6,4},{8,10},{10,8},{12,14},{14,12},{1,3},{3,1},... | collective-permute-start | bytes 1105928 | tf_op jit(solution)/shard_map/ppermute | solution.py:464
  72.5 11.2 %collective-permute-start.21 = (bf16[896,384]{1,0:T(8,128)(2,1)S(1)}, bf16[896,384]{1,0:T(8,128)(2,1)S(1)}, u32[]{:S(2)}, u32[]{:S(2)}) collective-permute-start(bf16[896,384]{1,0:T(8,128)(2,1)S(1)} %get-tuple-element.74), channel_id=1, source_target_pairs={{0,1},{1,0},{2,3},{3,2},{4,5},{5,4},{6,7},{7,6},{8,9},{9,8},{10,11... | collective-permute-start | bytes 2064392 | tf_op jit(solution)/shard_map/ppermute | solution.py:468
  79.3 7.4 %collective-permute-start.19 = (bf16[104,576]{1,0:T(8,128)(2,1)S(1)}, bf16[104,576]{1,0:T(8,128)(2,1)S(1)}, u32[]{:S(2)}, u32[]{:S(2)}) collective-permute-start(bf16[104,576]{1,0:T(8,128)(2,1)S(1)} %get-tuple-element.104), channel_id=1, source_target_pairs={{0,8},{2,10},{4,12},{6,14},{8,0},{10,2},{12,4},{14,6},{1,9},{3,11}... | collective-permute-start | bytes 359432 | tf_op jit(solution)/shard_map/ppermute | solution.py:464
  81.0 5.6 %collective-permute-start.18 = (bf16[104,576]{1,0:T(8,128)(2,1)S(1)}, bf16[104,576]{1,0:T(8,128)(2,1)S(1)}, u32[]{:S(2)}, u32[]{:S(2)}) collective-permute-start(bf16[104,576]{1,0:T(8,128)(2,1)S(1)} %get-tuple-element.105), channel_id=1, source_target_pairs={{0,4},{2,6},{4,0},{6,2},{8,12},{10,14},{12,8},{14,10},{1,5},{3,7},... | collective-permute-start | bytes 359432 | tf_op jit(solution)/shard_map/ppermute | solution.py:464
  81.7 7.4 %collective-permute-start.20 = (bf16[104,576]{1,0:T(8,128)(2,1)S(1)}, bf16[104,576]{1,0:T(8,128)(2,1)S(1)}, u32[]{:S(2)}, u32[]{:S(2)}) collective-permute-start(bf16[104,576]{1,0:T(8,128)(2,1)S(1)} %concatenate.20), channel_id=1, source_target_pairs={{0,12},{2,14},{4,8},{6,10},{8,4},{10,6},{12,0},{14,2},{1,13},{3,15... | collective-permute-start | bytes 359432 | tf_op jit(solution)/shard_map/ppermute | solution.py:464

commit v4 on v3

v4 whole, which is shorter than its diff:
```python
import functools
import math

import jax
import jax.numpy as jnp
from jax import lax
from jax.experimental import pallas as pl
from jax.experimental.pallas import tpu as pltpu
from jax.sharding import PartitionSpec as P

HEADS = 8
LANES = 128
F32 = jnp.float32
BF16 = jnp.bfloat16
PARAMS = pltpu.CompilerParams(vmem_limit_bytes=16 * 1024 * 1024)
NN = (((1,), (0,)), ((), ()))
NT = (((1,), (1,)), ((), ()))
TN = (((0,), (0,)), ((), ()))


def mul(left, right, dims=NN):
    return lax.dot_general(left, right, dims, preferred_element_type=F32)


def near_core(*arrays):
    return tuple(pltpu.with_memory_space_constraint(x, pltpu.VMEM) for x in arrays)


def vmem():
    return pl.BlockSpec(memory_space=pltpu.VMEM)


def smem():
    return pl.BlockSpec(memory_space=pltpu.SMEM)


def lane_tiles(channels):
    return [
        (k, k * LANES, min(LANES, channels - k * LANES)) for k in range(pl.cdiv(channels, LANES))
    ]


def round_up(size, step):
    return pl.cdiv(size, step) * step


def join_taps(taps, joint):
    local = taps.shape[2]
    for side in range(2):
        joint[0:27, side * local : (side + 1) * local] = taps[:, side, :]


def pool_body(
    geometry, place, own, other, weights, taps, to_pair, to_next, inner, stored, windows, joint, wide
):
    rows, cols, local = geometry
    pooled_rows, pooled_cols = rows // 4, cols // 4
    even = place[0] % 2 == 0
    first = place[1] == 0
    mine, theirs = own[:, :local].astype(F32), other[:, :local].astype(F32)
    low_half = jnp.where(first, mine, theirs)
    high_half = jnp.where(first, theirs, mine)
    tokens = jnp.concatenate([low_half, high_half], axis=1).astype(BF16)
    join_taps(taps, joint)
    starts = lax.broadcasted_iota(jnp.int32, (pooled_cols, LANES), 0) == 0
    both = weights[1:3].reshape(2 * local, 2 * local)
    full = mul(tokens, both, NT).astype(BF16).astype(F32)
    for tile, low, width in lane_tiles(2 * local):
        wide[tile, 0:8, :] = jnp.zeros((8, LANES), F32)
        wide[tile, 8:, :width] = full[:, low : low + width]
        for b in range(3):
            for e in range(3):
                for i in range(pooled_rows):
                    row = 4 * i + b - 1
                    if row < 0:
                        piece = jnp.zeros((pooled_cols, LANES), F32)
                    else:
                        piece = wide[tile, pl.ds(row * cols + e + 7, pooled_cols, stride=4), :]
                        if e == 0:
                            piece = jnp.where(starts, 0.0, piece)
                    at = slice(i * pooled_cols, (i + 1) * pooled_cols)
                    windows[3 * b + e, at, low : low + width] = piece[:, :width]
    for k in range(9):
        stored[k] = windows[k].astype(BF16)
    sums = []
    for a in range(3):
        total = windows[0] * joint[9 * a : 9 * a + 1, :]
        for k in range(1, 9):
            total = total + windows[k] * joint[9 * a + k : 9 * a + k + 1, :]
        sums.append(total)
    earlier, center, later = sums
    to_pair[...] = center.astype(BF16)
    to_next[...] = jnp.where(even, later, earlier).astype(BF16)
    inner[...] = jnp.where(even, earlier, later)


def pool_call(place, own, other, weights, taps, rows, cols):
    both = weights.shape[2]
    count = rows * cols // 16
    return pl.pallas_call(
        functools.partial(pool_body, (rows, cols, both // 2)),
        out_shape=(
            pltpu.VMEM((count, both), BF16),
            pltpu.VMEM((count, both), BF16),
            pltpu.VMEM((count, both), F32),
            jax.ShapeDtypeStruct((9, count, both), BF16),
        ),
        in_specs=[smem()] + [vmem()] * 4,
        out_specs=(vmem(),) * 4,
        scratch_shapes=[
            pltpu.VMEM((9, count, both), F32),
            pltpu.VMEM((32, both), F32),
            pltpu.VMEM((pl.cdiv(both, LANES), rows * cols + 8, LANES), F32),
        ],
        compiler_params=PARAMS,
        name="project_pool",
    )(place, *near_core(own, other), weights, taps)


def spread_rows(head_dim, local, heads):
    rows = lax.broadcasted_iota(jnp.int32, (heads * LANES, local), 0)
    cols = lax.broadcasted_iota(jnp.int32, (heads * LANES, local), 1)
    chosen = rows < 0
    for h in range(heads):
        inside = (cols >= h * head_dim) & (cols < (h + 1) * head_dim)
        chosen = chosen | (inside & (rows == cols + h * (LANES - head_dim)))
    return chosen.astype(F32).astype(BF16)


def identity(size):
    rows = lax.broadcasted_iota(jnp.int32, (size, size), 0)
    cols = lax.broadcasted_iota(jnp.int32, (size, size), 1)
    return (rows == cols).astype(F32).astype(BF16)


def turn_body(geometry, out_grad, grad_t):
    head_dim, local, heads = geometry
    grad_t[...] = mul(spread_rows(head_dim, local, heads), out_grad[...], NT).astype(BF16)


def turn_call(out_grad, head_dim):
    tokens, local = out_grad.shape
    heads = local // head_dim
    return pl.pallas_call(
        functools.partial(turn_body, (head_dim, local, heads)),
        out_shape=pltpu.VMEM((heads * LANES, tokens), BF16),
        in_specs=[vmem()],
        out_specs=vmem(),
        compiler_params=PARAMS,
        name="turn_grad",
    )(out_grad)


def query_body(geometry, place, own, other, weights, query_t, tokens_t):
    head_dim, local, heads = geometry
    spread = spread_rows(head_dim, local, heads)
    turn = identity(local)
    near = pl.multiple_of(place[1] * local, 16)
    far = pl.multiple_of((1 - place[1]) * local, 16)
    tokens_t[pl.ds(near, local), :] = mul(turn, own[:, :local], NT).astype(BF16)
    tokens_t[pl.ds(far, local), :] = mul(turn, other[:, :local], NT).astype(BF16)
    query_t[...] = mul(mul(spread, weights[0]).astype(BF16), tokens_t[...]).astype(BF16)


def query_call(place, own, other, weights, head_dim):
    tokens, local = own.shape[0], weights.shape[1]
    heads = local // head_dim
    return pl.pallas_call(
        functools.partial(query_body, (head_dim, local, heads)),
        out_shape=(
            pltpu.VMEM((heads * LANES, tokens), BF16),
            pltpu.VMEM((2 * local, tokens), BF16),
        ),
        in_specs=[smem()] + [vmem()] * 3,
        out_specs=(vmem(),) * 2,
        compiler_params=PARAMS,
        name="project_query",
    )(place, *near_core(own, other), weights)


def choose_head(head_dim, local, head):
    rows = lax.broadcasted_iota(jnp.int32, (2 * local, 2 * LANES), 0)
    cols = lax.broadcasted_iota(jnp.int32, (2 * local, 2 * LANES), 1)
    lane = cols % LANES
    source = lane + (cols // LANES) * local + head * head_dim
    return ((rows == source) & (lane < head_dim)).astype(F32).astype(BF16)


def head_products(head_dim, keys, chosen, query, grad):
    both = jnp.concatenate([mul(part[...], chosen) for part in keys], axis=0).astype(BF16)
    key, value = both[:, :LANES], both[:, LANES:]
    factor = head_dim ** (-0.5) * math.log2(math.e)
    raised = jnp.exp2(mul(key, query) * factor)
    return key, raised, mul(value, grad)


def measure_body(
    geometry, first, rest, query_t, grad_t, sums, raised_out, prob_grad_out, key_pad
):
    head_dim, local, heads = geometry
    chosen = choose_head(head_dim, local, pl.program_id(0))
    key, raised, prob_grad = head_products(
        head_dim, (first, rest), chosen, query_t[...], grad_t[...]
    )
    raised_out[0] = raised
    prob_grad_out[0] = prob_grad
    key_pad[...] = key
    sums[0, 0:1, :] = jnp.sum(raised, axis=0, keepdims=True)
    sums[0, 1:2, :] = jnp.sum(raised * prob_grad, axis=0, keepdims=True)


def attend_body(geometry, final, *refs):
    head_dim, local, heads = geometry
    head = pl.program_id(0)
    scale = head_dim ** (-0.5)
    chosen = choose_head(head_dim, local, head)
    if final:
        own_raised, own_prob_grad, own_pad, query_t, grad_t, sums, *refs = refs
        other_pad, other_scores, first_grads, rest_grads, query_grad, total = refs
        query, grad = query_t[...], grad_t[...]
        key, raised, prob_grad = own_pad[...], own_raised[0], own_prob_grad[0]
        inverse, centre = sums[0, 0:1, :], sums[0, 1:2, :]
    else:
        first, rest, query_t, grad_t, sums, *refs = refs
        first_grads, rest_grads, key_pad, score_grads, totals, total = refs
        query, grad = query_t[...], grad_t[...]
        key, raised, prob_grad = head_products(head_dim, (first, rest), chosen, query, grad)
        inverse = 1.0 / (sums[0, 0:1, :] + jnp.sum(raised, axis=0, keepdims=True))
        weighted = sums[0, 1:2, :] + jnp.sum(raised * prob_grad, axis=0, keepdims=True)
        centre = weighted * inverse
        totals[0, 0:1, :] = inverse
        totals[0, 1:2, :] = centre
    probs = raised * inverse
    score_grad = (probs * (prob_grad - centre) * scale).astype(BF16)
    if final:
        turn = identity(LANES)
        back_t = grad.astype(F32)
        for keys, scores in ((key, score_grad), (other_pad[...], other_scores[0])):
            back_t = back_t + mul(mul(turn, keys, NT).astype(BF16), scores)
        query_grad[...] = back_t.T.astype(BF16)
    else:
        key_pad[...] = key
        score_grads[0] = score_grad
    value_back = mul(probs.astype(BF16), grad, NT)
    key_back = mul(score_grad, query, NT)
    joined = jnp.concatenate([key_back, value_back], axis=1).astype(BF16)
    placed = mul(joined, chosen, NT)

    @pl.when(head == 0)
    def _():
        total[...] = placed

    @pl.when(head > 0)
    def _():
        total[...] += placed

    @pl.when(head == heads - 1)
    def _():
        split = first_grads.shape[0]
        first_grads[...] = total[:split, :].astype(BF16)
        rest_grads[...] = total[split:, :].astype(BF16)


def whole_spec(array):
    return pl.BlockSpec(array.shape, lambda h: (0,) * len(array.shape))


def head_specs(tokens, key_count):
    rows = pl.BlockSpec((LANES, tokens), lambda h: (h, 0))
    sums = pl.BlockSpec((1, 8, tokens), lambda h: (h, 0, 0))
    keys = pl.BlockSpec((key_count, LANES), lambda h: (0, h))
    scores = pl.BlockSpec((1, key_count, tokens), lambda h: (h, 0, 0))
    return rows, sums, keys, scores


def measure_call(first, rest, query_t, grad_t, head_dim):
    local, tokens = first.shape[1] // 2, query_t.shape[1]
    heads = local // head_dim
    key_count = first.shape[0] + rest.shape[0]
    row_spec, sum_spec, key_spec, score_spec = head_specs(tokens, key_count)
    return pl.pallas_call(
        functools.partial(measure_body, (head_dim, local, heads)),
        grid=(heads,),
        out_shape=(
            pltpu.VMEM((heads, 8, tokens), F32),
            pltpu.VMEM((heads, key_count, tokens), F32),
            pltpu.VMEM((heads, key_count, tokens), F32),
            pltpu.VMEM((key_count, heads * LANES), BF16),
        ),
        in_specs=[whole_spec(first), whole_spec(rest), row_spec, row_spec],
        out_specs=(sum_spec, score_spec, score_spec, key_spec),
        compiler_params=PARAMS,
        name="attend_measure",
    )(*near_core(first, rest, query_t, grad_t))


def attend_call(first, rest, query_t, grad_t, sums, head_dim):
    key_count, both = first.shape[0] + rest.shape[0], first.shape[1]
    local, tokens = both // 2, query_t.shape[1]
    heads = local // head_dim
    row_spec, sum_spec, key_spec, score_spec = head_specs(tokens, key_count)
    return pl.pallas_call(
        functools.partial(attend_body, (head_dim, local, heads), False),
        grid=(heads,),
        out_shape=(
            pltpu.VMEM(first.shape, BF16),
            pltpu.VMEM(rest.shape, BF16),
            pltpu.VMEM((key_count, heads * LANES), BF16),
            pltpu.VMEM((heads, key_count, tokens), BF16),
            pltpu.VMEM((heads, 8, tokens), F32),
        ),
        in_specs=[whole_spec(first), whole_spec(rest), row_spec, row_spec, sum_spec],
        out_specs=(whole_spec(first), whole_spec(rest), key_spec, score_spec, sum_spec),
        scratch_shapes=[pltpu.VMEM((key_count, both), F32)],
        compiler_params=PARAMS,
        name="attend_other",
    )(*near_core(first, rest, query_t, grad_t, sums))


def attend_final_call(saved, query_t, grad_t, totals, extra, head_dim, local, split):
    key_count, tokens = saved[0].shape[1:]
    heads = local // head_dim
    row_spec, sum_spec, key_spec, score_spec = head_specs(tokens, key_count)
    shapes = ((split, 2 * local), (key_count - split, 2 * local))
    outs = [pltpu.VMEM(shape, BF16) for shape in shapes]
    specs = [pl.BlockSpec(shape, lambda h: (0, 0)) for shape in shapes]
    in_specs = [score_spec, score_spec, key_spec, row_spec, row_spec, sum_spec]
    return pl.pallas_call(
        functools.partial(attend_body, (head_dim, local, heads), True),
        grid=(heads,),
        out_shape=(*outs, pltpu.VMEM((tokens, heads * LANES), BF16)),
        in_specs=[*in_specs, key_spec, score_spec],
        out_specs=(*specs, pl.BlockSpec((tokens, LANES), lambda h: (0, h))),
        scratch_shapes=[pltpu.VMEM((key_count, 2 * local), F32)],
        compiler_params=PARAMS,
        name="attend_same",
    )(*near_core(*saved, query_t, grad_t, totals, *extra))


def store_blocks(position, count, rows, column, here, away, away_own=None):
    padded = round_up(rows, 8)
    width = column.shape[1]
    for j in range(count):
        relative = position ^ j
        outer = relative // 2
        value = column[j * rows : (j + 1) * rows, :]

        @pl.when(relative % 2 == 0)
        def _(value=value, outer=outer):
            here[pl.ds(pl.multiple_of(outer * padded, 8), rows), :width] = value

        if away_own is None:

            @pl.when(relative % 2 == 1)
            def _(value=value, outer=outer):
                at = pl.multiple_of(outer * padded, 8)
                away[pl.ds(at, rows), :width] = value.astype(BF16)

        else:

            @pl.when(relative == 1)
            def _(value=value):
                away_own[:rows, :width] = value.astype(BF16)

            @pl.when((relative % 2 == 1) & (relative > 1))
            def _(value=value, outer=outer):
                at = pl.multiple_of((outer - 1) * padded, 8)
                away[pl.ds(at, rows), :width] = value.astype(BF16)


def query_side_body(geometry, place, query_pad, tokens_t, query_back, here, away):
    head_dim, local, heads, count = geometry
    spread = spread_rows(head_dim, local, heads)
    back = mul(query_pad[...], spread).astype(BF16)
    query_back[...] = back
    here[...] = jnp.zeros(here.shape, F32)
    away[...] = jnp.zeros(away.shape, BF16)
    column = mul(tokens_t[...], back)
    store_blocks(place[0], count, 2 * local // count, column, here, away)


def query_side_call(place, query_pad, tokens_t, head_dim, count):
    both, tokens = tokens_t.shape
    local = both // 2
    shape = (count // 2 * round_up(both // count, 8), round_up(local, LANES))
    return pl.pallas_call(
        functools.partial(query_side_body, (head_dim, local, local // head_dim, count)),
        out_shape=(
            pltpu.VMEM((tokens, local), BF16),
            pltpu.VMEM(shape, F32),
            pltpu.VMEM(shape, BF16),
        ),
        in_specs=[smem()] + [vmem()] * 2,
        out_specs=(vmem(),) * 3,
        compiler_params=PARAMS,
        name="query_side",
    )(place, *near_core(query_pad, tokens_t))


def pull_body(
    geometry,
    place,
    mine,
    swapped,
    beside,
    windows,
    taps,
    tokens_t,
    weights,
    query_back,
    here,
    away,
    away_own,
    token_near,
    token_far,
    wide,
    staged,
    joint,
    folded,
):
    rows, cols, local, count = geometry
    pooled_rows, pooled_cols = rows // 4, cols // 4
    position = place[0]
    even = position % 2 == 0
    pooled = pooled_rows * pooled_cols
    block_rows = 2 * local // count
    padded = round_up(block_rows, 8)
    outer = count // 2
    join_taps(taps, joint)
    starts = lax.broadcasted_iota(jnp.int32, (pooled, 2 * local), 0) % pooled_cols == 0
    folded[...] = jnp.zeros(folded.shape, F32)
    wide[...] = jnp.zeros(wide.shape, F32)
    if padded > block_rows:
        here[...] = jnp.zeros(here.shape, F32)
        away[...] = jnp.zeros(away.shape, BF16)
        away_own[...] = jnp.zeros(away_own.shape, BF16)
    partner, distant = swapped[...].astype(F32), beside[...].astype(F32)
    grads = [
        jnp.where(even, partner, distant),
        mine[...].astype(F32),
        jnp.where(even, distant, partner),
    ]
    for b in range(3):
        for e in range(3):
            k = 3 * b + e
            window = windows[k].astype(F32)
            spread = None
            for a in range(3):
                term = grads[a] * joint[9 * a + k : 9 * a + k + 1, :]
                spread = term if spread is None else spread + term
                folded[9 * a + k : 9 * a + k + 1, :] = jnp.sum(
                    grads[a] * window, axis=0, keepdims=True
                )
            if e == 0:
                spread = jnp.where(starts, 0.0, spread)
            for tile, low, width in lane_tiles(2 * local):
                staged[tile, :, :width] = spread[:, low : low + width]
                for i in range(pooled_rows):
                    row = 4 * i + b - 1
                    if row >= 0:
                        at = slice(i * pooled_cols, (i + 1) * pooled_cols)
                        wide[tile, pl.ds(row * cols + e + 7, pooled_cols, stride=4), :] = staged[
                            tile, at, :
                        ]
    back = jnp.concatenate(
        [wide[tile, 8:, :width] for tile, low, width in lane_tiles(2 * local)], axis=1
    ).astype(BF16)
    column = mul(tokens_t[...], back)
    here[outer * padded :, :] = folded[...]
    away[(outer - 1) * padded :, :] = folded[...].astype(BF16)
    store_blocks(position, count, block_rows, column, here, away, away_own)
    both = weights[1:3].reshape(2 * local, 2 * local)
    token_sum = mul(query_back[...], weights[0]) + mul(back, both)
    first = place[1] == 0
    low_half, high_half = token_sum[:, :local], token_sum[:, local:]
    token_near[...] = jnp.where(first, low_half, high_half)
    token_far[:, :local] = jnp.where(first, high_half, low_half).astype(BF16)
    token_far[:, local:] = jnp.zeros((token_far.shape[0], token_far.shape[1] - local), BF16)


def pull_call(
    place, mine, swapped, beside, windows, taps, tokens_t, weights, query_back, rows, cols, count
):
    both, tokens = tokens_t.shape
    local = both // 2
    padded = round_up(both // count, 8)
    size = count // 2 * padded + 32
    tiles = pl.cdiv(both, LANES)
    return pl.pallas_call(
        functools.partial(pull_body, (rows, cols, local, count)),
        out_shape=(
            pltpu.VMEM((size, both), F32),
            pltpu.VMEM((size - padded, both), BF16),
            pltpu.VMEM((padded, both), BF16),
            pltpu.VMEM((tokens, local), F32),
            pltpu.VMEM((tokens, round_up(local, LANES)), BF16),
        ),
        in_specs=[smem()] + [vmem()] * 8,
        out_specs=(vmem(),) * 5,
        scratch_shapes=[
            pltpu.VMEM((tiles, tokens + 8, LANES), F32),
            pltpu.VMEM((tiles, rows * cols // 16, LANES), F32),
            pltpu.VMEM((32, both), F32),
            pltpu.VMEM((32, both), F32),
        ],
        compiler_params=PARAMS,
        name="pull_back",
    )(
        place,
        *near_core(mine, swapped, beside),
        windows,
        taps,
        *near_core(tokens_t),
        weights,
        *near_core(query_back),
    )


def finish_body(rows, query_sum, own_sum, tail_sum, *refs):
    *pieces, weight_grad, kernel_grad = refs
    local = weight_grad.shape[2]
    padded = own_sum.shape[0]
    total, tail = own_sum[...], tail_sum[...]
    for piece in pieces:
        total = total + piece[:padded, :].astype(F32)
        tail = tail + piece[padded:, :].astype(F32)
    weight_grad[0] = query_sum[:rows, :local]
    weight_grad[1] = total[:rows, :local]
    weight_grad[2] = total[:rows, local:]
    for side in range(2):
        for k in range(kernel_grad.shape[0]):
            kernel_grad[k, side : side + 1, :] = tail[k : k + 1, side * local : (side + 1) * local]


def finish_call(query_sum, own_sum, tail_sum, pieces, rows, local):
    return pl.pallas_call(
        functools.partial(finish_body, rows),
        out_shape=(
            jax.ShapeDtypeStruct((3, rows, local), F32),
            jax.ShapeDtypeStruct((27, 2, local), F32),
        ),
        in_specs=[vmem()] * (3 + len(pieces)),
        out_specs=(vmem(),) * 2,
        compiler_params=PARAMS,
        name="finish",
    )(*near_core(query_sum, own_sum, tail_sum, *pieces))


def frame_pairs(step, flip):
    count = lax.axis_size("frames")
    return [(i, i ^ (2 * step + flip)) for i in range(count)]


def outer_pairs(direction):
    count = lax.axis_size("frames")
    moves = [(i, i + direction * (2 if i % 2 else -2)) for i in range(count)]
    return [(i, j) for i, j in moves if 0 <= j < count]


def exchange(block, pairs):
    return lax.ppermute(block, "frames", pairs)


def across(block):
    return lax.ppermute(block, "heads", [(0, 1), (1, 0)])


def scatter_weights(here, moved, rows):
    outer = lax.axis_size("frames") // 2
    summed = here + moved.astype(F32)
    end = outer * rows
    own = jnp.concatenate([summed[:rows], summed[end:]])
    low = summed.astype(BF16)
    pieces = []
    for step in range(1, outer):
        piece = jnp.concatenate([low[step * rows : (step + 1) * rows], low[end:]])
        pieces.append(exchange(piece, frame_pairs(step, 0)))
    return own, pieces


def add_all(own, pieces):
    for piece in pieces:
        own = own + piece.astype(F32)
    return own


def shards(tokens, out_grad, w_qkv, pool_kernel):
    local = tokens.shape[-1]
    heads_here = HEADS // lax.axis_size("heads")
    head_dim = local // heads_here
    rows, cols = tokens.shape[1], tokens.shape[2]
    token_count = rows * cols
    count = lax.axis_size("frames")
    frame = lax.axis_index("frames")
    core = lax.axis_index("heads")
    place = jnp.stack([frame, core]).astype(jnp.int32)
    outer = count // 2
    spare = round_up(local, LANES) - local
    own = jnp.pad(tokens.reshape(token_count, local), ((0, 0), (0, spare)))
    grad = out_grad.reshape(token_count, local)
    across_pair, barrier = frame_pairs(0, 1), lax.optimization_barrier
    other = across(own)
    grad_t = turn_call(grad, head_dim)
    other, grad_t = barrier((other, grad_t))
    weights = w_qkv.transpose(0, 2, 1)
    taps = pool_kernel.transpose(1, 0, 2)
    to_pair, to_next, inner, windows = pool_call(place, own, other, weights, taps, rows, cols)
    from_next = exchange(to_next, outer_pairs(1))
    from_pair = exchange(to_pair, across_pair)
    block = (inner + from_pair.astype(F32) + from_next.astype(F32)).astype(BF16)
    others = [exchange(block, frame_pairs(s, 0)) for s in range(1, outer)]
    other_first = exchange(block, across_pair)
    block, own, other = barrier((block, own, other))
    query_t, tokens_t = query_call(place, own, other, weights, head_dim)
    others, other_first, query_t, grad_t, tokens_t = barrier(
        (others, other_first, query_t, grad_t, tokens_t)
    )
    same_rest = jnp.concatenate(others)
    other_rest = exchange(same_rest, across_pair)
    sums, *saved = measure_call(block, same_rest, query_t, grad_t, head_dim)
    first_other, rest_other, *for_other, totals = attend_call(
        other_first, other_rest, query_t, grad_t, sums, head_dim
    )
    rest_moved = exchange(rest_other, across_pair)
    step_rows = block.shape[0]
    first_same, rest_same, query_pad = attend_final_call(
        saved, query_t, grad_t, totals, for_other, head_dim, local, step_rows
    )
    rest_moved, first_other = barrier((rest_moved, first_other))
    low = (rest_same.astype(F32) + rest_moved.astype(F32)).astype(BF16)
    pieces = [
        exchange(low[(s - 1) * step_rows : s * step_rows], frame_pairs(s, 0))
        for s in range(1, outer)
    ]
    first_moved = exchange(first_other, across_pair)
    query_back, query_here, query_away = query_side_call(
        place, query_pad, tokens_t, head_dim, count
    )
    pieces, first_moved, query_back, query_here, query_away = barrier(
        (pieces, first_moved, query_back, query_here, query_away)
    )
    summed = first_same.astype(F32) + first_moved.astype(F32)
    swapped = add_all(summed, pieces).astype(BF16)
    beside = exchange(swapped, outer_pairs(-1))
    mine = exchange(swapped, frame_pairs(0, 1))
    beside, mine, query_away = barrier((beside, mine, query_away))
    query_moved = exchange(query_away, across_pair)
    block_rows = 2 * local // count
    padded = round_up(block_rows, 8)
    here, away, away_own, near, far = pull_call(
        place, mine, swapped, beside, windows, taps, tokens_t, weights, query_back, rows, cols, count
    )
    moved = exchange(away, frame_pairs(0, 1))
    query_moved, near, far = barrier((query_moved, near, far))
    query_own, query_pieces = scatter_weights(query_here, query_moved, padded)
    moved, query_pieces = barrier((moved, query_pieces))
    query_sum = add_all(query_own, query_pieces)
    input_grad = (near + across(far)[:, :local].astype(F32)).astype(BF16)
    rest_sum = here[padded:] + moved.astype(F32)
    low, end = rest_sum.astype(BF16), (outer - 1) * padded
    pieces = [
        exchange(
            jnp.concatenate([low[(s - 1) * padded : s * padded], low[end:]]), frame_pairs(s, 0)
        )
        for s in range(1, outer)
    ]
    own_moved = exchange(barrier((away_own, moved))[0], across_pair)
    own_sum, tail_sum = here[:padded] + own_moved.astype(F32), rest_sum[end:]
    pieces, input_grad, query_sum, own_sum, tail_sum = barrier(
        (pieces, input_grad, query_sum, own_sum, tail_sum)
    )
    weight_grad, kernel_grad = finish_call(
        query_sum, own_sum, tail_sum, pieces, block_rows, local
    )
    return input_grad.reshape(tokens.shape), weight_grad, kernel_grad.transpose(1, 0, 2)


def solution(mesh):
    in_specs = (
        P(("clips", "frames"), None, None, "heads"),
        P(("clips", "frames"), None, None, "heads"),
        P(None, None, "heads"),
        P(None, None, "heads"),
    )
    out_specs = (
        P(("clips", "frames"), None, None, "heads"),
        P("clips", "frames", "heads"),
        P("clips", None, "heads"),
    )
    return jax.shard_map(shards, mesh=mesh, in_specs=in_specs, out_specs=out_specs, check_vma=False)
```

time: 91 us -> 86.4 us (0.949)
  waiting for transfers between devices: 24.7 us -> 22.9 us
  Pallas kernels: 27.3 us -> 25.7 us
    pallas_call x1 -> x3, Pallas kernels: 2.42 us -> 3.65 us  [the longest x1 2.07 us: pool_call(): pl.pallas_call(functools.partial(pool_body, (rows, cols, both // 2)), out...]
    ppermute x20 -> x23, waiting for transfers between devices: 23 us -> 21.9 us  [exchange(): return lax.ppermute(block, 'frames', pairs)]
    pallas_call x1, Pallas kernels: 5.59 us -> 4.56 us  [attend_final_call(): pl.pallas_call(functools.partial(attend_body, (head_dim, local, heads), T...]
    pallas_call x1, Pallas kernels: 5.89 us -> 4.94 us  [attend_call(): pl.pallas_call(functools.partial(attend_body, (head_dim, local, heads), F...]
    ppermute x20 -> x23, starting transfers between devices: 32.6 us -> 33.2 us  [exchange(): return lax.ppermute(block, 'frames', pairs)]
  transfers between devices with their start and end apart: 22 -> 25, of which waited for: 10 -> 14; matrix products, arithmetic and copies ran while one was open for 2% -> 2% of each run, Pallas kernels for 15% -> 21%
where the time goes in v4:
time: 86.4 us; the launch traced here: 86.2 us
  starting transfers between devices  33.8 us (39%)
  Pallas kernels  25.7 us (30%)
  waiting for transfers between devices  22.9 us (27%)
  other arithmetic  1.49 us (2%)
  local copies, waits for them, and re-layouts  1.44 us (2%)
  between operations  0.89 us (1%)
    ppermute x23, starting transfers between devices, exchange(): return lax.ppermute(block, 'frames', pairs)  33.2 us
    ppermute x23, waiting for transfers between devices, exchange(): return lax.ppermute(block, 'frames', pairs)  21.9 us
    pallas_call x1, Pallas kernels, pull_call(): pl.pallas_call(functools.partial(pull_body, (rows, cols, local, count)),...  5.56 us
    pallas_call x1, Pallas kernels, attend_call(): pl.pallas_call(functools.partial(attend_body, (head_dim, local, heads), F...  4.94 us
    pallas_call x1, Pallas kernels, attend_final_call(): pl.pallas_call(functools.partial(attend_body, (head_dim, local, heads), T...  4.56 us
    pallas_call x1, Pallas kernels, measure_call(): pl.pallas_call(functools.partial(measure_body, (head_dim, local, heads)),...  2.53 us
    pallas_call x1, Pallas kernels, query_call(): pl.pallas_call(functools.partial(query_body, (head_dim, local, heads)), o...  2.49 us
    pallas_call x1, Pallas kernels, pool_call(): pl.pallas_call(functools.partial(pool_body, (rows, cols, both // 2)), out...  2.07 us
  transfers between devices with their start and end apart: 25, of which 14 were waited for; matrix products, arithmetic and copies ran while one was open for 2% of the time, Pallas kernels for 21%

profile of v4, /device:TPU:0, one launch (start us, length us, event | category | flops | bytes accessed | tf_op | source)
XLA Modules:
  0.0 86.2 jit_solution(12616927529220746489)
XLA Ops:
  0.7 1.3 %pad.4.own = bf16[896,384]{1,0:T(8,128)(2,1)S(1)} pad(bf16[896,288]{1,0:T(8,128)(2,1)} %bitcast.14, bf16[]{:T(256)} %constant.10.clone.1), padding=0_0x0_96 | pad | bytes 1204226 | tf_op jit(solution)/shard_map/jit(_pad)/pad | solution.py:599
  2.0 0.5 collective-permute-start
  2.5 0.7 turn_grad.1.grad_t.refs_3_.refs_4_
  3.2 0.1 pad_add_fusion.place
  3.3 1.0 %collective-permute-done.other = bf16[896,384]{1,0:T(8,128)(2,1)S(1)} collective-permute-done((bf16[896,384]{1,0:T(8,128)(2,1)S(1)}, bf16[896,384]{1,0:T(8,128)(2,1)S(1)}, u32[]{:S(2)}, u32[]{:S(2)}) %collective-permute-start) | collective-permute-done | bytes 688160 | tf_op jit(solution)/shard_map/ppermute | solution.py:565
  4.3 2.1 %project_pool.1 = (bf16[56,576]{1,0:T(8,128)(2,1)S(1)}, bf16[56,576]{1,0:T(8,128)(2,1)S(1)}, f32[56,576]{1,0:T(8,128)S(1)}, bf16[9,56,576]{2,1,0:T(8,128)(2,1)S(1)}) custom-call(s32[2]{0:T(128)S(1)} %pad_add_fusion.place, bf16[896,384]{1,0:T(8,128)(2,1)S(1)} %pad.4.own, bf16[896,384]{1,0:T(8,128)(2,1)S(1)} %collective-permute-done.other, ...), custom_call_target="tpu_custom_call" | custom-call | tf_op jit(solution)/shard_map/project_pool/pallas_call | solution.py:100
  6.3 3.0 %collective-permute-start.1 = (bf16[56,576]{1,0:T(8,128)(2,1)S(1)}, bf16[56,576]{1,0:T(8,128)(2,1)S(1)}, u32[]{:S(2)}, u32[]{:S(2)}) collective-permute-start(bf16[56,576]{1,0:T(8,128)(2,1)S(1)} %get-tuple-element.72), channel_id=1, source_target_pairs={{0,2},{2,0},{4,6},{6,4},{8,10},{10,8},{12,14},{14,12},{1,3},{3,1},... | collective-permute-start | bytes 193544 | tf_op jit(solution)/shard_map/ppermute | solution.py:561
  9.3 1.3 %collective-permute-start.2 = (bf16[56,576]{1,0:T(8,128)(2,1)S(1)}, bf16[56,576]{1,0:T(8,128)(2,1)S(1)}, u32[]{:S(2)}, u32[]{:S(2)}) collective-permute-start(bf16[56,576]{1,0:T(8,128)(2,1)S(1)} %get-tuple-element.73), channel_id=1, source_target_pairs={{2,6},{4,0},{6,10},{8,4},{10,14},{12,8},{3,7},{5,1},{7,11},{9,5},{... | collective-permute-start | bytes 193544 | tf_op jit(solution)/shard_map/ppermute | solution.py:561
  10.6 1.2 %collective-permute-done.1 = bf16[56,576]{1,0:T(8,128)(2,1)S(1)} collective-permute-done((bf16[56,576]{1,0:T(8,128)(2,1)S(1)}, bf16[56,576]{1,0:T(8,128)(2,1)S(1)}, u32[]{:S(2)}, u32[]{:S(2)}) %collective-permute-start.1) | collective-permute-done | bytes 64544 | tf_op jit(solution)/shard_map/ppermute | solution.py:561
  11.8 3.7 %collective-permute-done.2 = bf16[56,576]{1,0:T(8,128)(2,1)S(1)} collective-permute-done((bf16[56,576]{1,0:T(8,128)(2,1)S(1)}, bf16[56,576]{1,0:T(8,128)(2,1)S(1)}, u32[]{:S(2)}, u32[]{:S(2)}) %collective-permute-start.2) | collective-permute-done | bytes 64544 | tf_op jit(solution)/shard_map/ppermute | solution.py:561
  15.5 0.1 collective-permute-start.6
  15.6 4.1 %collective-permute-start.5 = (bf16[56,576]{1,0:T(8,128)(2,1)S(1)}, bf16[56,576]{1,0:T(8,128)(2,1)S(1)}, u32[]{:S(2)}, u32[]{:S(2)}) collective-permute-start(bf16[56,576]{1,0:T(8,128)(2,1)S(1)} %add_convert_fusion.3.first), channel_id=1, source_target_pairs={{0,12},{2,14},{4,8},{6,10},{8,4},{10,6},{12,0},{14,2},{1,13},{3,15... | collective-permute-start | bytes 193544 | tf_op jit(solution)/shard_map/ppermute | solution.py:561
  19.7 0.6 collective-permute-start.3
  20.3 2.5 %project_query.1 = (bf16[512,896]{1,0:T(8,128)(2,1)S(1)}, bf16[576,896]{1,0:T(8,128)(2,1)S(1)}) custom-call(s32[2]{0:T(128)S(1)} %pad_add_fusion.place, bf16[896,384]{1,0:T(8,128)(2,1)S(1)} %pad.4.own, bf16[896,384]{1,0:T(8,128)(2,1)S(1)} %collective-permute-done.other, bf16[3,288,576]{2,1,0:T(8,128)(2,1)S(1)} %bitcast.9), custom_call_target="tpu_custom_call" | custom-call | tf_op jit(solution)/shard_map/project_query/pallas_call | solution.py:168
  22.8 2.2 %collective-permute-done.4 = bf16[56,576]{1,0:T(8,128)(2,1)S(1)} collective-permute-done((bf16[56,576]{1,0:T(8,128)(2,1)S(1)}, bf16[56,576]{1,0:T(8,128)(2,1)S(1)}, u32[]{:S(2)}, u32[]{:S(2)}) %collective-permute-start.4) | collective-permute-done | bytes 64544 | tf_op jit(solution)/shard_map/ppermute | solution.py:561
  25.0 1.4 %collective-permute-start.7 = (bf16[168,576]{1,0:T(8,128)(2,1)S(1)}, bf16[168,576]{1,0:T(8,128)(2,1)S(1)}, u32[]{:S(2)}, u32[]{:S(2)}) collective-permute-start(bf16[168,576]{1,0:T(8,128)(2,1)S(1)} %constant_dynamic-update-slice_fusion.rest), channel_id=1, source_target_pairs={{0,2},{2,0},{4,6},{6,4},{8,10},{10,8},{12,14},{14,12},{1,3},{3,1},... | collective-permute-start | bytes 580616 | tf_op jit(solution)/shard_map/ppermute | solution.py:561
  26.4 2.5 %attend_measure.1 = (f32[4,8,896]{2,1,0:T(8,128)S(1)}, f32[4,224,896]{2,1,0:T(8,128)S(1)}, f32[4,224,896]{2,1,0:T(8,128)S(1)}, bf16[224,512]{1,0:T(8,128)(2,1)S(1)}) custom-call(bf16[56,576]{1,0:T(8,128)(2,1)S(1)} %add_convert_fusion.3.first, bf16[168,576]{1,0:T(8,128)(2,1)S(1)} %constant_dynamic-update-slice_fusion.rest, ...), custom_call_target="tpu_custom_call" | custom-call | tf_op jit(solution)/shard_map/attend_measure/pallas_call | solution.py:281
  29.0 2.4 %collective-permute-done.7.refs_1_ = bf16[168,576]{1,0:T(8,128)(2,1)S(1)} collective-permute-done((bf16[168,576]{1,0:T(8,128)(2,1)S(1)}, bf16[168,576]{1,0:T(8,128)(2,1)S(1)}, u32[]{:S(2)}, u32[]{:S(2)}) %collective-permute-start.7) | collective-permute-done | bytes 193568 | tf_op jit(solution)/shard_map/ppermute | solution.py:561
  31.3 4.9 %attend_other.1 = (bf16[56,576]{1,0:T(8,128)(2,1)S(1)}, bf16[168,576]{1,0:T(8,128)(2,1)S(1)}, bf16[224,512]{1,0:T(8,128)(2,1)S(1)}, bf16[4,224,896]{2,1,0:T(8,128)(2,1)S(1)}, f32[4,8,896]{2,1,0:T(8,128)S(1)}) custom-call(bf16[56,576]{1,0:T(8,128)(2,1)S(1)} %collective-permute-done.6.refs_0_, bf16[168,576]{1,0:T(8,128)(2,1)S(1)} %collective-permute-done.7.refs_1_, ...), custom_call_target="tpu_custom_call" | custom-call | tf_op jit(solution)/shard_map/attend_other/pallas_call | solution.py:302
  36.3 1.0 %collective-permute-start.8 = (bf16[168,576]{1,0:T(8,128)(2,1)S(1)}, bf16[168,576]{1,0:T(8,128)(2,1)S(1)}, u32[]{:S(2)}, u32[]{:S(2)}) collective-permute-start(bf16[168,576]{1,0:T(8,128)(2,1)S(1)} %get-tuple-element.95), channel_id=1, source_target_pairs={{0,2},{2,0},{4,6},{6,4},{8,10},{10,8},{12,14},{14,12},{1,3},{3,1},... | collective-permute-start | bytes 580616 | tf_op jit(solution)/shard_map/ppermute | solution.py:561
  37.3 4.6 %attend_same.1 = (bf16[56,576]{1,0:T(8,128)(2,1)S(1)}, bf16[168,576]{1,0:T(8,128)(2,1)S(1)}, bf16[896,512]{1,0:T(8,128)(2,1)S(1)}) custom-call(f32[4,224,896]{2,1,0:T(8,128)S(1)} %get-tuple-element.85.refs_0_, f32[4,224,896]{2,1,0:T(8,128)S(1)} %get-tuple-element.86.refs_1_, bf16[224,512]{1,0:T(8,128)(2,1)S(1)} %get-tuple-element.87.refs_2_, ...), custom_call_target="tpu_custom_call" | custom-call | tf_op jit(solution)/shard_map/attend_same/pallas_call | solution.py:328
  41.9 0.3 collective-permute-done.8
  42.3 1.9 %collective-permute-start.11 = (bf16[56,576]{1,0:T(8,128)(2,1)S(1)}, bf16[56,576]{1,0:T(8,128)(2,1)S(1)}, u32[]{:S(2)}, u32[]{:S(2)}) collective-permute-start(bf16[56,576]{1,0:T(8,128)(2,1)S(1)} %get-tuple-element.146), channel_id=1, source_target_pairs={{0,12},{2,14},{4,8},{6,10},{8,4},{10,6},{12,0},{14,2},{1,13},{3,15... | collective-permute-start | bytes 193544 | tf_op jit(solution)/shard_map/ppermute | solution.py:561
  44.2 2.6 %collective-permute-start.9 = (bf16[56,576]{1,0:T(8,128)(2,1)S(1)}, bf16[56,576]{1,0:T(8,128)(2,1)S(1)}, u32[]{:S(2)}, u32[]{:S(2)}) collective-permute-start(bf16[56,576]{1,0:T(8,128)(2,1)S(1)} %get-tuple-element.148), channel_id=1, source_target_pairs={{0,4},{2,6},{4,0},{6,2},{8,12},{10,14},{12,8},{14,10},{1,5},{3,7},... | collective-permute-start | bytes 193544 | tf_op jit(solution)/shard_map/ppermute | solution.py:561
  46.8 1.0 %collective-permute-start.12 = (bf16[56,576]{1,0:T(8,128)(2,1)S(1)}, bf16[56,576]{1,0:T(8,128)(2,1)S(1)}, u32[]{:S(2)}, u32[]{:S(2)}) collective-permute-start(bf16[56,576]{1,0:T(8,128)(2,1)S(1)} %get-tuple-element.98), channel_id=1, source_target_pairs={{0,2},{2,0},{4,6},{6,4},{8,10},{10,8},{12,14},{14,12},{1,3},{3,1},... | collective-permute-start | bytes 193544 | tf_op jit(solution)/shard_map/ppermute | solution.py:561
  47.8 1.9 %query_side.1 = (bf16[896,288]{1,0:T(8,128)(2,1)S(1)}, f32[288,384]{1,0:T(8,128)S(1)}, bf16[288,384]{1,0:T(8,128)(2,1)S(1)}) custom-call(s32[2]{0:T(128)S(1)} %pad_add_fusion.place, bf16[896,512]{1,0:T(8,128)(2,1)S(1)} %get-tuple-element.99.query_pad, bf16[576,896]{1,0:T(8,128)(2,1)S(1)} %get-tuple-element.100.tokens_t), custom_call_target="tpu_custom_call" | custom-call | tf_op jit(solution)/shard_map/query_side/pallas_call | solution.py:386
  49.7 0.3 collective-permute-done.10
  50.1 1.1 %collective-permute-done.12 = bf16[56,576]{1,0:T(8,128)(2,1)S(1)} collective-permute-done((bf16[56,576]{1,0:T(8,128)(2,1)S(1)}, bf16[56,576]{1,0:T(8,128)(2,1)S(1)}, u32[]{:S(2)}, u32[]{:S(2)}) %collective-permute-start.12) | collective-permute-done | bytes 64544 | tf_op jit(solution)/shard_map/ppermute | solution.py:561
  51.2 1.0 %collective-permute-start.14 = (bf16[56,576]{1,0:T(8,128)(2,1)S(1)}, bf16[56,576]{1,0:T(8,128)(2,1)S(1)}, u32[]{:S(2)}, u32[]{:S(2)}) collective-permute-start(bf16[56,576]{1,0:T(8,128)(2,1)S(1)} %add_convert_fusion.2.swapped), channel_id=1, source_target_pairs={{0,2},{2,0},{4,6},{6,4},{8,10},{10,8},{12,14},{14,12},{1,3},{3,1},... | collective-permute-start | bytes 193544 | tf_op jit(solution)/shard_map/ppermute | solution.py:561
  52.2 2.4 %collective-permute-start.13 = (bf16[56,576]{1,0:T(8,128)(2,1)S(1)}, bf16[56,576]{1,0:T(8,128)(2,1)S(1)}, u32[]{:S(2)}, u32[]{:S(2)}) collective-permute-start(bf16[56,576]{1,0:T(8,128)(2,1)S(1)} %add_convert_fusion.2.swapped), channel_id=1, source_target_pairs={{0,4},{4,8},{6,2},{8,12},{10,6},{14,10},{1,5},{5,9},{7,3},{9,13},{... | collective-permute-start | bytes 193544 | tf_op jit(solution)/shard_map/ppermute | solution.py:561
  54.6 1.7 %collective-permute-done.14.mine = bf16[56,576]{1,0:T(8,128)(2,1)S(1)} collective-permute-done((bf16[56,576]{1,0:T(8,128)(2,1)S(1)}, bf16[56,576]{1,0:T(8,128)(2,1)S(1)}, u32[]{:S(2)}, u32[]{:S(2)}) %collective-permute-start.14) | collective-permute-done | bytes 64544 | tf_op jit(solution)/shard_map/ppermute | solution.py:561
  56.3 0.2 collective-permute-done.13.beside
  56.5 3.0 %collective-permute-start.16 = (bf16[288,384]{1,0:T(8,128)(2,1)S(1)}, bf16[288,384]{1,0:T(8,128)(2,1)S(1)}, u32[]{:S(2)}, u32[]{:S(2)}) collective-permute-start(bf16[288,384]{1,0:T(8,128)(2,1)S(1)} %get-tuple-element.116), channel_id=1, source_target_pairs={{0,2},{2,0},{4,6},{6,4},{8,10},{10,8},{12,14},{14,12},{1,3},{3,1},... | collective-permute-start | bytes 663560 | tf_op jit(solution)/shard_map/ppermute | solution.py:561
  59.5 5.6 %pull_back.1 = (f32[320,576]{1,0:T(8,128)S(1)}, bf16[248,576]{1,0:T(8,128)(2,1)S(1)}, bf16[72,576]{1,0:T(8,128)(2,1)S(1)}, f32[896,288]{1,0:T(8,128)S(1)}, bf16[896,384]{1,0:T(8,128)(2,1)S(1)}) custom-call(s32[2]{0:T(128)S(1)} %pad_add_fusion.place, bf16[56,576]{1,0:T(8,128)(2,1)S(1)} %collective-permute-done.14.mine, ...), custom_call_target="tpu_custom_call" | custom-call | tf_op jit(solution)/shard_map/pull_back/pallas_call | solution.py:489
  65.1 0.5 collective-permute-done.16
  65.7 2.7 %collective-permute-start.19 = (bf16[72,384]{1,0:T(8,128)(2,1)S(1)}, bf16[72,384]{1,0:T(8,128)(2,1)S(1)}, u32[]{:S(2)}, u32[]{:S(2)}) collective-permute-start(bf16[72,384]{1,0:T(8,128)(2,1)S(1)} %get-tuple-element.143), channel_id=1, source_target_pairs={{0,12},{2,14},{4,8},{6,10},{8,4},{10,6},{12,0},{14,2},{1,13},{3,15... | collective-permute-start | bytes 165896 | tf_op jit(solution)/shard_map/ppermute | solution.py:561
  68.4 0.4 collective-permute-start.18
  68.8 1.3 %collective-permute-start.17 = (bf16[72,384]{1,0:T(8,128)(2,1)S(1)}, bf16[72,384]{1,0:T(8,128)(2,1)S(1)}, u32[]{:S(2)}, u32[]{:S(2)}) collective-permute-start(bf16[72,384]{1,0:T(8,128)(2,1)S(1)} %get-tuple-element.145), channel_id=1, source_target_pairs={{0,4},{2,6},{4,0},{6,2},{8,12},{10,14},{12,8},{14,10},{1,5},{3,7},... | collective-permute-start | bytes 165896 | tf_op jit(solution)/shard_map/ppermute | solution.py:561
  70.1 1.6 %collective-permute-done.19 = bf16[72,384]{1,0:T(8,128)(2,1)S(1)} collective-permute-done((bf16[72,384]{1,0:T(8,128)(2,1)S(1)}, bf16[72,384]{1,0:T(8,128)(2,1)S(1)}, u32[]{:S(2)}, u32[]{:S(2)}) %collective-permute-start.19) | collective-permute-done | bytes 55328 | tf_op jit(solution)/shard_map/ppermute | solution.py:561
  71.7 1.8 %collective-permute-done.18 = bf16[72,384]{1,0:T(8,128)(2,1)S(1)} collective-permute-done((bf16[72,384]{1,0:T(8,128)(2,1)S(1)}, bf16[72,384]{1,0:T(8,128)(2,1)S(1)}, u32[]{:S(2)}, u32[]{:S(2)}) %collective-permute-start.18) | collective-permute-done | bytes 55328 | tf_op jit(solution)/shard_map/ppermute | solution.py:561
  73.5 0.1 fusion.2
  73.7 1.1 %collective-permute-start.24 = (bf16[72,576]{1,0:T(8,128)(2,1)S(1)}, bf16[72,576]{1,0:T(8,128)(2,1)S(1)}, u32[]{:S(2)}, u32[]{:S(2)}) collective-permute-start(bf16[72,576]{1,0:T(8,128)(2,1)S(1)} %get-tuple-element.127), channel_id=1, source_target_pairs={{0,2},{2,0},{4,6},{6,4},{8,10},{10,8},{12,14},{14,12},{1,3},{3,1},... | collective-permute-start | bytes 248840 | tf_op jit(solution)/shard_map/ppermute | solution.py:561
  74.8 1.6 %collective-permute-start.21 = (bf16[104,576]{1,0:T(8,128)(2,1)S(1)}, bf16[104,576]{1,0:T(8,128)(2,1)S(1)}, u32[]{:S(2)}, u32[]{:S(2)}) collective-permute-start(bf16[104,576]{1,0:T(8,128)(2,1)S(1)} %get-tuple-element.149), channel_id=1, source_target_pairs={{0,8},{2,10},{4,12},{6,14},{8,0},{10,2},{12,4},{14,6},{1,9},{3,11}... | collective-permute-start | bytes 359432 | tf_op jit(solution)/shard_map/ppermute | solution.py:561
  76.4 0.8 collective-permute-start.20
  77.2 2.1 %collective-permute-start.22 = (bf16[104,576]{1,0:T(8,128)(2,1)S(1)}, bf16[104,576]{1,0:T(8,128)(2,1)S(1)}, u32[]{:S(2)}, u32[]{:S(2)}) collective-permute-start(bf16[104,576]{1,0:T(8,128)(2,1)S(1)} %concatenate.16), channel_id=1, source_target_pairs={{0,12},{2,14},{4,8},{6,10},{8,4},{10,6},{12,0},{14,2},{1,13},{3,15... | collective-permute-start | bytes 359432 | tf_op jit(solution)/shard_map/ppermute | solution.py:561
  79.3 1.0 %add_convert_fusion = bf16[896,288]{1,0:T(8,128)(2,1)} fusion(f32[896,288]{1,0:T(8,128)S(1)} %get-tuple-element.121, bf16[896,384]{1,0:T(8,128)(2,1)S(1)} %collective-permute-done.23), kind=kLoop, calls=%fused_computation | loop fusion | flops 774144 | bytes 2064384 | tf_op jit(solution)/shard_map/convert_element_type | solution.py:658
  80.4 5.0 %collective-permute-done.21.refs_1_ = bf16[104,576]{1,0:T(8,128)(2,1)S(1)} collective-permute-done((bf16[104,576]{1,0:T(8,128)(2,1)S(1)}, bf16[104,576]{1,0:T(8,128)(2,1)S(1)}, u32[]{:S(2)}, u32[]{:S(2)}) %collective-permute-start.21) | collective-permute-done | bytes 119840 | tf_op jit(solution)/shard_map/ppermute | solution.py:561
  85.3 0.9 %finish.1 = (f32[3,72,288]{2,1,0:T(8,128)}, f32[27,2,288]{2,1,0:T(2,128)}) custom-call(f32[72,384]{1,0:T(8,128)S(1)} %fusion.1.query_sum, f32[72,576]{1,0:T(8,128)S(1)} %convert_add_fusion.2.own_sum, f32[32,576]{1,0:T(8,128)S(1)} %slice.71.tail_sum, bf16[104,576]{1,0:T(8,128)(2,1)S(1)} %collective-permute-done.20.refs_0_, ...), custom_call_target="tpu_custom_call" | custom-call | tf_op jit(solution)/shard_map/finish/pallas_call | solution.py:536
  (37 shorter events, 0.5 us)
Async XLA Ops:
  0.6 1.9 %copy-start.1 = (bf16[1,16,56,288]{3,2,1,0:T(8,128)(2,1)S(1)}, bf16[1,16,56,288]{3,2,1,0:T(8,128)(2,1)}, u32[]{:S(2)}) copy-start(bf16[1,16,56,288]{3,2,1,0:T(8,128)(2,1)} %param.5) | copy-start | bytes 1548292
  0.6 3.6 %copy-start = (bf16[3,576,288]{1,2,0:T(8,128)(2,1)S(1)}, bf16[3,576,288]{1,2,0:T(8,128)(2,1)}, u32[]{:S(2)}) copy-start(bf16[3,576,288]{1,2,0:T(8,128)(2,1)} %param.6) | copy-start | bytes 2985988
  0.7 3.6 %copy-start.2 = (f32[2,27,288]{2,0,1:T(2,128)S(1)}, f32[2,27,288]{2,0,1:T(2,128)}, u32[]{:S(2)}) copy-start(f32[2,27,288]{2,0,1:T(2,128)} %param.7) | copy-start | bytes 186628
  2.0 2.3 %collective-permute-start = (bf16[896,384]{1,0:T(8,128)(2,1)S(1)}, bf16[896,384]{1,0:T(8,128)(2,1)S(1)}, u32[]{:S(2)}, u32[]{:S(2)}) collective-permute-start(bf16[896,384]{1,0:T(8,128)(2,1)S(1)} %pad.4.own), channel_id=1, source_target_pairs={{0,1},{1,0},{2,3},{3,2},{4,5},{5,4},{6,7},{7,6},{8,9},{9,8},{10,11... | collective-permute-start | bytes 2064392 | tf_op jit(solution)/shard_map/ppermute | solution.py:565
  6.3 5.5 %collective-permute-start.1 = (bf16[56,576]{1,0:T(8,128)(2,1)S(1)}, bf16[56,576]{1,0:T(8,128)(2,1)S(1)}, u32[]{:S(2)}, u32[]{:S(2)}) collective-permute-start(bf16[56,576]{1,0:T(8,128)(2,1)S(1)} %get-tuple-element.72), channel_id=1, source_target_pairs={{0,2},{2,0},{4,6},{6,4},{8,10},{10,8},{12,14},{14,12},{1,3},{3,1},... | collective-permute-start | bytes 193544 | tf_op jit(solution)/shard_map/ppermute | solution.py:561
  9.3 6.2 %collective-permute-start.2 = (bf16[56,576]{1,0:T(8,128)(2,1)S(1)}, bf16[56,576]{1,0:T(8,128)(2,1)S(1)}, u32[]{:S(2)}, u32[]{:S(2)}) collective-permute-start(bf16[56,576]{1,0:T(8,128)(2,1)S(1)} %get-tuple-element.73), channel_id=1, source_target_pairs={{2,6},{4,0},{6,10},{8,4},{10,14},{12,8},{3,7},{5,1},{7,11},{9,5},{... | collective-permute-start | bytes 193544 | tf_op jit(solution)/shard_map/ppermute | solution.py:561
  15.5 7.2 %collective-permute-start.6 = (bf16[56,576]{1,0:T(8,128)(2,1)S(1)}, bf16[56,576]{1,0:T(8,128)(2,1)S(1)}, u32[]{:S(2)}, u32[]{:S(2)}) collective-permute-start(bf16[56,576]{1,0:T(8,128)(2,1)S(1)} %add_convert_fusion.3.first), channel_id=1, source_target_pairs={{0,2},{2,0},{4,6},{6,4},{8,10},{10,8},{12,14},{14,12},{1,3},{3,1},... | collective-permute-start | bytes 193544 | tf_op jit(solution)/shard_map/ppermute | solution.py:561
  15.6 7.2 %collective-permute-start.5 = (bf16[56,576]{1,0:T(8,128)(2,1)S(1)}, bf16[56,576]{1,0:T(8,128)(2,1)S(1)}, u32[]{:S(2)}, u32[]{:S(2)}) collective-permute-start(bf16[56,576]{1,0:T(8,128)(2,1)S(1)} %add_convert_fusion.3.first), channel_id=1, source_target_pairs={{0,12},{2,14},{4,8},{6,10},{8,4},{10,6},{12,0},{14,2},{1,13},{3,15... | collective-permute-start | bytes 193544 | tf_op jit(solution)/shard_map/ppermute | solution.py:561
  19.7 5.2 %collective-permute-start.4 = (bf16[56,576]{1,0:T(8,128)(2,1)S(1)}, bf16[56,576]{1,0:T(8,128)(2,1)S(1)}, u32[]{:S(2)}, u32[]{:S(2)}) collective-permute-start(bf16[56,576]{1,0:T(8,128)(2,1)S(1)} %add_convert_fusion.3.first), channel_id=1, source_target_pairs={{0,8},{2,10},{4,12},{6,14},{8,0},{10,2},{12,4},{14,6},{1,9},{3,11}... | collective-permute-start | bytes 193544 | tf_op jit(solution)/shard_map/ppermute | solution.py:561
  19.7 5.2 %collective-permute-start.3 = (bf16[56,576]{1,0:T(8,128)(2,1)S(1)}, bf16[56,576]{1,0:T(8,128)(2,1)S(1)}, u32[]{:S(2)}, u32[]{:S(2)}) collective-permute-start(bf16[56,576]{1,0:T(8,128)(2,1)S(1)} %add_convert_fusion.3.first), channel_id=1, source_target_pairs={{0,4},{2,6},{4,0},{6,2},{8,12},{10,14},{12,8},{14,10},{1,5},{3,7},... | collective-permute-start | bytes 193544 | tf_op jit(solution)/shard_map/ppermute | solution.py:561
  25.0 6.3 %collective-permute-start.7 = (bf16[168,576]{1,0:T(8,128)(2,1)S(1)}, bf16[168,576]{1,0:T(8,128)(2,1)S(1)}, u32[]{:S(2)}, u32[]{:S(2)}) collective-permute-start(bf16[168,576]{1,0:T(8,128)(2,1)S(1)} %constant_dynamic-update-slice_fusion.rest), channel_id=1, source_target_pairs={{0,2},{2,0},{4,6},{6,4},{8,10},{10,8},{12,14},{14,12},{1,3},{3,1},... | collective-permute-start | bytes 580616 | tf_op jit(solution)/shard_map/ppermute | solution.py:561
  36.3 5.9 %collective-permute-start.8 = (bf16[168,576]{1,0:T(8,128)(2,1)S(1)}, bf16[168,576]{1,0:T(8,128)(2,1)S(1)}, u32[]{:S(2)}, u32[]{:S(2)}) collective-permute-start(bf16[168,576]{1,0:T(8,128)(2,1)S(1)} %get-tuple-element.95), channel_id=1, source_target_pairs={{0,2},{2,0},{4,6},{6,4},{8,10},{10,8},{12,14},{14,12},{1,3},{3,1},... | collective-permute-start | bytes 580616 | tf_op jit(solution)/shard_map/ppermute | solution.py:561
  42.3 7.4 %collective-permute-start.11 = (bf16[56,576]{1,0:T(8,128)(2,1)S(1)}, bf16[56,576]{1,0:T(8,128)(2,1)S(1)}, u32[]{:S(2)}, u32[]{:S(2)}) collective-permute-start(bf16[56,576]{1,0:T(8,128)(2,1)S(1)} %get-tuple-element.146), channel_id=1, source_target_pairs={{0,12},{2,14},{4,8},{6,10},{8,4},{10,6},{12,0},{14,2},{1,13},{3,15... | collective-permute-start | bytes 193544 | tf_op jit(solution)/shard_map/ppermute | solution.py:561
  44.2 5.8 %collective-permute-start.10 = (bf16[56,576]{1,0:T(8,128)(2,1)S(1)}, bf16[56,576]{1,0:T(8,128)(2,1)S(1)}, u32[]{:S(2)}, u32[]{:S(2)}) collective-permute-start(bf16[56,576]{1,0:T(8,128)(2,1)S(1)} %get-tuple-element.147), channel_id=1, source_target_pairs={{0,8},{2,10},{4,12},{6,14},{8,0},{10,2},{12,4},{14,6},{1,9},{3,11}... | collective-permute-start | bytes 193544 | tf_op jit(solution)/shard_map/ppermute | solution.py:561
  44.2 5.8 %collective-permute-start.9 = (bf16[56,576]{1,0:T(8,128)(2,1)S(1)}, bf16[56,576]{1,0:T(8,128)(2,1)S(1)}, u32[]{:S(2)}, u32[]{:S(2)}) collective-permute-start(bf16[56,576]{1,0:T(8,128)(2,1)S(1)} %get-tuple-element.148), channel_id=1, source_target_pairs={{0,4},{2,6},{4,0},{6,2},{8,12},{10,14},{12,8},{14,10},{1,5},{3,7},... | collective-permute-start | bytes 193544 | tf_op jit(solution)/shard_map/ppermute | solution.py:561
  46.8 4.3 %collective-permute-start.12 = (bf16[56,576]{1,0:T(8,128)(2,1)S(1)}, bf16[56,576]{1,0:T(8,128)(2,1)S(1)}, u32[]{:S(2)}, u32[]{:S(2)}) collective-permute-start(bf16[56,576]{1,0:T(8,128)(2,1)S(1)} %get-tuple-element.98), channel_id=1, source_target_pairs={{0,2},{2,0},{4,6},{6,4},{8,10},{10,8},{12,14},{14,12},{1,3},{3,1},... | collective-permute-start | bytes 193544 | tf_op jit(solution)/shard_map/ppermute | solution.py:561
  51.2 5.1 %collective-permute-start.14 = (bf16[56,576]{1,0:T(8,128)(2,1)S(1)}, bf16[56,576]{1,0:T(8,128)(2,1)S(1)}, u32[]{:S(2)}, u32[]{:S(2)}) collective-permute-start(bf16[56,576]{1,0:T(8,128)(2,1)S(1)} %add_convert_fusion.2.swapped), channel_id=1, source_target_pairs={{0,2},{2,0},{4,6},{6,4},{8,10},{10,8},{12,14},{14,12},{1,3},{3,1},... | collective-permute-start | bytes 193544 | tf_op jit(solution)/shard_map/ppermute | solution.py:561
  52.2 4.3 %collective-permute-start.13 = (bf16[56,576]{1,0:T(8,128)(2,1)S(1)}, bf16[56,576]{1,0:T(8,128)(2,1)S(1)}, u32[]{:S(2)}, u32[]{:S(2)}) collective-permute-start(bf16[56,576]{1,0:T(8,128)(2,1)S(1)} %add_convert_fusion.2.swapped), channel_id=1, source_target_pairs={{0,4},{4,8},{6,2},{8,12},{10,6},{14,10},{1,5},{5,9},{7,3},{9,13},{... | collective-permute-start | bytes 193544 | tf_op jit(solution)/shard_map/ppermute | solution.py:561
  56.5 9.1 %collective-permute-start.16 = (bf16[288,384]{1,0:T(8,128)(2,1)S(1)}, bf16[288,384]{1,0:T(8,128)(2,1)S(1)}, u32[]{:S(2)}, u32[]{:S(2)}) collective-permute-start(bf16[288,384]{1,0:T(8,128)(2,1)S(1)} %get-tuple-element.116), channel_id=1, source_target_pairs={{0,2},{2,0},{4,6},{6,4},{8,10},{10,8},{12,14},{14,12},{1,3},{3,1},... | collective-permute-start | bytes 663560 | tf_op jit(solution)/shard_map/ppermute | solution.py:561
  65.0 8.5 %collective-permute-start.15 = (bf16[248,576]{1,0:T(8,128)(2,1)S(1)}, bf16[248,576]{1,0:T(8,128)(2,1)S(1)}, u32[]{:S(2)}, u32[]{:S(2)}) collective-permute-start(bf16[248,576]{1,0:T(8,128)(2,1)S(1)} %get-tuple-element.114), channel_id=1, source_target_pairs={{0,2},{2,0},{4,6},{6,4},{8,10},{10,8},{12,14},{14,12},{1,3},{3,1},... | collective-permute-start | bytes 857096 | tf_op jit(solution)/shard_map/ppermute | solution.py:561
  65.7 6.0 %collective-permute-start.19 = (bf16[72,384]{1,0:T(8,128)(2,1)S(1)}, bf16[72,384]{1,0:T(8,128)(2,1)S(1)}, u32[]{:S(2)}, u32[]{:S(2)}) collective-permute-start(bf16[72,384]{1,0:T(8,128)(2,1)S(1)} %get-tuple-element.143), channel_id=1, source_target_pairs={{0,12},{2,14},{4,8},{6,10},{8,4},{10,6},{12,0},{14,2},{1,13},{3,15... | collective-permute-start | bytes 165896 | tf_op jit(solution)/shard_map/ppermute | solution.py:561
  68.4 5.2 %collective-permute-start.18 = (bf16[72,384]{1,0:T(8,128)(2,1)S(1)}, bf16[72,384]{1,0:T(8,128)(2,1)S(1)}, u32[]{:S(2)}, u32[]{:S(2)}) collective-permute-start(bf16[72,384]{1,0:T(8,128)(2,1)S(1)} %get-tuple-element.144), channel_id=1, source_target_pairs={{0,8},{2,10},{4,12},{6,14},{8,0},{10,2},{12,4},{14,6},{1,9},{3,11}... | collective-permute-start | bytes 165896 | tf_op jit(solution)/shard_map/ppermute | solution.py:561
  68.8 4.7 %collective-permute-start.17 = (bf16[72,384]{1,0:T(8,128)(2,1)S(1)}, bf16[72,384]{1,0:T(8,128)(2,1)S(1)}, u32[]{:S(2)}, u32[]{:S(2)}) collective-permute-start(bf16[72,384]{1,0:T(8,128)(2,1)S(1)} %get-tuple-element.145), channel_id=1, source_target_pairs={{0,4},{2,6},{4,0},{6,2},{8,12},{10,14},{12,8},{14,10},{1,5},{3,7},... | collective-permute-start | bytes 165896 | tf_op jit(solution)/shard_map/ppermute | solution.py:561
  70.1 9.2 %collective-permute-start.23 = (bf16[896,384]{1,0:T(8,128)(2,1)S(1)}, bf16[896,384]{1,0:T(8,128)(2,1)S(1)}, u32[]{:S(2)}, u32[]{:S(2)}) collective-permute-start(bf16[896,384]{1,0:T(8,128)(2,1)S(1)} %get-tuple-element.122), channel_id=1, source_target_pairs={{0,1},{1,0},{2,3},{3,2},{4,5},{5,4},{6,7},{7,6},{8,9},{9,8},{10,11... | collective-permute-start | bytes 2064392 | tf_op jit(solution)/shard_map/ppermute | solution.py:565
  73.7 5.6 %collective-permute-start.24 = (bf16[72,576]{1,0:T(8,128)(2,1)S(1)}, bf16[72,576]{1,0:T(8,128)(2,1)S(1)}, u32[]{:S(2)}, u32[]{:S(2)}) collective-permute-start(bf16[72,576]{1,0:T(8,128)(2,1)S(1)} %get-tuple-element.127), channel_id=1, source_target_pairs={{0,2},{2,0},{4,6},{6,4},{8,10},{10,8},{12,14},{14,12},{1,3},{3,1},... | collective-permute-start | bytes 248840 | tf_op jit(solution)/shard_map/ppermute | solution.py:561
  74.8 10.5 %collective-permute-start.21 = (bf16[104,576]{1,0:T(8,128)(2,1)S(1)}, bf16[104,576]{1,0:T(8,128)(2,1)S(1)}, u32[]{:S(2)}, u32[]{:S(2)}) collective-permute-start(bf16[104,576]{1,0:T(8,128)(2,1)S(1)} %get-tuple-element.149), channel_id=1, source_target_pairs={{0,8},{2,10},{4,12},{6,14},{8,0},{10,2},{12,4},{14,6},{1,9},{3,11}... | collective-permute-start | bytes 359432 | tf_op jit(solution)/shard_map/ppermute | solution.py:561
  76.4 8.9 %collective-permute-start.20 = (bf16[104,576]{1,0:T(8,128)(2,1)S(1)}, bf16[104,576]{1,0:T(8,128)(2,1)S(1)}, u32[]{:S(2)}, u32[]{:S(2)}) collective-permute-start(bf16[104,576]{1,0:T(8,128)(2,1)S(1)} %get-tuple-element.150), channel_id=1, source_target_pairs={{0,4},{2,6},{4,0},{6,2},{8,12},{10,14},{12,8},{14,10},{1,5},{3,7},... | collective-permute-start | bytes 359432 | tf_op jit(solution)/shard_map/ppermute | solution.py:561
  77.2 8.1 %collective-permute-start.22 = (bf16[104,576]{1,0:T(8,128)(2,1)S(1)}, bf16[104,576]{1,0:T(8,128)(2,1)S(1)}, u32[]{:S(2)}, u32[]{:S(2)}) collective-permute-start(bf16[104,576]{1,0:T(8,128)(2,1)S(1)} %concatenate.16), channel_id=1, source_target_pairs={{0,12},{2,14},{4,8},{6,10},{8,4},{10,6},{12,0},{14,2},{1,13},{3,15... | collective-permute-start | bytes 359432 | tf_op jit(solution)/shard_map/ppermute | solution.py:561

commit v5 on v4

--- a/solution.py
+++ b/solution.py
@@ -10,9 +10,10 @@
 
 HEADS = 8
 LANES = 128
+STEP = 4
 F32 = jnp.float32
 BF16 = jnp.bfloat16
-PARAMS = pltpu.CompilerParams(vmem_limit_bytes=16 * 1024 * 1024)
+PARAMS = pltpu.CompilerParams(vmem_limit_bytes=24 * 1024 * 1024)
 NN = (((1,), (0,)), ((), ()))
 NT = (((1,), (1,)), ((), ()))
 TN = (((0,), (0,)), ((), ()))
@@ -198,63 +199,70 @@
     geometry, first, rest, query_t, grad_t, sums, raised_out, prob_grad_out, key_pad
 ):
     head_dim, local, heads = geometry
-    chosen = choose_head(head_dim, local, pl.program_id(0))
-    key, raised, prob_grad = head_products(
-        head_dim, (first, rest), chosen, query_t[...], grad_t[...]
-    )
-    raised_out[0] = raised
-    prob_grad_out[0] = prob_grad
-    key_pad[...] = key
-    sums[0, 0:1, :] = jnp.sum(raised, axis=0, keepdims=True)
-    sums[0, 1:2, :] = jnp.sum(raised * prob_grad, axis=0, keepdims=True)
+    for sub in range(STEP):
+        rows = slice(sub * LANES, (sub + 1) * LANES)
+        chosen = choose_head(head_dim, local, STEP * pl.program_id(0) + sub)
+        key, raised, prob_grad = head_products(
+            head_dim, (first, rest), chosen, query_t[rows, :], grad_t[rows, :]
+        )
+        raised_out[sub] = raised
+        prob_grad_out[sub] = prob_grad
+        key_pad[:, rows] = key
+        sums[sub, 0:1, :] = jnp.sum(raised, axis=0, keepdims=True)
+        sums[sub, 1:2, :] = jnp.sum(raised * prob_grad, axis=0, keepdims=True)
 
 
 def attend_body(geometry, final, *refs):
     head_dim, local, heads = geometry
-    head = pl.program_id(0)
+    step = pl.program_id(0)
     scale = head_dim ** (-0.5)
-    chosen = choose_head(head_dim, local, head)
     if final:
         own_raised, own_prob_grad, own_pad, query_t, grad_t, sums, *refs = refs
         other_pad, other_scores, first_grads, rest_grads, query_grad, total = refs
-        query, grad = query_t[...], grad_t[...]
-        key, raised, prob_grad = own_pad[...], own_raised[0], own_prob_grad[0]
-        inverse, centre = sums[0, 0:1, :], sums[0, 1:2, :]
     else:
         first, rest, query_t, grad_t, sums, *refs = refs
         first_grads, rest_grads, key_pad, score_grads, totals, total = refs
-        query, grad = query_t[...], grad_t[...]
-        key, raised, prob_grad = head_products(head_dim, (first, rest), chosen, query, grad)
-        inverse = 1.0 / (sums[0, 0:1, :] + jnp.sum(raised, axis=0, keepdims=True))
-        weighted = sums[0, 1:2, :] + jnp.sum(raised * prob_grad, axis=0, keepdims=True)
-        centre = weighted * inverse
-        totals[0, 0:1, :] = inverse
-        totals[0, 1:2, :] = centre
-    probs = raised * inverse
-    score_grad = (probs * (prob_grad - centre) * scale).astype(BF16)
-    if final:
-        turn = identity(LANES)
-        back_t = grad.astype(F32)
-        for keys, scores in ((key, score_grad), (other_pad[...], other_scores[0])):
-            back_t = back_t + mul(mul(turn, keys, NT).astype(BF16), scores)
-        query_grad[...] = back_t.T.astype(BF16)
-    else:
-        key_pad[...] = key
-        score_grads[0] = score_grad
-    value_back = mul(probs.astype(BF16), grad, NT)
-    key_back = mul(score_grad, query, NT)
-    joined = jnp.concatenate([key_back, value_back], axis=1).astype(BF16)
-    placed = mul(joined, chosen, NT)
-
-    @pl.when(head == 0)
+    joined, choices = [], []
+    for sub in range(STEP):
+        rows = slice(sub * LANES, (sub + 1) * LANES)
+        chosen = choose_head(head_dim, local, STEP * step + sub)
+        query, grad = query_t[rows, :], grad_t[rows, :]
+        if final:
+            key, raised, prob_grad = own_pad[:, rows], own_raised[sub], own_prob_grad[sub]
+            inverse, centre = sums[sub, 0:1, :], sums[sub, 1:2, :]
+        else:
+            key, raised, prob_grad = head_products(head_dim, (first, rest), chosen, query, grad)
+            inverse = 1.0 / (sums[sub, 0:1, :] + jnp.sum(raised, axis=0, keepdims=True))
+            weighted = sums[sub, 1:2, :] + jnp.sum(raised * prob_grad, axis=0, keepdims=True)
+            centre = weighted * inverse
+            totals[sub, 0:1, :] = inverse
+            totals[sub, 1:2, :] = centre
+        probs = raised * inverse
+        score_grad = (probs * (prob_grad - centre) * scale).astype(BF16)
+        if final:
+            turn = identity(LANES)
+            back_t = grad.astype(F32)
+            for keys, scores in ((key, score_grad), (other_pad[:, rows], other_scores[sub])):
+                back_t = back_t + mul(mul(turn, keys, NT).astype(BF16), scores)
+            query_grad[:, rows] = back_t.T.astype(BF16)
+        else:
+            key_pad[:, rows] = key
+            score_grads[sub] = score_grad
+        value_back = mul(probs.astype(BF16), grad, NT)
+        key_back = mul(score_grad, query, NT)
+        joined += [key_back.astype(BF16), value_back.astype(BF16)]
+        choices.append(chosen)
+    placed = mul(jnp.concatenate(joined, axis=1), jnp.concatenate(choices, axis=1), NT)
+
+    @pl.when(step == 0)
     def _():
         total[...] = placed
 
-    @pl.when(head > 0)
+    @pl.when(step > 0)
     def _():
         total[...] += placed
 
-    @pl.when(head == heads - 1)
+    @pl.when(step == heads // STEP - 1)
     def _():
         split = first_grads.shape[0]
         first_grads[...] = total[:split, :].astype(BF16)
@@ -266,10 +274,10 @@
 
 
 def head_specs(tokens, key_count):
-    rows = pl.BlockSpec((LANES, tokens), lambda h: (h, 0))
-    sums = pl.BlockSpec((1, 8, tokens), lambda h: (h, 0, 0))
-    keys = pl.BlockSpec((key_count, LANES), lambda h: (0, h))
-    scores = pl.BlockSpec((1, key_count, tokens), lambda h: (h, 0, 0))
+    rows = pl.BlockSpec((STEP * LANES, tokens), lambda h: (h, 0))
+    sums = pl.BlockSpec((STEP, 8, tokens), lambda h: (h, 0, 0))
+    keys = pl.BlockSpec((key_count, STEP * LANES), lambda h: (0, h))
+    scores = pl.BlockSpec((STEP, key_count, tokens), lambda h: (h, 0, 0))
     return rows, sums, keys, scores
 
 
@@ -280,7 +288,7 @@
     row_spec, sum_spec, key_spec, score_spec = head_specs(tokens, key_count)
     return pl.pallas_call(
         functools.partial(measure_body, (head_dim, local, heads)),
-        grid=(heads,),
+        grid=(heads // STEP,),
         out_shape=(
             pltpu.VMEM((heads, 8, tokens), F32),
             pltpu.VMEM((heads, key_count, tokens), F32),
@@ -301,7 +309,7 @@
     row_spec, sum_spec, key_spec, score_spec = head_specs(tokens, key_count)
     return pl.pallas_call(
         functools.partial(attend_body, (head_dim, local, heads), False),
-        grid=(heads,),
+        grid=(heads // STEP,),
         out_shape=(
             pltpu.VMEM(first.shape, BF16),
             pltpu.VMEM(rest.shape, BF16),
@@ -327,45 +335,31 @@
     in_specs = [score_spec, score_spec, key_spec, row_spec, row_spec, sum_spec]
     return pl.pallas_call(
         functools.partial(attend_body, (head_dim, local, heads), True),
-        grid=(heads,),
+        grid=(heads // STEP,),
         out_shape=(*outs, pltpu.VMEM((tokens, heads * LANES), BF16)),
         in_specs=[*in_specs, key_spec, score_spec],
-        out_specs=(*specs, pl.BlockSpec((tokens, LANES), lambda h: (0, h))),
+        out_specs=(*specs, pl.BlockSpec((tokens, STEP * LANES), lambda h: (0, h))),
         scratch_shapes=[pltpu.VMEM((key_count, 2 * local), F32)],
         compiler_params=PARAMS,
         name="attend_same",
     )(*near_core(*saved, query_t, grad_t, totals, *extra))
 
 
-def store_blocks(position, count, rows, column, here, away, away_own=None):
+def store_blocks(position, count, rows, column, here, away):
     padded = round_up(rows, 8)
     width = column.shape[1]
     for j in range(count):
         relative = position ^ j
-        outer = relative // 2
+        at = pl.multiple_of((relative // 2) * padded, 8)
         value = column[j * rows : (j + 1) * rows, :]
 
         @pl.when(relative % 2 == 0)
-        def _(value=value, outer=outer):
-            here[pl.ds(pl.multiple_of(outer * padded, 8), rows), :width] = value
-
-        if away_own is None:
-
-            @pl.when(relative % 2 == 1)
-            def _(value=value, outer=outer):
-                at = pl.multiple_of(outer * padded, 8)
-                away[pl.ds(at, rows), :width] = value.astype(BF16)
-
-        else:
-
-            @pl.when(relative == 1)
-            def _(value=value):
-                away_own[:rows, :width] = value.astype(BF16)
-
-            @pl.when((relative % 2 == 1) & (relative > 1))
-            def _(value=value, outer=outer):
-                at = pl.multiple_of((outer - 1) * padded, 8)
-                away[pl.ds(at, rows), :width] = value.astype(BF16)
+        def _(value=value, at=at):
+            here[pl.ds(at, rows), :width] = value
+
+        @pl.when(relative % 2 == 1)
+        def _(value=value, at=at):
+            away[pl.ds(at, rows), :width] = value.astype(BF16)
 
 
 def query_side_body(geometry, place, query_pad, tokens_t, query_back, here, away):
@@ -406,13 +400,9 @@
     windows,
     taps,
     tokens_t,
-    weights,
-    query_back,
     here,
     away,
-    away_own,
-    token_near,
-    token_far,
+    backs,
     wide,
     staged,
     joint,
@@ -433,7 +423,6 @@
     if padded > block_rows:
         here[...] = jnp.zeros(here.shape, F32)
         away[...] = jnp.zeros(away.shape, BF16)
-        away_own[...] = jnp.zeros(away_own.shape, BF16)
     partner, distant = swapped[...].astype(F32), beside[...].astype(F32)
     grads = [
         jnp.where(even, partner, distant),
@@ -465,12 +454,17 @@
     back = jnp.concatenate(
         [wide[tile, 8:, :width] for tile, low, width in lane_tiles(2 * local)], axis=1
     ).astype(BF16)
+    backs[...] = back
     column = mul(tokens_t[...], back)
     here[outer * padded :, :] = folded[...]
-    away[(outer - 1) * padded :, :] = folded[...].astype(BF16)
-    store_blocks(position, count, block_rows, column, here, away, away_own)
+    away[outer * padded :, :] = folded[...].astype(BF16)
+    store_blocks(position, count, block_rows, column, here, away)
+
+
+def token_body(place, query_back, backs, weights, token_near, token_far):
+    local = weights.shape[1]
     both = weights[1:3].reshape(2 * local, 2 * local)
-    token_sum = mul(query_back[...], weights[0]) + mul(back, both)
+    token_sum = mul(query_back[...], weights[0]) + mul(backs[...], both)
     first = place[1] == 0
     low_half, high_half = token_sum[:, :local], token_sum[:, local:]
     token_near[...] = jnp.where(first, low_half, high_half)
@@ -478,8 +472,23 @@
     token_far[:, local:] = jnp.zeros((token_far.shape[0], token_far.shape[1] - local), BF16)
 
 
+def token_call(place, query_back, backs, weights):
+    tokens, local = query_back.shape
+    return pl.pallas_call(
+        token_body,
+        out_shape=(
+            pltpu.VMEM((tokens, local), F32),
+            pltpu.VMEM((tokens, round_up(local, LANES)), BF16),
+        ),
+        in_specs=[smem()] + [vmem()] * 3,
+        out_specs=(vmem(),) * 2,
+        compiler_params=PARAMS,
+        name="token_side",
+    )(place, *near_core(query_back, backs), weights)
+
+
 def pull_call(
-    place, mine, swapped, beside, windows, taps, tokens_t, weights, query_back, rows, cols, count
+    place, mine, swapped, beside, windows, taps, tokens_t, rows, cols, count
 ):
     both, tokens = tokens_t.shape
     local = both // 2
@@ -490,13 +499,11 @@
         functools.partial(pull_body, (rows, cols, local, count)),
         out_shape=(
             pltpu.VMEM((size, both), F32),
-            pltpu.VMEM((size - padded, both), BF16),
-            pltpu.VMEM((padded, both), BF16),
-            pltpu.VMEM((tokens, local), F32),
-            pltpu.VMEM((tokens, round_up(local, LANES)), BF16),
-        ),
-        in_specs=[smem()] + [vmem()] * 8,
-        out_specs=(vmem(),) * 5,
+            pltpu.VMEM((size, both), BF16),
+            pltpu.VMEM((tokens, both), BF16),
+        ),
+        in_specs=[smem()] + [vmem()] * 6,
+        out_specs=(vmem(),) * 3,
         scratch_shapes=[
             pltpu.VMEM((tiles, tokens + 8, LANES), F32),
             pltpu.VMEM((tiles, rows * cols // 16, LANES), F32),
@@ -511,8 +518,6 @@
         windows,
         taps,
         *near_core(tokens_t),
-        weights,
-        *near_core(query_back),
     )
 
 
@@ -621,51 +626,43 @@
     first_other, rest_other, *for_other, totals = attend_call(
         other_first, other_rest, query_t, grad_t, sums, head_dim
     )
-    rest_moved = exchange(rest_other, across_pair)
+    all_moved = exchange(jnp.concatenate([first_other, rest_other]), across_pair)
     step_rows = block.shape[0]
     first_same, rest_same, query_pad = attend_final_call(
         saved, query_t, grad_t, totals, for_other, head_dim, local, step_rows
     )
-    rest_moved, first_other = barrier((rest_moved, first_other))
+    first_moved, rest_moved = all_moved[:step_rows], all_moved[step_rows:]
     low = (rest_same.astype(F32) + rest_moved.astype(F32)).astype(BF16)
     pieces = [
         exchange(low[(s - 1) * step_rows : s * step_rows], frame_pairs(s, 0))
         for s in range(1, outer)
     ]
-    first_moved = exchange(first_other, across_pair)
     query_back, query_here, query_away = query_side_call(
         place, query_pad, tokens_t, head_dim, count
     )
-    pieces, first_moved, query_back, query_here, query_away = barrier(
-        (pieces, first_moved, query_back, query_here, query_away)
+    query_moved = exchange(query_away, across_pair)
+    pieces, first_moved, query_back, query_here = barrier(
+        (pieces, first_moved, query_back, query_here)
     )
     summed = first_same.astype(F32) + first_moved.astype(F32)
     swapped = add_all(summed, pieces).astype(BF16)
     beside = exchange(swapped, outer_pairs(-1))
     mine = exchange(swapped, frame_pairs(0, 1))
-    beside, mine, query_away = barrier((beside, mine, query_away))
-    query_moved = exchange(query_away, across_pair)
+    beside, mine = barrier((beside, mine))
     block_rows = 2 * local // count
     padded = round_up(block_rows, 8)
-    here, away, away_own, near, far = pull_call(
-        place, mine, swapped, beside, windows, taps, tokens_t, weights, query_back, rows, cols, count
-    )
+    here, away, backs = pull_call(
+        place, mine, swapped, beside, windows, taps, tokens_t, rows, cols, count
+    )
+    query_moved, backs = barrier((query_moved, backs))
+    near, far = token_call(place, query_back, backs, weights)
     moved = exchange(away, frame_pairs(0, 1))
-    query_moved, near, far = barrier((query_moved, near, far))
     query_own, query_pieces = scatter_weights(query_here, query_moved, padded)
     moved, query_pieces = barrier((moved, query_pieces))
     query_sum = add_all(query_own, query_pieces)
     input_grad = (near + across(far)[:, :local].astype(F32)).astype(BF16)
-    rest_sum = here[padded:] + moved.astype(F32)
-    low, end = rest_sum.astype(BF16), (outer - 1) * padded
-    pieces = [
-        exchange(
-            jnp.concatenate([low[(s - 1) * padded : s * padded], low[end:]]), frame_pairs(s, 0)
-        )
-        for s in range(1, outer)
-    ]
-    own_moved = exchange(barrier((away_own, moved))[0], across_pair)
-    own_sum, tail_sum = here[:padded] + own_moved.astype(F32), rest_sum[end:]
+    own_sum, pieces = scatter_weights(here, moved, padded)
+    own_sum, tail_sum = own_sum[:padded], own_sum[padded:]
     pieces, input_grad, query_sum, own_sum, tail_sum = barrier(
         (pieces, input_grad, query_sum, own_sum, tail_sum)
     )

time: 86.4 us -> 83.2 us (0.963)
  Pallas kernels: 25.7 us -> 23.5 us
    pallas_call x0 -> x1, Pallas kernels: none -> 2.79 us  [token_call(): pl.pallas_call(token_body, out_shape=(pltpu.VMEM((tokens, local), F32), p...]
    pallas_call x1, Pallas kernels: 5.56 us -> 2.97 us  [pull_call(): pl.pallas_call(functools.partial(pull_body, (rows, cols, local, count)),...]
    pallas_call x1, Pallas kernels: 4.56 us -> 3.31 us  [attend_final_call(): pl.pallas_call(functools.partial(attend_body, (head_dim, local, heads), T...]
    pallas_call x1, Pallas kernels: 4.94 us -> 4.04 us  [attend_call(): pl.pallas_call(functools.partial(attend_body, (head_dim, local, heads), F...]
    ppermute x23 -> x21, starting transfers between devices: 33.2 us -> 32.4 us  [exchange(): return lax.ppermute(block, 'frames', pairs)]
    ppermute x23 -> x21, waiting for transfers between devices: 21.9 us -> 21.2 us  [exchange(): return lax.ppermute(block, 'frames', pairs)]
  transfers between devices with their start and end apart: 25 -> 23, of which waited for: 14 -> 11; matrix products, arithmetic and copies ran while one was open for 2% -> 2% of each run, Pallas kernels for 21% -> 20%
where the time goes in v5:
time: 83.2 us; the launch traced here: 82.6 us
  starting transfers between devices  33 us (40%)
  Pallas kernels  23.5 us (28%)
  waiting for transfers between devices  22.2 us (27%)
  other arithmetic  1.49 us (2%)
  local copies, waits for them, and re-layouts  1.46 us (2%)
  between operations  0.93 us (1%)
    ppermute x21, starting transfers between devices, exchange(): return lax.ppermute(block, 'frames', pairs)  32.4 us
    ppermute x21, waiting for transfers between devices, exchange(): return lax.ppermute(block, 'frames', pairs)  21.2 us
    pallas_call x1, Pallas kernels, attend_call(): pl.pallas_call(functools.partial(attend_body, (head_dim, local, heads), F...  4.04 us
    pallas_call x1, Pallas kernels, attend_final_call(): pl.pallas_call(functools.partial(attend_body, (head_dim, local, heads), T...  3.31 us
    pallas_call x1, Pallas kernels, pull_call(): pl.pallas_call(functools.partial(pull_body, (rows, cols, local, count)),...  2.97 us
    pallas_call x1, Pallas kernels, token_call(): pl.pallas_call(token_body, out_shape=(pltpu.VMEM((tokens, local), F32), p...  2.79 us
    pallas_call x1, Pallas kernels, query_call(): pl.pallas_call(functools.partial(query_body, (head_dim, local, heads)), o...  2.49 us
    pallas_call x1, Pallas kernels, measure_call(): pl.pallas_call(functools.partial(measure_body, (head_dim, local, heads)),...  2.29 us
  transfers between devices with their start and end apart: 23, of which 11 were waited for; matrix products, arithmetic and copies ran while one was open for 2% of the time, Pallas kernels for 20%

profile of v5, /device:TPU:0, one launch (start us, length us, event | category | flops | bytes accessed | tf_op | source)
XLA Modules:
  0.0 82.6 jit_solution(16320632556520059172)
XLA Ops:
  0.7 1.3 %pad.4.own = bf16[896,384]{1,0:T(8,128)(2,1)S(1)} pad(bf16[896,288]{1,0:T(8,128)(2,1)} %bitcast.14, bf16[]{:T(256)} %constant.10.clone.1), padding=0_0x0_96 | pad | bytes 1204226 | tf_op jit(solution)/shard_map/jit(_pad)/pad | solution.py:604
  2.0 0.5 collective-permute-start
  2.5 0.7 turn_grad.1.grad_t.refs_3_.refs_4_
  3.2 0.1 pad_add_fusion.place
  3.3 1.0 %collective-permute-done.other = bf16[896,384]{1,0:T(8,128)(2,1)S(1)} collective-permute-done((bf16[896,384]{1,0:T(8,128)(2,1)S(1)}, bf16[896,384]{1,0:T(8,128)(2,1)S(1)}, u32[]{:S(2)}, u32[]{:S(2)}) %collective-permute-start) | collective-permute-done | bytes 688160 | tf_op jit(solution)/shard_map/ppermute | solution.py:570
  4.3 2.1 %project_pool.1 = (bf16[56,576]{1,0:T(8,128)(2,1)S(1)}, bf16[56,576]{1,0:T(8,128)(2,1)S(1)}, f32[56,576]{1,0:T(8,128)S(1)}, bf16[9,56,576]{2,1,0:T(8,128)(2,1)S(1)}) custom-call(s32[2]{0:T(128)S(1)} %pad_add_fusion.place, bf16[896,384]{1,0:T(8,128)(2,1)S(1)} %pad.4.own, bf16[896,384]{1,0:T(8,128)(2,1)S(1)} %collective-permute-done.other, ...), custom_call_target="tpu_custom_call" | custom-call | tf_op jit(solution)/shard_map/project_pool/pallas_call | solution.py:101
  6.3 3.0 %collective-permute-start.1 = (bf16[56,576]{1,0:T(8,128)(2,1)S(1)}, bf16[56,576]{1,0:T(8,128)(2,1)S(1)}, u32[]{:S(2)}, u32[]{:S(2)}) collective-permute-start(bf16[56,576]{1,0:T(8,128)(2,1)S(1)} %get-tuple-element.66), channel_id=1, source_target_pairs={{0,2},{2,0},{4,6},{6,4},{8,10},{10,8},{12,14},{14,12},{1,3},{3,1},... | collective-permute-start | bytes 193544 | tf_op jit(solution)/shard_map/ppermute | solution.py:566
  9.3 1.5 %collective-permute-start.2 = (bf16[56,576]{1,0:T(8,128)(2,1)S(1)}, bf16[56,576]{1,0:T(8,128)(2,1)S(1)}, u32[]{:S(2)}, u32[]{:S(2)}) collective-permute-start(bf16[56,576]{1,0:T(8,128)(2,1)S(1)} %get-tuple-element.67), channel_id=1, source_target_pairs={{2,6},{4,0},{6,10},{8,4},{10,14},{12,8},{3,7},{5,1},{7,11},{9,5},{... | collective-permute-start | bytes 193544 | tf_op jit(solution)/shard_map/ppermute | solution.py:566
  10.8 1.1 %collective-permute-done.1 = bf16[56,576]{1,0:T(8,128)(2,1)S(1)} collective-permute-done((bf16[56,576]{1,0:T(8,128)(2,1)S(1)}, bf16[56,576]{1,0:T(8,128)(2,1)S(1)}, u32[]{:S(2)}, u32[]{:S(2)}) %collective-permute-start.1) | collective-permute-done | bytes 64544 | tf_op jit(solution)/shard_map/ppermute | solution.py:566
  11.8 3.7 %collective-permute-done.2 = bf16[56,576]{1,0:T(8,128)(2,1)S(1)} collective-permute-done((bf16[56,576]{1,0:T(8,128)(2,1)S(1)}, bf16[56,576]{1,0:T(8,128)(2,1)S(1)}, u32[]{:S(2)}, u32[]{:S(2)}) %collective-permute-start.2) | collective-permute-done | bytes 64544 | tf_op jit(solution)/shard_map/ppermute | solution.py:566
  15.5 0.1 collective-permute-start.6
  15.6 4.1 %collective-permute-start.5 = (bf16[56,576]{1,0:T(8,128)(2,1)S(1)}, bf16[56,576]{1,0:T(8,128)(2,1)S(1)}, u32[]{:S(2)}, u32[]{:S(2)}) collective-permute-start(bf16[56,576]{1,0:T(8,128)(2,1)S(1)} %add_convert_fusion.3.first), channel_id=1, source_target_pairs={{0,12},{2,14},{4,8},{6,10},{8,4},{10,6},{12,0},{14,2},{1,13},{3,15... | collective-permute-start | bytes 193544 | tf_op jit(solution)/shard_map/ppermute | solution.py:566
  19.7 0.6 collective-permute-start.3
  20.3 2.5 %project_query.1 = (bf16[512,896]{1,0:T(8,128)(2,1)S(1)}, bf16[576,896]{1,0:T(8,128)(2,1)S(1)}) custom-call(s32[2]{0:T(128)S(1)} %pad_add_fusion.place, bf16[896,384]{1,0:T(8,128)(2,1)S(1)} %pad.4.own, bf16[896,384]{1,0:T(8,128)(2,1)S(1)} %collective-permute-done.other, bf16[3,288,576]{2,1,0:T(8,128)(2,1)S(1)} %bitcast.9), custom_call_target="tpu_custom_call" | custom-call | tf_op jit(solution)/shard_map/project_query/pallas_call | solution.py:169
  22.8 2.2 %collective-permute-done.4 = bf16[56,576]{1,0:T(8,128)(2,1)S(1)} collective-permute-done((bf16[56,576]{1,0:T(8,128)(2,1)S(1)}, bf16[56,576]{1,0:T(8,128)(2,1)S(1)}, u32[]{:S(2)}, u32[]{:S(2)}) %collective-permute-start.4) | collective-permute-done | bytes 64544 | tf_op jit(solution)/shard_map/ppermute | solution.py:566
  25.0 1.4 %collective-permute-start.7 = (bf16[168,576]{1,0:T(8,128)(2,1)S(1)}, bf16[168,576]{1,0:T(8,128)(2,1)S(1)}, u32[]{:S(2)}, u32[]{:S(2)}) collective-permute-start(bf16[168,576]{1,0:T(8,128)(2,1)S(1)} %constant_dynamic-update-slice_fusion.rest), channel_id=1, source_target_pairs={{0,2},{2,0},{4,6},{6,4},{8,10},{10,8},{12,14},{14,12},{1,3},{3,1},... | collective-permute-start | bytes 580616 | tf_op jit(solution)/shard_map/ppermute | solution.py:566
  26.4 2.3 %attend_measure.1 = (f32[4,8,896]{2,1,0:T(8,128)S(1)}, f32[4,224,896]{2,1,0:T(8,128)S(1)}, f32[4,224,896]{2,1,0:T(8,128)S(1)}, bf16[224,512]{1,0:T(8,128)(2,1)S(1)}) custom-call(bf16[56,576]{1,0:T(8,128)(2,1)S(1)} %add_convert_fusion.3.first, bf16[168,576]{1,0:T(8,128)(2,1)S(1)} %constant_dynamic-update-slice_fusion.rest, ...), custom_call_target="tpu_custom_call" | custom-call | tf_op jit(solution)/shard_map/attend_measure/pallas_call | solution.py:289
  28.7 2.6 %collective-permute-done.7.refs_1_ = bf16[168,576]{1,0:T(8,128)(2,1)S(1)} collective-permute-done((bf16[168,576]{1,0:T(8,128)(2,1)S(1)}, bf16[168,576]{1,0:T(8,128)(2,1)S(1)}, u32[]{:S(2)}, u32[]{:S(2)}) %collective-permute-start.7) | collective-permute-done | bytes 193568 | tf_op jit(solution)/shard_map/ppermute | solution.py:566
  31.3 4.0 %attend_other.1 = (bf16[56,576]{1,0:T(8,128)(2,1)S(1)}, bf16[168,576]{1,0:T(8,128)(2,1)S(1)}, bf16[224,512]{1,0:T(8,128)(2,1)S(1)}, bf16[4,224,896]{2,1,0:T(8,128)(2,1)S(1)}, f32[4,8,896]{2,1,0:T(8,128)S(1)}) custom-call(bf16[56,576]{1,0:T(8,128)(2,1)S(1)} %collective-permute-done.6.refs_0_, bf16[168,576]{1,0:T(8,128)(2,1)S(1)} %collective-permute-done.7.refs_1_, ...), custom_call_target="tpu_custom_call" | custom-call | tf_op jit(solution)/shard_map/attend_other/pallas_call | solution.py:310
  35.4 1.0 %collective-permute-start.8 = (bf16[224,576]{1,0:T(8,128)(2,1)S(1)}, bf16[224,576]{1,0:T(8,128)(2,1)S(1)}, u32[]{:S(2)}, u32[]{:S(2)}) collective-permute-start(bf16[224,576]{1,0:T(8,128)(2,1)S(1)} %pad_maximum_fusion), channel_id=1, source_target_pairs={{0,2},{2,0},{4,6},{6,4},{8,10},{10,8},{12,14},{14,12},{1,3},{3,1},... | collective-permute-start | bytes 774152 | tf_op jit(solution)/shard_map/ppermute | solution.py:566
  36.5 3.3 %attend_same.1 = (bf16[56,576]{1,0:T(8,128)(2,1)S(1)}, bf16[168,576]{1,0:T(8,128)(2,1)S(1)}, bf16[896,512]{1,0:T(8,128)(2,1)S(1)}) custom-call(f32[4,224,896]{2,1,0:T(8,128)S(1)} %get-tuple-element.79.refs_0_, f32[4,224,896]{2,1,0:T(8,128)S(1)} %get-tuple-element.80.refs_1_, bf16[224,512]{1,0:T(8,128)(2,1)S(1)} %get-tuple-element.81.refs_2_, ...), custom_call_target="tpu_custom_call" | custom-call | tf_op jit(solution)/shard_map/attend_same/pallas_call | solution.py:336
  39.8 2.6 %collective-permute-done.8 = bf16[224,576]{1,0:T(8,128)(2,1)S(1)} collective-permute-done((bf16[224,576]{1,0:T(8,128)(2,1)S(1)}, bf16[224,576]{1,0:T(8,128)(2,1)S(1)}, u32[]{:S(2)}, u32[]{:S(2)}) %collective-permute-start.8) | collective-permute-done | bytes 258080 | tf_op jit(solution)/shard_map/ppermute | solution.py:566
  42.4 0.1 add_convert_fusion.1
  42.4 1.6 %collective-permute-start.11 = (bf16[56,576]{1,0:T(8,128)(2,1)S(1)}, bf16[56,576]{1,0:T(8,128)(2,1)S(1)}, u32[]{:S(2)}, u32[]{:S(2)}) collective-permute-start(bf16[56,576]{1,0:T(8,128)(2,1)S(1)} %get-tuple-element.134), channel_id=1, source_target_pairs={{0,12},{2,14},{4,8},{6,10},{8,4},{10,6},{12,0},{14,2},{1,13},{3,15... | collective-permute-start | bytes 193544 | tf_op jit(solution)/shard_map/ppermute | solution.py:566
  44.1 2.8 %collective-permute-start.9 = (bf16[56,576]{1,0:T(8,128)(2,1)S(1)}, bf16[56,576]{1,0:T(8,128)(2,1)S(1)}, u32[]{:S(2)}, u32[]{:S(2)}) collective-permute-start(bf16[56,576]{1,0:T(8,128)(2,1)S(1)} %get-tuple-element.136), channel_id=1, source_target_pairs={{0,4},{2,6},{4,0},{6,2},{8,12},{10,14},{12,8},{14,10},{1,5},{3,7},... | collective-permute-start | bytes 193544 | tf_op jit(solution)/shard_map/ppermute | solution.py:566
  46.9 1.9 %query_side.1 = (bf16[896,288]{1,0:T(8,128)(2,1)S(1)}, f32[288,384]{1,0:T(8,128)S(1)}, bf16[288,384]{1,0:T(8,128)(2,1)S(1)}) custom-call(s32[2]{0:T(128)S(1)} %pad_add_fusion.place, bf16[896,512]{1,0:T(8,128)(2,1)S(1)} %get-tuple-element.91.query_pad, bf16[576,896]{1,0:T(8,128)(2,1)S(1)} %get-tuple-element.92.tokens_t), custom_call_target="tpu_custom_call" | custom-call | tf_op jit(solution)/shard_map/query_side/pallas_call | solution.py:380
  48.8 0.8 %collective-permute-start.15 = (bf16[288,384]{1,0:T(8,128)(2,1)S(1)}, bf16[288,384]{1,0:T(8,128)(2,1)S(1)}, u32[]{:S(2)}, u32[]{:S(2)}) collective-permute-start(bf16[288,384]{1,0:T(8,128)(2,1)S(1)} %get-tuple-element.105), channel_id=1, source_target_pairs={{0,2},{2,0},{4,6},{6,4},{8,10},{10,8},{12,14},{14,12},{1,3},{3,1},... | collective-permute-start | bytes 663560 | tf_op jit(solution)/shard_map/ppermute | solution.py:566
  49.7 0.5 collective-permute-done.10
  50.2 0.9 %collective-permute-start.13 = (bf16[56,576]{1,0:T(8,128)(2,1)S(1)}, bf16[56,576]{1,0:T(8,128)(2,1)S(1)}, u32[]{:S(2)}, u32[]{:S(2)}) collective-permute-start(bf16[56,576]{1,0:T(8,128)(2,1)S(1)} %add_convert_fusion.2.swapped), channel_id=1, source_target_pairs={{0,2},{2,0},{4,6},{6,4},{8,10},{10,8},{12,14},{14,12},{1,3},{3,1},... | collective-permute-start | bytes 193544 | tf_op jit(solution)/shard_map/ppermute | solution.py:566
  51.1 3.1 %collective-permute-start.12 = (bf16[56,576]{1,0:T(8,128)(2,1)S(1)}, bf16[56,576]{1,0:T(8,128)(2,1)S(1)}, u32[]{:S(2)}, u32[]{:S(2)}) collective-permute-start(bf16[56,576]{1,0:T(8,128)(2,1)S(1)} %add_convert_fusion.2.swapped), channel_id=1, source_target_pairs={{0,4},{4,8},{6,2},{8,12},{10,6},{14,10},{1,5},{5,9},{7,3},{9,13},{... | collective-permute-start | bytes 193544 | tf_op jit(solution)/shard_map/ppermute | solution.py:566
  54.2 1.4 %collective-permute-done.13.mine = bf16[56,576]{1,0:T(8,128)(2,1)S(1)} collective-permute-done((bf16[56,576]{1,0:T(8,128)(2,1)S(1)}, bf16[56,576]{1,0:T(8,128)(2,1)S(1)}, u32[]{:S(2)}, u32[]{:S(2)}) %collective-permute-start.13) | collective-permute-done | bytes 64544 | tf_op jit(solution)/shard_map/ppermute | solution.py:566
  55.6 0.3 collective-permute-done.12.beside
  56.0 3.0 %pull_back.1 = (f32[320,576]{1,0:T(8,128)S(1)}, bf16[320,576]{1,0:T(8,128)(2,1)S(1)}, bf16[896,576]{1,0:T(8,128)(2,1)S(1)}) custom-call(s32[2]{0:T(128)S(1)} %pad_add_fusion.place, bf16[56,576]{1,0:T(8,128)(2,1)S(1)} %collective-permute-done.13.mine, bf16[56,576]{1,0:T(8,128)(2,1)S(1)} %add_convert_fusion.2.swapped, ...), custom_call_target="tpu_custom_call" | custom-call | tf_op jit(solution)/shard_map/pull_back/pallas_call | solution.py:498
  58.9 2.7 %collective-permute-start.14 = (bf16[320,576]{1,0:T(8,128)(2,1)S(1)}, bf16[320,576]{1,0:T(8,128)(2,1)S(1)}, u32[]{:S(2)}, u32[]{:S(2)}) collective-permute-start(bf16[320,576]{1,0:T(8,128)(2,1)S(1)} %get-tuple-element.103), channel_id=1, source_target_pairs={{0,2},{2,0},{4,6},{6,4},{8,10},{10,8},{12,14},{14,12},{1,3},{3,1},... | collective-permute-start | bytes 1105928 | tf_op jit(solution)/shard_map/ppermute | solution.py:566
  61.6 0.1 fusion.3
  61.7 1.0 %collective-permute-start.18 = (bf16[72,384]{1,0:T(8,128)(2,1)S(1)}, bf16[72,384]{1,0:T(8,128)(2,1)S(1)}, u32[]{:S(2)}, u32[]{:S(2)}) collective-permute-start(bf16[72,384]{1,0:T(8,128)(2,1)S(1)} %get-tuple-element.131), channel_id=1, source_target_pairs={{0,12},{2,14},{4,8},{6,10},{8,4},{10,6},{12,0},{14,2},{1,13},{3,15... | collective-permute-start | bytes 165896 | tf_op jit(solution)/shard_map/ppermute | solution.py:566
  62.6 1.6 %collective-permute-start.17 = (bf16[72,384]{1,0:T(8,128)(2,1)S(1)}, bf16[72,384]{1,0:T(8,128)(2,1)S(1)}, u32[]{:S(2)}, u32[]{:S(2)}) collective-permute-start(bf16[72,384]{1,0:T(8,128)(2,1)S(1)} %get-tuple-element.132), channel_id=1, source_target_pairs={{0,8},{2,10},{4,12},{6,14},{8,0},{10,2},{12,4},{14,6},{1,9},{3,11}... | collective-permute-start | bytes 165896 | tf_op jit(solution)/shard_map/ppermute | solution.py:566
  64.3 1.9 %collective-permute-start.16 = (bf16[72,384]{1,0:T(8,128)(2,1)S(1)}, bf16[72,384]{1,0:T(8,128)(2,1)S(1)}, u32[]{:S(2)}, u32[]{:S(2)}) collective-permute-start(bf16[72,384]{1,0:T(8,128)(2,1)S(1)} %get-tuple-element.133), channel_id=1, source_target_pairs={{0,4},{2,6},{4,0},{6,2},{8,12},{10,14},{12,8},{14,10},{1,5},{3,7},... | collective-permute-start | bytes 165896 | tf_op jit(solution)/shard_map/ppermute | solution.py:566
  66.1 2.8 %token_side.1 = (f32[896,288]{1,0:T(8,128)S(1)}, bf16[896,384]{1,0:T(8,128)(2,1)S(1)}) custom-call(s32[2]{0:T(128)S(1)} %pad_add_fusion.place, bf16[896,288]{1,0:T(8,128)(2,1)S(1)} %get-tuple-element.109.query_back, bf16[896,576]{1,0:T(8,128)(2,1)S(1)} %get-tuple-element.110.backs, bf16[3,288,576]{2,1,0:T(8,128)(2,1)S(1)} %bitcast.10), custom_call_target="tpu_custom_call" | custom-call | tf_op jit(solution)/shard_map/token_side/pallas_call | solution.py:477
  68.9 0.1 collective-permute-start.22
  69.1 0.1 fusion.2
  69.3 1.0 %collective-permute-start.20 = (bf16[104,576]{1,0:T(8,128)(2,1)S(1)}, bf16[104,576]{1,0:T(8,128)(2,1)S(1)}, u32[]{:S(2)}, u32[]{:S(2)}) collective-permute-start(bf16[104,576]{1,0:T(8,128)(2,1)S(1)} %get-tuple-element.137), channel_id=1, source_target_pairs={{0,8},{2,10},{4,12},{6,14},{8,0},{10,2},{12,4},{14,6},{1,9},{3,11}... | collective-permute-start | bytes 359432 | tf_op jit(solution)/shard_map/ppermute | solution.py:566
  70.3 1.4 %collective-permute-start.19 = (bf16[104,576]{1,0:T(8,128)(2,1)S(1)}, bf16[104,576]{1,0:T(8,128)(2,1)S(1)}, u32[]{:S(2)}, u32[]{:S(2)}) collective-permute-start(bf16[104,576]{1,0:T(8,128)(2,1)S(1)} %get-tuple-element.138), channel_id=1, source_target_pairs={{0,4},{2,6},{4,0},{6,2},{8,12},{10,14},{12,8},{14,10},{1,5},{3,7},... | collective-permute-start | bytes 359432 | tf_op jit(solution)/shard_map/ppermute | solution.py:566
  71.7 2.1 %collective-permute-start.21 = (bf16[104,576]{1,0:T(8,128)(2,1)S(1)}, bf16[104,576]{1,0:T(8,128)(2,1)S(1)}, u32[]{:S(2)}, u32[]{:S(2)}) collective-permute-start(bf16[104,576]{1,0:T(8,128)(2,1)S(1)} %concatenate.20), channel_id=1, source_target_pairs={{0,12},{2,14},{4,8},{6,10},{8,4},{10,6},{12,0},{14,2},{1,13},{3,15... | collective-permute-start | bytes 359432 | tf_op jit(solution)/shard_map/ppermute | solution.py:566
  73.8 1.0 %add_convert_fusion = bf16[896,288]{1,0:T(8,128)(2,1)} fusion(f32[896,288]{1,0:T(8,128)S(1)} %get-tuple-element.111, bf16[896,384]{1,0:T(8,128)(2,1)S(1)} %collective-permute-done.22), kind=kLoop, calls=%fused_computation | loop fusion | flops 774144 | bytes 2064384 | tf_op jit(solution)/shard_map/convert_element_type | solution.py:663
  74.8 5.2 %collective-permute-done.20.refs_1_ = bf16[104,576]{1,0:T(8,128)(2,1)S(1)} collective-permute-done((bf16[104,576]{1,0:T(8,128)(2,1)S(1)}, bf16[104,576]{1,0:T(8,128)(2,1)S(1)}, u32[]{:S(2)}, u32[]{:S(2)}) %collective-permute-start.20) | collective-permute-done | bytes 119840 | tf_op jit(solution)/shard_map/ppermute | solution.py:566
  80.0 1.7 %collective-permute-done.21.refs_2_ = bf16[104,576]{1,0:T(8,128)(2,1)S(1)} collective-permute-done((bf16[104,576]{1,0:T(8,128)(2,1)S(1)}, bf16[104,576]{1,0:T(8,128)(2,1)S(1)}, u32[]{:S(2)}, u32[]{:S(2)}) %collective-permute-start.21) | collective-permute-done | bytes 119840 | tf_op jit(solution)/shard_map/ppermute | solution.py:566
  81.7 0.9 %finish.1 = (f32[3,72,288]{2,1,0:T(8,128)}, f32[27,2,288]{2,1,0:T(2,128)}) custom-call(f32[72,384]{1,0:T(8,128)S(1)} %fusion.1.query_sum, f32[72,576]{1,0:T(8,128)S(1)} %slice.77.own_sum, f32[32,576]{1,0:T(8,128)S(1)} %slice.78.tail_sum, bf16[104,576]{1,0:T(8,128)(2,1)S(1)} %collective-permute-done.19.refs_0_, ...), custom_call_target="tpu_custom_call" | custom-call | tf_op jit(solution)/shard_map/finish/pallas_call | solution.py:541
  (36 shorter events, 0.4 us)
Async XLA Ops:
  0.6 1.9 %copy-start.1 = (bf16[1,16,56,288]{3,2,1,0:T(8,128)(2,1)S(1)}, bf16[1,16,56,288]{3,2,1,0:T(8,128)(2,1)}, u32[]{:S(2)}) copy-start(bf16[1,16,56,288]{3,2,1,0:T(8,128)(2,1)} %param.5) | copy-start | bytes 1548292
  0.6 3.6 %copy-start = (bf16[3,576,288]{1,2,0:T(8,128)(2,1)S(1)}, bf16[3,576,288]{1,2,0:T(8,128)(2,1)}, u32[]{:S(2)}) copy-start(bf16[3,576,288]{1,2,0:T(8,128)(2,1)} %param.6) | copy-start | bytes 2985988
  0.7 3.6 %copy-start.2 = (f32[2,27,288]{2,0,1:T(2,128)S(1)}, f32[2,27,288]{2,0,1:T(2,128)}, u32[]{:S(2)}) copy-start(f32[2,27,288]{2,0,1:T(2,128)} %param.7) | copy-start | bytes 186628
  2.0 2.3 %collective-permute-start = (bf16[896,384]{1,0:T(8,128)(2,1)S(1)}, bf16[896,384]{1,0:T(8,128)(2,1)S(1)}, u32[]{:S(2)}, u32[]{:S(2)}) collective-permute-start(bf16[896,384]{1,0:T(8,128)(2,1)S(1)} %pad.4.own), channel_id=1, source_target_pairs={{0,1},{1,0},{2,3},{3,2},{4,5},{5,4},{6,7},{7,6},{8,9},{9,8},{10,11... | collective-permute-start | bytes 2064392 | tf_op jit(solution)/shard_map/ppermute | solution.py:570
  6.3 5.5 %collective-permute-start.1 = (bf16[56,576]{1,0:T(8,128)(2,1)S(1)}, bf16[56,576]{1,0:T(8,128)(2,1)S(1)}, u32[]{:S(2)}, u32[]{:S(2)}) collective-permute-start(bf16[56,576]{1,0:T(8,128)(2,1)S(1)} %get-tuple-element.66), channel_id=1, source_target_pairs={{0,2},{2,0},{4,6},{6,4},{8,10},{10,8},{12,14},{14,12},{1,3},{3,1},... | collective-permute-start | bytes 193544 | tf_op jit(solution)/shard_map/ppermute | solution.py:566
  9.3 6.2 %collective-permute-start.2 = (bf16[56,576]{1,0:T(8,128)(2,1)S(1)}, bf16[56,576]{1,0:T(8,128)(2,1)S(1)}, u32[]{:S(2)}, u32[]{:S(2)}) collective-permute-start(bf16[56,576]{1,0:T(8,128)(2,1)S(1)} %get-tuple-element.67), channel_id=1, source_target_pairs={{2,6},{4,0},{6,10},{8,4},{10,14},{12,8},{3,7},{5,1},{7,11},{9,5},{... | collective-permute-start | bytes 193544 | tf_op jit(solution)/shard_map/ppermute | solution.py:566
  15.5 7.2 %collective-permute-start.6 = (bf16[56,576]{1,0:T(8,128)(2,1)S(1)}, bf16[56,576]{1,0:T(8,128)(2,1)S(1)}, u32[]{:S(2)}, u32[]{:S(2)}) collective-permute-start(bf16[56,576]{1,0:T(8,128)(2,1)S(1)} %add_convert_fusion.3.first), channel_id=1, source_target_pairs={{0,2},{2,0},{4,6},{6,4},{8,10},{10,8},{12,14},{14,12},{1,3},{3,1},... | collective-permute-start | bytes 193544 | tf_op jit(solution)/shard_map/ppermute | solution.py:566
  15.6 7.2 %collective-permute-start.5 = (bf16[56,576]{1,0:T(8,128)(2,1)S(1)}, bf16[56,576]{1,0:T(8,128)(2,1)S(1)}, u32[]{:S(2)}, u32[]{:S(2)}) collective-permute-start(bf16[56,576]{1,0:T(8,128)(2,1)S(1)} %add_convert_fusion.3.first), channel_id=1, source_target_pairs={{0,12},{2,14},{4,8},{6,10},{8,4},{10,6},{12,0},{14,2},{1,13},{3,15... | collective-permute-start | bytes 193544 | tf_op jit(solution)/shard_map/ppermute | solution.py:566
  19.7 5.2 %collective-permute-start.4 = (bf16[56,576]{1,0:T(8,128)(2,1)S(1)}, bf16[56,576]{1,0:T(8,128)(2,1)S(1)}, u32[]{:S(2)}, u32[]{:S(2)}) collective-permute-start(bf16[56,576]{1,0:T(8,128)(2,1)S(1)} %add_convert_fusion.3.first), channel_id=1, source_target_pairs={{0,8},{2,10},{4,12},{6,14},{8,0},{10,2},{12,4},{14,6},{1,9},{3,11}... | collective-permute-start | bytes 193544 | tf_op jit(solution)/shard_map/ppermute | solution.py:566
  19.7 5.2 %collective-permute-start.3 = (bf16[56,576]{1,0:T(8,128)(2,1)S(1)}, bf16[56,576]{1,0:T(8,128)(2,1)S(1)}, u32[]{:S(2)}, u32[]{:S(2)}) collective-permute-start(bf16[56,576]{1,0:T(8,128)(2,1)S(1)} %add_convert_fusion.3.first), channel_id=1, source_target_pairs={{0,4},{2,6},{4,0},{6,2},{8,12},{10,14},{12,8},{14,10},{1,5},{3,7},... | collective-permute-start | bytes 193544 | tf_op jit(solution)/shard_map/ppermute | solution.py:566
  25.0 6.3 %collective-permute-start.7 = (bf16[168,576]{1,0:T(8,128)(2,1)S(1)}, bf16[168,576]{1,0:T(8,128)(2,1)S(1)}, u32[]{:S(2)}, u32[]{:S(2)}) collective-permute-start(bf16[168,576]{1,0:T(8,128)(2,1)S(1)} %constant_dynamic-update-slice_fusion.rest), channel_id=1, source_target_pairs={{0,2},{2,0},{4,6},{6,4},{8,10},{10,8},{12,14},{14,12},{1,3},{3,1},... | collective-permute-start | bytes 580616 | tf_op jit(solution)/shard_map/ppermute | solution.py:566
  35.4 6.9 %collective-permute-start.8 = (bf16[224,576]{1,0:T(8,128)(2,1)S(1)}, bf16[224,576]{1,0:T(8,128)(2,1)S(1)}, u32[]{:S(2)}, u32[]{:S(2)}) collective-permute-start(bf16[224,576]{1,0:T(8,128)(2,1)S(1)} %pad_maximum_fusion), channel_id=1, source_target_pairs={{0,2},{2,0},{4,6},{6,4},{8,10},{10,8},{12,14},{14,12},{1,3},{3,1},... | collective-permute-start | bytes 774152 | tf_op jit(solution)/shard_map/ppermute | solution.py:566
  42.4 7.2 %collective-permute-start.11 = (bf16[56,576]{1,0:T(8,128)(2,1)S(1)}, bf16[56,576]{1,0:T(8,128)(2,1)S(1)}, u32[]{:S(2)}, u32[]{:S(2)}) collective-permute-start(bf16[56,576]{1,0:T(8,128)(2,1)S(1)} %get-tuple-element.134), channel_id=1, source_target_pairs={{0,12},{2,14},{4,8},{6,10},{8,4},{10,6},{12,0},{14,2},{1,13},{3,15... | collective-permute-start | bytes 193544 | tf_op jit(solution)/shard_map/ppermute | solution.py:566
  44.1 6.1 %collective-permute-start.10 = (bf16[56,576]{1,0:T(8,128)(2,1)S(1)}, bf16[56,576]{1,0:T(8,128)(2,1)S(1)}, u32[]{:S(2)}, u32[]{:S(2)}) collective-permute-start(bf16[56,576]{1,0:T(8,128)(2,1)S(1)} %get-tuple-element.135), channel_id=1, source_target_pairs={{0,8},{2,10},{4,12},{6,14},{8,0},{10,2},{12,4},{14,6},{1,9},{3,11}... | collective-permute-start | bytes 193544 | tf_op jit(solution)/shard_map/ppermute | solution.py:566
  44.1 6.1 %collective-permute-start.9 = (bf16[56,576]{1,0:T(8,128)(2,1)S(1)}, bf16[56,576]{1,0:T(8,128)(2,1)S(1)}, u32[]{:S(2)}, u32[]{:S(2)}) collective-permute-start(bf16[56,576]{1,0:T(8,128)(2,1)S(1)} %get-tuple-element.136), channel_id=1, source_target_pairs={{0,4},{2,6},{4,0},{6,2},{8,12},{10,14},{12,8},{14,10},{1,5},{3,7},... | collective-permute-start | bytes 193544 | tf_op jit(solution)/shard_map/ppermute | solution.py:566
  48.8 10.1 %collective-permute-start.15 = (bf16[288,384]{1,0:T(8,128)(2,1)S(1)}, bf16[288,384]{1,0:T(8,128)(2,1)S(1)}, u32[]{:S(2)}, u32[]{:S(2)}) collective-permute-start(bf16[288,384]{1,0:T(8,128)(2,1)S(1)} %get-tuple-element.105), channel_id=1, source_target_pairs={{0,2},{2,0},{4,6},{6,4},{8,10},{10,8},{12,14},{14,12},{1,3},{3,1},... | collective-permute-start | bytes 663560 | tf_op jit(solution)/shard_map/ppermute | solution.py:566
  50.2 5.4 %collective-permute-start.13 = (bf16[56,576]{1,0:T(8,128)(2,1)S(1)}, bf16[56,576]{1,0:T(8,128)(2,1)S(1)}, u32[]{:S(2)}, u32[]{:S(2)}) collective-permute-start(bf16[56,576]{1,0:T(8,128)(2,1)S(1)} %add_convert_fusion.2.swapped), channel_id=1, source_target_pairs={{0,2},{2,0},{4,6},{6,4},{8,10},{10,8},{12,14},{14,12},{1,3},{3,1},... | collective-permute-start | bytes 193544 | tf_op jit(solution)/shard_map/ppermute | solution.py:566
  51.1 4.9 %collective-permute-start.12 = (bf16[56,576]{1,0:T(8,128)(2,1)S(1)}, bf16[56,576]{1,0:T(8,128)(2,1)S(1)}, u32[]{:S(2)}, u32[]{:S(2)}) collective-permute-start(bf16[56,576]{1,0:T(8,128)(2,1)S(1)} %add_convert_fusion.2.swapped), channel_id=1, source_target_pairs={{0,4},{4,8},{6,2},{8,12},{10,6},{14,10},{1,5},{5,9},{7,3},{9,13},{... | collective-permute-start | bytes 193544 | tf_op jit(solution)/shard_map/ppermute | solution.py:566
  58.9 10.1 %collective-permute-start.14 = (bf16[320,576]{1,0:T(8,128)(2,1)S(1)}, bf16[320,576]{1,0:T(8,128)(2,1)S(1)}, u32[]{:S(2)}, u32[]{:S(2)}) collective-permute-start(bf16[320,576]{1,0:T(8,128)(2,1)S(1)} %get-tuple-element.103), channel_id=1, source_target_pairs={{0,2},{2,0},{4,6},{6,4},{8,10},{10,8},{12,14},{14,12},{1,3},{3,1},... | collective-permute-start | bytes 1105928 | tf_op jit(solution)/shard_map/ppermute | solution.py:566
  61.7 7.3 %collective-permute-start.18 = (bf16[72,384]{1,0:T(8,128)(2,1)S(1)}, bf16[72,384]{1,0:T(8,128)(2,1)S(1)}, u32[]{:S(2)}, u32[]{:S(2)}) collective-permute-start(bf16[72,384]{1,0:T(8,128)(2,1)S(1)} %get-tuple-element.131), channel_id=1, source_target_pairs={{0,12},{2,14},{4,8},{6,10},{8,4},{10,6},{12,0},{14,2},{1,13},{3,15... | collective-permute-start | bytes 165896 | tf_op jit(solution)/shard_map/ppermute | solution.py:566
  62.6 6.4 %collective-permute-start.17 = (bf16[72,384]{1,0:T(8,128)(2,1)S(1)}, bf16[72,384]{1,0:T(8,128)(2,1)S(1)}, u32[]{:S(2)}, u32[]{:S(2)}) collective-permute-start(bf16[72,384]{1,0:T(8,128)(2,1)S(1)} %get-tuple-element.132), channel_id=1, source_target_pairs={{0,8},{2,10},{4,12},{6,14},{8,0},{10,2},{12,4},{14,6},{1,9},{3,11}... | collective-permute-start | bytes 165896 | tf_op jit(solution)/shard_map/ppermute | solution.py:566
  64.3 4.8 %collective-permute-start.16 = (bf16[72,384]{1,0:T(8,128)(2,1)S(1)}, bf16[72,384]{1,0:T(8,128)(2,1)S(1)}, u32[]{:S(2)}, u32[]{:S(2)}) collective-permute-start(bf16[72,384]{1,0:T(8,128)(2,1)S(1)} %get-tuple-element.133), channel_id=1, source_target_pairs={{0,4},{2,6},{4,0},{6,2},{8,12},{10,14},{12,8},{14,10},{1,5},{3,7},... | collective-permute-start | bytes 165896 | tf_op jit(solution)/shard_map/ppermute | solution.py:566
  68.9 4.9 %collective-permute-start.22 = (bf16[896,384]{1,0:T(8,128)(2,1)S(1)}, bf16[896,384]{1,0:T(8,128)(2,1)S(1)}, u32[]{:S(2)}, u32[]{:S(2)}) collective-permute-start(bf16[896,384]{1,0:T(8,128)(2,1)S(1)} %get-tuple-element.112), channel_id=1, source_target_pairs={{0,1},{1,0},{2,3},{3,2},{4,5},{5,4},{6,7},{7,6},{8,9},{9,8},{10,11... | collective-permute-start | bytes 2064392 | tf_op jit(solution)/shard_map/ppermute | solution.py:570
  69.3 10.7 %collective-permute-start.20 = (bf16[104,576]{1,0:T(8,128)(2,1)S(1)}, bf16[104,576]{1,0:T(8,128)(2,1)S(1)}, u32[]{:S(2)}, u32[]{:S(2)}) collective-permute-start(bf16[104,576]{1,0:T(8,128)(2,1)S(1)} %get-tuple-element.137), channel_id=1, source_target_pairs={{0,8},{2,10},{4,12},{6,14},{8,0},{10,2},{12,4},{14,6},{1,9},{3,11}... | collective-permute-start | bytes 359432 | tf_op jit(solution)/shard_map/ppermute | solution.py:566
  70.3 9.7 %collective-permute-start.19 = (bf16[104,576]{1,0:T(8,128)(2,1)S(1)}, bf16[104,576]{1,0:T(8,128)(2,1)S(1)}, u32[]{:S(2)}, u32[]{:S(2)}) collective-permute-start(bf16[104,576]{1,0:T(8,128)(2,1)S(1)} %get-tuple-element.138), channel_id=1, source_target_pairs={{0,4},{2,6},{4,0},{6,2},{8,12},{10,14},{12,8},{14,10},{1,5},{3,7},... | collective-permute-start | bytes 359432 | tf_op jit(solution)/shard_map/ppermute | solution.py:566
  71.7 10.0 %collective-permute-start.21 = (bf16[104,576]{1,0:T(8,128)(2,1)S(1)}, bf16[104,576]{1,0:T(8,128)(2,1)S(1)}, u32[]{:S(2)}, u32[]{:S(2)}) collective-permute-start(bf16[104,576]{1,0:T(8,128)(2,1)S(1)} %concatenate.20), channel_id=1, source_target_pairs={{0,12},{2,14},{4,8},{6,10},{8,4},{10,6},{12,0},{14,2},{1,13},{3,15... | collective-permute-start | bytes 359432 | tf_op jit(solution)/shard_map/ppermute | solution.py:566

commit v6 on v5

--- a/solution.py
+++ b/solution.py
@@ -195,8 +195,17 @@
     return key, raised, mul(value, grad)
 
 
+def range_factor(total):
+    return jnp.where(total > 1.0, 2.0**-16, 2.0**16)
+
+
+def normalised(raised, total):
+    factor = range_factor(total)
+    return (raised * factor) * (1.0 / (jnp.maximum(total, 2.0**-125) * factor))
+
+
 def measure_body(
-    geometry, first, rest, query_t, grad_t, sums, raised_out, prob_grad_out, key_pad
+    geometry, first, rest, query_t, grad_t, sums, share_out, prob_grad_out, key_pad
 ):
     head_dim, local, heads = geometry
     for sub in range(STEP):
@@ -205,11 +214,13 @@
         key, raised, prob_grad = head_products(
             head_dim, (first, rest), chosen, query_t[rows, :], grad_t[rows, :]
         )
-        raised_out[sub] = raised
+        total = jnp.sum(raised, axis=0, keepdims=True)
+        shares = normalised(raised, total)
+        share_out[sub] = shares
         prob_grad_out[sub] = prob_grad
         key_pad[:, rows] = key
-        sums[sub, 0:1, :] = jnp.sum(raised, axis=0, keepdims=True)
-        sums[sub, 1:2, :] = jnp.sum(raised * prob_grad, axis=0, keepdims=True)
+        sums[sub, 0:1, :] = total
+        sums[sub, 1:2, :] = jnp.sum(shares * prob_grad, axis=0, keepdims=True)
 
 
 def attend_body(geometry, final, *refs):
@@ -217,7 +228,7 @@
     step = pl.program_id(0)
     scale = head_dim ** (-0.5)
     if final:
-        own_raised, own_prob_grad, own_pad, query_t, grad_t, sums, *refs = refs
+        own_shares, own_prob_grad, own_pad, query_t, grad_t, sums, *refs = refs
         other_pad, other_scores, first_grads, rest_grads, query_grad, total = refs
     else:
         first, rest, query_t, grad_t, sums, *refs = refs
@@ -228,16 +239,22 @@
         chosen = choose_head(head_dim, local, STEP * step + sub)
         query, grad = query_t[rows, :], grad_t[rows, :]
         if final:
-            key, raised, prob_grad = own_pad[:, rows], own_raised[sub], own_prob_grad[sub]
-            inverse, centre = sums[sub, 0:1, :], sums[sub, 1:2, :]
+            key, shares, prob_grad = own_pad[:, rows], own_shares[sub], own_prob_grad[sub]
+            weight, centre = sums[sub, 0:1, :], sums[sub, 1:2, :]
         else:
             key, raised, prob_grad = head_products(head_dim, (first, rest), chosen, query, grad)
-            inverse = 1.0 / (sums[sub, 0:1, :] + jnp.sum(raised, axis=0, keepdims=True))
-            weighted = sums[sub, 1:2, :] + jnp.sum(raised * prob_grad, axis=0, keepdims=True)
-            centre = weighted * inverse
-            totals[sub, 0:1, :] = inverse
+            first_sum, here_sum = sums[sub, 0:1, :], jnp.sum(raised, axis=0, keepdims=True)
+            shares = normalised(raised, here_sum)
+            whole = first_sum + here_sum
+            factor = range_factor(whole)
+            inverse = 1.0 / (whole * factor)
+            first_weight, weight = first_sum * factor * inverse, here_sum * factor * inverse
+            centre = sums[sub, 1:2, :] * first_weight + weight * jnp.sum(
+                shares * prob_grad, axis=0, keepdims=True
+            )
+            totals[sub, 0:1, :] = first_weight
             totals[sub, 1:2, :] = centre
-        probs = raised * inverse
+        probs = shares * weight
         score_grad = (probs * (prob_grad - centre) * scale).astype(BF16)
         if final:
             turn = identity(LANES)

time: 83.2 us -> 83.3 us (level)
  no operation moved by 1% of the time
where the time goes in v6:
time: 83.3 us; the launch traced here: 82.7 us
  starting transfers between devices  33 us (40%)
  Pallas kernels  23.7 us (28%)
  waiting for transfers between devices  22.1 us (27%)
  other arithmetic  1.49 us (2%)
  local copies, waits for them, and re-layouts  1.46 us (2%)
  between operations  0.93 us (1%)
    ppermute x21, starting transfers between devices, exchange(): return lax.ppermute(block, 'frames', pairs)  32.4 us
    ppermute x21, waiting for transfers between devices, exchange(): return lax.ppermute(block, 'frames', pairs)  21.1 us
    pallas_call x1, Pallas kernels, attend_call(): pl.pallas_call(functools.partial(attend_body, (head_dim, local, heads), F...  4.15 us
    pallas_call x1, Pallas kernels, attend_final_call(): pl.pallas_call(functools.partial(attend_body, (head_dim, local, heads), T...  3.31 us
    pallas_call x1, Pallas kernels, pull_call(): pl.pallas_call(functools.partial(pull_body, (rows, cols, local, count)),...  2.97 us
    pallas_call x1, Pallas kernels, token_call(): pl.pallas_call(token_body, out_shape=(pltpu.VMEM((tokens, local), F32), p...  2.79 us
    pallas_call x1, Pallas kernels, query_call(): pl.pallas_call(functools.partial(query_body, (head_dim, local, heads)), o...  2.49 us
    pallas_call x1, Pallas kernels, measure_call(): pl.pallas_call(functools.partial(measure_body, (head_dim, local, heads)),...  2.4 us
  transfers between devices with their start and end apart: 23, of which 11 were waited for; matrix products, arithmetic and copies ran while one was open for 2% of the time, Pallas kernels for 20%

profile of v6, /device:TPU:0, one launch (start us, length us, event | category | flops | bytes accessed | tf_op | source)
XLA Modules:
  0.0 82.7 jit_solution(17928382675185931333)
XLA Ops:
  0.7 1.3 %pad.4.own = bf16[896,384]{1,0:T(8,128)(2,1)S(1)} pad(bf16[896,288]{1,0:T(8,128)(2,1)} %bitcast.14, bf16[]{:T(256)} %constant.10.clone.1), padding=0_0x0_96 | pad | bytes 1204226 | tf_op jit(solution)/shard_map/jit(_pad)/pad | solution.py:621
  2.0 0.5 collective-permute-start
  2.5 0.7 turn_grad.1.grad_t.refs_3_.refs_4_
  3.2 0.1 pad_add_fusion.place
  3.3 1.0 %collective-permute-done.other = bf16[896,384]{1,0:T(8,128)(2,1)S(1)} collective-permute-done((bf16[896,384]{1,0:T(8,128)(2,1)S(1)}, bf16[896,384]{1,0:T(8,128)(2,1)S(1)}, u32[]{:S(2)}, u32[]{:S(2)}) %collective-permute-start) | collective-permute-done | bytes 688160 | tf_op jit(solution)/shard_map/ppermute | solution.py:587
  4.3 2.1 %project_pool.1 = (bf16[56,576]{1,0:T(8,128)(2,1)S(1)}, bf16[56,576]{1,0:T(8,128)(2,1)S(1)}, f32[56,576]{1,0:T(8,128)S(1)}, bf16[9,56,576]{2,1,0:T(8,128)(2,1)S(1)}) custom-call(s32[2]{0:T(128)S(1)} %pad_add_fusion.place, bf16[896,384]{1,0:T(8,128)(2,1)S(1)} %pad.4.own, bf16[896,384]{1,0:T(8,128)(2,1)S(1)} %collective-permute-done.other, ...), custom_call_target="tpu_custom_call" | custom-call | tf_op jit(solution)/shard_map/project_pool/pallas_call | solution.py:101
  6.3 3.0 %collective-permute-start.1 = (bf16[56,576]{1,0:T(8,128)(2,1)S(1)}, bf16[56,576]{1,0:T(8,128)(2,1)S(1)}, u32[]{:S(2)}, u32[]{:S(2)}) collective-permute-start(bf16[56,576]{1,0:T(8,128)(2,1)S(1)} %get-tuple-element.66), channel_id=1, source_target_pairs={{0,2},{2,0},{4,6},{6,4},{8,10},{10,8},{12,14},{14,12},{1,3},{3,1},... | collective-permute-start | bytes 193544 | tf_op jit(solution)/shard_map/ppermute | solution.py:583
  9.3 1.5 %collective-permute-start.2 = (bf16[56,576]{1,0:T(8,128)(2,1)S(1)}, bf16[56,576]{1,0:T(8,128)(2,1)S(1)}, u32[]{:S(2)}, u32[]{:S(2)}) collective-permute-start(bf16[56,576]{1,0:T(8,128)(2,1)S(1)} %get-tuple-element.67), channel_id=1, source_target_pairs={{2,6},{4,0},{6,10},{8,4},{10,14},{12,8},{3,7},{5,1},{7,11},{9,5},{... | collective-permute-start | bytes 193544 | tf_op jit(solution)/shard_map/ppermute | solution.py:583
  10.8 1.1 %collective-permute-done.1 = bf16[56,576]{1,0:T(8,128)(2,1)S(1)} collective-permute-done((bf16[56,576]{1,0:T(8,128)(2,1)S(1)}, bf16[56,576]{1,0:T(8,128)(2,1)S(1)}, u32[]{:S(2)}, u32[]{:S(2)}) %collective-permute-start.1) | collective-permute-done | bytes 64544 | tf_op jit(solution)/shard_map/ppermute | solution.py:583
  11.8 3.7 %collective-permute-done.2 = bf16[56,576]{1,0:T(8,128)(2,1)S(1)} collective-permute-done((bf16[56,576]{1,0:T(8,128)(2,1)S(1)}, bf16[56,576]{1,0:T(8,128)(2,1)S(1)}, u32[]{:S(2)}, u32[]{:S(2)}) %collective-permute-start.2) | collective-permute-done | bytes 64544 | tf_op jit(solution)/shard_map/ppermute | solution.py:583
  15.5 0.1 collective-permute-start.6
  15.6 4.1 %collective-permute-start.5 = (bf16[56,576]{1,0:T(8,128)(2,1)S(1)}, bf16[56,576]{1,0:T(8,128)(2,1)S(1)}, u32[]{:S(2)}, u32[]{:S(2)}) collective-permute-start(bf16[56,576]{1,0:T(8,128)(2,1)S(1)} %add_convert_fusion.3.first), channel_id=1, source_target_pairs={{0,12},{2,14},{4,8},{6,10},{8,4},{10,6},{12,0},{14,2},{1,13},{3,15... | collective-permute-start | bytes 193544 | tf_op jit(solution)/shard_map/ppermute | solution.py:583
  19.7 0.6 collective-permute-start.3
  20.3 2.5 %project_query.1 = (bf16[512,896]{1,0:T(8,128)(2,1)S(1)}, bf16[576,896]{1,0:T(8,128)(2,1)S(1)}) custom-call(s32[2]{0:T(128)S(1)} %pad_add_fusion.place, bf16[896,384]{1,0:T(8,128)(2,1)S(1)} %pad.4.own, bf16[896,384]{1,0:T(8,128)(2,1)S(1)} %collective-permute-done.other, bf16[3,288,576]{2,1,0:T(8,128)(2,1)S(1)} %bitcast.9), custom_call_target="tpu_custom_call" | custom-call | tf_op jit(solution)/shard_map/project_query/pallas_call | solution.py:169
  22.8 2.2 %collective-permute-done.4 = bf16[56,576]{1,0:T(8,128)(2,1)S(1)} collective-permute-done((bf16[56,576]{1,0:T(8,128)(2,1)S(1)}, bf16[56,576]{1,0:T(8,128)(2,1)S(1)}, u32[]{:S(2)}, u32[]{:S(2)}) %collective-permute-start.4) | collective-permute-done | bytes 64544 | tf_op jit(solution)/shard_map/ppermute | solution.py:583
  25.0 1.4 %collective-permute-start.7 = (bf16[168,576]{1,0:T(8,128)(2,1)S(1)}, bf16[168,576]{1,0:T(8,128)(2,1)S(1)}, u32[]{:S(2)}, u32[]{:S(2)}) collective-permute-start(bf16[168,576]{1,0:T(8,128)(2,1)S(1)} %constant_dynamic-update-slice_fusion.rest), channel_id=1, source_target_pairs={{0,2},{2,0},{4,6},{6,4},{8,10},{10,8},{12,14},{14,12},{1,3},{3,1},... | collective-permute-start | bytes 580616 | tf_op jit(solution)/shard_map/ppermute | solution.py:583
  26.4 2.4 %attend_measure.1 = (f32[4,8,896]{2,1,0:T(8,128)S(1)}, f32[4,224,896]{2,1,0:T(8,128)S(1)}, f32[4,224,896]{2,1,0:T(8,128)S(1)}, bf16[224,512]{1,0:T(8,128)(2,1)S(1)}) custom-call(bf16[56,576]{1,0:T(8,128)(2,1)S(1)} %add_convert_fusion.3.first, bf16[168,576]{1,0:T(8,128)(2,1)S(1)} %constant_dynamic-update-slice_fusion.rest, ...), custom_call_target="tpu_custom_call" | custom-call | tf_op jit(solution)/shard_map/attend_measure/pallas_call | solution.py:306
  28.8 2.5 %collective-permute-done.7.refs_1_ = bf16[168,576]{1,0:T(8,128)(2,1)S(1)} collective-permute-done((bf16[168,576]{1,0:T(8,128)(2,1)S(1)}, bf16[168,576]{1,0:T(8,128)(2,1)S(1)}, u32[]{:S(2)}, u32[]{:S(2)}) %collective-permute-start.7) | collective-permute-done | bytes 193568 | tf_op jit(solution)/shard_map/ppermute | solution.py:583
  31.3 4.2 %attend_other.1 = (bf16[56,576]{1,0:T(8,128)(2,1)S(1)}, bf16[168,576]{1,0:T(8,128)(2,1)S(1)}, bf16[224,512]{1,0:T(8,128)(2,1)S(1)}, bf16[4,224,896]{2,1,0:T(8,128)(2,1)S(1)}, f32[4,8,896]{2,1,0:T(8,128)S(1)}) custom-call(bf16[56,576]{1,0:T(8,128)(2,1)S(1)} %collective-permute-done.6.refs_0_, bf16[168,576]{1,0:T(8,128)(2,1)S(1)} %collective-permute-done.7.refs_1_, ...), custom_call_target="tpu_custom_call" | custom-call | tf_op jit(solution)/shard_map/attend_other/pallas_call | solution.py:327
  35.5 1.0 %collective-permute-start.8 = (bf16[224,576]{1,0:T(8,128)(2,1)S(1)}, bf16[224,576]{1,0:T(8,128)(2,1)S(1)}, u32[]{:S(2)}, u32[]{:S(2)}) collective-permute-start(bf16[224,576]{1,0:T(8,128)(2,1)S(1)} %pad_maximum_fusion), channel_id=1, source_target_pairs={{0,2},{2,0},{4,6},{6,4},{8,10},{10,8},{12,14},{14,12},{1,3},{3,1},... | collective-permute-start | bytes 774152 | tf_op jit(solution)/shard_map/ppermute | solution.py:583
  36.6 3.3 %attend_same.1 = (bf16[56,576]{1,0:T(8,128)(2,1)S(1)}, bf16[168,576]{1,0:T(8,128)(2,1)S(1)}, bf16[896,512]{1,0:T(8,128)(2,1)S(1)}) custom-call(f32[4,224,896]{2,1,0:T(8,128)S(1)} %get-tuple-element.79.refs_0_, f32[4,224,896]{2,1,0:T(8,128)S(1)} %get-tuple-element.80.refs_1_, bf16[224,512]{1,0:T(8,128)(2,1)S(1)} %get-tuple-element.81.refs_2_, ...), custom_call_target="tpu_custom_call" | custom-call | tf_op jit(solution)/shard_map/attend_same/pallas_call | solution.py:353
  39.9 2.6 %collective-permute-done.8 = bf16[224,576]{1,0:T(8,128)(2,1)S(1)} collective-permute-done((bf16[224,576]{1,0:T(8,128)(2,1)S(1)}, bf16[224,576]{1,0:T(8,128)(2,1)S(1)}, u32[]{:S(2)}, u32[]{:S(2)}) %collective-permute-start.8) | collective-permute-done | bytes 258080 | tf_op jit(solution)/shard_map/ppermute | solution.py:583
  42.5 0.1 add_convert_fusion.1
  42.6 1.6 %collective-permute-start.11 = (bf16[56,576]{1,0:T(8,128)(2,1)S(1)}, bf16[56,576]{1,0:T(8,128)(2,1)S(1)}, u32[]{:S(2)}, u32[]{:S(2)}) collective-permute-start(bf16[56,576]{1,0:T(8,128)(2,1)S(1)} %get-tuple-element.134), channel_id=1, source_target_pairs={{0,12},{2,14},{4,8},{6,10},{8,4},{10,6},{12,0},{14,2},{1,13},{3,15... | collective-permute-start | bytes 193544 | tf_op jit(solution)/shard_map/ppermute | solution.py:583
  44.2 2.8 %collective-permute-start.9 = (bf16[56,576]{1,0:T(8,128)(2,1)S(1)}, bf16[56,576]{1,0:T(8,128)(2,1)S(1)}, u32[]{:S(2)}, u32[]{:S(2)}) collective-permute-start(bf16[56,576]{1,0:T(8,128)(2,1)S(1)} %get-tuple-element.136), channel_id=1, source_target_pairs={{0,4},{2,6},{4,0},{6,2},{8,12},{10,14},{12,8},{14,10},{1,5},{3,7},... | collective-permute-start | bytes 193544 | tf_op jit(solution)/shard_map/ppermute | solution.py:583
  47.0 1.9 %query_side.1 = (bf16[896,288]{1,0:T(8,128)(2,1)S(1)}, f32[288,384]{1,0:T(8,128)S(1)}, bf16[288,384]{1,0:T(8,128)(2,1)S(1)}) custom-call(s32[2]{0:T(128)S(1)} %pad_add_fusion.place, bf16[896,512]{1,0:T(8,128)(2,1)S(1)} %get-tuple-element.91.query_pad, bf16[576,896]{1,0:T(8,128)(2,1)S(1)} %get-tuple-element.92.tokens_t), custom_call_target="tpu_custom_call" | custom-call | tf_op jit(solution)/shard_map/query_side/pallas_call | solution.py:397
  49.0 0.8 collective-permute-start.15
  49.8 0.5 collective-permute-done.10
  50.4 0.9 %collective-permute-start.13 = (bf16[56,576]{1,0:T(8,128)(2,1)S(1)}, bf16[56,576]{1,0:T(8,128)(2,1)S(1)}, u32[]{:S(2)}, u32[]{:S(2)}) collective-permute-start(bf16[56,576]{1,0:T(8,128)(2,1)S(1)} %add_convert_fusion.2.swapped), channel_id=1, source_target_pairs={{0,2},{2,0},{4,6},{6,4},{8,10},{10,8},{12,14},{14,12},{1,3},{3,1},... | collective-permute-start | bytes 193544 | tf_op jit(solution)/shard_map/ppermute | solution.py:583
  51.2 3.1 %collective-permute-start.12 = (bf16[56,576]{1,0:T(8,128)(2,1)S(1)}, bf16[56,576]{1,0:T(8,128)(2,1)S(1)}, u32[]{:S(2)}, u32[]{:S(2)}) collective-permute-start(bf16[56,576]{1,0:T(8,128)(2,1)S(1)} %add_convert_fusion.2.swapped), channel_id=1, source_target_pairs={{0,4},{4,8},{6,2},{8,12},{10,6},{14,10},{1,5},{5,9},{7,3},{9,13},{... | collective-permute-start | bytes 193544 | tf_op jit(solution)/shard_map/ppermute | solution.py:583
  54.3 1.4 %collective-permute-done.13.mine = bf16[56,576]{1,0:T(8,128)(2,1)S(1)} collective-permute-done((bf16[56,576]{1,0:T(8,128)(2,1)S(1)}, bf16[56,576]{1,0:T(8,128)(2,1)S(1)}, u32[]{:S(2)}, u32[]{:S(2)}) %collective-permute-start.13) | collective-permute-done | bytes 64544 | tf_op jit(solution)/shard_map/ppermute | solution.py:583
  55.7 0.3 collective-permute-done.12.beside
  56.1 3.0 %pull_back.1 = (f32[320,576]{1,0:T(8,128)S(1)}, bf16[320,576]{1,0:T(8,128)(2,1)S(1)}, bf16[896,576]{1,0:T(8,128)(2,1)S(1)}) custom-call(s32[2]{0:T(128)S(1)} %pad_add_fusion.place, bf16[56,576]{1,0:T(8,128)(2,1)S(1)} %collective-permute-done.13.mine, bf16[56,576]{1,0:T(8,128)(2,1)S(1)} %add_convert_fusion.2.swapped, ...), custom_call_target="tpu_custom_call" | custom-call | tf_op jit(solution)/shard_map/pull_back/pallas_call | solution.py:515
  59.1 2.7 %collective-permute-start.14 = (bf16[320,576]{1,0:T(8,128)(2,1)S(1)}, bf16[320,576]{1,0:T(8,128)(2,1)S(1)}, u32[]{:S(2)}, u32[]{:S(2)}) collective-permute-start(bf16[320,576]{1,0:T(8,128)(2,1)S(1)} %get-tuple-element.103), channel_id=1, source_target_pairs={{0,2},{2,0},{4,6},{6,4},{8,10},{10,8},{12,14},{14,12},{1,3},{3,1},... | collective-permute-start | bytes 1105928 | tf_op jit(solution)/shard_map/ppermute | solution.py:583
  61.7 0.1 fusion.3
  61.8 0.9 %collective-permute-start.18 = (bf16[72,384]{1,0:T(8,128)(2,1)S(1)}, bf16[72,384]{1,0:T(8,128)(2,1)S(1)}, u32[]{:S(2)}, u32[]{:S(2)}) collective-permute-start(bf16[72,384]{1,0:T(8,128)(2,1)S(1)} %get-tuple-element.131), channel_id=1, source_target_pairs={{0,12},{2,14},{4,8},{6,10},{8,4},{10,6},{12,0},{14,2},{1,13},{3,15... | collective-permute-start | bytes 165896 | tf_op jit(solution)/shard_map/ppermute | solution.py:583
  62.7 1.6 %collective-permute-start.17 = (bf16[72,384]{1,0:T(8,128)(2,1)S(1)}, bf16[72,384]{1,0:T(8,128)(2,1)S(1)}, u32[]{:S(2)}, u32[]{:S(2)}) collective-permute-start(bf16[72,384]{1,0:T(8,128)(2,1)S(1)} %get-tuple-element.132), channel_id=1, source_target_pairs={{0,8},{2,10},{4,12},{6,14},{8,0},{10,2},{12,4},{14,6},{1,9},{3,11}... | collective-permute-start | bytes 165896 | tf_op jit(solution)/shard_map/ppermute | solution.py:583
  64.4 1.9 %collective-permute-start.16 = (bf16[72,384]{1,0:T(8,128)(2,1)S(1)}, bf16[72,384]{1,0:T(8,128)(2,1)S(1)}, u32[]{:S(2)}, u32[]{:S(2)}) collective-permute-start(bf16[72,384]{1,0:T(8,128)(2,1)S(1)} %get-tuple-element.133), channel_id=1, source_target_pairs={{0,4},{2,6},{4,0},{6,2},{8,12},{10,14},{12,8},{14,10},{1,5},{3,7},... | collective-permute-start | bytes 165896 | tf_op jit(solution)/shard_map/ppermute | solution.py:583
  66.3 2.8 %token_side.1 = (f32[896,288]{1,0:T(8,128)S(1)}, bf16[896,384]{1,0:T(8,128)(2,1)S(1)}) custom-call(s32[2]{0:T(128)S(1)} %pad_add_fusion.place, bf16[896,288]{1,0:T(8,128)(2,1)S(1)} %get-tuple-element.109.query_back, bf16[896,576]{1,0:T(8,128)(2,1)S(1)} %get-tuple-element.110.backs, bf16[3,288,576]{2,1,0:T(8,128)(2,1)S(1)} %bitcast.10), custom_call_target="tpu_custom_call" | custom-call | tf_op jit(solution)/shard_map/token_side/pallas_call | solution.py:494
  69.1 0.1 collective-permute-start.22
  69.2 0.1 fusion.2
  69.4 1.0 %collective-permute-start.20 = (bf16[104,576]{1,0:T(8,128)(2,1)S(1)}, bf16[104,576]{1,0:T(8,128)(2,1)S(1)}, u32[]{:S(2)}, u32[]{:S(2)}) collective-permute-start(bf16[104,576]{1,0:T(8,128)(2,1)S(1)} %get-tuple-element.137), channel_id=1, source_target_pairs={{0,8},{2,10},{4,12},{6,14},{8,0},{10,2},{12,4},{14,6},{1,9},{3,11}... | collective-permute-start | bytes 359432 | tf_op jit(solution)/shard_map/ppermute | solution.py:583
  70.4 1.4 %collective-permute-start.19 = (bf16[104,576]{1,0:T(8,128)(2,1)S(1)}, bf16[104,576]{1,0:T(8,128)(2,1)S(1)}, u32[]{:S(2)}, u32[]{:S(2)}) collective-permute-start(bf16[104,576]{1,0:T(8,128)(2,1)S(1)} %get-tuple-element.138), channel_id=1, source_target_pairs={{0,4},{2,6},{4,0},{6,2},{8,12},{10,14},{12,8},{14,10},{1,5},{3,7},... | collective-permute-start | bytes 359432 | tf_op jit(solution)/shard_map/ppermute | solution.py:583
  71.8 2.1 %collective-permute-start.21 = (bf16[104,576]{1,0:T(8,128)(2,1)S(1)}, bf16[104,576]{1,0:T(8,128)(2,1)S(1)}, u32[]{:S(2)}, u32[]{:S(2)}) collective-permute-start(bf16[104,576]{1,0:T(8,128)(2,1)S(1)} %concatenate.20), channel_id=1, source_target_pairs={{0,12},{2,14},{4,8},{6,10},{8,4},{10,6},{12,0},{14,2},{1,13},{3,15... | collective-permute-start | bytes 359432 | tf_op jit(solution)/shard_map/ppermute | solution.py:583
  73.9 1.0 %add_convert_fusion = bf16[896,288]{1,0:T(8,128)(2,1)} fusion(f32[896,288]{1,0:T(8,128)S(1)} %get-tuple-element.111, bf16[896,384]{1,0:T(8,128)(2,1)S(1)} %collective-permute-done.22), kind=kLoop, calls=%fused_computation | loop fusion | flops 774144 | bytes 2064384 | tf_op jit(solution)/shard_map/convert_element_type | solution.py:680
  74.9 5.2 %collective-permute-done.20.refs_1_ = bf16[104,576]{1,0:T(8,128)(2,1)S(1)} collective-permute-done((bf16[104,576]{1,0:T(8,128)(2,1)S(1)}, bf16[104,576]{1,0:T(8,128)(2,1)S(1)}, u32[]{:S(2)}, u32[]{:S(2)}) %collective-permute-start.20) | collective-permute-done | bytes 119840 | tf_op jit(solution)/shard_map/ppermute | solution.py:583
  80.1 1.7 %collective-permute-done.21.refs_2_ = bf16[104,576]{1,0:T(8,128)(2,1)S(1)} collective-permute-done((bf16[104,576]{1,0:T(8,128)(2,1)S(1)}, bf16[104,576]{1,0:T(8,128)(2,1)S(1)}, u32[]{:S(2)}, u32[]{:S(2)}) %collective-permute-start.21) | collective-permute-done | bytes 119840 | tf_op jit(solution)/shard_map/ppermute | solution.py:583
  81.8 0.9 %finish.1 = (f32[3,72,288]{2,1,0:T(8,128)}, f32[27,2,288]{2,1,0:T(2,128)}) custom-call(f32[72,384]{1,0:T(8,128)S(1)} %fusion.1.query_sum, f32[72,576]{1,0:T(8,128)S(1)} %slice.77.own_sum, f32[32,576]{1,0:T(8,128)S(1)} %slice.78.tail_sum, bf16[104,576]{1,0:T(8,128)(2,1)S(1)} %collective-permute-done.19.refs_0_, ...), custom_call_target="tpu_custom_call" | custom-call | tf_op jit(solution)/shard_map/finish/pallas_call | solution.py:558
  (36 shorter events, 0.4 us)
Async XLA Ops:
  0.6 1.9 %copy-start.1 = (bf16[1,16,56,288]{3,2,1,0:T(8,128)(2,1)S(1)}, bf16[1,16,56,288]{3,2,1,0:T(8,128)(2,1)}, u32[]{:S(2)}) copy-start(bf16[1,16,56,288]{3,2,1,0:T(8,128)(2,1)} %param.5) | copy-start | bytes 1548292
  0.6 3.6 %copy-start = (bf16[3,576,288]{1,2,0:T(8,128)(2,1)S(1)}, bf16[3,576,288]{1,2,0:T(8,128)(2,1)}, u32[]{:S(2)}) copy-start(bf16[3,576,288]{1,2,0:T(8,128)(2,1)} %param.6) | copy-start | bytes 2985988
  0.7 3.6 %copy-start.2 = (f32[2,27,288]{2,0,1:T(2,128)S(1)}, f32[2,27,288]{2,0,1:T(2,128)}, u32[]{:S(2)}) copy-start(f32[2,27,288]{2,0,1:T(2,128)} %param.7) | copy-start | bytes 186628
  2.0 2.3 %collective-permute-start = (bf16[896,384]{1,0:T(8,128)(2,1)S(1)}, bf16[896,384]{1,0:T(8,128)(2,1)S(1)}, u32[]{:S(2)}, u32[]{:S(2)}) collective-permute-start(bf16[896,384]{1,0:T(8,128)(2,1)S(1)} %pad.4.own), channel_id=1, source_target_pairs={{0,1},{1,0},{2,3},{3,2},{4,5},{5,4},{6,7},{7,6},{8,9},{9,8},{10,11... | collective-permute-start | bytes 2064392 | tf_op jit(solution)/shard_map/ppermute | solution.py:587
  6.3 5.5 %collective-permute-start.1 = (bf16[56,576]{1,0:T(8,128)(2,1)S(1)}, bf16[56,576]{1,0:T(8,128)(2,1)S(1)}, u32[]{:S(2)}, u32[]{:S(2)}) collective-permute-start(bf16[56,576]{1,0:T(8,128)(2,1)S(1)} %get-tuple-element.66), channel_id=1, source_target_pairs={{0,2},{2,0},{4,6},{6,4},{8,10},{10,8},{12,14},{14,12},{1,3},{3,1},... | collective-permute-start | bytes 193544 | tf_op jit(solution)/shard_map/ppermute | solution.py:583
  9.3 6.2 %collective-permute-start.2 = (bf16[56,576]{1,0:T(8,128)(2,1)S(1)}, bf16[56,576]{1,0:T(8,128)(2,1)S(1)}, u32[]{:S(2)}, u32[]{:S(2)}) collective-permute-start(bf16[56,576]{1,0:T(8,128)(2,1)S(1)} %get-tuple-element.67), channel_id=1, source_target_pairs={{2,6},{4,0},{6,10},{8,4},{10,14},{12,8},{3,7},{5,1},{7,11},{9,5},{... | collective-permute-start | bytes 193544 | tf_op jit(solution)/shard_map/ppermute | solution.py:583
  15.5 7.2 %collective-permute-start.6 = (bf16[56,576]{1,0:T(8,128)(2,1)S(1)}, bf16[56,576]{1,0:T(8,128)(2,1)S(1)}, u32[]{:S(2)}, u32[]{:S(2)}) collective-permute-start(bf16[56,576]{1,0:T(8,128)(2,1)S(1)} %add_convert_fusion.3.first), channel_id=1, source_target_pairs={{0,2},{2,0},{4,6},{6,4},{8,10},{10,8},{12,14},{14,12},{1,3},{3,1},... | collective-permute-start | bytes 193544 | tf_op jit(solution)/shard_map/ppermute | solution.py:583
  15.6 7.2 %collective-permute-start.5 = (bf16[56,576]{1,0:T(8,128)(2,1)S(1)}, bf16[56,576]{1,0:T(8,128)(2,1)S(1)}, u32[]{:S(2)}, u32[]{:S(2)}) collective-permute-start(bf16[56,576]{1,0:T(8,128)(2,1)S(1)} %add_convert_fusion.3.first), channel_id=1, source_target_pairs={{0,12},{2,14},{4,8},{6,10},{8,4},{10,6},{12,0},{14,2},{1,13},{3,15... | collective-permute-start | bytes 193544 | tf_op jit(solution)/shard_map/ppermute | solution.py:583
  19.7 5.2 %collective-permute-start.4 = (bf16[56,576]{1,0:T(8,128)(2,1)S(1)}, bf16[56,576]{1,0:T(8,128)(2,1)S(1)}, u32[]{:S(2)}, u32[]{:S(2)}) collective-permute-start(bf16[56,576]{1,0:T(8,128)(2,1)S(1)} %add_convert_fusion.3.first), channel_id=1, source_target_pairs={{0,8},{2,10},{4,12},{6,14},{8,0},{10,2},{12,4},{14,6},{1,9},{3,11}... | collective-permute-start | bytes 193544 | tf_op jit(solution)/shard_map/ppermute | solution.py:583
  19.7 5.2 %collective-permute-start.3 = (bf16[56,576]{1,0:T(8,128)(2,1)S(1)}, bf16[56,576]{1,0:T(8,128)(2,1)S(1)}, u32[]{:S(2)}, u32[]{:S(2)}) collective-permute-start(bf16[56,576]{1,0:T(8,128)(2,1)S(1)} %add_convert_fusion.3.first), channel_id=1, source_target_pairs={{0,4},{2,6},{4,0},{6,2},{8,12},{10,14},{12,8},{14,10},{1,5},{3,7},... | collective-permute-start | bytes 193544 | tf_op jit(solution)/shard_map/ppermute | solution.py:583
  25.0 6.3 %collective-permute-start.7 = (bf16[168,576]{1,0:T(8,128)(2,1)S(1)}, bf16[168,576]{1,0:T(8,128)(2,1)S(1)}, u32[]{:S(2)}, u32[]{:S(2)}) collective-permute-start(bf16[168,576]{1,0:T(8,128)(2,1)S(1)} %constant_dynamic-update-slice_fusion.rest), channel_id=1, source_target_pairs={{0,2},{2,0},{4,6},{6,4},{8,10},{10,8},{12,14},{14,12},{1,3},{3,1},... | collective-permute-start | bytes 580616 | tf_op jit(solution)/shard_map/ppermute | solution.py:583
  35.5 6.9 %collective-permute-start.8 = (bf16[224,576]{1,0:T(8,128)(2,1)S(1)}, bf16[224,576]{1,0:T(8,128)(2,1)S(1)}, u32[]{:S(2)}, u32[]{:S(2)}) collective-permute-start(bf16[224,576]{1,0:T(8,128)(2,1)S(1)} %pad_maximum_fusion), channel_id=1, source_target_pairs={{0,2},{2,0},{4,6},{6,4},{8,10},{10,8},{12,14},{14,12},{1,3},{3,1},... | collective-permute-start | bytes 774152 | tf_op jit(solution)/shard_map/ppermute | solution.py:583
  42.6 7.2 %collective-permute-start.11 = (bf16[56,576]{1,0:T(8,128)(2,1)S(1)}, bf16[56,576]{1,0:T(8,128)(2,1)S(1)}, u32[]{:S(2)}, u32[]{:S(2)}) collective-permute-start(bf16[56,576]{1,0:T(8,128)(2,1)S(1)} %get-tuple-element.134), channel_id=1, source_target_pairs={{0,12},{2,14},{4,8},{6,10},{8,4},{10,6},{12,0},{14,2},{1,13},{3,15... | collective-permute-start | bytes 193544 | tf_op jit(solution)/shard_map/ppermute | solution.py:583
  44.2 6.1 %collective-permute-start.10 = (bf16[56,576]{1,0:T(8,128)(2,1)S(1)}, bf16[56,576]{1,0:T(8,128)(2,1)S(1)}, u32[]{:S(2)}, u32[]{:S(2)}) collective-permute-start(bf16[56,576]{1,0:T(8,128)(2,1)S(1)} %get-tuple-element.135), channel_id=1, source_target_pairs={{0,8},{2,10},{4,12},{6,14},{8,0},{10,2},{12,4},{14,6},{1,9},{3,11}... | collective-permute-start | bytes 193544 | tf_op jit(solution)/shard_map/ppermute | solution.py:583
  44.2 6.1 %collective-permute-start.9 = (bf16[56,576]{1,0:T(8,128)(2,1)S(1)}, bf16[56,576]{1,0:T(8,128)(2,1)S(1)}, u32[]{:S(2)}, u32[]{:S(2)}) collective-permute-start(bf16[56,576]{1,0:T(8,128)(2,1)S(1)} %get-tuple-element.136), channel_id=1, source_target_pairs={{0,4},{2,6},{4,0},{6,2},{8,12},{10,14},{12,8},{14,10},{1,5},{3,7},... | collective-permute-start | bytes 193544 | tf_op jit(solution)/shard_map/ppermute | solution.py:583
  49.0 10.1 %collective-permute-start.15 = (bf16[288,384]{1,0:T(8,128)(2,1)S(1)}, bf16[288,384]{1,0:T(8,128)(2,1)S(1)}, u32[]{:S(2)}, u32[]{:S(2)}) collective-permute-start(bf16[288,384]{1,0:T(8,128)(2,1)S(1)} %get-tuple-element.105), channel_id=1, source_target_pairs={{0,2},{2,0},{4,6},{6,4},{8,10},{10,8},{12,14},{14,12},{1,3},{3,1},... | collective-permute-start | bytes 663560 | tf_op jit(solution)/shard_map/ppermute | solution.py:583
  50.4 5.4 %collective-permute-start.13 = (bf16[56,576]{1,0:T(8,128)(2,1)S(1)}, bf16[56,576]{1,0:T(8,128)(2,1)S(1)}, u32[]{:S(2)}, u32[]{:S(2)}) collective-permute-start(bf16[56,576]{1,0:T(8,128)(2,1)S(1)} %add_convert_fusion.2.swapped), channel_id=1, source_target_pairs={{0,2},{2,0},{4,6},{6,4},{8,10},{10,8},{12,14},{14,12},{1,3},{3,1},... | collective-permute-start | bytes 193544 | tf_op jit(solution)/shard_map/ppermute | solution.py:583
  51.2 4.8 %collective-permute-start.12 = (bf16[56,576]{1,0:T(8,128)(2,1)S(1)}, bf16[56,576]{1,0:T(8,128)(2,1)S(1)}, u32[]{:S(2)}, u32[]{:S(2)}) collective-permute-start(bf16[56,576]{1,0:T(8,128)(2,1)S(1)} %add_convert_fusion.2.swapped), channel_id=1, source_target_pairs={{0,4},{4,8},{6,2},{8,12},{10,6},{14,10},{1,5},{5,9},{7,3},{9,13},{... | collective-permute-start | bytes 193544 | tf_op jit(solution)/shard_map/ppermute | solution.py:583
  59.1 10.1 %collective-permute-start.14 = (bf16[320,576]{1,0:T(8,128)(2,1)S(1)}, bf16[320,576]{1,0:T(8,128)(2,1)S(1)}, u32[]{:S(2)}, u32[]{:S(2)}) collective-permute-start(bf16[320,576]{1,0:T(8,128)(2,1)S(1)} %get-tuple-element.103), channel_id=1, source_target_pairs={{0,2},{2,0},{4,6},{6,4},{8,10},{10,8},{12,14},{14,12},{1,3},{3,1},... | collective-permute-start | bytes 1105928 | tf_op jit(solution)/shard_map/ppermute | solution.py:583
  61.8 7.3 %collective-permute-start.18 = (bf16[72,384]{1,0:T(8,128)(2,1)S(1)}, bf16[72,384]{1,0:T(8,128)(2,1)S(1)}, u32[]{:S(2)}, u32[]{:S(2)}) collective-permute-start(bf16[72,384]{1,0:T(8,128)(2,1)S(1)} %get-tuple-element.131), channel_id=1, source_target_pairs={{0,12},{2,14},{4,8},{6,10},{8,4},{10,6},{12,0},{14,2},{1,13},{3,15... | collective-permute-start | bytes 165896 | tf_op jit(solution)/shard_map/ppermute | solution.py:583
  62.7 6.4 %collective-permute-start.17 = (bf16[72,384]{1,0:T(8,128)(2,1)S(1)}, bf16[72,384]{1,0:T(8,128)(2,1)S(1)}, u32[]{:S(2)}, u32[]{:S(2)}) collective-permute-start(bf16[72,384]{1,0:T(8,128)(2,1)S(1)} %get-tuple-element.132), channel_id=1, source_target_pairs={{0,8},{2,10},{4,12},{6,14},{8,0},{10,2},{12,4},{14,6},{1,9},{3,11}... | collective-permute-start | bytes 165896 | tf_op jit(solution)/shard_map/ppermute | solution.py:583
  64.4 4.8 %collective-permute-start.16 = (bf16[72,384]{1,0:T(8,128)(2,1)S(1)}, bf16[72,384]{1,0:T(8,128)(2,1)S(1)}, u32[]{:S(2)}, u32[]{:S(2)}) collective-permute-start(bf16[72,384]{1,0:T(8,128)(2,1)S(1)} %get-tuple-element.133), channel_id=1, source_target_pairs={{0,4},{2,6},{4,0},{6,2},{8,12},{10,14},{12,8},{14,10},{1,5},{3,7},... | collective-permute-start | bytes 165896 | tf_op jit(solution)/shard_map/ppermute | solution.py:583
  69.1 4.9 %collective-permute-start.22 = (bf16[896,384]{1,0:T(8,128)(2,1)S(1)}, bf16[896,384]{1,0:T(8,128)(2,1)S(1)}, u32[]{:S(2)}, u32[]{:S(2)}) collective-permute-start(bf16[896,384]{1,0:T(8,128)(2,1)S(1)} %get-tuple-element.112), channel_id=1, source_target_pairs={{0,1},{1,0},{2,3},{3,2},{4,5},{5,4},{6,7},{7,6},{8,9},{9,8},{10,11... | collective-permute-start | bytes 2064392 | tf_op jit(solution)/shard_map/ppermute | solution.py:587
  69.4 10.7 %collective-permute-start.20 = (bf16[104,576]{1,0:T(8,128)(2,1)S(1)}, bf16[104,576]{1,0:T(8,128)(2,1)S(1)}, u32[]{:S(2)}, u32[]{:S(2)}) collective-permute-start(bf16[104,576]{1,0:T(8,128)(2,1)S(1)} %get-tuple-element.137), channel_id=1, source_target_pairs={{0,8},{2,10},{4,12},{6,14},{8,0},{10,2},{12,4},{14,6},{1,9},{3,11}... | collective-permute-start | bytes 359432 | tf_op jit(solution)/shard_map/ppermute | solution.py:583
  70.4 9.7 %collective-permute-start.19 = (bf16[104,576]{1,0:T(8,128)(2,1)S(1)}, bf16[104,576]{1,0:T(8,128)(2,1)S(1)}, u32[]{:S(2)}, u32[]{:S(2)}) collective-permute-start(bf16[104,576]{1,0:T(8,128)(2,1)S(1)} %get-tuple-element.138), channel_id=1, source_target_pairs={{0,4},{2,6},{4,0},{6,2},{8,12},{10,14},{12,8},{14,10},{1,5},{3,7},... | collective-permute-start | bytes 359432 | tf_op jit(solution)/shard_map/ppermute | solution.py:583
  71.8 10.0 %collective-permute-start.21 = (bf16[104,576]{1,0:T(8,128)(2,1)S(1)}, bf16[104,576]{1,0:T(8,128)(2,1)S(1)}, u32[]{:S(2)}, u32[]{:S(2)}) collective-permute-start(bf16[104,576]{1,0:T(8,128)(2,1)S(1)} %concatenate.20), channel_id=1, source_target_pairs={{0,12},{2,14},{4,8},{6,10},{8,4},{10,6},{12,0},{14,2},{1,13},{3,15... | collective-permute-start | bytes 359432 | tf_op jit(solution)/shard_map/ppermute | solution.py:583

commit v7 on v6

--- a/solution.py
+++ b/solution.py
@@ -229,10 +229,10 @@
     scale = head_dim ** (-0.5)
     if final:
         own_shares, own_prob_grad, own_pad, query_t, grad_t, sums, *refs = refs
-        other_pad, other_scores, first_grads, rest_grads, query_grad, total = refs
+        other_pad, other_scores, key_grads, query_grad, total = refs
     else:
         first, rest, query_t, grad_t, sums, *refs = refs
-        first_grads, rest_grads, key_pad, score_grads, totals, total = refs
+        key_grads, key_pad, score_grads, totals, total = refs
     joined, choices = [], []
     for sub in range(STEP):
         rows = slice(sub * LANES, (sub + 1) * LANES)
@@ -281,9 +281,7 @@
 
     @pl.when(step == heads // STEP - 1)
     def _():
-        split = first_grads.shape[0]
-        first_grads[...] = total[:split, :].astype(BF16)
-        rest_grads[...] = total[split:, :].astype(BF16)
+        key_grads[...] = total[...].astype(BF16)
 
 
 def whole_spec(array):
@@ -328,27 +326,31 @@
         functools.partial(attend_body, (head_dim, local, heads), False),
         grid=(heads // STEP,),
         out_shape=(
-            pltpu.VMEM(first.shape, BF16),
-            pltpu.VMEM(rest.shape, BF16),
+            pltpu.VMEM((key_count, both), BF16),
             pltpu.VMEM((key_count, heads * LANES), BF16),
             pltpu.VMEM((heads, key_count, tokens), BF16),
             pltpu.VMEM((heads, 8, tokens), F32),
         ),
         in_specs=[whole_spec(first), whole_spec(rest), row_spec, row_spec, sum_spec],
-        out_specs=(whole_spec(first), whole_spec(rest), key_spec, score_spec, sum_spec),
+        out_specs=(
+            pl.BlockSpec((key_count, both), lambda h: (0, 0)),
+            key_spec,
+            score_spec,
+            sum_spec,
+        ),
         scratch_shapes=[pltpu.VMEM((key_count, both), F32)],
         compiler_params=PARAMS,
         name="attend_other",
     )(*near_core(first, rest, query_t, grad_t, sums))
 
 
-def attend_final_call(saved, query_t, grad_t, totals, extra, head_dim, local, split):
+def attend_final_call(saved, query_t, grad_t, totals, extra, head_dim, local):
     key_count, tokens = saved[0].shape[1:]
     heads = local // head_dim
     row_spec, sum_spec, key_spec, score_spec = head_specs(tokens, key_count)
-    shapes = ((split, 2 * local), (key_count - split, 2 * local))
-    outs = [pltpu.VMEM(shape, BF16) for shape in shapes]
-    specs = [pl.BlockSpec(shape, lambda h: (0, 0)) for shape in shapes]
+    shape = (key_count, 2 * local)
+    outs = [pltpu.VMEM(shape, BF16)]
+    specs = [pl.BlockSpec(shape, lambda h: (0, 0))]
     in_specs = [score_spec, score_spec, key_spec, row_spec, row_spec, sum_spec]
     return pl.pallas_call(
         functools.partial(attend_body, (head_dim, local, heads), True),
@@ -406,6 +408,12 @@
         compiler_params=PARAMS,
         name="query_side",
     )(place, *near_core(query_pad, tokens_t))
+
+
+def tap_packing(both, padded):
+    spare = round_up(both, LANES) - both
+    fits = spare > 0 and both % spare == 0 and padded >= 8 * (both // spare)
+    return spare, 8 if fits else 0
 
 
 def pull_body(
@@ -473,8 +481,18 @@
     ).astype(BF16)
     backs[...] = back
     column = mul(tokens_t[...], back)
-    here[outer * padded :, :] = folded[...]
-    away[outer * padded :, :] = folded[...].astype(BF16)
+    both, end = 2 * local, outer * padded
+    spare, packed = tap_packing(both, padded)
+    tail = here.shape[0] - end
+    for target in (here, away):
+        if spare > 0:
+            target[:, both:] = jnp.zeros((target.shape[0], spare), target.dtype)
+        target[end:, :both] = folded[packed : packed + tail, :].astype(target.dtype)
+        for g in range(both // spare if packed else 0):
+            part = folded[0:8, g * spare : (g + 1) * spare].astype(target.dtype)
+            for s in range(outer):
+                at = s * padded + 8 * g
+                target[at : at + 8, both:] = part
     store_blocks(position, count, block_rows, column, here, away)
 
 
@@ -510,13 +528,14 @@
     both, tokens = tokens_t.shape
     local = both // 2
     padded = round_up(both // count, 8)
-    size = count // 2 * padded + 32
+    spare, packed = tap_packing(both, padded)
+    size = count // 2 * padded + 32 - packed
     tiles = pl.cdiv(both, LANES)
     return pl.pallas_call(
         functools.partial(pull_body, (rows, cols, local, count)),
         out_shape=(
-            pltpu.VMEM((size, both), F32),
-            pltpu.VMEM((size, both), BF16),
+            pltpu.VMEM((size, both + spare), F32),
+            pltpu.VMEM((size, both + spare), BF16),
             pltpu.VMEM((tokens, both), BF16),
         ),
         in_specs=[smem()] + [vmem()] * 6,
@@ -548,7 +567,13 @@
         tail = tail + piece[padded:, :].astype(F32)
     weight_grad[0] = query_sum[:rows, :local]
     weight_grad[1] = total[:rows, :local]
-    weight_grad[2] = total[:rows, local:]
+    weight_grad[2] = total[:rows, local : 2 * local]
+    both = 2 * local
+    spare, packed = tap_packing(both, padded)
+    tail = tail[:, :both]
+    if packed:
+        parts = [total[8 * g : 8 * g + 8, both:] for g in range(both // spare)]
+        tail = jnp.concatenate([jnp.concatenate(parts, axis=1), tail], axis=0)
     for side in range(2):
         for k in range(kernel_grad.shape[0]):
             kernel_grad[k, side : side + 1, :] = tail[k : k + 1, side * local : (side + 1) * local]
@@ -640,16 +665,16 @@
     same_rest = jnp.concatenate(others)
     other_rest = exchange(same_rest, across_pair)
     sums, *saved = measure_call(block, same_rest, query_t, grad_t, head_dim)
-    first_other, rest_other, *for_other, totals = attend_call(
+    other_grads, *for_other, totals = attend_call(
         other_first, other_rest, query_t, grad_t, sums, head_dim
     )
-    all_moved = exchange(jnp.concatenate([first_other, rest_other]), across_pair)
+    all_moved = exchange(other_grads, across_pair)
     step_rows = block.shape[0]
-    first_same, rest_same, query_pad = attend_final_call(
-        saved, query_t, grad_t, totals, for_other, head_dim, local, step_rows
-    )
-    first_moved, rest_moved = all_moved[:step_rows], all_moved[step_rows:]
-    low = (rest_same.astype(F32) + rest_moved.astype(F32)).astype(BF16)
+    same_grads, query_pad = attend_final_call(
+        saved, query_t, grad_t, totals, for_other, head_dim, local
+    )
+    all_sum = same_grads.astype(F32) + all_moved.astype(F32)
+    low = all_sum[step_rows:].astype(BF16)
     pieces = [
         exchange(low[(s - 1) * step_rows : s * step_rows], frame_pairs(s, 0))
         for s in range(1, outer)
@@ -658,11 +683,8 @@
         place, query_pad, tokens_t, head_dim, count
     )
     query_moved = exchange(query_away, across_pair)
-    pieces, first_moved, query_back, query_here = barrier(
-        (pieces, first_moved, query_back, query_here)
-    )
-    summed = first_same.astype(F32) + first_moved.astype(F32)
-    swapped = add_all(summed, pieces).astype(BF16)
+    pieces, query_back, query_here = barrier((pieces, query_back, query_here))
+    swapped = add_all(all_sum[:step_rows], pieces).astype(BF16)
     beside = exchange(swapped, outer_pairs(-1))
     mine = exchange(swapped, frame_pairs(0, 1))
     beside, mine = barrier((beside, mine))

time: 83.3 us -> 82.5 us (level)
  no operation moved by 1% of the time
where the time goes in v7:
time: 82.5 us; the launch traced here: 82.2 us
  starting transfers between devices  33 us (40%)
  Pallas kernels  23.8 us (29%)
  waiting for transfers between devices  21.5 us (26%)
  other arithmetic  1.47 us (2%)
  local copies, waits for them, and re-layouts  1.45 us (2%)
  between operations  0.92 us (1%)
    ppermute x21, starting transfers between devices, exchange(): return lax.ppermute(block, 'frames', pairs)  32.4 us
    ppermute x21, waiting for transfers between devices, exchange(): return lax.ppermute(block, 'frames', pairs)  20.5 us
    pallas_call x1, Pallas kernels, attend_call(): pl.pallas_call(functools.partial(attend_body, (head_dim, local, heads), F...  4.18 us
    pallas_call x1, Pallas kernels, attend_final_call(): pl.pallas_call(functools.partial(attend_body, (head_dim, local, heads), T...  3.33 us
    pallas_call x1, Pallas kernels, pull_call(): pl.pallas_call(functools.partial(pull_body, (rows, cols, local, count)),...  3.01 us
    pallas_call x1, Pallas kernels, token_call(): pl.pallas_call(token_body, out_shape=(pltpu.VMEM((tokens, local), F32), p...  2.79 us
    pallas_call x1, Pallas kernels, query_call(): pl.pallas_call(functools.partial(query_body, (head_dim, local, heads)), o...  2.49 us
    pallas_call x1, Pallas kernels, measure_call(): pl.pallas_call(functools.partial(measure_body, (head_dim, local, heads)),...  2.42 us
  transfers between devices with their start and end apart: 23, of which 11 were waited for; matrix products, arithmetic and copies ran while one was open for 2% of the time, Pallas kernels for 20%

profile of v7, /device:TPU:0, one launch (start us, length us, event | category | flops | bytes accessed | tf_op | source)
XLA Modules:
  0.0 82.2 jit_solution(1631995118891032914)
XLA Ops:
  0.7 1.3 %pad.4.own = bf16[896,384]{1,0:T(8,128)(2,1)S(1)} pad(bf16[896,288]{1,0:T(8,128)(2,1)} %bitcast.14, bf16[]{:T(256)} %constant.10.clone.1), padding=0_0x0_96 | pad | bytes 1204226 | tf_op jit(solution)/shard_map/jit(_pad)/pad | solution.py:646
  2.0 0.5 collective-permute-start
  2.5 0.7 turn_grad.1.grad_t.refs_3_.refs_4_
  3.2 0.1 pad_add_fusion.place
  3.3 1.0 %collective-permute-done.other = bf16[896,384]{1,0:T(8,128)(2,1)S(1)} collective-permute-done((bf16[896,384]{1,0:T(8,128)(2,1)S(1)}, bf16[896,384]{1,0:T(8,128)(2,1)S(1)}, u32[]{:S(2)}, u32[]{:S(2)}) %collective-permute-start) | collective-permute-done | bytes 688160 | tf_op jit(solution)/shard_map/ppermute | solution.py:612
  4.3 2.1 %project_pool.1 = (bf16[56,576]{1,0:T(8,128)(2,1)S(1)}, bf16[56,576]{1,0:T(8,128)(2,1)S(1)}, f32[56,576]{1,0:T(8,128)S(1)}, bf16[9,56,576]{2,1,0:T(8,128)(2,1)S(1)}) custom-call(s32[2]{0:T(128)S(1)} %pad_add_fusion.place, bf16[896,384]{1,0:T(8,128)(2,1)S(1)} %pad.4.own, bf16[896,384]{1,0:T(8,128)(2,1)S(1)} %collective-permute-done.other, ...), custom_call_target="tpu_custom_call" | custom-call | tf_op jit(solution)/shard_map/project_pool/pallas_call | solution.py:101
  6.3 3.0 %collective-permute-start.1 = (bf16[56,576]{1,0:T(8,128)(2,1)S(1)}, bf16[56,576]{1,0:T(8,128)(2,1)S(1)}, u32[]{:S(2)}, u32[]{:S(2)}) collective-permute-start(bf16[56,576]{1,0:T(8,128)(2,1)S(1)} %get-tuple-element.63), channel_id=1, source_target_pairs={{0,2},{2,0},{4,6},{6,4},{8,10},{10,8},{12,14},{14,12},{1,3},{3,1},... | collective-permute-start | bytes 193544 | tf_op jit(solution)/shard_map/ppermute | solution.py:608
  9.3 1.5 %collective-permute-start.2 = (bf16[56,576]{1,0:T(8,128)(2,1)S(1)}, bf16[56,576]{1,0:T(8,128)(2,1)S(1)}, u32[]{:S(2)}, u32[]{:S(2)}) collective-permute-start(bf16[56,576]{1,0:T(8,128)(2,1)S(1)} %get-tuple-element.64), channel_id=1, source_target_pairs={{2,6},{4,0},{6,10},{8,4},{10,14},{12,8},{3,7},{5,1},{7,11},{9,5},{... | collective-permute-start | bytes 193544 | tf_op jit(solution)/shard_map/ppermute | solution.py:608
  10.8 1.1 %collective-permute-done.1 = bf16[56,576]{1,0:T(8,128)(2,1)S(1)} collective-permute-done((bf16[56,576]{1,0:T(8,128)(2,1)S(1)}, bf16[56,576]{1,0:T(8,128)(2,1)S(1)}, u32[]{:S(2)}, u32[]{:S(2)}) %collective-permute-start.1) | collective-permute-done | bytes 64544 | tf_op jit(solution)/shard_map/ppermute | solution.py:608
  11.8 3.7 %collective-permute-done.2 = bf16[56,576]{1,0:T(8,128)(2,1)S(1)} collective-permute-done((bf16[56,576]{1,0:T(8,128)(2,1)S(1)}, bf16[56,576]{1,0:T(8,128)(2,1)S(1)}, u32[]{:S(2)}, u32[]{:S(2)}) %collective-permute-start.2) | collective-permute-done | bytes 64544 | tf_op jit(solution)/shard_map/ppermute | solution.py:608
  15.5 0.1 collective-permute-start.6
  15.6 4.1 %collective-permute-start.5 = (bf16[56,576]{1,0:T(8,128)(2,1)S(1)}, bf16[56,576]{1,0:T(8,128)(2,1)S(1)}, u32[]{:S(2)}, u32[]{:S(2)}) collective-permute-start(bf16[56,576]{1,0:T(8,128)(2,1)S(1)} %add_convert_fusion.1.first), channel_id=1, source_target_pairs={{0,12},{2,14},{4,8},{6,10},{8,4},{10,6},{12,0},{14,2},{1,13},{3,15... | collective-permute-start | bytes 193544 | tf_op jit(solution)/shard_map/ppermute | solution.py:608
  19.7 0.6 collective-permute-start.3
  20.3 2.5 %project_query.1 = (bf16[512,896]{1,0:T(8,128)(2,1)S(1)}, bf16[576,896]{1,0:T(8,128)(2,1)S(1)}) custom-call(s32[2]{0:T(128)S(1)} %pad_add_fusion.place, bf16[896,384]{1,0:T(8,128)(2,1)S(1)} %pad.4.own, bf16[896,384]{1,0:T(8,128)(2,1)S(1)} %collective-permute-done.other, bf16[3,288,576]{2,1,0:T(8,128)(2,1)S(1)} %bitcast.9), custom_call_target="tpu_custom_call" | custom-call | tf_op jit(solution)/shard_map/project_query/pallas_call | solution.py:169
  22.8 2.2 %collective-permute-done.4 = bf16[56,576]{1,0:T(8,128)(2,1)S(1)} collective-permute-done((bf16[56,576]{1,0:T(8,128)(2,1)S(1)}, bf16[56,576]{1,0:T(8,128)(2,1)S(1)}, u32[]{:S(2)}, u32[]{:S(2)}) %collective-permute-start.4) | collective-permute-done | bytes 64544 | tf_op jit(solution)/shard_map/ppermute | solution.py:608
  25.0 1.4 %collective-permute-start.7 = (bf16[168,576]{1,0:T(8,128)(2,1)S(1)}, bf16[168,576]{1,0:T(8,128)(2,1)S(1)}, u32[]{:S(2)}, u32[]{:S(2)}) collective-permute-start(bf16[168,576]{1,0:T(8,128)(2,1)S(1)} %constant_dynamic-update-slice_fusion.rest), channel_id=1, source_target_pairs={{0,2},{2,0},{4,6},{6,4},{8,10},{10,8},{12,14},{14,12},{1,3},{3,1},... | collective-permute-start | bytes 580616 | tf_op jit(solution)/shard_map/ppermute | solution.py:608
  26.4 2.4 %attend_measure.1 = (f32[4,8,896]{2,1,0:T(8,128)S(1)}, f32[4,224,896]{2,1,0:T(8,128)S(1)}, f32[4,224,896]{2,1,0:T(8,128)S(1)}, bf16[224,512]{1,0:T(8,128)(2,1)S(1)}) custom-call(bf16[56,576]{1,0:T(8,128)(2,1)S(1)} %add_convert_fusion.1.first, bf16[168,576]{1,0:T(8,128)(2,1)S(1)} %constant_dynamic-update-slice_fusion.rest, ...), custom_call_target="tpu_custom_call" | custom-call | tf_op jit(solution)/shard_map/attend_measure/pallas_call | solution.py:304
  28.9 2.5 %collective-permute-done.7.refs_1_ = bf16[168,576]{1,0:T(8,128)(2,1)S(1)} collective-permute-done((bf16[168,576]{1,0:T(8,128)(2,1)S(1)}, bf16[168,576]{1,0:T(8,128)(2,1)S(1)}, u32[]{:S(2)}, u32[]{:S(2)}) %collective-permute-start.7) | collective-permute-done | bytes 193568 | tf_op jit(solution)/shard_map/ppermute | solution.py:608
  31.3 4.2 %attend_other.1 = (bf16[224,576]{1,0:T(8,128)(2,1)S(1)}, bf16[224,512]{1,0:T(8,128)(2,1)S(1)}, bf16[4,224,896]{2,1,0:T(8,128)(2,1)S(1)}, f32[4,8,896]{2,1,0:T(8,128)S(1)}) custom-call(bf16[56,576]{1,0:T(8,128)(2,1)S(1)} %collective-permute-done.6.refs_0_, bf16[168,576]{1,0:T(8,128)(2,1)S(1)} %collective-permute-done.7.refs_1_, ...), custom_call_target="tpu_custom_call" | custom-call | tf_op jit(solution)/shard_map/attend_other/pallas_call | solution.py:325
  35.5 1.0 %collective-permute-start.8 = (bf16[224,576]{1,0:T(8,128)(2,1)S(1)}, bf16[224,576]{1,0:T(8,128)(2,1)S(1)}, u32[]{:S(2)}, u32[]{:S(2)}) collective-permute-start(bf16[224,576]{1,0:T(8,128)(2,1)S(1)} %get-tuple-element.85), channel_id=1, source_target_pairs={{0,2},{2,0},{4,6},{6,4},{8,10},{10,8},{12,14},{14,12},{1,3},{3,1},... | collective-permute-start | bytes 774152 | tf_op jit(solution)/shard_map/ppermute | solution.py:608
  36.6 3.3 %attend_same.1 = (bf16[224,576]{1,0:T(8,128)(2,1)S(1)}, bf16[896,512]{1,0:T(8,128)(2,1)S(1)}) custom-call(f32[4,224,896]{2,1,0:T(8,128)S(1)} %get-tuple-element.76.refs_0_, f32[4,224,896]{2,1,0:T(8,128)S(1)} %get-tuple-element.77.refs_1_, bf16[224,512]{1,0:T(8,128)(2,1)S(1)} %get-tuple-element.78.refs_2_, ...), custom_call_target="tpu_custom_call" | custom-call | tf_op jit(solution)/shard_map/attend_same/pallas_call | solution.py:355
  39.9 2.6 %collective-permute-done.8 = bf16[224,576]{1,0:T(8,128)(2,1)S(1)} collective-permute-done((bf16[224,576]{1,0:T(8,128)(2,1)S(1)}, bf16[224,576]{1,0:T(8,128)(2,1)S(1)}, u32[]{:S(2)}, u32[]{:S(2)}) %collective-permute-start.8) | collective-permute-done | bytes 258080 | tf_op jit(solution)/shard_map/ppermute | solution.py:608
  42.5 0.1 fusion.5
  42.6 1.6 %collective-permute-start.11 = (bf16[56,576]{1,0:T(8,128)(2,1)S(1)}, bf16[56,576]{1,0:T(8,128)(2,1)S(1)}, u32[]{:S(2)}, u32[]{:S(2)}) collective-permute-start(bf16[56,576]{1,0:T(8,128)(2,1)S(1)} %get-tuple-element.127), channel_id=1, source_target_pairs={{0,12},{2,14},{4,8},{6,10},{8,4},{10,6},{12,0},{14,2},{1,13},{3,15... | collective-permute-start | bytes 193544 | tf_op jit(solution)/shard_map/ppermute | solution.py:608
  44.2 2.8 %collective-permute-start.9 = (bf16[56,576]{1,0:T(8,128)(2,1)S(1)}, bf16[56,576]{1,0:T(8,128)(2,1)S(1)}, u32[]{:S(2)}, u32[]{:S(2)}) collective-permute-start(bf16[56,576]{1,0:T(8,128)(2,1)S(1)} %get-tuple-element.129), channel_id=1, source_target_pairs={{0,4},{2,6},{4,0},{6,2},{8,12},{10,14},{12,8},{14,10},{1,5},{3,7},... | collective-permute-start | bytes 193544 | tf_op jit(solution)/shard_map/ppermute | solution.py:608
  47.0 1.9 %query_side.1 = (bf16[896,288]{1,0:T(8,128)(2,1)S(1)}, f32[288,384]{1,0:T(8,128)S(1)}, bf16[288,384]{1,0:T(8,128)(2,1)S(1)}) custom-call(s32[2]{0:T(128)S(1)} %pad_add_fusion.place, bf16[896,512]{1,0:T(8,128)(2,1)S(1)} %get-tuple-element.86.query_pad, bf16[576,896]{1,0:T(8,128)(2,1)S(1)} %get-tuple-element.87.tokens_t), custom_call_target="tpu_custom_call" | custom-call | tf_op jit(solution)/shard_map/query_side/pallas_call | solution.py:399
  49.0 0.8 collective-permute-start.15
  49.8 0.5 collective-permute-done.10
  50.4 0.8 %collective-permute-start.13 = (bf16[56,576]{1,0:T(8,128)(2,1)S(1)}, bf16[56,576]{1,0:T(8,128)(2,1)S(1)}, u32[]{:S(2)}, u32[]{:S(2)}) collective-permute-start(bf16[56,576]{1,0:T(8,128)(2,1)S(1)} %fusion.2.swapped), channel_id=1, source_target_pairs={{0,2},{2,0},{4,6},{6,4},{8,10},{10,8},{12,14},{14,12},{1,3},{3,1},... | collective-permute-start | bytes 193544 | tf_op jit(solution)/shard_map/ppermute | solution.py:608
  51.2 3.1 %collective-permute-start.12 = (bf16[56,576]{1,0:T(8,128)(2,1)S(1)}, bf16[56,576]{1,0:T(8,128)(2,1)S(1)}, u32[]{:S(2)}, u32[]{:S(2)}) collective-permute-start(bf16[56,576]{1,0:T(8,128)(2,1)S(1)} %fusion.2.swapped), channel_id=1, source_target_pairs={{0,4},{4,8},{6,2},{8,12},{10,6},{14,10},{1,5},{5,9},{7,3},{9,13},{... | collective-permute-start | bytes 193544 | tf_op jit(solution)/shard_map/ppermute | solution.py:608
  54.3 1.4 %collective-permute-done.13.mine = bf16[56,576]{1,0:T(8,128)(2,1)S(1)} collective-permute-done((bf16[56,576]{1,0:T(8,128)(2,1)S(1)}, bf16[56,576]{1,0:T(8,128)(2,1)S(1)}, u32[]{:S(2)}, u32[]{:S(2)}) %collective-permute-start.13) | collective-permute-done | bytes 64544 | tf_op jit(solution)/shard_map/ppermute | solution.py:608
  55.8 0.3 collective-permute-done.12.beside
  56.1 3.0 %pull_back.1 = (f32[312,640]{1,0:T(8,128)S(1)}, bf16[312,640]{1,0:T(8,128)(2,1)S(1)}, bf16[896,576]{1,0:T(8,128)(2,1)S(1)}) custom-call(s32[2]{0:T(128)S(1)} %pad_add_fusion.place, bf16[56,576]{1,0:T(8,128)(2,1)S(1)} %collective-permute-done.13.mine, bf16[56,576]{1,0:T(8,128)(2,1)S(1)} %fusion.2.swapped, bf16[56,576]{1,0:T(8,128)(2,1)S(1)} %collective-permute-done.12.beside, ...), custom_call_target="tpu_custom_call" | custom-call | tf_op jit(solution)/shard_map/pull_back/pallas_call | solution.py:534
  59.1 2.7 %collective-permute-start.14 = (bf16[312,640]{1,0:T(8,128)(2,1)S(1)}, bf16[312,640]{1,0:T(8,128)(2,1)S(1)}, u32[]{:S(2)}, u32[]{:S(2)}) collective-permute-start(bf16[312,640]{1,0:T(8,128)(2,1)S(1)} %get-tuple-element.97), channel_id=1, source_target_pairs={{0,2},{2,0},{4,6},{6,4},{8,10},{10,8},{12,14},{14,12},{1,3},{3,1},... | collective-permute-start | bytes 1198088 | tf_op jit(solution)/shard_map/ppermute | solution.py:608
  61.8 0.1 fusion.7
  61.8 0.9 %collective-permute-start.18 = (bf16[72,384]{1,0:T(8,128)(2,1)S(1)}, bf16[72,384]{1,0:T(8,128)(2,1)S(1)}, u32[]{:S(2)}, u32[]{:S(2)}) collective-permute-start(bf16[72,384]{1,0:T(8,128)(2,1)S(1)} %get-tuple-element.130), channel_id=1, source_target_pairs={{0,12},{2,14},{4,8},{6,10},{8,4},{10,6},{12,0},{14,2},{1,13},{3,15... | collective-permute-start | bytes 165896 | tf_op jit(solution)/shard_map/ppermute | solution.py:608
  62.8 1.6 %collective-permute-start.17 = (bf16[72,384]{1,0:T(8,128)(2,1)S(1)}, bf16[72,384]{1,0:T(8,128)(2,1)S(1)}, u32[]{:S(2)}, u32[]{:S(2)}) collective-permute-start(bf16[72,384]{1,0:T(8,128)(2,1)S(1)} %get-tuple-element.131), channel_id=1, source_target_pairs={{0,8},{2,10},{4,12},{6,14},{8,0},{10,2},{12,4},{14,6},{1,9},{3,11}... | collective-permute-start | bytes 165896 | tf_op jit(solution)/shard_map/ppermute | solution.py:608
  64.4 1.9 %collective-permute-start.16 = (bf16[72,384]{1,0:T(8,128)(2,1)S(1)}, bf16[72,384]{1,0:T(8,128)(2,1)S(1)}, u32[]{:S(2)}, u32[]{:S(2)}) collective-permute-start(bf16[72,384]{1,0:T(8,128)(2,1)S(1)} %get-tuple-element.132), channel_id=1, source_target_pairs={{0,4},{2,6},{4,0},{6,2},{8,12},{10,14},{12,8},{14,10},{1,5},{3,7},... | collective-permute-start | bytes 165896 | tf_op jit(solution)/shard_map/ppermute | solution.py:608
  66.3 2.8 %token_side.1 = (f32[896,288]{1,0:T(8,128)S(1)}, bf16[896,384]{1,0:T(8,128)(2,1)S(1)}) custom-call(s32[2]{0:T(128)S(1)} %pad_add_fusion.place, bf16[896,288]{1,0:T(8,128)(2,1)S(1)} %get-tuple-element.103.query_back, bf16[896,576]{1,0:T(8,128)(2,1)S(1)} %get-tuple-element.104.backs, bf16[3,288,576]{2,1,0:T(8,128)(2,1)S(1)} %bitcast.10), custom_call_target="tpu_custom_call" | custom-call | tf_op jit(solution)/shard_map/token_side/pallas_call | solution.py:512
  69.1 0.1 collective-permute-start.22
  69.2 0.1 fusion.6
  69.5 0.9 %collective-permute-start.20 = (bf16[96,640]{1,0:T(8,128)(2,1)S(1)}, bf16[96,640]{1,0:T(8,128)(2,1)S(1)}, u32[]{:S(2)}, u32[]{:S(2)}) collective-permute-start(bf16[96,640]{1,0:T(8,128)(2,1)S(1)} %get-tuple-element.133), channel_id=1, source_target_pairs={{0,8},{2,10},{4,12},{6,14},{8,0},{10,2},{12,4},{14,6},{1,9},{3,11}... | collective-permute-start | bytes 368648 | tf_op jit(solution)/shard_map/ppermute | solution.py:608
  70.4 1.5 %collective-permute-start.19 = (bf16[96,640]{1,0:T(8,128)(2,1)S(1)}, bf16[96,640]{1,0:T(8,128)(2,1)S(1)}, u32[]{:S(2)}, u32[]{:S(2)}) collective-permute-start(bf16[96,640]{1,0:T(8,128)(2,1)S(1)} %get-tuple-element.134), channel_id=1, source_target_pairs={{0,4},{2,6},{4,0},{6,2},{8,12},{10,14},{12,8},{14,10},{1,5},{3,7},... | collective-permute-start | bytes 368648 | tf_op jit(solution)/shard_map/ppermute | solution.py:608
  71.9 2.1 %collective-permute-start.21 = (bf16[96,640]{1,0:T(8,128)(2,1)S(1)}, bf16[96,640]{1,0:T(8,128)(2,1)S(1)}, u32[]{:S(2)}, u32[]{:S(2)}) collective-permute-start(bf16[96,640]{1,0:T(8,128)(2,1)S(1)} %concatenate.16), channel_id=1, source_target_pairs={{0,12},{2,14},{4,8},{6,10},{8,4},{10,6},{12,0},{14,2},{1,13},{3,15... | collective-permute-start | bytes 368648 | tf_op jit(solution)/shard_map/ppermute | solution.py:608
  74.0 1.0 %add_convert_fusion = bf16[896,288]{1,0:T(8,128)(2,1)} fusion(f32[896,288]{1,0:T(8,128)S(1)} %get-tuple-element.105, bf16[896,384]{1,0:T(8,128)(2,1)S(1)} %collective-permute-done.22), kind=kLoop, calls=%fused_computation | loop fusion | flops 774144 | bytes 2064384 | tf_op jit(solution)/shard_map/convert_element_type | solution.py:702
  75.0 4.5 %collective-permute-done.20.refs_1_ = bf16[96,640]{1,0:T(8,128)(2,1)S(1)} collective-permute-done((bf16[96,640]{1,0:T(8,128)(2,1)S(1)}, bf16[96,640]{1,0:T(8,128)(2,1)S(1)}, u32[]{:S(2)}, u32[]{:S(2)}) %collective-permute-start.20) | collective-permute-done | bytes 122912 | tf_op jit(solution)/shard_map/ppermute | solution.py:608
  79.5 1.9 %collective-permute-done.21.refs_2_ = bf16[96,640]{1,0:T(8,128)(2,1)S(1)} collective-permute-done((bf16[96,640]{1,0:T(8,128)(2,1)S(1)}, bf16[96,640]{1,0:T(8,128)(2,1)S(1)}, u32[]{:S(2)}, u32[]{:S(2)}) %collective-permute-start.21) | collective-permute-done | bytes 122912 | tf_op jit(solution)/shard_map/ppermute | solution.py:608
  81.3 0.9 %finish.1 = (f32[3,72,288]{2,1,0:T(8,128)}, f32[27,2,288]{2,1,0:T(2,128)}) custom-call(f32[72,384]{1,0:T(8,128)S(1)} %fusion.4.query_sum, f32[72,640]{1,0:T(8,128)S(1)} %slice.77.own_sum, f32[24,640]{1,0:T(8,128)S(1)} %slice.78.tail_sum, bf16[96,640]{1,0:T(8,128)(2,1)S(1)} %collective-permute-done.19.refs_0_, ...), custom_call_target="tpu_custom_call" | custom-call | tf_op jit(solution)/shard_map/finish/pallas_call | solution.py:583
  (34 shorter events, 0.3 us)
Async XLA Ops:
  0.6 1.9 %copy-start.1 = (bf16[1,16,56,288]{3,2,1,0:T(8,128)(2,1)S(1)}, bf16[1,16,56,288]{3,2,1,0:T(8,128)(2,1)}, u32[]{:S(2)}) copy-start(bf16[1,16,56,288]{3,2,1,0:T(8,128)(2,1)} %param.5) | copy-start | bytes 1548292
  0.6 3.6 %copy-start = (bf16[3,576,288]{1,2,0:T(8,128)(2,1)S(1)}, bf16[3,576,288]{1,2,0:T(8,128)(2,1)}, u32[]{:S(2)}) copy-start(bf16[3,576,288]{1,2,0:T(8,128)(2,1)} %param.6) | copy-start | bytes 2985988
  0.7 3.6 %copy-start.2 = (f32[2,27,288]{2,0,1:T(2,128)S(1)}, f32[2,27,288]{2,0,1:T(2,128)}, u32[]{:S(2)}) copy-start(f32[2,27,288]{2,0,1:T(2,128)} %param.7) | copy-start | bytes 186628
  2.0 2.3 %collective-permute-start = (bf16[896,384]{1,0:T(8,128)(2,1)S(1)}, bf16[896,384]{1,0:T(8,128)(2,1)S(1)}, u32[]{:S(2)}, u32[]{:S(2)}) collective-permute-start(bf16[896,384]{1,0:T(8,128)(2,1)S(1)} %pad.4.own), channel_id=1, source_target_pairs={{0,1},{1,0},{2,3},{3,2},{4,5},{5,4},{6,7},{7,6},{8,9},{9,8},{10,11... | collective-permute-start | bytes 2064392 | tf_op jit(solution)/shard_map/ppermute | solution.py:612
  6.3 5.5 %collective-permute-start.1 = (bf16[56,576]{1,0:T(8,128)(2,1)S(1)}, bf16[56,576]{1,0:T(8,128)(2,1)S(1)}, u32[]{:S(2)}, u32[]{:S(2)}) collective-permute-start(bf16[56,576]{1,0:T(8,128)(2,1)S(1)} %get-tuple-element.63), channel_id=1, source_target_pairs={{0,2},{2,0},{4,6},{6,4},{8,10},{10,8},{12,14},{14,12},{1,3},{3,1},... | collective-permute-start | bytes 193544 | tf_op jit(solution)/shard_map/ppermute | solution.py:608
  9.3 6.2 %collective-permute-start.2 = (bf16[56,576]{1,0:T(8,128)(2,1)S(1)}, bf16[56,576]{1,0:T(8,128)(2,1)S(1)}, u32[]{:S(2)}, u32[]{:S(2)}) collective-permute-start(bf16[56,576]{1,0:T(8,128)(2,1)S(1)} %get-tuple-element.64), channel_id=1, source_target_pairs={{2,6},{4,0},{6,10},{8,4},{10,14},{12,8},{3,7},{5,1},{7,11},{9,5},{... | collective-permute-start | bytes 193544 | tf_op jit(solution)/shard_map/ppermute | solution.py:608
  15.5 7.2 %collective-permute-start.6 = (bf16[56,576]{1,0:T(8,128)(2,1)S(1)}, bf16[56,576]{1,0:T(8,128)(2,1)S(1)}, u32[]{:S(2)}, u32[]{:S(2)}) collective-permute-start(bf16[56,576]{1,0:T(8,128)(2,1)S(1)} %add_convert_fusion.1.first), channel_id=1, source_target_pairs={{0,2},{2,0},{4,6},{6,4},{8,10},{10,8},{12,14},{14,12},{1,3},{3,1},... | collective-permute-start | bytes 193544 | tf_op jit(solution)/shard_map/ppermute | solution.py:608
  15.6 7.2 %collective-permute-start.5 = (bf16[56,576]{1,0:T(8,128)(2,1)S(1)}, bf16[56,576]{1,0:T(8,128)(2,1)S(1)}, u32[]{:S(2)}, u32[]{:S(2)}) collective-permute-start(bf16[56,576]{1,0:T(8,128)(2,1)S(1)} %add_convert_fusion.1.first), channel_id=1, source_target_pairs={{0,12},{2,14},{4,8},{6,10},{8,4},{10,6},{12,0},{14,2},{1,13},{3,15... | collective-permute-start | bytes 193544 | tf_op jit(solution)/shard_map/ppermute | solution.py:608
  19.7 5.2 %collective-permute-start.4 = (bf16[56,576]{1,0:T(8,128)(2,1)S(1)}, bf16[56,576]{1,0:T(8,128)(2,1)S(1)}, u32[]{:S(2)}, u32[]{:S(2)}) collective-permute-start(bf16[56,576]{1,0:T(8,128)(2,1)S(1)} %add_convert_fusion.1.first), channel_id=1, source_target_pairs={{0,8},{2,10},{4,12},{6,14},{8,0},{10,2},{12,4},{14,6},{1,9},{3,11}... | collective-permute-start | bytes 193544 | tf_op jit(solution)/shard_map/ppermute | solution.py:608
  19.7 5.2 %collective-permute-start.3 = (bf16[56,576]{1,0:T(8,128)(2,1)S(1)}, bf16[56,576]{1,0:T(8,128)(2,1)S(1)}, u32[]{:S(2)}, u32[]{:S(2)}) collective-permute-start(bf16[56,576]{1,0:T(8,128)(2,1)S(1)} %add_convert_fusion.1.first), channel_id=1, source_target_pairs={{0,4},{2,6},{4,0},{6,2},{8,12},{10,14},{12,8},{14,10},{1,5},{3,7},... | collective-permute-start | bytes 193544 | tf_op jit(solution)/shard_map/ppermute | solution.py:608
  25.0 6.3 %collective-permute-start.7 = (bf16[168,576]{1,0:T(8,128)(2,1)S(1)}, bf16[168,576]{1,0:T(8,128)(2,1)S(1)}, u32[]{:S(2)}, u32[]{:S(2)}) collective-permute-start(bf16[168,576]{1,0:T(8,128)(2,1)S(1)} %constant_dynamic-update-slice_fusion.rest), channel_id=1, source_target_pairs={{0,2},{2,0},{4,6},{6,4},{8,10},{10,8},{12,14},{14,12},{1,3},{3,1},... | collective-permute-start | bytes 580616 | tf_op jit(solution)/shard_map/ppermute | solution.py:608
  35.5 6.9 %collective-permute-start.8 = (bf16[224,576]{1,0:T(8,128)(2,1)S(1)}, bf16[224,576]{1,0:T(8,128)(2,1)S(1)}, u32[]{:S(2)}, u32[]{:S(2)}) collective-permute-start(bf16[224,576]{1,0:T(8,128)(2,1)S(1)} %get-tuple-element.85), channel_id=1, source_target_pairs={{0,2},{2,0},{4,6},{6,4},{8,10},{10,8},{12,14},{14,12},{1,3},{3,1},... | collective-permute-start | bytes 774152 | tf_op jit(solution)/shard_map/ppermute | solution.py:608
  42.6 7.2 %collective-permute-start.11 = (bf16[56,576]{1,0:T(8,128)(2,1)S(1)}, bf16[56,576]{1,0:T(8,128)(2,1)S(1)}, u32[]{:S(2)}, u32[]{:S(2)}) collective-permute-start(bf16[56,576]{1,0:T(8,128)(2,1)S(1)} %get-tuple-element.127), channel_id=1, source_target_pairs={{0,12},{2,14},{4,8},{6,10},{8,4},{10,6},{12,0},{14,2},{1,13},{3,15... | collective-permute-start | bytes 193544 | tf_op jit(solution)/shard_map/ppermute | solution.py:608
  44.2 6.1 %collective-permute-start.10 = (bf16[56,576]{1,0:T(8,128)(2,1)S(1)}, bf16[56,576]{1,0:T(8,128)(2,1)S(1)}, u32[]{:S(2)}, u32[]{:S(2)}) collective-permute-start(bf16[56,576]{1,0:T(8,128)(2,1)S(1)} %get-tuple-element.128), channel_id=1, source_target_pairs={{0,8},{2,10},{4,12},{6,14},{8,0},{10,2},{12,4},{14,6},{1,9},{3,11}... | collective-permute-start | bytes 193544 | tf_op jit(solution)/shard_map/ppermute | solution.py:608
  44.2 6.1 %collective-permute-start.9 = (bf16[56,576]{1,0:T(8,128)(2,1)S(1)}, bf16[56,576]{1,0:T(8,128)(2,1)S(1)}, u32[]{:S(2)}, u32[]{:S(2)}) collective-permute-start(bf16[56,576]{1,0:T(8,128)(2,1)S(1)} %get-tuple-element.129), channel_id=1, source_target_pairs={{0,4},{2,6},{4,0},{6,2},{8,12},{10,14},{12,8},{14,10},{1,5},{3,7},... | collective-permute-start | bytes 193544 | tf_op jit(solution)/shard_map/ppermute | solution.py:608
  49.0 10.1 %collective-permute-start.15 = (bf16[288,384]{1,0:T(8,128)(2,1)S(1)}, bf16[288,384]{1,0:T(8,128)(2,1)S(1)}, u32[]{:S(2)}, u32[]{:S(2)}) collective-permute-start(bf16[288,384]{1,0:T(8,128)(2,1)S(1)} %get-tuple-element.99), channel_id=1, source_target_pairs={{0,2},{2,0},{4,6},{6,4},{8,10},{10,8},{12,14},{14,12},{1,3},{3,1},... | collective-permute-start | bytes 663560 | tf_op jit(solution)/shard_map/ppermute | solution.py:608
  50.4 5.4 %collective-permute-start.13 = (bf16[56,576]{1,0:T(8,128)(2,1)S(1)}, bf16[56,576]{1,0:T(8,128)(2,1)S(1)}, u32[]{:S(2)}, u32[]{:S(2)}) collective-permute-start(bf16[56,576]{1,0:T(8,128)(2,1)S(1)} %fusion.2.swapped), channel_id=1, source_target_pairs={{0,2},{2,0},{4,6},{6,4},{8,10},{10,8},{12,14},{14,12},{1,3},{3,1},... | collective-permute-start | bytes 193544 | tf_op jit(solution)/shard_map/ppermute | solution.py:608
  51.2 4.9 %collective-permute-start.12 = (bf16[56,576]{1,0:T(8,128)(2,1)S(1)}, bf16[56,576]{1,0:T(8,128)(2,1)S(1)}, u32[]{:S(2)}, u32[]{:S(2)}) collective-permute-start(bf16[56,576]{1,0:T(8,128)(2,1)S(1)} %fusion.2.swapped), channel_id=1, source_target_pairs={{0,4},{4,8},{6,2},{8,12},{10,6},{14,10},{1,5},{5,9},{7,3},{9,13},{... | collective-permute-start | bytes 193544 | tf_op jit(solution)/shard_map/ppermute | solution.py:608
  59.1 10.1 %collective-permute-start.14 = (bf16[312,640]{1,0:T(8,128)(2,1)S(1)}, bf16[312,640]{1,0:T(8,128)(2,1)S(1)}, u32[]{:S(2)}, u32[]{:S(2)}) collective-permute-start(bf16[312,640]{1,0:T(8,128)(2,1)S(1)} %get-tuple-element.97), channel_id=1, source_target_pairs={{0,2},{2,0},{4,6},{6,4},{8,10},{10,8},{12,14},{14,12},{1,3},{3,1},... | collective-permute-start | bytes 1198088 | tf_op jit(solution)/shard_map/ppermute | solution.py:608
  61.8 7.3 %collective-permute-start.18 = (bf16[72,384]{1,0:T(8,128)(2,1)S(1)}, bf16[72,384]{1,0:T(8,128)(2,1)S(1)}, u32[]{:S(2)}, u32[]{:S(2)}) collective-permute-start(bf16[72,384]{1,0:T(8,128)(2,1)S(1)} %get-tuple-element.130), channel_id=1, source_target_pairs={{0,12},{2,14},{4,8},{6,10},{8,4},{10,6},{12,0},{14,2},{1,13},{3,15... | collective-permute-start | bytes 165896 | tf_op jit(solution)/shard_map/ppermute | solution.py:608
  62.8 6.4 %collective-permute-start.17 = (bf16[72,384]{1,0:T(8,128)(2,1)S(1)}, bf16[72,384]{1,0:T(8,128)(2,1)S(1)}, u32[]{:S(2)}, u32[]{:S(2)}) collective-permute-start(bf16[72,384]{1,0:T(8,128)(2,1)S(1)} %get-tuple-element.131), channel_id=1, source_target_pairs={{0,8},{2,10},{4,12},{6,14},{8,0},{10,2},{12,4},{14,6},{1,9},{3,11}... | collective-permute-start | bytes 165896 | tf_op jit(solution)/shard_map/ppermute | solution.py:608
  64.4 4.8 %collective-permute-start.16 = (bf16[72,384]{1,0:T(8,128)(2,1)S(1)}, bf16[72,384]{1,0:T(8,128)(2,1)S(1)}, u32[]{:S(2)}, u32[]{:S(2)}) collective-permute-start(bf16[72,384]{1,0:T(8,128)(2,1)S(1)} %get-tuple-element.132), channel_id=1, source_target_pairs={{0,4},{2,6},{4,0},{6,2},{8,12},{10,14},{12,8},{14,10},{1,5},{3,7},... | collective-permute-start | bytes 165896 | tf_op jit(solution)/shard_map/ppermute | solution.py:608
  69.1 4.9 %collective-permute-start.22 = (bf16[896,384]{1,0:T(8,128)(2,1)S(1)}, bf16[896,384]{1,0:T(8,128)(2,1)S(1)}, u32[]{:S(2)}, u32[]{:S(2)}) collective-permute-start(bf16[896,384]{1,0:T(8,128)(2,1)S(1)} %get-tuple-element.106), channel_id=1, source_target_pairs={{0,1},{1,0},{2,3},{3,2},{4,5},{5,4},{6,7},{7,6},{8,9},{9,8},{10,11... | collective-permute-start | bytes 2064392 | tf_op jit(solution)/shard_map/ppermute | solution.py:612
  69.5 10.0 %collective-permute-start.20 = (bf16[96,640]{1,0:T(8,128)(2,1)S(1)}, bf16[96,640]{1,0:T(8,128)(2,1)S(1)}, u32[]{:S(2)}, u32[]{:S(2)}) collective-permute-start(bf16[96,640]{1,0:T(8,128)(2,1)S(1)} %get-tuple-element.133), channel_id=1, source_target_pairs={{0,8},{2,10},{4,12},{6,14},{8,0},{10,2},{12,4},{14,6},{1,9},{3,11}... | collective-permute-start | bytes 368648 | tf_op jit(solution)/shard_map/ppermute | solution.py:608
  70.4 9.1 %collective-permute-start.19 = (bf16[96,640]{1,0:T(8,128)(2,1)S(1)}, bf16[96,640]{1,0:T(8,128)(2,1)S(1)}, u32[]{:S(2)}, u32[]{:S(2)}) collective-permute-start(bf16[96,640]{1,0:T(8,128)(2,1)S(1)} %get-tuple-element.134), channel_id=1, source_target_pairs={{0,4},{2,6},{4,0},{6,2},{8,12},{10,14},{12,8},{14,10},{1,5},{3,7},... | collective-permute-start | bytes 368648 | tf_op jit(solution)/shard_map/ppermute | solution.py:608
  71.9 9.5 %collective-permute-start.21 = (bf16[96,640]{1,0:T(8,128)(2,1)S(1)}, bf16[96,640]{1,0:T(8,128)(2,1)S(1)}, u32[]{:S(2)}, u32[]{:S(2)}) collective-permute-start(bf16[96,640]{1,0:T(8,128)(2,1)S(1)} %concatenate.16), channel_id=1, source_target_pairs={{0,12},{2,14},{4,8},{6,10},{8,4},{10,6},{12,0},{14,2},{1,13},{3,15... | collective-permute-start | bytes 368648 | tf_op jit(solution)/shard_map/ppermute | solution.py:608

commit v8 on v7

--- a/solution.py
+++ b/solution.py
@@ -498,8 +498,8 @@
 
 def token_body(place, query_back, backs, weights, token_near, token_far):
     local = weights.shape[1]
-    both = weights[1:3].reshape(2 * local, 2 * local)
-    token_sum = mul(query_back[...], weights[0]) + mul(backs[...], both)
+    joined = jnp.concatenate([query_back[...], backs[...]], axis=1)
+    token_sum = mul(joined, weights[...].reshape(3 * local, 2 * local))
     first = place[1] == 0
     low_half, high_half = token_sum[:, :local], token_sum[:, local:]
     token_near[...] = jnp.where(first, low_half, high_half)

time: 82.5 us -> 85.8 us (1.040)
  Pallas kernels: 23.8 us -> 27.1 us
    pallas_call x1, Pallas kernels: 2.79 us -> 6.04 us  [token_call(): pl.pallas_call(token_body, out_shape=(pltpu.VMEM((tokens, local), F32), p...]
  transfers between devices with their start and end apart: 23 -> 23, of which waited for: 11 -> 11; matrix products, arithmetic and copies ran while one was open for 2% -> 2% of each run, Pallas kernels for 20% -> 23%
where the time goes in v8:
time: 85.8 us; the launch traced here: 85.3 us
  starting transfers between devices  33 us (38%)
  Pallas kernels  27.1 us (32%)
  waiting for transfers between devices  21.4 us (25%)
  other arithmetic  1.47 us (2%)
  local copies, waits for them, and re-layouts  1.45 us (2%)
  between operations  0.92 us (1%)
    ppermute x21, starting transfers between devices, exchange(): return lax.ppermute(block, 'frames', pairs)  32.4 us
    ppermute x21, waiting for transfers between devices, exchange(): return lax.ppermute(block, 'frames', pairs)  20.4 us
    pallas_call x1, Pallas kernels, token_call(): pl.pallas_call(token_body, out_shape=(pltpu.VMEM((tokens, local), F32), p...  6.04 us
    pallas_call x1, Pallas kernels, attend_call(): pl.pallas_call(functools.partial(attend_body, (head_dim, local, heads), F...  4.18 us
    pallas_call x1, Pallas kernels, attend_final_call(): pl.pallas_call(functools.partial(attend_body, (head_dim, local, heads), T...  3.33 us
    pallas_call x1, Pallas kernels, pull_call(): pl.pallas_call(functools.partial(pull_body, (rows, cols, local, count)),...  3.01 us
    pallas_call x1, Pallas kernels, query_call(): pl.pallas_call(functools.partial(query_body, (head_dim, local, heads)), o...  2.49 us
    pallas_call x1, Pallas kernels, measure_call(): pl.pallas_call(functools.partial(measure_body, (head_dim, local, heads)),...  2.42 us
  transfers between devices with their start and end apart: 23, of which 11 were waited for; matrix products, arithmetic and copies ran while one was open for 2% of the time, Pallas kernels for 23%

profile of v8, /device:TPU:0, one launch (start us, length us, event | category | flops | bytes accessed | tf_op | source)
XLA Modules:
  0.0 85.3 jit_solution(1959327931815325748)
XLA Ops:
  0.7 1.3 %pad.4.own = bf16[896,384]{1,0:T(8,128)(2,1)S(1)} pad(bf16[896,288]{1,0:T(8,128)(2,1)} %bitcast.14, bf16[]{:T(256)} %constant.10.clone.1), padding=0_0x0_96 | pad | bytes 1204226 | tf_op jit(solution)/shard_map/jit(_pad)/pad | solution.py:646
  2.0 0.5 collective-permute-start
  2.5 0.7 turn_grad.1.grad_t.refs_3_.refs_4_
  3.2 0.1 pad_add_fusion.place
  3.3 1.0 %collective-permute-done.other = bf16[896,384]{1,0:T(8,128)(2,1)S(1)} collective-permute-done((bf16[896,384]{1,0:T(8,128)(2,1)S(1)}, bf16[896,384]{1,0:T(8,128)(2,1)S(1)}, u32[]{:S(2)}, u32[]{:S(2)}) %collective-permute-start) | collective-permute-done | bytes 688160 | tf_op jit(solution)/shard_map/ppermute | solution.py:612
  4.3 2.1 %project_pool.1 = (bf16[56,576]{1,0:T(8,128)(2,1)S(1)}, bf16[56,576]{1,0:T(8,128)(2,1)S(1)}, f32[56,576]{1,0:T(8,128)S(1)}, bf16[9,56,576]{2,1,0:T(8,128)(2,1)S(1)}) custom-call(s32[2]{0:T(128)S(1)} %pad_add_fusion.place, bf16[896,384]{1,0:T(8,128)(2,1)S(1)} %pad.4.own, bf16[896,384]{1,0:T(8,128)(2,1)S(1)} %collective-permute-done.other, ...), custom_call_target="tpu_custom_call" | custom-call | tf_op jit(solution)/shard_map/project_pool/pallas_call | solution.py:101
  6.3 3.0 %collective-permute-start.1 = (bf16[56,576]{1,0:T(8,128)(2,1)S(1)}, bf16[56,576]{1,0:T(8,128)(2,1)S(1)}, u32[]{:S(2)}, u32[]{:S(2)}) collective-permute-start(bf16[56,576]{1,0:T(8,128)(2,1)S(1)} %get-tuple-element.63), channel_id=1, source_target_pairs={{0,2},{2,0},{4,6},{6,4},{8,10},{10,8},{12,14},{14,12},{1,3},{3,1},... | collective-permute-start | bytes 193544 | tf_op jit(solution)/shard_map/ppermute | solution.py:608
  9.3 1.5 %collective-permute-start.2 = (bf16[56,576]{1,0:T(8,128)(2,1)S(1)}, bf16[56,576]{1,0:T(8,128)(2,1)S(1)}, u32[]{:S(2)}, u32[]{:S(2)}) collective-permute-start(bf16[56,576]{1,0:T(8,128)(2,1)S(1)} %get-tuple-element.64), channel_id=1, source_target_pairs={{2,6},{4,0},{6,10},{8,4},{10,14},{12,8},{3,7},{5,1},{7,11},{9,5},{... | collective-permute-start | bytes 193544 | tf_op jit(solution)/shard_map/ppermute | solution.py:608
  10.8 1.1 %collective-permute-done.1 = bf16[56,576]{1,0:T(8,128)(2,1)S(1)} collective-permute-done((bf16[56,576]{1,0:T(8,128)(2,1)S(1)}, bf16[56,576]{1,0:T(8,128)(2,1)S(1)}, u32[]{:S(2)}, u32[]{:S(2)}) %collective-permute-start.1) | collective-permute-done | bytes 64544 | tf_op jit(solution)/shard_map/ppermute | solution.py:608
  11.8 3.7 %collective-permute-done.2 = bf16[56,576]{1,0:T(8,128)(2,1)S(1)} collective-permute-done((bf16[56,576]{1,0:T(8,128)(2,1)S(1)}, bf16[56,576]{1,0:T(8,128)(2,1)S(1)}, u32[]{:S(2)}, u32[]{:S(2)}) %collective-permute-start.2) | collective-permute-done | bytes 64544 | tf_op jit(solution)/shard_map/ppermute | solution.py:608
  15.5 0.1 collective-permute-start.6
  15.6 4.1 %collective-permute-start.5 = (bf16[56,576]{1,0:T(8,128)(2,1)S(1)}, bf16[56,576]{1,0:T(8,128)(2,1)S(1)}, u32[]{:S(2)}, u32[]{:S(2)}) collective-permute-start(bf16[56,576]{1,0:T(8,128)(2,1)S(1)} %add_convert_fusion.1.first), channel_id=1, source_target_pairs={{0,12},{2,14},{4,8},{6,10},{8,4},{10,6},{12,0},{14,2},{1,13},{3,15... | collective-permute-start | bytes 193544 | tf_op jit(solution)/shard_map/ppermute | solution.py:608
  19.7 0.6 collective-permute-start.3
  20.3 2.5 %project_query.1 = (bf16[512,896]{1,0:T(8,128)(2,1)S(1)}, bf16[576,896]{1,0:T(8,128)(2,1)S(1)}) custom-call(s32[2]{0:T(128)S(1)} %pad_add_fusion.place, bf16[896,384]{1,0:T(8,128)(2,1)S(1)} %pad.4.own, bf16[896,384]{1,0:T(8,128)(2,1)S(1)} %collective-permute-done.other, bf16[3,288,576]{2,1,0:T(8,128)(2,1)S(1)} %bitcast.9), custom_call_target="tpu_custom_call" | custom-call | tf_op jit(solution)/shard_map/project_query/pallas_call | solution.py:169
  22.8 2.2 %collective-permute-done.4 = bf16[56,576]{1,0:T(8,128)(2,1)S(1)} collective-permute-done((bf16[56,576]{1,0:T(8,128)(2,1)S(1)}, bf16[56,576]{1,0:T(8,128)(2,1)S(1)}, u32[]{:S(2)}, u32[]{:S(2)}) %collective-permute-start.4) | collective-permute-done | bytes 64544 | tf_op jit(solution)/shard_map/ppermute | solution.py:608
  25.0 1.4 %collective-permute-start.7 = (bf16[168,576]{1,0:T(8,128)(2,1)S(1)}, bf16[168,576]{1,0:T(8,128)(2,1)S(1)}, u32[]{:S(2)}, u32[]{:S(2)}) collective-permute-start(bf16[168,576]{1,0:T(8,128)(2,1)S(1)} %constant_dynamic-update-slice_fusion.rest), channel_id=1, source_target_pairs={{0,2},{2,0},{4,6},{6,4},{8,10},{10,8},{12,14},{14,12},{1,3},{3,1},... | collective-permute-start | bytes 580616 | tf_op jit(solution)/shard_map/ppermute | solution.py:608
  26.4 2.4 %attend_measure.1 = (f32[4,8,896]{2,1,0:T(8,128)S(1)}, f32[4,224,896]{2,1,0:T(8,128)S(1)}, f32[4,224,896]{2,1,0:T(8,128)S(1)}, bf16[224,512]{1,0:T(8,128)(2,1)S(1)}) custom-call(bf16[56,576]{1,0:T(8,128)(2,1)S(1)} %add_convert_fusion.1.first, bf16[168,576]{1,0:T(8,128)(2,1)S(1)} %constant_dynamic-update-slice_fusion.rest, ...), custom_call_target="tpu_custom_call" | custom-call | tf_op jit(solution)/shard_map/attend_measure/pallas_call | solution.py:304
  28.9 2.5 %collective-permute-done.7.refs_1_ = bf16[168,576]{1,0:T(8,128)(2,1)S(1)} collective-permute-done((bf16[168,576]{1,0:T(8,128)(2,1)S(1)}, bf16[168,576]{1,0:T(8,128)(2,1)S(1)}, u32[]{:S(2)}, u32[]{:S(2)}) %collective-permute-start.7) | collective-permute-done | bytes 193568 | tf_op jit(solution)/shard_map/ppermute | solution.py:608
  31.3 4.2 %attend_other.1 = (bf16[224,576]{1,0:T(8,128)(2,1)S(1)}, bf16[224,512]{1,0:T(8,128)(2,1)S(1)}, bf16[4,224,896]{2,1,0:T(8,128)(2,1)S(1)}, f32[4,8,896]{2,1,0:T(8,128)S(1)}) custom-call(bf16[56,576]{1,0:T(8,128)(2,1)S(1)} %collective-permute-done.6.refs_0_, bf16[168,576]{1,0:T(8,128)(2,1)S(1)} %collective-permute-done.7.refs_1_, ...), custom_call_target="tpu_custom_call" | custom-call | tf_op jit(solution)/shard_map/attend_other/pallas_call | solution.py:325
  35.5 1.0 %collective-permute-start.8 = (bf16[224,576]{1,0:T(8,128)(2,1)S(1)}, bf16[224,576]{1,0:T(8,128)(2,1)S(1)}, u32[]{:S(2)}, u32[]{:S(2)}) collective-permute-start(bf16[224,576]{1,0:T(8,128)(2,1)S(1)} %get-tuple-element.85), channel_id=1, source_target_pairs={{0,2},{2,0},{4,6},{6,4},{8,10},{10,8},{12,14},{14,12},{1,3},{3,1},... | collective-permute-start | bytes 774152 | tf_op jit(solution)/shard_map/ppermute | solution.py:608
  36.6 3.3 %attend_same.1 = (bf16[224,576]{1,0:T(8,128)(2,1)S(1)}, bf16[896,512]{1,0:T(8,128)(2,1)S(1)}) custom-call(f32[4,224,896]{2,1,0:T(8,128)S(1)} %get-tuple-element.76.refs_0_, f32[4,224,896]{2,1,0:T(8,128)S(1)} %get-tuple-element.77.refs_1_, bf16[224,512]{1,0:T(8,128)(2,1)S(1)} %get-tuple-element.78.refs_2_, ...), custom_call_target="tpu_custom_call" | custom-call | tf_op jit(solution)/shard_map/attend_same/pallas_call | solution.py:355
  39.9 2.6 %collective-permute-done.8 = bf16[224,576]{1,0:T(8,128)(2,1)S(1)} collective-permute-done((bf16[224,576]{1,0:T(8,128)(2,1)S(1)}, bf16[224,576]{1,0:T(8,128)(2,1)S(1)}, u32[]{:S(2)}, u32[]{:S(2)}) %collective-permute-start.8) | collective-permute-done | bytes 258080 | tf_op jit(solution)/shard_map/ppermute | solution.py:608
  42.5 0.1 fusion.5
  42.6 1.6 %collective-permute-start.11 = (bf16[56,576]{1,0:T(8,128)(2,1)S(1)}, bf16[56,576]{1,0:T(8,128)(2,1)S(1)}, u32[]{:S(2)}, u32[]{:S(2)}) collective-permute-start(bf16[56,576]{1,0:T(8,128)(2,1)S(1)} %get-tuple-element.127), channel_id=1, source_target_pairs={{0,12},{2,14},{4,8},{6,10},{8,4},{10,6},{12,0},{14,2},{1,13},{3,15... | collective-permute-start | bytes 193544 | tf_op jit(solution)/shard_map/ppermute | solution.py:608
  44.2 2.8 %collective-permute-start.9 = (bf16[56,576]{1,0:T(8,128)(2,1)S(1)}, bf16[56,576]{1,0:T(8,128)(2,1)S(1)}, u32[]{:S(2)}, u32[]{:S(2)}) collective-permute-start(bf16[56,576]{1,0:T(8,128)(2,1)S(1)} %get-tuple-element.129), channel_id=1, source_target_pairs={{0,4},{2,6},{4,0},{6,2},{8,12},{10,14},{12,8},{14,10},{1,5},{3,7},... | collective-permute-start | bytes 193544 | tf_op jit(solution)/shard_map/ppermute | solution.py:608
  47.0 1.9 %query_side.1 = (bf16[896,288]{1,0:T(8,128)(2,1)S(1)}, f32[288,384]{1,0:T(8,128)S(1)}, bf16[288,384]{1,0:T(8,128)(2,1)S(1)}) custom-call(s32[2]{0:T(128)S(1)} %pad_add_fusion.place, bf16[896,512]{1,0:T(8,128)(2,1)S(1)} %get-tuple-element.86.query_pad, bf16[576,896]{1,0:T(8,128)(2,1)S(1)} %get-tuple-element.87.tokens_t), custom_call_target="tpu_custom_call" | custom-call | tf_op jit(solution)/shard_map/query_side/pallas_call | solution.py:399
  49.0 0.8 collective-permute-start.15
  49.8 0.5 collective-permute-done.10
  50.4 0.8 collective-permute-start.13
  51.2 3.1 %collective-permute-start.12 = (bf16[56,576]{1,0:T(8,128)(2,1)S(1)}, bf16[56,576]{1,0:T(8,128)(2,1)S(1)}, u32[]{:S(2)}, u32[]{:S(2)}) collective-permute-start(bf16[56,576]{1,0:T(8,128)(2,1)S(1)} %fusion.2.swapped), channel_id=1, source_target_pairs={{0,4},{4,8},{6,2},{8,12},{10,6},{14,10},{1,5},{5,9},{7,3},{9,13},{... | collective-permute-start | bytes 193544 | tf_op jit(solution)/shard_map/ppermute | solution.py:608
  54.3 1.4 %collective-permute-done.13.mine = bf16[56,576]{1,0:T(8,128)(2,1)S(1)} collective-permute-done((bf16[56,576]{1,0:T(8,128)(2,1)S(1)}, bf16[56,576]{1,0:T(8,128)(2,1)S(1)}, u32[]{:S(2)}, u32[]{:S(2)}) %collective-permute-start.13) | collective-permute-done | bytes 64544 | tf_op jit(solution)/shard_map/ppermute | solution.py:608
  55.8 0.3 collective-permute-done.12.beside
  56.1 3.0 %pull_back.1 = (f32[312,640]{1,0:T(8,128)S(1)}, bf16[312,640]{1,0:T(8,128)(2,1)S(1)}, bf16[896,576]{1,0:T(8,128)(2,1)S(1)}) custom-call(s32[2]{0:T(128)S(1)} %pad_add_fusion.place, bf16[56,576]{1,0:T(8,128)(2,1)S(1)} %collective-permute-done.13.mine, bf16[56,576]{1,0:T(8,128)(2,1)S(1)} %fusion.2.swapped, bf16[56,576]{1,0:T(8,128)(2,1)S(1)} %collective-permute-done.12.beside, ...), custom_call_target="tpu_custom_call" | custom-call | tf_op jit(solution)/shard_map/pull_back/pallas_call | solution.py:534
  59.1 2.7 %collective-permute-start.14 = (bf16[312,640]{1,0:T(8,128)(2,1)S(1)}, bf16[312,640]{1,0:T(8,128)(2,1)S(1)}, u32[]{:S(2)}, u32[]{:S(2)}) collective-permute-start(bf16[312,640]{1,0:T(8,128)(2,1)S(1)} %get-tuple-element.97), channel_id=1, source_target_pairs={{0,2},{2,0},{4,6},{6,4},{8,10},{10,8},{12,14},{14,12},{1,3},{3,1},... | collective-permute-start | bytes 1198088 | tf_op jit(solution)/shard_map/ppermute | solution.py:608
  61.8 0.1 fusion.7
  61.8 0.9 %collective-permute-start.18 = (bf16[72,384]{1,0:T(8,128)(2,1)S(1)}, bf16[72,384]{1,0:T(8,128)(2,1)S(1)}, u32[]{:S(2)}, u32[]{:S(2)}) collective-permute-start(bf16[72,384]{1,0:T(8,128)(2,1)S(1)} %get-tuple-element.130), channel_id=1, source_target_pairs={{0,12},{2,14},{4,8},{6,10},{8,4},{10,6},{12,0},{14,2},{1,13},{3,15... | collective-permute-start | bytes 165896 | tf_op jit(solution)/shard_map/ppermute | solution.py:608
  62.8 1.6 %collective-permute-start.17 = (bf16[72,384]{1,0:T(8,128)(2,1)S(1)}, bf16[72,384]{1,0:T(8,128)(2,1)S(1)}, u32[]{:S(2)}, u32[]{:S(2)}) collective-permute-start(bf16[72,384]{1,0:T(8,128)(2,1)S(1)} %get-tuple-element.131), channel_id=1, source_target_pairs={{0,8},{2,10},{4,12},{6,14},{8,0},{10,2},{12,4},{14,6},{1,9},{3,11}... | collective-permute-start | bytes 165896 | tf_op jit(solution)/shard_map/ppermute | solution.py:608
  64.4 1.9 %collective-permute-start.16 = (bf16[72,384]{1,0:T(8,128)(2,1)S(1)}, bf16[72,384]{1,0:T(8,128)(2,1)S(1)}, u32[]{:S(2)}, u32[]{:S(2)}) collective-permute-start(bf16[72,384]{1,0:T(8,128)(2,1)S(1)} %get-tuple-element.132), channel_id=1, source_target_pairs={{0,4},{2,6},{4,0},{6,2},{8,12},{10,14},{12,8},{14,10},{1,5},{3,7},... | collective-permute-start | bytes 165896 | tf_op jit(solution)/shard_map/ppermute | solution.py:608
  66.3 6.0 %token_side.1 = (f32[896,288]{1,0:T(8,128)S(1)}, bf16[896,384]{1,0:T(8,128)(2,1)S(1)}) custom-call(s32[2]{0:T(128)S(1)} %pad_add_fusion.place, bf16[896,288]{1,0:T(8,128)(2,1)S(1)} %get-tuple-element.103.query_back, bf16[896,576]{1,0:T(8,128)(2,1)S(1)} %get-tuple-element.104.backs, bf16[3,288,576]{2,1,0:T(8,128)(2,1)S(1)} %bitcast.10), custom_call_target="tpu_custom_call" | custom-call | tf_op jit(solution)/shard_map/token_side/pallas_call | solution.py:512
  72.3 0.1 collective-permute-start.22
  72.5 0.1 fusion.6
  72.7 0.3 collective-permute-start.20
  73.0 1.2 %collective-permute-start.19 = (bf16[96,640]{1,0:T(8,128)(2,1)S(1)}, bf16[96,640]{1,0:T(8,128)(2,1)S(1)}, u32[]{:S(2)}, u32[]{:S(2)}) collective-permute-start(bf16[96,640]{1,0:T(8,128)(2,1)S(1)} %get-tuple-element.134), channel_id=1, source_target_pairs={{0,4},{2,6},{4,0},{6,2},{8,12},{10,14},{12,8},{14,10},{1,5},{3,7},... | collective-permute-start | bytes 368648 | tf_op jit(solution)/shard_map/ppermute | solution.py:608
  74.2 2.9 %collective-permute-start.21 = (bf16[96,640]{1,0:T(8,128)(2,1)S(1)}, bf16[96,640]{1,0:T(8,128)(2,1)S(1)}, u32[]{:S(2)}, u32[]{:S(2)}) collective-permute-start(bf16[96,640]{1,0:T(8,128)(2,1)S(1)} %concatenate.16), channel_id=1, source_target_pairs={{0,12},{2,14},{4,8},{6,10},{8,4},{10,6},{12,0},{14,2},{1,13},{3,15... | collective-permute-start | bytes 368648 | tf_op jit(solution)/shard_map/ppermute | solution.py:608
  77.2 1.0 %add_convert_fusion = bf16[896,288]{1,0:T(8,128)(2,1)} fusion(f32[896,288]{1,0:T(8,128)S(1)} %get-tuple-element.105, bf16[896,384]{1,0:T(8,128)(2,1)S(1)} %collective-permute-done.22), kind=kLoop, calls=%fused_computation | loop fusion | flops 774144 | bytes 2064384 | tf_op jit(solution)/shard_map/convert_element_type | solution.py:702
  78.2 3.9 %collective-permute-done.20.refs_1_ = bf16[96,640]{1,0:T(8,128)(2,1)S(1)} collective-permute-done((bf16[96,640]{1,0:T(8,128)(2,1)S(1)}, bf16[96,640]{1,0:T(8,128)(2,1)S(1)}, u32[]{:S(2)}, u32[]{:S(2)}) %collective-permute-start.20) | collective-permute-done | bytes 122912 | tf_op jit(solution)/shard_map/ppermute | solution.py:608
  82.1 2.3 %collective-permute-done.21.refs_2_ = bf16[96,640]{1,0:T(8,128)(2,1)S(1)} collective-permute-done((bf16[96,640]{1,0:T(8,128)(2,1)S(1)}, bf16[96,640]{1,0:T(8,128)(2,1)S(1)}, u32[]{:S(2)}, u32[]{:S(2)}) %collective-permute-start.21) | collective-permute-done | bytes 122912 | tf_op jit(solution)/shard_map/ppermute | solution.py:608
  84.4 0.9 %finish.1 = (f32[3,72,288]{2,1,0:T(8,128)}, f32[27,2,288]{2,1,0:T(2,128)}) custom-call(f32[72,384]{1,0:T(8,128)S(1)} %fusion.4.query_sum, f32[72,640]{1,0:T(8,128)S(1)} %slice.77.own_sum, f32[24,640]{1,0:T(8,128)S(1)} %slice.78.tail_sum, bf16[96,640]{1,0:T(8,128)(2,1)S(1)} %collective-permute-done.19.refs_0_, ...), custom_call_target="tpu_custom_call" | custom-call | tf_op jit(solution)/shard_map/finish/pallas_call | solution.py:583
  (34 shorter events, 0.3 us)
Async XLA Ops:
  0.6 1.9 %copy-start.1 = (bf16[1,16,56,288]{3,2,1,0:T(8,128)(2,1)S(1)}, bf16[1,16,56,288]{3,2,1,0:T(8,128)(2,1)}, u32[]{:S(2)}) copy-start(bf16[1,16,56,288]{3,2,1,0:T(8,128)(2,1)} %param.5) | copy-start | bytes 1548292
  0.6 3.6 %copy-start = (bf16[3,576,288]{1,2,0:T(8,128)(2,1)S(1)}, bf16[3,576,288]{1,2,0:T(8,128)(2,1)}, u32[]{:S(2)}) copy-start(bf16[3,576,288]{1,2,0:T(8,128)(2,1)} %param.6) | copy-start | bytes 2985988
  0.7 3.6 %copy-start.2 = (f32[2,27,288]{2,0,1:T(2,128)S(1)}, f32[2,27,288]{2,0,1:T(2,128)}, u32[]{:S(2)}) copy-start(f32[2,27,288]{2,0,1:T(2,128)} %param.7) | copy-start | bytes 186628
  2.0 2.3 %collective-permute-start = (bf16[896,384]{1,0:T(8,128)(2,1)S(1)}, bf16[896,384]{1,0:T(8,128)(2,1)S(1)}, u32[]{:S(2)}, u32[]{:S(2)}) collective-permute-start(bf16[896,384]{1,0:T(8,128)(2,1)S(1)} %pad.4.own), channel_id=1, source_target_pairs={{0,1},{1,0},{2,3},{3,2},{4,5},{5,4},{6,7},{7,6},{8,9},{9,8},{10,11... | collective-permute-start | bytes 2064392 | tf_op jit(solution)/shard_map/ppermute | solution.py:612
  6.3 5.5 %collective-permute-start.1 = (bf16[56,576]{1,0:T(8,128)(2,1)S(1)}, bf16[56,576]{1,0:T(8,128)(2,1)S(1)}, u32[]{:S(2)}, u32[]{:S(2)}) collective-permute-start(bf16[56,576]{1,0:T(8,128)(2,1)S(1)} %get-tuple-element.63), channel_id=1, source_target_pairs={{0,2},{2,0},{4,6},{6,4},{8,10},{10,8},{12,14},{14,12},{1,3},{3,1},... | collective-permute-start | bytes 193544 | tf_op jit(solution)/shard_map/ppermute | solution.py:608
  9.3 6.2 %collective-permute-start.2 = (bf16[56,576]{1,0:T(8,128)(2,1)S(1)}, bf16[56,576]{1,0:T(8,128)(2,1)S(1)}, u32[]{:S(2)}, u32[]{:S(2)}) collective-permute-start(bf16[56,576]{1,0:T(8,128)(2,1)S(1)} %get-tuple-element.64), channel_id=1, source_target_pairs={{2,6},{4,0},{6,10},{8,4},{10,14},{12,8},{3,7},{5,1},{7,11},{9,5},{... | collective-permute-start | bytes 193544 | tf_op jit(solution)/shard_map/ppermute | solution.py:608
  15.5 7.2 %collective-permute-start.6 = (bf16[56,576]{1,0:T(8,128)(2,1)S(1)}, bf16[56,576]{1,0:T(8,128)(2,1)S(1)}, u32[]{:S(2)}, u32[]{:S(2)}) collective-permute-start(bf16[56,576]{1,0:T(8,128)(2,1)S(1)} %add_convert_fusion.1.first), channel_id=1, source_target_pairs={{0,2},{2,0},{4,6},{6,4},{8,10},{10,8},{12,14},{14,12},{1,3},{3,1},... | collective-permute-start | bytes 193544 | tf_op jit(solution)/shard_map/ppermute | solution.py:608
  15.6 7.2 %collective-permute-start.5 = (bf16[56,576]{1,0:T(8,128)(2,1)S(1)}, bf16[56,576]{1,0:T(8,128)(2,1)S(1)}, u32[]{:S(2)}, u32[]{:S(2)}) collective-permute-start(bf16[56,576]{1,0:T(8,128)(2,1)S(1)} %add_convert_fusion.1.first), channel_id=1, source_target_pairs={{0,12},{2,14},{4,8},{6,10},{8,4},{10,6},{12,0},{14,2},{1,13},{3,15... | collective-permute-start | bytes 193544 | tf_op jit(solution)/shard_map/ppermute | solution.py:608
  19.7 5.2 %collective-permute-start.4 = (bf16[56,576]{1,0:T(8,128)(2,1)S(1)}, bf16[56,576]{1,0:T(8,128)(2,1)S(1)}, u32[]{:S(2)}, u32[]{:S(2)}) collective-permute-start(bf16[56,576]{1,0:T(8,128)(2,1)S(1)} %add_convert_fusion.1.first), channel_id=1, source_target_pairs={{0,8},{2,10},{4,12},{6,14},{8,0},{10,2},{12,4},{14,6},{1,9},{3,11}... | collective-permute-start | bytes 193544 | tf_op jit(solution)/shard_map/ppermute | solution.py:608
  19.7 5.2 %collective-permute-start.3 = (bf16[56,576]{1,0:T(8,128)(2,1)S(1)}, bf16[56,576]{1,0:T(8,128)(2,1)S(1)}, u32[]{:S(2)}, u32[]{:S(2)}) collective-permute-start(bf16[56,576]{1,0:T(8,128)(2,1)S(1)} %add_convert_fusion.1.first), channel_id=1, source_target_pairs={{0,4},{2,6},{4,0},{6,2},{8,12},{10,14},{12,8},{14,10},{1,5},{3,7},... | collective-permute-start | bytes 193544 | tf_op jit(solution)/shard_map/ppermute | solution.py:608
  25.0 6.3 %collective-permute-start.7 = (bf16[168,576]{1,0:T(8,128)(2,1)S(1)}, bf16[168,576]{1,0:T(8,128)(2,1)S(1)}, u32[]{:S(2)}, u32[]{:S(2)}) collective-permute-start(bf16[168,576]{1,0:T(8,128)(2,1)S(1)} %constant_dynamic-update-slice_fusion.rest), channel_id=1, source_target_pairs={{0,2},{2,0},{4,6},{6,4},{8,10},{10,8},{12,14},{14,12},{1,3},{3,1},... | collective-permute-start | bytes 580616 | tf_op jit(solution)/shard_map/ppermute | solution.py:608
  35.5 6.9 %collective-permute-start.8 = (bf16[224,576]{1,0:T(8,128)(2,1)S(1)}, bf16[224,576]{1,0:T(8,128)(2,1)S(1)}, u32[]{:S(2)}, u32[]{:S(2)}) collective-permute-start(bf16[224,576]{1,0:T(8,128)(2,1)S(1)} %get-tuple-element.85), channel_id=1, source_target_pairs={{0,2},{2,0},{4,6},{6,4},{8,10},{10,8},{12,14},{14,12},{1,3},{3,1},... | collective-permute-start | bytes 774152 | tf_op jit(solution)/shard_map/ppermute | solution.py:608
  42.6 7.2 %collective-permute-start.11 = (bf16[56,576]{1,0:T(8,128)(2,1)S(1)}, bf16[56,576]{1,0:T(8,128)(2,1)S(1)}, u32[]{:S(2)}, u32[]{:S(2)}) collective-permute-start(bf16[56,576]{1,0:T(8,128)(2,1)S(1)} %get-tuple-element.127), channel_id=1, source_target_pairs={{0,12},{2,14},{4,8},{6,10},{8,4},{10,6},{12,0},{14,2},{1,13},{3,15... | collective-permute-start | bytes 193544 | tf_op jit(solution)/shard_map/ppermute | solution.py:608
  44.2 6.1 %collective-permute-start.10 = (bf16[56,576]{1,0:T(8,128)(2,1)S(1)}, bf16[56,576]{1,0:T(8,128)(2,1)S(1)}, u32[]{:S(2)}, u32[]{:S(2)}) collective-permute-start(bf16[56,576]{1,0:T(8,128)(2,1)S(1)} %get-tuple-element.128), channel_id=1, source_target_pairs={{0,8},{2,10},{4,12},{6,14},{8,0},{10,2},{12,4},{14,6},{1,9},{3,11}... | collective-permute-start | bytes 193544 | tf_op jit(solution)/shard_map/ppermute | solution.py:608
  44.2 6.1 %collective-permute-start.9 = (bf16[56,576]{1,0:T(8,128)(2,1)S(1)}, bf16[56,576]{1,0:T(8,128)(2,1)S(1)}, u32[]{:S(2)}, u32[]{:S(2)}) collective-permute-start(bf16[56,576]{1,0:T(8,128)(2,1)S(1)} %get-tuple-element.129), channel_id=1, source_target_pairs={{0,4},{2,6},{4,0},{6,2},{8,12},{10,14},{12,8},{14,10},{1,5},{3,7},... | collective-permute-start | bytes 193544 | tf_op jit(solution)/shard_map/ppermute | solution.py:608
  49.0 10.1 %collective-permute-start.15 = (bf16[288,384]{1,0:T(8,128)(2,1)S(1)}, bf16[288,384]{1,0:T(8,128)(2,1)S(1)}, u32[]{:S(2)}, u32[]{:S(2)}) collective-permute-start(bf16[288,384]{1,0:T(8,128)(2,1)S(1)} %get-tuple-element.99), channel_id=1, source_target_pairs={{0,2},{2,0},{4,6},{6,4},{8,10},{10,8},{12,14},{14,12},{1,3},{3,1},... | collective-permute-start | bytes 663560 | tf_op jit(solution)/shard_map/ppermute | solution.py:608
  50.4 5.4 %collective-permute-start.13 = (bf16[56,576]{1,0:T(8,128)(2,1)S(1)}, bf16[56,576]{1,0:T(8,128)(2,1)S(1)}, u32[]{:S(2)}, u32[]{:S(2)}) collective-permute-start(bf16[56,576]{1,0:T(8,128)(2,1)S(1)} %fusion.2.swapped), channel_id=1, source_target_pairs={{0,2},{2,0},{4,6},{6,4},{8,10},{10,8},{12,14},{14,12},{1,3},{3,1},... | collective-permute-start | bytes 193544 | tf_op jit(solution)/shard_map/ppermute | solution.py:608
  51.2 4.9 %collective-permute-start.12 = (bf16[56,576]{1,0:T(8,128)(2,1)S(1)}, bf16[56,576]{1,0:T(8,128)(2,1)S(1)}, u32[]{:S(2)}, u32[]{:S(2)}) collective-permute-start(bf16[56,576]{1,0:T(8,128)(2,1)S(1)} %fusion.2.swapped), channel_id=1, source_target_pairs={{0,4},{4,8},{6,2},{8,12},{10,6},{14,10},{1,5},{5,9},{7,3},{9,13},{... | collective-permute-start | bytes 193544 | tf_op jit(solution)/shard_map/ppermute | solution.py:608
  59.1 13.4 %collective-permute-start.14 = (bf16[312,640]{1,0:T(8,128)(2,1)S(1)}, bf16[312,640]{1,0:T(8,128)(2,1)S(1)}, u32[]{:S(2)}, u32[]{:S(2)}) collective-permute-start(bf16[312,640]{1,0:T(8,128)(2,1)S(1)} %get-tuple-element.97), channel_id=1, source_target_pairs={{0,2},{2,0},{4,6},{6,4},{8,10},{10,8},{12,14},{14,12},{1,3},{3,1},... | collective-permute-start | bytes 1198088 | tf_op jit(solution)/shard_map/ppermute | solution.py:608
  61.8 10.6 %collective-permute-start.18 = (bf16[72,384]{1,0:T(8,128)(2,1)S(1)}, bf16[72,384]{1,0:T(8,128)(2,1)S(1)}, u32[]{:S(2)}, u32[]{:S(2)}) collective-permute-start(bf16[72,384]{1,0:T(8,128)(2,1)S(1)} %get-tuple-element.130), channel_id=1, source_target_pairs={{0,12},{2,14},{4,8},{6,10},{8,4},{10,6},{12,0},{14,2},{1,13},{3,15... | collective-permute-start | bytes 165896 | tf_op jit(solution)/shard_map/ppermute | solution.py:608
  62.8 9.6 %collective-permute-start.17 = (bf16[72,384]{1,0:T(8,128)(2,1)S(1)}, bf16[72,384]{1,0:T(8,128)(2,1)S(1)}, u32[]{:S(2)}, u32[]{:S(2)}) collective-permute-start(bf16[72,384]{1,0:T(8,128)(2,1)S(1)} %get-tuple-element.131), channel_id=1, source_target_pairs={{0,8},{2,10},{4,12},{6,14},{8,0},{10,2},{12,4},{14,6},{1,9},{3,11}... | collective-permute-start | bytes 165896 | tf_op jit(solution)/shard_map/ppermute | solution.py:608
  64.4 8.0 %collective-permute-start.16 = (bf16[72,384]{1,0:T(8,128)(2,1)S(1)}, bf16[72,384]{1,0:T(8,128)(2,1)S(1)}, u32[]{:S(2)}, u32[]{:S(2)}) collective-permute-start(bf16[72,384]{1,0:T(8,128)(2,1)S(1)} %get-tuple-element.132), channel_id=1, source_target_pairs={{0,4},{2,6},{4,0},{6,2},{8,12},{10,14},{12,8},{14,10},{1,5},{3,7},... | collective-permute-start | bytes 165896 | tf_op jit(solution)/shard_map/ppermute | solution.py:608
  72.3 4.9 %collective-permute-start.22 = (bf16[896,384]{1,0:T(8,128)(2,1)S(1)}, bf16[896,384]{1,0:T(8,128)(2,1)S(1)}, u32[]{:S(2)}, u32[]{:S(2)}) collective-permute-start(bf16[896,384]{1,0:T(8,128)(2,1)S(1)} %get-tuple-element.106), channel_id=1, source_target_pairs={{0,1},{1,0},{2,3},{3,2},{4,5},{5,4},{6,7},{7,6},{8,9},{9,8},{10,11... | collective-permute-start | bytes 2064392 | tf_op jit(solution)/shard_map/ppermute | solution.py:612
  72.7 9.4 %collective-permute-start.20 = (bf16[96,640]{1,0:T(8,128)(2,1)S(1)}, bf16[96,640]{1,0:T(8,128)(2,1)S(1)}, u32[]{:S(2)}, u32[]{:S(2)}) collective-permute-start(bf16[96,640]{1,0:T(8,128)(2,1)S(1)} %get-tuple-element.133), channel_id=1, source_target_pairs={{0,8},{2,10},{4,12},{6,14},{8,0},{10,2},{12,4},{14,6},{1,9},{3,11}... | collective-permute-start | bytes 368648 | tf_op jit(solution)/shard_map/ppermute | solution.py:608
  73.0 9.0 %collective-permute-start.19 = (bf16[96,640]{1,0:T(8,128)(2,1)S(1)}, bf16[96,640]{1,0:T(8,128)(2,1)S(1)}, u32[]{:S(2)}, u32[]{:S(2)}) collective-permute-start(bf16[96,640]{1,0:T(8,128)(2,1)S(1)} %get-tuple-element.134), channel_id=1, source_target_pairs={{0,4},{2,6},{4,0},{6,2},{8,12},{10,14},{12,8},{14,10},{1,5},{3,7},... | collective-permute-start | bytes 368648 | tf_op jit(solution)/shard_map/ppermute | solution.py:608
  74.2 10.2 %collective-permute-start.21 = (bf16[96,640]{1,0:T(8,128)(2,1)S(1)}, bf16[96,640]{1,0:T(8,128)(2,1)S(1)}, u32[]{:S(2)}, u32[]{:S(2)}) collective-permute-start(bf16[96,640]{1,0:T(8,128)(2,1)S(1)} %concatenate.16), channel_id=1, source_target_pairs={{0,12},{2,14},{4,8},{6,10},{8,4},{10,6},{12,0},{14,2},{1,13},{3,15... | collective-permute-start | bytes 368648 | tf_op jit(solution)/shard_map/ppermute | solution.py:608
